TPU v7x, 32 devices: a whole 2x2x4 slice. The times are simulated.
32 devices in a mesh: dp: 16 (over z, x, core), tensor: 2 (over y).
Axes of the slice: x: 2, y: 2, z: 4, core: 2. Of those that a mesh axis runs over, the one named last changes fastest.
Arguments:
- tokens: bfloat16 [10240, 2048], P(('dp', 'tensor')), may hold values from -6 to 6
- cotangent: bfloat16 [10240, 2048], P(('dp', 'tensor')), may hold values from -6 to 6
- cont_ids: int32 [16, 512], P('dp'), may hold values from 0 to 3, never falling along the last dimension, each value on 1 to 256 neighbouring positions
- q_weight: bfloat16 [2048, 2048], P('dp', 'tensor'), may hold values from -0.125 to 0.125
- k_weight: bfloat16 [2048, 2048], P('dp', 'tensor'), may hold values from -0.125 to 0.125
- v_weight: bfloat16 [2048, 2048], P('dp', 'tensor'), may hold values from -0.125 to 0.125
- out_weight: bfloat16 [2048, 2048], P('dp', 'tensor'), may hold values from -0.125 to 0.125
- attn_gain: bfloat16 [2048], P('dp'), may hold values from 0.25 to 1.75
- head_gain: bfloat16 [256, 8], P('dp', 'tensor'), may hold values from 0.25 to 1.75
- lam_q1: bfloat16 [128, 8], P('dp', 'tensor'), may hold values from -1 to 1
- lam_k1: bfloat16 [128, 8], P('dp', 'tensor'), may hold values from -1 to 1
- lam_q2: bfloat16 [128, 8], P('dp', 'tensor'), may hold values from -1 to 1
- lam_k2: bfloat16 [128, 8], P('dp', 'tensor'), may hold values from -1 to 1
- gate_weight: bfloat16 [2048, 5632], P('dp', 'tensor'), may hold values from -0.125 to 0.125
- up_weight: bfloat16 [2048, 5632], P('dp', 'tensor'), may hold values from -0.125 to 0.125
- down_weight: bfloat16 [2048, 5632], P('dp', 'tensor'), may hold values from -0.078125 to 0.078125
- ffn_gain: bfloat16 [2048], P('dp'), may hold values from 0.25 to 1.75
Outputs:
- output: bfloat16 [10240, 2048], P(('dp', 'tensor'))
- tokens_grad: bfloat16 [10240, 2048], P(('dp', 'tensor'))
- grad_q: float32 [2048, 2048], P('dp', 'tensor')
- grad_k: float32 [2048, 2048], P('dp', 'tensor')
- grad_v: float32 [2048, 2048], P('dp', 'tensor')
- grad_out: float32 [2048, 2048], P('dp', 'tensor')
- grad_attn_gain: float32 [2048], P('dp')
- grad_head_gain: float32 [256, 8], P('dp', 'tensor')
- grad_lam_q1: float32 [128, 8], P('dp', 'tensor')
- grad_lam_k1: float32 [128, 8], P('dp', 'tensor')
- grad_lam_q2: float32 [128, 8], P('dp', 'tensor')
- grad_lam_k2: float32 [128, 8], P('dp', 'tensor')
- grad_gate: float32 [2048, 5632], P('dp', 'tensor')
- grad_up: float32 [2048, 5632], P('dp', 'tensor')
- grad_down: float32 [2048, 5632], P('dp', 'tensor')
- grad_ffn_gain: float32 [2048], P('dp')
Inputs may be any that keep to these rules, and one draw needn't show every extreme that they name: `cont_ids`: in each row the ids never fall; each of the 4 continuations holds 1 to 256 tokens, and one continuation of each row holds exactly 256.
All inputs are finite; a program needn't handle non-finite values.
Results may differ from a plain program's by a relative error of at most 0.01345.
The roundings to bfloat16 on the way count: a program that leaves them out, or rounds other values in their place, can miss the bound.
Values may be sent and summed in bfloat16 or wider, within the bound.
No kernel may reach another device: no remote copies, remote signals or barrier semaphores. Data moves between devices by JAX's collectives and lax.ppermute only.
A program may use at most 320 MiB of HBM per device.

v0:
```python
import jax
import jax.numpy as jnp
from jax import lax
from jax.sharding import PartitionSpec as P

D = 2048
DK = 128
DV = 256


norm_eps = 1e-06
head_eps = 1e-05
lambda_init = 0.2
masked_value = -1e30


def shortened(array):

    def short(part):
        return part.astype(jnp.bfloat16) if part.dtype == jnp.float32 else part

    return jax.tree.map(short, array)


def fetch(weight_list):
    return jax.tree.map(
        lambda part, own: part.astype(own.dtype),
        lax.all_gather(shortened(weight_list), "dp", axis=0, tiled=True),
        weight_list,
    )


def rows_in(row_values):
    return lax.all_gather(row_values, "tensor", axis=0, tiled=True)


def rows_out(term_fn, local_rows):
    return lax.psum_scatter(
        term_fn(jnp.int32(0), local_rows * lax.axis_size("tensor")),
        "tensor",
        scatter_dimension=0,
        tiled=True,
    )


def gains_total(gain_parts):
    return lax.psum((gain_parts[0], gain_parts[1]), "tensor")


def reduce_grads(grad_list):
    return (
        lax.psum_scatter(grad_list[0], "dp", scatter_dimension=0, tiled=True),
        lax.psum_scatter(grad_list[1], "dp", scatter_dimension=0, tiled=True),
        lax.psum_scatter(grad_list[2], "dp", scatter_dimension=0, tiled=True),
        lax.psum_scatter(grad_list[3], "dp", scatter_dimension=0, tiled=True),
        lax.psum_scatter(grad_list[4], "dp", scatter_dimension=0, tiled=True),
        lax.psum_scatter(grad_list[5], "dp", scatter_dimension=0, tiled=True),
        lax.psum_scatter(grad_list[6], "dp", scatter_dimension=0, tiled=True),
        lax.psum_scatter(grad_list[7], "dp", scatter_dimension=0, tiled=True),
        lax.psum_scatter(grad_list[8], "dp", scatter_dimension=0, tiled=True),
        lax.psum_scatter(grad_list[9], "dp", scatter_dimension=0, tiled=True),
        lax.psum_scatter(grad_list[10], "dp", scatter_dimension=0, tiled=True),
        lax.psum_scatter(grad_list[11], "dp", scatter_dimension=0, tiled=True),
        lax.psum_scatter(grad_list[12], "dp", scatter_dimension=0, tiled=True),
        lax.psum_scatter(grad_list[13], "dp", scatter_dimension=0, tiled=True),
    )


def inv_rms(entries, eps_value):
    return lax.rsqrt(jnp.mean(entries * entries, axis=-1, keepdims=True) + eps_value)


def norm_back(entries, inverse, gain_row, incoming):
    scaled = gain_row * incoming
    return inverse * scaled - entries * inverse**3 * jnp.mean(
        entries * scaled, axis=-1, keepdims=True
    )


def rows_product(first_arg, second_arg):
    return lax.dot_general(
        first_arg, second_arg, (((0,), (0,)), ((), ())), preferred_element_type=jnp.float32
    )


def cols_product(first_arg, second_arg):
    return lax.dot_general(
        first_arg, second_arg, (((1,), (1,)), ((), ())), preferred_element_type=jnp.float32
    )


def key_mask(block_rows, prompt_part, prompt_len, cont_row_ids, block_index):
    row_index = lax.broadcasted_iota(jnp.int32, (block_rows, 1), 0)
    prompt_key = lax.broadcasted_iota(jnp.int32, (1, prompt_len), 1)
    position = block_index * prompt_part + row_index
    prompt_cols = jnp.where(row_index < prompt_part, prompt_key <= position, True)
    cont_len = cont_row_ids.shape[0]
    cont_key = lax.broadcasted_iota(jnp.int32, (1, cont_len), 1)
    row_ids = jnp.concatenate([jnp.full((prompt_part,), -1, jnp.int32), cont_row_ids])[:, None]
    cont_cols = (row_ids == cont_row_ids[None, :]) & (cont_key <= row_index - prompt_part)
    return jnp.concatenate([prompt_cols, cont_cols], axis=1)


def head_scores(query_head, key_head, allowed, score_scale):
    scores = (
        jnp.einsum("qcd,kcd->cqk", query_head, key_head, preferred_element_type=jnp.float32)
        * score_scale
    )
    return jnp.where(allowed[None], scores, masked_value)


def head_forward(query_head, key_head, value_head, lam_head, allowed, score_scale):
    scores = head_scores(query_head, key_head, allowed, score_scale)
    row_top = jnp.max(scores, axis=-1, keepdims=True)
    exp_terms = jnp.exp(scores - row_top)
    row_total = jnp.sum(exp_terms, axis=-1, keepdims=True)
    weights = exp_terms / row_total
    mixed_map = (weights[0] - lam_head * weights[1]).astype(jnp.bfloat16)
    heads_out = jnp.dot(mixed_map, value_head, preferred_element_type=jnp.float32)
    return (heads_out, (row_top + jnp.log(row_total))[:, :, 0])


def head_backward(
    query_head, key_head, value_head, lam_head, lse_head, grad_head, allowed, score_scale
):
    scores = head_scores(query_head, key_head, allowed, score_scale)
    weights = jnp.exp(scores - lse_head[:, :, None])
    mixed_map = (weights[0] - lam_head * weights[1]).astype(jnp.bfloat16)
    mixed_grad = cols_product(grad_head, value_head)
    value_grad = rows_product(mixed_map, grad_head)
    lam_grad = -jnp.sum(weights[1] * mixed_grad)
    first_grad = weights[0] * (
        mixed_grad - jnp.sum(mixed_grad * weights[0], axis=-1, keepdims=True)
    )
    second_in = -lam_head * mixed_grad
    second_grad = weights[1] * (second_in - jnp.sum(second_in * weights[1], axis=-1, keepdims=True))
    score_grad = jnp.stack([first_grad, second_grad]).astype(jnp.bfloat16)
    query_grad = (
        jnp.einsum("cqk,kcd->qcd", score_grad, key_head, preferred_element_type=jnp.float32)
        * score_scale
    )
    key_grad = (
        jnp.einsum("cqk,qcd->kcd", score_grad, query_head, preferred_element_type=jnp.float32)
        * score_scale
    )
    return (query_grad, key_grad, value_grad, lam_grad)


def attn_unpack(fetched, heads_here):
    return (
        fetched[0].reshape(D, heads_here, 2, DK),
        fetched[1].reshape(D, heads_here, 2, DK),
        fetched[2].reshape(D, heads_here, DV),
        fetched[3],
    )


def per_device(
    tokens,
    cotangent,
    cont_ids,
    q_weight,
    k_weight,
    v_weight,
    out_weight,
    attn_gain,
    head_gain,
    lam_q1,
    lam_k1,
    lam_q2,
    lam_k2,
    gate_weight,
    up_weight,
    down_weight,
    ffn_gain,
):
    local_rows = tokens.shape[0]
    block_rows = local_rows * lax.axis_size("tensor")
    row_ids = cont_ids[0]
    prompt_part = block_rows - row_ids.shape[0]
    prompt_len = prompt_part * lax.axis_size("dp")
    block_index = lax.axis_index("dp")
    score_scale = DK ** (-0.5)
    heads_here = q_weight.shape[1] // (2 * DK)
    allowed = key_mask(block_rows, prompt_part, prompt_len, row_ids, block_index)
    attn_fetched = fetch(
        (
            q_weight,
            k_weight,
            v_weight,
            out_weight,
            attn_gain,
            head_gain,
            lam_q1,
            lam_k1,
            lam_q2,
            lam_k2,
        )
    )
    q_four, k_four, v_three, out_full = attn_unpack(attn_fetched, heads_here)
    attn_gain_row = attn_fetched[4].astype(jnp.float32)
    head_gain_rows = attn_fetched[5].astype(jnp.float32).T[:, None, :]
    query_lam_one = attn_fetched[6].astype(jnp.float32)
    key_lam_one = attn_fetched[7].astype(jnp.float32)
    query_lam_two = attn_fetched[8].astype(jnp.float32)
    key_lam_two = attn_fetched[9].astype(jnp.float32)
    first_exp = jnp.exp(jnp.sum(query_lam_one * key_lam_one, axis=0))
    second_exp = jnp.exp(jnp.sum(query_lam_two * key_lam_two, axis=0))
    lam_vec = first_exp - second_exp + lambda_init
    tokens_f32 = tokens.astype(jnp.float32)
    inv_first = inv_rms(tokens_f32, norm_eps)
    normed = rows_in((tokens_f32 * inv_first * attn_gain_row).astype(jnp.bfloat16))
    queries = jnp.einsum(
        "re,ehcd->hrcd", normed, q_four, preferred_element_type=jnp.float32
    ).astype(jnp.bfloat16)
    keys_here = jnp.einsum(
        "re,ehcd->hrcd", normed, k_four, preferred_element_type=jnp.float32
    ).astype(jnp.bfloat16)
    values_here = jnp.einsum(
        "re,ehd->hrd", normed, v_three, preferred_element_type=jnp.float32
    ).astype(jnp.bfloat16)
    prompt_keys, prompt_values = (
        lax.all_gather(keys_here[:, :prompt_part], "dp", axis=1, tiled=True),
        lax.all_gather(values_here[:, :prompt_part], "dp", axis=1, tiled=True),
    )
    key_block = jnp.concatenate([prompt_keys, keys_here[:, prompt_part:]], axis=1)
    value_block = jnp.concatenate([prompt_values, values_here[:, prompt_part:]], axis=1)

    def forward_head(pieces):
        return head_forward(pieces[0], pieces[1], pieces[2], pieces[3], allowed, score_scale)

    heads_out, head_lse = lax.map(forward_head, (queries, key_block, value_block, lam_vec))
    head_inv = inv_rms(heads_out, head_eps)
    attn_vec = jnp.transpose(heads_out * head_inv * head_gain_rows * (1.0 - lambda_init), (1, 0, 2))
    attn_vec = attn_vec.reshape(block_rows, heads_here * DV).astype(jnp.bfloat16)

    def project_out(first_row, row_count):
        return cols_product(attn_vec, out_full)

    residual = tokens_f32 + rows_out(project_out, local_rows)
    ffn_fetched = fetch((gate_weight, up_weight, down_weight, ffn_gain))
    gate_full, up_full, down_full = (ffn_fetched[0], ffn_fetched[1], ffn_fetched[2])
    ffn_gain_row = ffn_fetched[3].astype(jnp.float32)
    inv_second = inv_rms(residual, norm_eps)
    ffn_in = rows_in((residual * inv_second * ffn_gain_row).astype(jnp.bfloat16))
    gate_proj = jnp.dot(ffn_in, gate_full, preferred_element_type=jnp.float32)
    up_proj = jnp.dot(ffn_in, up_full, preferred_element_type=jnp.float32)
    gate_sigmoid = jax.nn.sigmoid(gate_proj)
    hidden = (gate_proj * gate_sigmoid * up_proj).astype(jnp.bfloat16)

    def project_down(first_row, row_count):
        return cols_product(hidden, down_full)

    output = (residual + rows_out(project_down, local_rows)).astype(jnp.bfloat16)
    cot_rows = rows_in(cotangent)
    hidden_grad = jnp.dot(cot_rows, down_full, preferred_element_type=jnp.float32)
    grad_down = rows_product(cot_rows, hidden)
    gate_grad = (
        hidden_grad * up_proj * gate_sigmoid * (1.0 + gate_proj * (1.0 - gate_sigmoid))
    ).astype(jnp.bfloat16)
    up_grad = (hidden_grad * gate_proj * gate_sigmoid).astype(jnp.bfloat16)
    grad_gate = rows_product(ffn_in, gate_grad)
    grad_up = rows_product(ffn_in, up_grad)

    def back_ffn(first_row, row_count):
        return cols_product(gate_grad, gate_full) + cols_product(up_grad, up_full)

    ffn_in_grad = rows_out(back_ffn, local_rows)
    residual_grad = cotangent.astype(jnp.float32) + norm_back(
        residual, inv_second, ffn_gain_row, ffn_in_grad
    )
    ffn_gain_part = jnp.sum(ffn_in_grad * residual * inv_second, axis=0)
    branch_grad = rows_in(residual_grad.astype(jnp.bfloat16))
    vec_grad = jnp.dot(branch_grad, out_full, preferred_element_type=jnp.float32)
    grad_out = rows_product(branch_grad, attn_vec)
    vec_heads = jnp.transpose(vec_grad.reshape(block_rows, heads_here, DV), (1, 0, 2))
    scaled_grad = vec_heads * head_gain_rows * (1.0 - lambda_init)
    heads_grad = (
        head_inv * scaled_grad
        - heads_out * head_inv**3 * jnp.mean(heads_out * scaled_grad, axis=-1, keepdims=True)
    ).astype(jnp.bfloat16)
    grad_head_gain = jnp.sum(vec_heads * heads_out * head_inv * (1.0 - lambda_init), axis=1).T

    def backward_head(pieces):
        return head_backward(
            pieces[0], pieces[1], pieces[2], pieces[3], pieces[4], pieces[5], allowed, score_scale
        )

    queries_grad, keys_grad, values_grad, lam_grad = lax.map(
        backward_head, (queries, key_block, value_block, lam_vec, head_lse, heads_grad)
    )
    prompt_key_sum, prompt_value_sum = (
        lax.psum_scatter(keys_grad[:, :prompt_len], "dp", scatter_dimension=1, tiled=True),
        lax.psum_scatter(values_grad[:, :prompt_len], "dp", scatter_dimension=1, tiled=True),
    )
    keys_grad_here = jnp.concatenate([prompt_key_sum, keys_grad[:, prompt_len:]], axis=1).astype(
        jnp.bfloat16
    )
    values_grad_here = jnp.concatenate(
        [prompt_value_sum, values_grad[:, prompt_len:]], axis=1
    ).astype(jnp.bfloat16)
    queries_grad = queries_grad.astype(jnp.bfloat16)
    grad_q = jnp.einsum(
        "re,hrcd->ehcd", normed, queries_grad, preferred_element_type=jnp.float32
    ).reshape(D, -1)
    grad_k = jnp.einsum(
        "re,hrcd->ehcd", normed, keys_grad_here, preferred_element_type=jnp.float32
    ).reshape(D, -1)
    grad_v = jnp.einsum(
        "re,hrd->ehd", normed, values_grad_here, preferred_element_type=jnp.float32
    ).reshape(D, -1)
    grad_query_lam_one = lam_grad * first_exp * key_lam_one
    grad_key_lam_one = lam_grad * first_exp * query_lam_one
    grad_query_lam_two = -lam_grad * second_exp * key_lam_two
    grad_key_lam_two = -lam_grad * second_exp * query_lam_two

    def back_attn(first_row, row_count):
        return (
            jnp.einsum("hrcd,ehcd->re", queries_grad, q_four, preferred_element_type=jnp.float32)
            + jnp.einsum(
                "hrcd,ehcd->re", keys_grad_here, k_four, preferred_element_type=jnp.float32
            )
            + jnp.einsum(
                "hrd,ehd->re", values_grad_here, v_three, preferred_element_type=jnp.float32
            )
        )

    normed_grad = rows_out(back_attn, local_rows)
    tokens_grad = (
        residual_grad + norm_back(tokens_f32, inv_first, attn_gain_row, normed_grad)
    ).astype(jnp.bfloat16)
    attn_gain_part = jnp.sum(normed_grad * tokens_f32 * inv_first, axis=0)
    attn_gain_sum, ffn_gain_sum = gains_total((attn_gain_part, ffn_gain_part))
    grads_all = reduce_grads(
        (
            grad_q,
            grad_k,
            grad_v,
            grad_out,
            attn_gain_sum,
            grad_head_gain,
            grad_query_lam_one,
            grad_key_lam_one,
            grad_query_lam_two,
            grad_key_lam_two,
            grad_gate,
            grad_up,
            grad_down,
            ffn_gain_sum,
        )
    )
    attn_grads = grads_all[:10]
    ffn_grads = grads_all[10:]
    return (
        output,
        tokens_grad,
        attn_grads[0],
        attn_grads[1],
        attn_grads[2],
        attn_grads[3],
        attn_grads[4],
        attn_grads[5],
        attn_grads[6],
        attn_grads[7],
        attn_grads[8],
        attn_grads[9],
        ffn_grads[0],
        ffn_grads[1],
        ffn_grads[2],
        ffn_grads[3],
    )


def solution(mesh):
    placed = (
        P(("dp", "tensor"), None),
        P(("dp", "tensor"), None),
        P("dp", None),
        P("dp", "tensor"),
        P("dp", "tensor"),
        P("dp", "tensor"),
        P("dp", "tensor"),
        P("dp"),
        P("dp", "tensor"),
        P("dp", "tensor"),
        P("dp", "tensor"),
        P("dp", "tensor"),
        P("dp", "tensor"),
        P("dp", "tensor"),
        P("dp", "tensor"),
        P("dp", "tensor"),
        P("dp"),
    )
    return jax.shard_map(
        per_device,
        mesh=mesh,
        in_specs=placed,
        out_specs=(
            P(("dp", "tensor"), None),
            P(("dp", "tensor"), None),
            P("dp", "tensor"),
            P("dp", "tensor"),
            P("dp", "tensor"),
            P("dp", "tensor"),
            P("dp"),
            P("dp", "tensor"),
            P("dp", "tensor"),
            P("dp", "tensor"),
            P("dp", "tensor"),
            P("dp", "tensor"),
            P("dp", "tensor"),
            P("dp", "tensor"),
            P("dp", "tensor"),
            P("dp"),
        ),
        check_vma=False,
    )
```

profile of v0, /device:TPU:0, one launch (start us, length us, event | category | flops | bytes accessed | tf_op | source)
XLA Modules:
  0.0 2810.8 jit_solution(15380109284307870582)
XLA Ops:
  7.2 23.1 all-gather
  38.9 33.6 %all-gather.21.cloned.1.call-done = bf16[640,2048]{1,0:T(8,128)(2,1)} async-done(((bf16[320,2048]{1,0:T(8,128)(2,1)}), bf16[640,2048]{1,0:T(8,128)(2,1)}) %all-gather.21.cloned.1.call-update) | async-done | bytes 2621456 | tf_op jit(solution)/shard_map/all_gather | solution.py:34
  72.6 56.0 %all-gather.25.cloned.1.call-done = bf16[2048,1024]{0,1:T(8,128)(2,1)} async-done(((bf16[128,1024]{0,1:T(8,128)(2,1)}), bf16[2048,1024]{0,1:T(8,128)(2,1)}) %all-gather.25.cloned.1.call-update) | async-done | bytes 4194320 | tf_op jit(solution)/shard_map/all_gather | solution.py:28
  135.9 46.8 %all-gather.29.cloned.1.call-done = bf16[2048,1024]{0,1:T(8,128)(2,1)} async-done(((bf16[128,1024]{0,1:T(8,128)(2,1)}), bf16[2048,1024]{0,1:T(8,128)(2,1)}) %all-gather.29.cloned.1.call-update) | async-done | bytes 4194320 | tf_op jit(solution)/shard_map/all_gather | solution.py:28
  190.4 18.7 all-gather.3
  209.4 17.7 all-gather.4
  227.4 18.7 all-gather.1
  246.4 17.6 all-gather.2
  264.2 18.8 all-gather.5
  300.0 40.2 %all-gather.31.cloned.1.call-done = bf16[4,2048,256]{2,1,0:T(8,128)(2,1)} async-done(((bf16[4,128,256]{2,1,0:T(8,128)(2,1)}), bf16[4,2048,256]{2,1,0:T(8,128)(2,1)}) %all-gather.31.cloned.1.call-update) | async-done | bytes 4194320 | tf_op jit(solution)/shard_map/all_gather | solution.py:224
  344.9 119.4 %while.28 = (s32[]{:T(128)}, f32[4,640,256]{2,1,0:T(8,128)}, f32[4,2,640]{2,1,0:T(2,128)}, pred[640,2560]{1,0:T(8,128)(4,1)S(1)}, bf16[4,640,2,128]{3,1,2,0:T(8,...) while((s32[]{:T(128)}, f32[4,640,256]{2,1,0:T(8,128)}, ...), condition=%wide.region_6.7_spmd, body=%wide.region_3.6_spmd.sunk | while | flops 1718680320 | bytes 74099312 | solution.py:232
  464.4 14.8 copy.125
  491.2 18.2 all-gather.6
  509.5 44.9 %reduce-scatter.21.cloned.1.call-done = f32[320,2048]{1,0:T(8,128)} async-done(((f32[640,2048]{1,0:T(8,128)}), f32[320,2048]{1,0:T(8,128)}) %reduce-scatter.21.cloned.1.call-update) | async-done | bytes 2621456 | tf_op jit(solution)/shard_map/reduce_scatter | solution.py:38
  560.4 90.9 %all-gather.37.cloned.1.call-done = bf16[2048,2816]{1,0:T(8,128)(2,1)} async-done(((bf16[128,2816]{1,0:T(8,128)(2,1)}), bf16[2048,2816]{1,0:T(8,128)(2,1)}) %all-gather.37.cloned.1.call-update) | async-done | bytes 11534352 | tf_op jit(solution)/shard_map/all_gather | solution.py:28
  651.3 39.3 %all-gather.35.cloned.1.call-done = bf16[640,2048]{1,0:T(8,128)(2,1)} async-done(((bf16[320,2048]{1,0:T(8,128)(2,1)}), bf16[640,2048]{1,0:T(8,128)(2,1)}) %all-gather.35.cloned.1.call-update) | async-done | bytes 2621456 | tf_op jit(solution)/shard_map/all_gather | solution.py:34
  690.5 13.8 fusion.121
  704.3 83.1 %all-gather.39.cloned.1.call-done = bf16[2048,2816]{1,0:T(8,128)(2,1)} async-done(((bf16[128,2816]{1,0:T(8,128)(2,1)}), bf16[2048,2816]{1,0:T(8,128)(2,1)}) %all-gather.39.cloned.1.call-update) | async-done | bytes 11534352 | tf_op jit(solution)/shard_map/all_gather | solution.py:28
  787.4 13.7 fusion.122
  801.2 25.0 all-gather.43.cloned.1.call-done
  826.1 96.9 %all-gather.41.cloned.1.call-done = bf16[2048,2816]{1,0:T(8,128)(2,1)} async-done(((bf16[128,2816]{1,0:T(8,128)(2,1)}), bf16[2048,2816]{1,0:T(8,128)(2,1)}) %all-gather.41.cloned.1.call-update) | async-done | bytes 11534352 | tf_op jit(solution)/shard_map/all_gather | solution.py:28
  923.0 19.2 multiply_convert_fusion
  942.3 14.4 fusion.124
  956.6 11.5 convolution_add_fusion
  968.2 13.1 fusion.123
  981.4 50.8 %reduce-scatter.25.cloned.1.call-done = f32[320,2048]{1,0:T(8,128)} async-done(((f32[640,2048]{1,0:T(8,128)}), f32[320,2048]{1,0:T(8,128)}) %reduce-scatter.25.cloned.1.call-update) | async-done | bytes 2621456 | tf_op jit(solution)/shard_map/reduce_scatter | solution.py:38
  1035.2 64.8 %reduce-scatter.23.cloned.1.call-done = f32[320,2048]{1,0:T(8,128)} async-done(((f32[640,2048]{1,0:T(8,128)}), f32[320,2048]{1,0:T(8,128)}) %reduce-scatter.23.cloned.1.call-update) | async-done | bytes 2621456 | tf_op jit(solution)/shard_map/reduce_scatter | solution.py:38
  1106.4 39.1 %all-gather.45.cloned.1.call-done = bf16[640,2048]{1,0:T(8,128)(2,1)} async-done(((bf16[320,2048]{1,0:T(8,128)(2,1)}), bf16[640,2048]{1,0:T(8,128)(2,1)}) %all-gather.45.cloned.1.call-update) | async-done | bytes 2621456 | tf_op jit(solution)/shard_map/all_gather | solution.py:34
  1155.1 173.8 %while.29 = (s32[]{:T(128)}, bf16[4,640,2,128]{1,3,2,0:T(8,128)(2,1)}, f32[4,2560,2,128]{3,1,0,2:T(8,128)}, f32[4,2560,256]{2,1,0:T(8,128)}, f32[4]{0:T(128)S(1)...) while((s32[]{:T(128)}, ...), condition=%wide.region_18.19_spmd, body=%wide.region_14.18_spmd.sunk | while | flops 4239358720 | bytes 167475456 | solution.py:289
  1156.0 9.8 subtract_exponential_fusion.3
  1199.3 9.8 subtract_exponential_fusion.3
  1242.7 9.8 subtract_exponential_fusion.3
  1286.1 9.8 subtract_exponential_fusion.3
  1345.7 14.8 convolution_bitcast_fusion.1
  1370.5 70.5 %reduce-scatter.27.cloned.1.call-done = f32[4,128,2,128]{3,1,0,2:T(8,128)} async-done(((f32[4,2048,2,128]{3,1,0,2:T(8,128)}), f32[4,128,2,128]{3,1,0,2:T(8,128)}) %reduce-scatter.27.cloned.1.call-update) | async-done | bytes 524304 | tf_op jit(solution)/shard_map/reduce_scatter | solution.py:293
  1442.2 107.8 %reduce-scatter.29.cloned.1.call-done = f32[4,128,256]{2,1,0:T(8,128)} async-done(((f32[4,2048,256]{2,1,0:T(8,128)}), f32[4,128,256]{2,1,0:T(8,128)}) %reduce-scatter.29.cloned.1.call-update) | async-done | bytes 524304 | tf_op jit(solution)/shard_map/reduce_scatter | solution.py:294
  1578.7 16.5 fusion.127
  1595.3 16.1 fusion.128
  1630.4 10.4 copy.141
  1644.9 194.3 %reduce-scatter.45.cloned.1.call-done = f32[128,2816]{0,1:T(8,128)} async-done(((f32[2048,2816]{0,1:T(8,128)}), f32[128,2816]{0,1:T(8,128)}) %reduce-scatter.45.cloned.1.call-update) | async-done | bytes 1441808 | tf_op jit(solution)/shard_map/reduce_scatter | solution.py:64
  1842.1 64.3 %reduce-scatter.31.cloned.1.call-done = f32[320,2048]{1,0:T(8,128)} async-done(((f32[640,2048]{1,0:T(8,128)}), f32[320,2048]{1,0:T(8,128)}) %reduce-scatter.31.cloned.1.call-update) | async-done | bytes 2621456 | tf_op jit(solution)/shard_map/reduce_scatter | solution.py:38
  1908.9 63.1 %all-reduce.7 = (f32[2048]{0:T(1024)S(1)}, f32[128,4]{0,1:T(4,128)S(1)}, f32[128,4]{0,1:T(4,128)S(1)}, f32[128,4]{0,1:T(4,128)S(1)}, f32[128,4]{0,1:T(4,128)S(1)}, /*index=5*/f32[2048]{0:T(1024)S(1)}) all-reduce(f32[2048]{0:T(1024)S(1)} %get-tuple-element.235, ...), channel_id=12, replica_groups=mesh['dp'=16,'tensor'=2] {'dp'}, use_global_device_ids=true, to_apply=%region_29.30.clone | all-reduce | flops 6144 | bytes 49152
  1984.6 31.2 %reduce-scatter.33.cloned.1.call-done = f32[128,1024]{1,0:T(8,128)} async-done(((f32[2048,1024]{1,0:T(8,128)}), f32[128,1024]{1,0:T(8,128)}) %reduce-scatter.33.cloned.1.call-update) | async-done | bytes 524304 | tf_op jit(solution)/shard_map/reduce_scatter | solution.py:52
  2015.8 109.0 %reduce-scatter.39.cloned.1.call-done = f32[128,1024]{1,0:T(8,128)} async-done(((f32[2048,1024]{1,0:T(8,128)}), f32[128,1024]{1,0:T(8,128)}) %reduce-scatter.39.cloned.1.call-update) | async-done | bytes 524304 | tf_op jit(solution)/shard_map/reduce_scatter | solution.py:55
  2124.8 231.1 %reduce-scatter.41.cloned.1.call-done = f32[128,2816]{1,0:T(8,128)} async-done(((f32[2048,2816]{1,0:T(8,128)}), f32[128,2816]{1,0:T(8,128)}) %reduce-scatter.41.cloned.1.call-update) | async-done | bytes 1441808 | tf_op jit(solution)/shard_map/reduce_scatter | solution.py:62
  2355.9 230.7 %reduce-scatter.43.cloned.1.call-done = f32[128,2816]{1,0:T(8,128)} async-done(((f32[2048,2816]{1,0:T(8,128)}), f32[128,2816]{1,0:T(8,128)}) %reduce-scatter.43.cloned.1.call-update) | async-done | bytes 1441808 | tf_op jit(solution)/shard_map/reduce_scatter | solution.py:63
  2586.6 108.3 %reduce-scatter.35.cloned.1.call-done = f32[128,1024]{1,0:T(8,128)} async-done(((f32[2048,1024]{1,0:T(8,128)}), f32[128,1024]{1,0:T(8,128)}) %reduce-scatter.35.cloned.1.call-update) | async-done | bytes 524304 | tf_op jit(solution)/shard_map/reduce_scatter | solution.py:53
  2694.9 108.9 %reduce-scatter.37.cloned.1.call-done = f32[128,1024]{1,0:T(8,128)} async-done(((f32[2048,1024]{1,0:T(8,128)}), f32[128,1024]{1,0:T(8,128)}) %reduce-scatter.37.cloned.1.call-update) | async-done | bytes 524304 | tf_op jit(solution)/shard_map/reduce_scatter | solution.py:54
  (340 shorter events, 427.5 us)
Async XLA Ops:
  7.2 65.4 %all-gather.21.cloned.1.call-start = ((), (), s32[]{:S(2)}) async-start(), calls=%async_computation.14 | async-start | bytes 3932160 | tf_op jit(solution)/shard_map/all_gather | solution.py:34
  36.1 92.4 %all-gather.25.cloned.1.call-start = ((), (), s32[]{:S(2)}) async-start(), calls=%async_computation.16 | async-start | bytes 4456448 | tf_op jit(solution)/shard_map/all_gather | solution.py:28
  37.0 145.7 %all-gather.29.cloned.1.call-start = ((), (), s32[]{:S(2)}) async-start(), calls=%async_computation.18 | async-start | bytes 4456448 | tf_op jit(solution)/shard_map/all_gather | solution.py:28
  37.9 249.7 %all-gather.23.cloned.1.call-start = ((), (), s32[]{:S(2)}) async-start(), calls=%async_computation.15 | async-start | bytes 4456448 | tf_op jit(solution)/shard_map/all_gather | solution.py:28
  38.9 255.7 %all-gather.27.cloned.1.call-start = ((), (), s32[]{:S(2)}) async-start(), calls=%async_computation.17 | async-start | bytes 4456448 | tf_op jit(solution)/shard_map/all_gather | solution.py:223
  135.9 204.3 %all-gather.31.cloned.1.call-start = ((), (), s32[]{:S(2)}) async-start(), calls=%async_computation.19 | async-start | bytes 4456448 | tf_op jit(solution)/shard_map/all_gather | solution.py:224
  182.7 26.7 copy-start.40
  182.7 44.7 %copy-start.41 = (bf16[8,4]{0,1:T(4,128)(2,1)S(1)}, bf16[8,4]{0,1:T(4,128)(2,1)}, u32[]{:S(2)}) copy-start(bf16[8,4]{0,1:T(4,128)(2,1)} %param.30) | copy-start | bytes 196
  182.7 63.7 %copy-start.42 = (bf16[8,4]{0,1:T(4,128)(2,1)S(1)}, bf16[8,4]{0,1:T(4,128)(2,1)}, u32[]{:S(2)}) copy-start(bf16[8,4]{0,1:T(4,128)(2,1)} %param.31) | copy-start | bytes 196
  182.7 81.5 %copy-start.43 = (bf16[16,4]{0,1:T(4,128)(2,1)S(1)}, bf16[16,4]{0,1:T(4,128)(2,1)}, u32[]{:S(2)}) copy-start(bf16[16,4]{0,1:T(4,128)(2,1)} %param.29) | copy-start | bytes 388
  182.7 100.4 %copy-start.34 = (s32[1,512]{1,0:T(1,128)S(1)}, s32[1,512]{1,0:T(1,128)}, u32[]{:S(2)}) copy-start(s32[1,512]{1,0:T(1,128)} %param.23) | copy-start | bytes 6148
  188.7 98.9 %copy-start.8 = (bf16[4,640,256]{2,1,0:T(8,128)(2,1)}, bf16[4,640,256]{2,1,0:T(8,128)(2,1)S(1)}, u32[]{:S(2)}) copy-start(bf16[4,640,256]{2,1,0:T(8,128)(2,1)S(1)} %fusion.106) | copy-start | bytes 3932164
  189.5 293.1 %all-gather.33.cloned.1.call-start = ((), (), s32[]{:S(2)}) async-start(), calls=%async_computation.20 | async-start | bytes 4456448 | tf_op jit(solution)/shard_map/all_gather | solution.py:28
  190.2 364.1 %reduce-scatter.21.cloned.1.call-start = ((), (), s32[]{:S(2)}) async-start(), calls=%async_computation.21 | async-start | bytes 7864320 | tf_op jit(solution)/shard_map/reduce_scatter | solution.py:38
  209.3 75.2 %copy-start.24 = (f32[128,4]{0,1:T(4,128)}, f32[128,4]{0,1:T(4,128)S(1)}, u32[]{:S(2)}) copy-start(f32[128,4]{0,1:T(4,128)S(1)} %reshape.185) | copy-start | bytes 6148
  227.4 57.2 %copy-start.26 = (f32[128,4]{0,1:T(4,128)}, f32[128,4]{0,1:T(4,128)S(1)}, u32[]{:S(2)}) copy-start(f32[128,4]{0,1:T(4,128)S(1)} %reshape.186) | copy-start | bytes 6148
  246.4 41.2 %copy-start.28 = (f32[128,4]{0,1:T(4,128)}, f32[128,4]{0,1:T(4,128)S(1)}, u32[]{:S(2)}) copy-start(f32[128,4]{0,1:T(4,128)S(1)} %reshape.183) | copy-start | bytes 6148
  264.2 23.4 copy-start.30
  294.5 45.6 %slice-start = ((bf16[4,640,256]{2,1,0:T(8,128)(2,1)}), bf16[4,512,256]{2,1,0:T(8,128)(2,1)S(1)}, s32[]{:S(2)}) async-start(bf16[4,640,256]{2,1,0:T(8,128)(2,1)} %copy-done.8), calls=%async_computation.41 | async-start | bytes 2097152 | tf_op jit(solution)/shard_map/slice | solution.py:227
  464.4 14.8 copy-start.1
  464.4 14.8 copy-start.51
  490.4 160.8 %all-gather.37.cloned.1.call-start = ((), (), s32[]{:S(2)}) async-start(), calls=%async_computation.23 | async-start | bytes 12255232 | tf_op jit(solution)/shard_map/all_gather | solution.py:28
  491.2 199.4 %all-gather.35.cloned.1.call-start = ((), (), s32[]{:S(2)}) async-start(), calls=%async_computation.22 | async-start | bytes 3932160 | tf_op jit(solution)/shard_map/all_gather | solution.py:34
  558.3 229.2 %all-gather.39.cloned.1.call-start = ((), (), s32[]{:S(2)}) async-start(), calls=%async_computation.24 | async-start | bytes 12255232 | tf_op jit(solution)/shard_map/all_gather | solution.py:28
  559.0 267.1 %all-gather.43.cloned.1.call-start = ((), (), s32[]{:S(2)}) async-start(), calls=%async_computation.27 | async-start | bytes 3932160 | tf_op jit(solution)/shard_map/all_gather | solution.py:34
  559.6 363.4 %all-gather.41.cloned.1.call-start = ((), (), s32[]{:S(2)}) async-start(), calls=%async_computation.25 | async-start | bytes 12255232 | tf_op jit(solution)/shard_map/all_gather | solution.py:28
  560.3 471.9 %reduce-scatter.25.cloned.1.call-start = ((), (), s32[]{:S(2)}) async-start(), calls=%async_computation.28 | async-start | bytes 7864320 | tf_op jit(solution)/shard_map/reduce_scatter | solution.py:38
  942.2 14.4 copy-start.45
  968.2 131.9 %reduce-scatter.23.cloned.1.call-start = ((), (), s32[]{:S(2)}) async-start(), calls=%async_computation.26 | async-start | bytes 7864320 | tf_op jit(solution)/shard_map/reduce_scatter | solution.py:38
  981.3 164.2 %all-gather.45.cloned.1.call-start = ((), (), s32[]{:S(2)}) async-start(), calls=%async_computation.29 | async-start | bytes 3932160 | tf_op jit(solution)/shard_map/all_gather | solution.py:34
  1106.3 334.8 %reduce-scatter.27.cloned.1.call-start = ((), (), s32[]{:S(2)}) async-start(), calls=%async_computation.30 | async-start | bytes 8912896 | tf_op jit(solution)/shard_map/reduce_scatter | solution.py:293
  1106.4 45.2 %copy-start.5 = (f32[4,640,256]{1,2,0:T(8,128)S(1)}, f32[4,640,256]{1,2,0:T(8,128)}, u32[]{:S(2)}) copy-start(f32[4,640,256]{1,2,0:T(8,128)} %copy.125) | copy-start | bytes 7864324
  1336.2 213.8 %reduce-scatter.29.cloned.1.call-start = ((), (), s32[]{:S(2)}) async-start(), calls=%async_computation.31 | async-start | bytes 8912896 | tf_op jit(solution)/shard_map/reduce_scatter | solution.py:294
  1343.7 299.9 %reduce-scatter.47.cloned.1.call-start = ((), (), s32[]{:S(2)}) async-start(), calls=%async_computation.40 | async-start | bytes 139264
  1345.1 494.0 %reduce-scatter.45.cloned.1.call-start = ((), (), s32[]{:S(2)}) async-start(), calls=%async_computation.39 | async-start | bytes 24510464 | tf_op jit(solution)/shard_map/reduce_scatter | solution.py:64
  1360.6 545.9 %reduce-scatter.31.cloned.1.call-start = ((), (), s32[]{:S(2)}) async-start(), calls=%async_computation.32 | async-start | bytes 7864320 | tf_op jit(solution)/shard_map/reduce_scatter | solution.py:38
  1364.3 191.9 %copy-start.12 = (bf16[4,512,256]{2,1,0:T(8,128)(2,1)}, bf16[4,512,256]{2,1,0:T(8,128)(2,1)S(1)}, u32[]{:S(2)}) copy-start(bf16[4,512,256]{2,1,0:T(8,128)(2,1)S(1)} %slice.100) | copy-start | bytes 3145732
  1561.1 454.7 %reduce-scatter.33.cloned.1.call-start = ((), (), s32[]{:S(2)}) async-start(), calls=%async_computation.33 | async-start | bytes 8912896 | tf_op jit(solution)/shard_map/reduce_scatter | solution.py:52
  1569.9 555.0 %reduce-scatter.39.cloned.1.call-start = ((), (), s32[]{:S(2)}) async-start(), calls=%async_computation.36 | async-start | bytes 8912896 | tf_op jit(solution)/shard_map/reduce_scatter | solution.py:55
  1578.6 777.3 %reduce-scatter.41.cloned.1.call-start = ((), (), s32[]{:S(2)}) async-start(), calls=%async_computation.37 | async-start | bytes 24510464 | tf_op jit(solution)/shard_map/reduce_scatter | solution.py:62
  1595.2 991.4 %reduce-scatter.43.cloned.1.call-start = ((), (), s32[]{:S(2)}) async-start(), calls=%async_computation.38 | async-start | bytes 24510464 | tf_op jit(solution)/shard_map/reduce_scatter | solution.py:63
  1611.4 1083.5 %reduce-scatter.35.cloned.1.call-start = ((), (), s32[]{:S(2)}) async-start(), calls=%async_computation.34 | async-start | bytes 8912896 | tf_op jit(solution)/shard_map/reduce_scatter | solution.py:53
  1619.7 1184.1 %reduce-scatter.37.cloned.1.call-start = ((), (), s32[]{:S(2)}) async-start(), calls=%async_computation.35 | async-start | bytes 8912896 | tf_op jit(solution)/shard_map/reduce_scatter | solution.py:54
  1640.9 265.6 %copy-start.7 = (bf16[320,2048]{1,0:T(8,128)(2,1)S(1)}, bf16[320,2048]{1,0:T(8,128)(2,1)}, u32[]{:S(2)}) copy-start(bf16[320,2048]{1,0:T(8,128)(2,1)} %param.21) | copy-start | bytes 3932164
  1640.9 265.6 %copy-start.18 = (f32[16,1,128]{2,1,0:T(1,128)S(1)}, f32[16,1,128]{2,1,0:T(1,128)}, u32[]{:S(2)}) copy-start(f32[16,1,128]{2,1,0:T(1,128)} %copy-done.17) | copy-start | bytes 24580
  1640.9 265.6 %copy-start.23 = (f32[320]{0:T(512)S(1)}, f32[320]{0:T(512)}, u32[]{:S(2)}) copy-start(f32[320]{0:T(512)} %copy-done.22) | copy-start | bytes 3844
  1842.1 66.8 %copy-start.21 = (f32[2048]{0:T(1024)S(1)}, f32[2048]{0:T(1024)}, u32[]{:S(2)}) copy-start(f32[2048]{0:T(1024)} %get-tuple-element.233) | copy-start | bytes 24580
  1842.1 138.1 %copy-start.33 = (f32[320]{0:T(512)S(1)}, f32[320]{0:T(512)}, u32[]{:S(2)}) copy-start(f32[320]{0:T(512)} %get-tuple-element.303) | copy-start | bytes 3844
  (42 other events, 179.3 us)
Sparse Core Ops, SparseCore 0:
  36.2 36.3 all-gather.20
  75.3 53.2 all-gather.24
  131.3 51.3 all-gather.28
  185.3 51.3 all-gather.22
  239.3 49.0 all-gather.26
  291.0 49.1 all-gather.30
  342.3 49.0 all-gather.32
  490.6 63.7 reduce-scatter.20
  556.9 94.3 all-gather.36
  653.3 37.1 all-gather.34
  693.1 94.3 all-gather.38
  788.9 37.1 all-gather.42
  828.7 94.3 all-gather.40
  968.3 63.8 reduce-scatter.24
  1034.4 65.6 reduce-scatter.22
  1106.4 39.0 all-gather.44
  1336.4 104.6 reduce-scatter.26
  1445.5 104.4 reduce-scatter.28
  1553.9 54.8 reduce-scatter.46
  1613.3 225.8 reduce-scatter.44
  1841.6 64.7 reduce-scatter.30
  1911.1 104.6 reduce-scatter.32
  2020.5 104.3 reduce-scatter.38
  2129.4 226.5 reduce-scatter.40
  2360.6 225.9 reduce-scatter.42
  2591.1 103.7 reduce-scatter.34
  2699.4 104.3 reduce-scatter.36
where the time goes:
time: 2820 us; the launch traced here: 2810 us
  waiting for transfers between devices  1970 us (70%)
  matrix products  404 us (14%)
  blocking collectives  201 us (7%)
  other arithmetic  117 us (4%)
  local copies, waits for them, and re-layouts  93.2 us (3%)
    all_gather x7, waiting for transfers between devices, fetch(): lax.all_gather(shortened(weight_list), 'dp', axis=0, tiled=True)  374 us
    reduce_scatter x1, waiting for transfers between devices, reduce_grads(): lax.psum_scatter(grad_list[10], 'dp', scatter_dimension=0, tiled=True)  231 us
    reduce_scatter x1, waiting for transfers between devices, reduce_grads(): lax.psum_scatter(grad_list[11], 'dp', scatter_dimension=0, tiled=True)  231 us
    reduce_scatter x4, waiting for transfers between devices, rows_out(): lax.psum_scatter(term_fn(jnp.int32(0), local_rows * lax.axis_size('tensor...  225 us
    reduce_scatter x1, waiting for transfers between devices, reduce_grads(): lax.psum_scatter(grad_list[12], 'dp', scatter_dimension=0, tiled=True)  194 us
    all_gather x4, waiting for transfers between devices, rows_in(): return lax.all_gather(row_values, 'tensor', axis=0, tiled=True)  137 us
    all_gather x7, blocking collectives, fetch(): lax.all_gather(shortened(weight_list), 'dp', axis=0, tiled=True)  133 us
    reduce_scatter x1, waiting for transfers between devices, reduce_grads(): lax.psum_scatter(grad_list[3], 'dp', scatter_dimension=0, tiled=True)  109 us
  transfers between devices with their start and end apart: 27, of which 23 were waited for; matrix products, arithmetic and copies ran while one was open for 13% of the time, Pallas kernels for 0%

commit v1 on v0

v1 whole, which is shorter than its diff:
```python
import jax
import jax.numpy as jnp
from jax import lax
from jax.sharding import PartitionSpec as P

D = 2048
DK = 128
DV = 256

norm_eps = 1e-06
head_eps = 1e-05
lambda_init = 0.2
masked_value = -1e30
f32 = jnp.float32
bf16 = jnp.bfloat16


def inv_rms(entries, eps_value):
    return lax.rsqrt(jnp.mean(entries * entries, axis=-1, keepdims=True) + eps_value)


def norm_back(entries, inverse, gain_row, incoming):
    scaled = gain_row * incoming
    return inverse * scaled - entries * inverse**3 * jnp.mean(
        entries * scaled, axis=-1, keepdims=True
    )


def plain_product(first_arg, second_arg):
    return jnp.dot(first_arg, second_arg, preferred_element_type=f32)


def rows_product(first_arg, second_arg):
    return lax.dot_general(
        first_arg, second_arg, (((0,), (0,)), ((), ())), preferred_element_type=f32
    )


def cols_product(first_arg, second_arg):
    return lax.dot_general(
        first_arg, second_arg, (((1,), (1,)), ((), ())), preferred_element_type=f32
    )


class Places:
    def __init__(self):
        self.count = lax.axis_size("dp")
        self.upper = self.count // 4
        index = lax.axis_index("dp")
        self.index = index
        self.core = index % 2
        self.side = (index // 2) % 2
        self.tensor = lax.axis_index("tensor")
        self.upper_groups = [
            [low + 4 * high for high in range(self.upper)] for low in range(4)
        ]
        self.core_pairs = [(k, k ^ 1) for k in range(self.count)]
        self.side_pairs = [(k, k ^ 2) for k in range(self.count)]

    def swap_core(self, value):
        return lax.ppermute(value, "dp", self.core_pairs)

    def swap_side(self, value):
        return lax.ppermute(value, "dp", self.side_pairs)

    def swap_tensor(self, value):
        return lax.ppermute(value, "tensor", [(0, 1), (1, 0)])

    def gather(self, shard):
        here = lax.all_gather(
            shard, "dp", axis=0, tiled=True, axis_index_groups=self.upper_groups
        )
        aside = self.swap_side(here)
        return jnp.concatenate(
            [here, aside, self.swap_core(here), self.swap_core(aside)], axis=0
        )

    def scatter_upper(self, value):
        return lax.psum_scatter(
            value, "dp", scatter_dimension=0, tiled=True, axis_index_groups=self.upper_groups
        )

    def scatter_product(self, first_arg, second_arg):
        width = first_arg.shape[1]
        half, quarter = width // 2, width // 4
        far = self.swap_core(rows_product(first_arg[:, half:], second_arg).astype(bf16))
        aside = rows_product(first_arg[:, quarter:half], second_arg) + far[quarter:].astype(f32)
        aside = self.swap_side(aside.astype(bf16))
        near = rows_product(first_arg[:, :quarter], second_arg) + far[:quarter].astype(f32)
        near = (near + aside.astype(f32)).astype(bf16)
        return self.scatter_upper(near)

    def scatter_rows(self, value):
        half, quarter = value.shape[0] // 2, value.shape[0] // 4
        far = self.swap_core(value[half:])
        near = (value[:half].astype(f32) + far.astype(f32)).astype(bf16)
        aside = self.swap_side(near[quarter:])
        near = (near[:quarter].astype(f32) + aside.astype(f32)).astype(bf16)
        return self.scatter_upper(near)

    def flip(self, value, axis, bit):
        return jnp.where(bit == 1, jnp.flip(value, axis), value)

    def to_relative(self, value):
        lead = value.shape[:-1]
        parts = value.reshape(lead + (self.upper, 2, 2, value.shape[-1] // self.count))
        k = len(lead)
        order = tuple(range(k)) + (k + 2, k + 1, k, k + 3)
        parts = jnp.transpose(parts, order)
        parts = self.flip(self.flip(parts, k, self.core), k + 1, self.side)
        return parts.reshape(value.shape)

    def from_relative(self, value):
        lead = value.shape[:-1]
        parts = value.reshape(lead + (2, 2, self.upper, value.shape[-1] // self.count))
        k = len(lead)
        parts = self.flip(self.flip(parts, k, self.core), k + 1, self.side)
        order = tuple(range(k)) + (k + 2, k + 1, k, k + 3)
        return jnp.transpose(parts, order).reshape(value.shape)

    def relative_blocks(self):
        spot = jnp.arange(self.count, dtype=jnp.int32)
        core = spot // (2 * self.upper)
        side = (spot // self.upper) % 2
        high = spot % self.upper
        return high * 4 + (side ^ self.side) * 2 + (core ^ self.core)

    def own_half(self, rows):
        half = rows.shape[0] // 2
        return lax.dynamic_slice_in_dim(rows, self.tensor * half, half, 0)

    def other_half(self, rows):
        half = rows.shape[0] // 2
        return lax.dynamic_slice_in_dim(rows, (1 - self.tensor) * half, half, 0)

    def in_order(self, own, other):
        return jnp.where(
            self.tensor == 0,
            jnp.concatenate([own, other], axis=0),
            jnp.concatenate([other, own], axis=0),
        )


def key_mask(block_rows, prompt_part, key_blocks, cont_row_ids, block_index):
    row_index = lax.broadcasted_iota(jnp.int32, (block_rows, 1), 0)
    prompt_key = (
        key_blocks[:, None] * prompt_part + jnp.arange(prompt_part, dtype=jnp.int32)[None]
    ).reshape(1, -1)
    position = block_index * prompt_part + row_index
    prompt_cols = jnp.where(row_index < prompt_part, prompt_key <= position, True)
    cont_len = cont_row_ids.shape[0]
    cont_key = lax.broadcasted_iota(jnp.int32, (1, cont_len), 1)
    row_ids = jnp.concatenate([jnp.full((prompt_part,), -1, jnp.int32), cont_row_ids])[:, None]
    cont_cols = (row_ids == cont_row_ids[None, :]) & (cont_key <= row_index - prompt_part)
    return jnp.concatenate([prompt_cols, cont_cols], axis=1)


def head_scores(query_head, key_head, allowed, score_scale):
    scores = (
        jnp.einsum("qcd,kcd->cqk", query_head, key_head, preferred_element_type=f32)
        * score_scale
    )
    return jnp.where(allowed[None], scores, masked_value)


def head_forward(query_head, key_head, value_head, lam_head, allowed, score_scale):
    scores = head_scores(query_head, key_head, allowed, score_scale)
    row_top = jnp.max(scores, axis=-1, keepdims=True)
    exp_terms = jnp.exp(scores - row_top)
    row_total = jnp.sum(exp_terms, axis=-1, keepdims=True)
    weights = exp_terms / row_total
    mixed_map = (weights[0] - lam_head * weights[1]).astype(bf16)
    heads_out = jnp.dot(mixed_map, value_head, preferred_element_type=f32)
    return (heads_out, (row_top + jnp.log(row_total))[:, :, 0])


def head_backward(
    query_head, key_head, value_head, lam_head, lse_head, grad_head, allowed, score_scale
):
    scores = head_scores(query_head, key_head, allowed, score_scale)
    weights = jnp.exp(scores - lse_head[:, :, None])
    mixed_map = (weights[0] - lam_head * weights[1]).astype(bf16)
    mixed_grad = cols_product(grad_head, value_head)
    value_grad = rows_product(mixed_map, grad_head)
    lam_grad = -jnp.sum(weights[1] * mixed_grad)
    first_grad = weights[0] * (
        mixed_grad - jnp.sum(mixed_grad * weights[0], axis=-1, keepdims=True)
    )
    second_in = -lam_head * mixed_grad
    second_grad = weights[1] * (second_in - jnp.sum(second_in * weights[1], axis=-1, keepdims=True))
    score_grad = jnp.stack([first_grad, second_grad]).astype(bf16)
    query_grad = (
        jnp.einsum("cqk,kcd->qcd", score_grad, key_head, preferred_element_type=f32) * score_scale
    )
    key_grad = (
        jnp.einsum("cqk,qcd->kcd", score_grad, query_head, preferred_element_type=f32)
        * score_scale
    )
    return (query_grad, key_grad, value_grad, lam_grad)


def attend(queries, keys_values, lam_vec, allowed, score_scale):
    heads = lam_vec.shape[0]
    rows, keys = queries.shape[0], keys_values.shape[0]
    width = heads * 2 * DK
    q_four = queries.reshape(rows, heads, 2, DK).transpose(1, 0, 2, 3)
    k_four = keys_values[:, :width].reshape(keys, heads, 2, DK).transpose(1, 0, 2, 3)
    v_three = keys_values[:, width:].reshape(keys, heads, DV).transpose(1, 0, 2)

    def one(pieces):
        return head_forward(pieces[0], pieces[1], pieces[2], pieces[3], allowed, score_scale)

    out, lse = lax.map(one, (q_four, k_four, v_three, lam_vec))
    return out.transpose(1, 0, 2).reshape(rows, heads * DV), lse


def attend_back(queries, keys_values, lam_vec, lse, heads_grad, allowed, score_scale):
    heads = lam_vec.shape[0]
    rows, keys = queries.shape[0], keys_values.shape[0]
    width = heads * 2 * DK
    q_four = queries.reshape(rows, heads, 2, DK).transpose(1, 0, 2, 3)
    k_four = keys_values[:, :width].reshape(keys, heads, 2, DK).transpose(1, 0, 2, 3)
    v_three = keys_values[:, width:].reshape(keys, heads, DV).transpose(1, 0, 2)
    g_three = heads_grad.reshape(rows, heads, DV).transpose(1, 0, 2)

    def one(pieces):
        return head_backward(*pieces, allowed, score_scale)

    dq, dk, dv, dlam = lax.map(one, (q_four, k_four, v_three, lam_vec, lse, g_three))
    dq = dq.transpose(1, 0, 2, 3).reshape(rows, width).astype(bf16)
    dk = dk.transpose(1, 0, 2, 3).reshape(keys, width).astype(bf16)
    dv = dv.transpose(1, 0, 2).reshape(keys, heads * DV).astype(bf16)
    return dq, jnp.concatenate([dk, dv], axis=1), dlam


def per_device(
    tokens,
    cotangent,
    cont_ids,
    q_weight,
    k_weight,
    v_weight,
    out_weight,
    attn_gain,
    head_gain,
    lam_q1,
    lam_k1,
    lam_q2,
    lam_k2,
    gate_weight,
    up_weight,
    down_weight,
    ffn_gain,
):
    at = Places()
    local_rows = tokens.shape[0]
    block_rows = 2 * local_rows
    row_ids = cont_ids[0]
    prompt_part = block_rows - row_ids.shape[0]
    prompt_len = prompt_part * at.count
    score_scale = DK ** (-0.5)
    heads = q_weight.shape[1] // (2 * DK)
    width = heads * 2 * DK

    prompt_sent = lax.ppermute(tokens[:prompt_part], "tensor", [(0, 1)])
    prompt_own = jnp.where(at.tensor == 0, tokens[:prompt_part], prompt_sent)
    prompt_all = at.gather(prompt_own)
    kv_full = at.gather(jnp.concatenate([k_weight, v_weight], axis=1))
    qo_full = at.gather(jnp.concatenate([q_weight, out_weight], axis=1))
    q_full, out_full = qo_full[:, :width], qo_full[:, width:]
    gate_full = at.gather(gate_weight)
    up_full = at.gather(up_weight)
    down_full = at.gather(down_weight)
    small_parts = (attn_gain, ffn_gain, head_gain, lam_q1, lam_k1, lam_q2, lam_k2)
    small_all = lax.all_gather(
        jnp.concatenate([part.reshape(-1) for part in small_parts]), "dp", axis=0
    ).astype(f32)
    small_full = []
    start = 0
    for part in small_parts:
        small_full.append(
            small_all[:, start : start + part.size].reshape((-1,) + part.shape[1:])
        )
        start += part.size
    attn_gain_row = at.to_relative(small_full[0])
    ffn_gain_row = at.to_relative(small_full[1])
    head_gain_row = small_full[2].T.reshape(-1)
    first_exp = jnp.exp(jnp.sum(small_full[3] * small_full[4], axis=0))
    second_exp = jnp.exp(jnp.sum(small_full[5] * small_full[6], axis=0))
    lam_vec = first_exp - second_exp + lambda_init

    tokens_rel = at.to_relative(tokens)
    tokens_f32 = tokens_rel.astype(f32)
    tokens_all = at.in_order(tokens_rel, at.swap_tensor(tokens_rel)).astype(f32)
    normed = (tokens_all * inv_rms(tokens_all, norm_eps) * attn_gain_row).astype(bf16)
    prompt_f32 = at.to_relative(prompt_all).astype(f32)
    prompt_normed = (prompt_f32 * inv_rms(prompt_f32, norm_eps) * attn_gain_row).astype(bf16)
    normed_keys = jnp.concatenate([prompt_normed, normed[prompt_part:]], axis=0)
    queries = plain_product(normed, q_full).astype(bf16)
    keys_values = plain_product(normed_keys, kv_full).astype(bf16)
    allowed = key_mask(block_rows, prompt_part, at.relative_blocks(), row_ids, at.index)
    heads_out, lse = attend(queries, keys_values, lam_vec, allowed, score_scale)

    def per_head(rows):
        return rows.reshape(rows.shape[0], heads, DV)

    heads_three = per_head(heads_out)
    head_gain_three = head_gain_row.reshape(1, heads, DV)
    head_inv = inv_rms(heads_three, head_eps)
    attn_vec = (heads_three * head_inv * head_gain_three * (1.0 - lambda_init)).astype(bf16)
    attn_vec = attn_vec.reshape(block_rows, heads * DV)
    attn_own, attn_other = at.own_half(attn_vec), at.other_half(attn_vec)
    attn_two = jnp.concatenate([attn_own, attn_other], axis=0)
    out_sent = at.swap_tensor(cols_product(attn_other, out_full).astype(bf16))
    residual = tokens_f32 + (cols_product(attn_own, out_full) + out_sent.astype(f32))

    inv_second = inv_rms(residual, norm_eps)
    ffn_own = (residual * inv_second * ffn_gain_row).astype(bf16)
    ffn_in = jnp.concatenate([ffn_own, at.swap_tensor(ffn_own)], axis=0)
    gate_proj = plain_product(ffn_in, gate_full)
    up_proj = plain_product(ffn_in, up_full)
    gate_sigmoid = jax.nn.sigmoid(gate_proj)
    hidden = (gate_proj * gate_sigmoid * up_proj).astype(bf16)
    down_sent = at.swap_tensor(cols_product(hidden[local_rows:], down_full).astype(bf16))
    output = residual + (cols_product(hidden[:local_rows], down_full) + down_sent.astype(f32))
    output = at.from_relative(output.astype(bf16))

    cot_rel = at.to_relative(cotangent)
    cot_rows = jnp.concatenate([cot_rel, at.swap_tensor(cot_rel)], axis=0)
    hidden_grad = plain_product(cot_rows, down_full)
    grad_down = at.scatter_product(cot_rows, hidden)
    gate_grad = (
        hidden_grad * up_proj * gate_sigmoid * (1.0 + gate_proj * (1.0 - gate_sigmoid))
    ).astype(bf16)
    up_grad = (hidden_grad * gate_proj * gate_sigmoid).astype(bf16)

    def back_ffn(rows):
        return cols_product(gate_grad[rows], gate_full) + cols_product(up_grad[rows], up_full)

    ffn_sent = at.swap_tensor(back_ffn(slice(local_rows, None)).astype(bf16))
    ffn_in_grad = back_ffn(slice(0, local_rows)) + ffn_sent.astype(f32)
    grad_gate = at.scatter_product(ffn_in, gate_grad)
    grad_up = at.scatter_product(ffn_in, up_grad)
    residual_grad = cot_rel.astype(f32) + norm_back(
        residual, inv_second, ffn_gain_row, ffn_in_grad
    )
    ffn_gain_part = jnp.sum(ffn_in_grad * residual * inv_second, axis=0)

    branch_own = residual_grad.astype(bf16)
    branch = jnp.concatenate([branch_own, at.swap_tensor(branch_own)], axis=0)
    grad_out = at.scatter_product(branch, attn_two)
    vec_two = plain_product(branch, out_full)
    vec_three = per_head(at.in_order(vec_two[:local_rows], vec_two[local_rows:]))
    scaled_grad = vec_three * head_gain_three * (1.0 - lambda_init)
    heads_grad = (
        head_inv * scaled_grad
        - heads_three
        * head_inv**3
        * jnp.mean(heads_three * scaled_grad, axis=-1, keepdims=True)
    ).astype(bf16)
    head_gain_part = jnp.sum(vec_three * heads_three * head_inv * (1.0 - lambda_init), axis=0)
    queries_grad, kv_grad, lam_grad = attend_back(
        queries,
        keys_values,
        lam_vec,
        lse,
        heads_grad.reshape(block_rows, heads * DV),
        allowed,
        score_scale,
    )
    prompt_grad = at.scatter_rows(kv_grad[:prompt_len])
    grad_kv = at.scatter_product(normed_keys, kv_grad)
    grad_q = at.scatter_product(normed, queries_grad)
    kv_here = jnp.concatenate([prompt_grad, kv_grad[prompt_len:]], axis=0)
    joint_grad = jnp.concatenate([queries_grad, kv_here], axis=1)
    back_own, back_other = at.own_half(joint_grad), at.other_half(joint_grad)

    def back_attn(rows):
        return cols_product(rows[:, :width], q_full) + cols_product(rows[:, width:], kv_full)

    normed_sent = at.swap_tensor(back_attn(back_other).astype(bf16))
    normed_grad = back_attn(back_own) + normed_sent.astype(f32)
    inv_first = inv_rms(tokens_f32, norm_eps)
    tokens_grad = residual_grad + norm_back(tokens_f32, inv_first, attn_gain_row, normed_grad)
    tokens_grad = at.from_relative(tokens_grad.astype(bf16))
    attn_gain_part = jnp.sum(normed_grad * tokens_f32 * inv_first, axis=0)

    head_rows = head_gain.shape[0]
    gain_rows = attn_gain.shape[0]
    attn_gain_sum, ffn_gain_sum, head_gain_sum, lam_sum = lax.psum(
        (
            at.from_relative(attn_gain_part),
            at.from_relative(ffn_gain_part),
            head_gain_part.T,
            lam_grad,
        ),
        "dp",
    )
    gain_two = jnp.stack([attn_gain_sum, ffn_gain_sum])
    gain_two = lax.psum(
        lax.dynamic_slice_in_dim(gain_two, at.index * gain_rows, gain_rows, 1), "tensor"
    )
    grad_head_gain = lax.dynamic_slice_in_dim(head_gain_sum, at.index * head_rows, head_rows, 0)
    one_scale, two_scale = lam_sum * first_exp, -lam_sum * second_exp
    return (
        output,
        tokens_grad,
        grad_q.astype(f32),
        grad_kv[:, :width].astype(f32),
        grad_kv[:, width:].astype(f32),
        grad_out.astype(f32),
        gain_two[0],
        grad_head_gain,
        one_scale * lam_k1.astype(f32),
        one_scale * lam_q1.astype(f32),
        two_scale * lam_k2.astype(f32),
        two_scale * lam_q2.astype(f32),
        grad_gate.astype(f32),
        grad_up.astype(f32),
        grad_down.astype(f32),
        gain_two[1],
    )


def solution(mesh):
    rows = P(("dp", "tensor"), None)
    both = P("dp", "tensor")
    placed = (
        (rows, rows, P("dp", None))
        + (both,) * 4
        + (P("dp"),)
        + (both,) * 5
        + (both,) * 3
        + (P("dp"),)
    )
    return jax.shard_map(
        per_device,
        mesh=mesh,
        in_specs=placed,
        out_specs=(rows, rows)
        + (both,) * 4
        + (P("dp"),)
        + (both,) * 5
        + (both,) * 3
        + (P("dp"),),
        check_vma=False,
    )
```

time: 2820 us -> 1590 us (0.56)
  waiting for transfers between devices: 1970 us -> 537 us
  other arithmetic: 117 us -> 224 us
  matrix products: 404 us -> 490 us
  blocking collectives: 201 us -> 125 us
  local copies, waits for them, and re-layouts: 93.2 us -> 152 us
  starting transfers between devices: 1.11 us -> 32.9 us
    reduce_scatter x13 -> x6, waiting for transfers between devices: 1420 us -> 0.03 us  [scatter_upper(): lax.psum_scatter(value, 'dp', scatter_dimension=0, tiled=True, axis_index...]
    all_gather x13 -> x6, waiting for transfers between devices: 551 us -> 184 us  [gather(): lax.all_gather(shard, 'dp', axis=0, tiled=True, axis_index_groups=self.up...]
    ppermute x0 -> x41, waiting for transfers between devices: none -> 352 us  [the longest x13 248 us: swap_side(): return lax.ppermute(value, 'dp', self.side_pairs)]
    all_gather x7 -> x0, blocking collectives: 133 us -> none  [fetch(): lax.all_gather(shortened(weight_list), 'dp', axis=0, tiled=True)]
    dot_general x8 -> x16, matrix products: 80.7 us -> 140 us  [cols_product(): lax.dot_general(first_arg, second_arg, (((1,), (1,)), ((), ())), preferre...]
    convert_element_type x8 -> x21, other arithmetic: 16.9 us -> 74.5 us  [the longest x6 23.8 us: scatter_product(): near = (near + aside.astype(f32)).astype(bf16)]
    psum x1 -> x2, blocking collectives: 5.42 us -> 62.6 us  [the longest x1 57.7 us: per_device(): lax.psum((at.from_relative(attn_gain_part), at.from_relative(ffn_gain_par...]
    dot_general x8 -> x22, matrix products: 89.5 us -> 142 us  [rows_product(): lax.dot_general(first_arg, second_arg, (((0,), (0,)), ((), ())), preferre...]
  transfers between devices with their start and end apart: 27 -> 54, of which waited for: 23 -> 16; matrix products, arithmetic and copies ran while one was open for 13% -> 46% of each run, Pallas kernels for 0% -> 0%
where the time goes in v1:
time: 1590 us; the launch traced here: 1580 us
  waiting for transfers between devices  537 us (34%)
  matrix products  490 us (31%)
  other arithmetic  224 us (14%)
  local copies, waits for them, and re-layouts  152 us (10%)
  blocking collectives  125 us (8%)
  starting transfers between devices  32.9 us (2%)
  between operations  16.2 us (1%)
    ppermute x13, waiting for transfers between devices, swap_side(): return lax.ppermute(value, 'dp', self.side_pairs)  248 us
    all_gather x6, waiting for transfers between devices, gather(): lax.all_gather(shard, 'dp', axis=0, tiled=True, axis_index_groups=self.up...  184 us
    dot_general x22, matrix products, rows_product(): lax.dot_general(first_arg, second_arg, (((0,), (0,)), ((), ())), preferre...  142 us
    dot_general x16, matrix products, cols_product(): lax.dot_general(first_arg, second_arg, (((1,), (1,)), ((), ())), preferre...  140 us
    ppermute x8, waiting for transfers between devices, swap_tensor(): return lax.ppermute(value, 'tensor', [(0, 1), (1, 0)])  93.2 us
    dot_general x6, matrix products, plain_product(): return jnp.dot(first_arg, second_arg, preferred_element_type=f32)  82.6 us
    dot_general x8, matrix products, head_scores(): jnp.einsum('qcd,kcd->cqk', query_head, key_head, preferred_element_type=f32)  75.4 us
    unnamed x1, blocking collectives  62.3 us
  transfers between devices with their start and end apart: 54, of which 16 were waited for; matrix products, arithmetic and copies ran while one was open for 46% of the time, Pallas kernels for 0%

profile of v1, /device:TPU:0, one launch (start us, length us, event | category | flops | bytes accessed | tf_op | source)
XLA Modules:
  0.0 1582.8 jit_solution(5884250352109504785)
XLA Ops:
  16.5 11.1 collective-permute-done.4
  50.5 62.3 %all-reduce.1 = bf16[7168]{0:T(1024)(128)(2,1)S(1)} all-reduce(bf16[7168]{0:T(1024)(128)(2,1)S(1)} %dynamic-update-slice), channel_id=2, replica_groups=mesh['dp'=16,'tensor'=2] {'dp'}, use_global_device_ids=true, to_apply=%add.1 | all-reduce | flops 7168 | bytes 28672
  132.1 21.2 %all-gather.10.cloned.1.call-done = bf16[512,2048]{0,1:T(8,128)(2,1)} async-done(((bf16[128,2048]{0,1:T(8,128)(2,1)}), bf16[512,2048]{0,1:T(8,128)(2,1)}) %all-gather.10.cloned.1.call-update) | async-done | bytes 2097168 | tf_op jit(solution)/shard_map/all_gather | solution.py:70
  154.8 57.4 %all-gather.16.cloned.1.call-done = bf16[512,2816]{1,0:T(8,128)(2,1)} async-done(((bf16[128,2816]{1,0:T(8,128)(2,1)}), bf16[512,2816]{1,0:T(8,128)(2,1)}) %all-gather.16.cloned.1.call-update) | async-done | bytes 2883600 | tf_op jit(solution)/shard_map/all_gather | solution.py:70
  222.1 49.4 %all-gather.14.cloned.1.call-done = bf16[512,2816]{1,0:T(8,128)(2,1)} async-done(((bf16[128,2816]{1,0:T(8,128)(2,1)}), bf16[512,2816]{1,0:T(8,128)(2,1)}) %all-gather.14.cloned.1.call-update) | async-done | bytes 2883600 | tf_op jit(solution)/shard_map/all_gather | solution.py:70
  275.0 55.8 %all-gather.18.cloned.1.call-done = bf16[512,2816]{1,0:T(8,128)(2,1)} async-done(((bf16[128,2816]{1,0:T(8,128)(2,1)}), bf16[512,2816]{1,0:T(8,128)(2,1)}) %all-gather.18.cloned.1.call-update) | async-done | bytes 2883600 | tf_op jit(solution)/shard_map/all_gather | solution.py:70
  373.9 14.2 reverse_select_fusion.1
  388.1 16.0 %fusion.77 = f32[2048,2,2,4,128]{0,4,1,2,3:T(8,128)} fusion(bf16[2048,2,2,4,128]{0,4,1,2,3:T(8,128)(2,1)} %reverse_select_fusion.1, pred[]{:T(512)S(6)} %eq.18), kind=kLoop, calls=%fused_computation.92 | loop fusion | flops 8388608 | bytes 25165824 | tf_op jit(solution)/shard_map/convert_element_type | solution.py:296
  404.1 10.0 multiply_reduce_fusion
  427.4 26.0 %convolution_convert_fusion = bf16[2560,2048]{0,1:T(8,128)(2,1)} fusion(bf16[2048,2048]{1,0:T(8,128)(2,1)} %constant_dynamic-update-slice_fusion.4, bf16[512,2048]{0,1:T(8,128)(2,1)S(1)} %copy-done.43, bf16[2048,2048]{0,1:T(8,128)(2,1)S(1)} %fusion.75), kind=kOutput, calls=%fused_computation.88 | convolution fusion | flops 21501050880 | bytes 29360128 | tf_op jit(solution)/shard_map/dot_general | solution.py:30
  453.4 8.7 fusion.223
  478.1 121.0 %while.28 = (s32[]{:T(128)}, f32[4,640,256]{1,2,0:T(8,128)}, f32[4,2,640]{2,1,0:T(2,128)}, pred[640,2560]{1,0:T(8,128)(4,1)S(1)}, bf16[4,640,2,128]{3,1,2,0:T(8,...) while((s32[]{:T(128)}, f32[4,640,256]{1,2,0:T(8,128)}, ...), condition=%wide.region_7.8_spmd, body=%wide.region_4.7_spmd.sunk | while | flops 1718680320 | bytes 74099816 | solution.py:213
  478.3 9.2 fusion.277
  508.5 9.2 fusion.277
  538.6 9.1 fusion.277
  568.8 9.2 fusion.277
  623.0 15.8 collective-permute-done.11
  650.8 22.9 %collective-permute-done.12 = bf16[320,2048]{1,0:T(8,128)(2,1)S(1)} collective-permute-done((bf16[320,2048]{1,0:T(8,128)(2,1)S(1)}, bf16[320,2048]{1,0:T(8,128)(2,1)S(1)}, u32[]{:S(2)}, u32[]{:S(2)}) %collective-permute-start.12) | collective-permute-done | bytes 1310752 | tf_op jit(solution)/shard_map/ppermute | solution.py:67
  673.7 13.5 fusion.159
  687.2 13.4 fusion.160
  700.6 19.3 %multiply_convert_fusion.1 = (bf16[640,2816]{1,0:T(8,128)(2,1)S(1)}, bf16[640,2816]{1,0:T(8,128)(2,1)}, bf16[640,2816]{1,0:T(8,128)(2,1)}) fusion(f32[640,2816]{1,0:T(8,128)} %fusion.160, f32[640,2816]{1,0:T(8,128)} %fusion.159, bf16[640,2048]{1,0:T(8,128)(2,1)} %constant_dynamic-update-slice_fusion.20, bf16[2048,2816]{1,0:T(8,128)(2,1)} %copy-done.45), kind=kOutput, calls=%fused_computation.96 | convolution fusion | flops 7410810880 | bytes 39387136 | tf_op jit(solution)/shard_map/dot_general | solution.py:30
  719.8 11.5 fusion.151
  731.3 12.7 fusion.120
  745.5 10.2 fusion.154
  755.7 17.8 %collective-permute-done.24 = bf16[320,2048]{1,0:T(8,128)(2,1)} collective-permute-done((bf16[320,2048]{1,0:T(8,128)(2,1)S(1)}, bf16[320,2048]{1,0:T(8,128)(2,1)}, u32[]{:S(2)}, u32[]{:S(2)}) %collective-permute-start.24) | collective-permute-done | bytes 1310752 | tf_op jit(solution)/shard_map/ppermute | solution.py:67
  773.5 12.6 multiply_reduce_fusion.1
  793.1 27.3 %collective-permute-done.25 = bf16[320,2048]{1,0:T(8,128)(2,1)} collective-permute-done((bf16[320,2048]{1,0:T(8,128)(2,1)}, bf16[320,2048]{1,0:T(8,128)(2,1)}, u32[]{:S(2)}, u32[]{:S(2)}) %collective-permute-start.25) | collective-permute-done | bytes 1310752 | tf_op jit(solution)/shard_map/ppermute | solution.py:67
  847.8 160.4 %while.29 = (s32[]{:T(128)}, bf16[4,640,2,128]{1,3,2,0:T(8,128)(2,1)S(1)}, bf16[4,2560,2,128]{1,3,2,0:T(8,128)(2,1)}, bf16[4,2560,256]{1,2,0:T(8,128)(2,1)}, f32...) while((s32[]{:T(128)}, ...), condition=%wide.region_17.18_spmd, body=%wide.region_13.17_spmd.sunk | while | flops 4239358720 | bytes 163543792 | solution.py:229
  848.9 9.7 subtract_exponential_fusion.3
  888.9 9.7 subtract_exponential_fusion.3
  928.9 9.7 subtract_exponential_fusion.3
  968.9 9.7 subtract_exponential_fusion.3
  1023.2 16.9 %fusion.86 = bf16[1024,2048]{1,0:T(8,128)(2,1)} fusion(bf16[2048,2048]{0,1:T(8,128)(2,1)} %copy-done.26, bf16[512,2048]{0,1:T(8,128)(2,1)} %copy.111, bf16[2560,1024]{0,1:T(8,128)(2,1)} %bitcast.288, bf16[2560,1024]{0,1:T(8,128)(2,1)} %bitcast.294), kind=kOutput, calls=%fused_computation.127 | convolution fusion | flops 10770972672 | bytes 25165824 | tf_op jit(solution)/shard_map/dot_general | solution.py:34
  1052.8 16.4 %collective-permute-done.30 = bf16[512,1024]{1,0:T(8,128)(2,1)S(1)} collective-permute-done((bf16[512,1024]{1,0:T(8,128)(2,1)S(1)}, bf16[512,1024]{1,0:T(8,128)(2,1)S(1)}, u32[]{:S(2)}, u32[]{:S(2)}) %collective-permute-start.30) | collective-permute-done | bytes 1048608 | tf_op jit(solution)/shard_map/ppermute | solution.py:64
  1072.0 9.7 convolution_convert_fusion.1
  1081.7 31.8 %collective-permute-done.27 = bf16[512,2048]{0,1:T(8,128)(2,1)} collective-permute-done((bf16[512,2048]{0,1:T(8,128)(2,1)S(1)}, bf16[512,2048]{0,1:T(8,128)(2,1)}, u32[]{:S(2)}, u32[]{:S(2)}) %collective-permute-start.27) | collective-permute-done | bytes 2097184 | tf_op jit(solution)/shard_map/ppermute | solution.py:64
  1119.0 12.9 add_convert_fusion.8
  1141.1 10.4 fusion.101
  1151.5 27.7 %collective-permute-done.32 = bf16[512,2048]{1,0:T(8,128)(2,1)} collective-permute-done((bf16[512,2048]{1,0:T(8,128)(2,1)}, bf16[512,2048]{1,0:T(8,128)(2,1)}, u32[]{:S(2)}, u32[]{:S(2)}) %collective-permute-start.32) | collective-permute-done | bytes 2097184 | tf_op jit(solution)/shard_map/ppermute | solution.py:64
  1193.9 59.0 %collective-permute-done.40 = bf16[512,2816]{1,0:T(8,128)(2,1)S(1)} collective-permute-done((bf16[512,2816]{1,0:T(8,128)(2,1)S(1)}, bf16[512,2816]{1,0:T(8,128)(2,1)S(1)}, u32[]{:S(2)}, u32[]{:S(2)}) %collective-permute-start.40) | collective-permute-done | bytes 2883616 | tf_op jit(solution)/shard_map/ppermute | solution.py:64
  1273.4 62.1 %collective-permute-done.38 = bf16[512,2816]{1,0:T(8,128)(2,1)S(1)} collective-permute-done((bf16[512,2816]{1,0:T(8,128)(2,1)S(1)}, bf16[512,2816]{1,0:T(8,128)(2,1)S(1)}, u32[]{:S(2)}, u32[]{:S(2)}) %collective-permute-start.38) | collective-permute-done | bytes 2883616 | tf_op jit(solution)/shard_map/ppermute | solution.py:64
  1347.8 9.5 convolution_convert_fusion.4
  1360.9 50.9 %collective-permute-done.36 = bf16[512,2816]{1,0:T(8,128)(2,1)S(1)} collective-permute-done((bf16[512,2816]{1,0:T(8,128)(2,1)}, bf16[512,2816]{1,0:T(8,128)(2,1)S(1)}, u32[]{:S(2)}, u32[]{:S(2)}) %collective-permute-start.36) | collective-permute-done | bytes 2883616 | tf_op jit(solution)/shard_map/ppermute | solution.py:64
  1418.1 10.6 fusion.119
  1445.2 8.8 fusion.164
  1460.6 9.9 fusion.166
  1477.5 9.4 collective-permute-done.28
  1494.7 57.7 %all-reduce.2 = (f32[1,2048]{1,0:T(1,128)S(1)}, f32[1,2048]{1,0:T(1,128)S(1)}, f32[256,4]{0,1:T(4,128)S(1)}, f32[4]{0:T(128)S(1)}) all-reduce(f32[1,2048]{1,0:T(1,128)S(1)} %bitcast.333, f32[1,2048]{1,0:T(1,128)S(1)} %bitcast.332, f32[256,4]{0,1:T(4,128)S(1)} %bitcast.334, ...), channel_id=1, replica_groups=mesh['dp'=16,'tensor'=2] {'dp'}, use_global_device_ids=true, to_apply=%region_24.25 | all-reduce | flops 5124 | bytes 40992 | tf_op jit(solution)/shard_map/psum | solution.py:390
  (509 shorter events, 572.3 us)
Async XLA Ops:
  7.2 108.5 %all-gather.12.cloned.1.call-start = ((), (), s32[]{:S(2)}) async-start(), calls=%async_computation.9 | async-start | bytes 2621440 | tf_op jit(solution)/shard_map/all_gather | solution.py:70
  9.2 109.9 %all-gather.8.cloned.1.call-start = ((), (), s32[]{:S(2)}) async-start(), calls=%async_computation.7 | async-start | bytes 2621440 | tf_op jit(solution)/shard_map/all_gather | solution.py:70
  11.1 142.2 %all-gather.10.cloned.1.call-start = ((), (), s32[]{:S(2)}) async-start(), calls=%async_computation.8 | async-start | bytes 2621440 | tf_op jit(solution)/shard_map/all_gather | solution.py:70
  28.5 183.7 %all-gather.16.cloned.1.call-start = ((), (), s32[]{:S(2)}) async-start(), calls=%async_computation.11 | async-start | bytes 3604480 | tf_op jit(solution)/shard_map/all_gather | solution.py:70
  29.1 242.4 %all-gather.14.cloned.1.call-start = ((), (), s32[]{:S(2)}) async-start(), calls=%async_computation.10 | async-start | bytes 3604480 | tf_op jit(solution)/shard_map/all_gather | solution.py:70
  29.7 301.1 %all-gather.18.cloned.1.call-start = ((), (), s32[]{:S(2)}) async-start(), calls=%async_computation.12 | async-start | bytes 3604480 | tf_op jit(solution)/shard_map/all_gather | solution.py:70
  35.4 85.7 %collective-permute-start = (bf16[320,2048]{1,0:T(8,128)(2,1)S(1)}, bf16[320,2048]{1,0:T(8,128)(2,1)}, u32[]{:S(2)}, u32[]{:S(2)}) collective-permute-start(bf16[320,2048]{1,0:T(8,128)(2,1)S(1)} %reshape.307), channel_id=1, source_target_pairs={{0,1},{1,0},{2,3},{3,2},{4,5},{5,4},{6,7},{7,6},{8,9},{9,8},{10,11... | collective-permute-start | bytes 3932168 | tf_op jit(solution)/shard_map/ppermute | solution.py:67
  47.3 78.6 %collective-permute-start.23 = (bf16[320,2048]{1,0:T(8,128)(2,1)S(1)}, bf16[320,2048]{1,0:T(8,128)(2,1)}, u32[]{:S(2)}, u32[]{:S(2)}) collective-permute-start(bf16[320,2048]{1,0:T(8,128)(2,1)S(1)} %reshape.322), channel_id=1, source_target_pairs={{0,1},{1,0},{2,3},{3,2},{4,5},{5,4},{6,7},{7,6},{8,9},{9,8},{10,11... | collective-permute-start | bytes 3932168 | tf_op jit(solution)/shard_map/ppermute | solution.py:67
  47.8 1386.9 %reduce-scatter.14.cloned.1.call-start = ((), (), s32[]{:S(2)}) async-start(), calls=%async_computation.15 | async-start | bytes 1310720 | tf_op jit(solution)/shard_map/reduce_scatter | solution.py:79
  115.7 96.5 %collective-permute-start.8 = (bf16[512,2048]{1,0:T(8,128)(2,1)}, bf16[512,2048]{1,0:T(8,128)(2,1)}, u32[]{:S(2)}, u32[]{:S(2)}) collective-permute-start(bf16[512,2048]{1,0:T(8,128)(2,1)} %all-gather.12.cloned.1.call-done), channel_id=1, source_target_pairs={{0,4},{2,6},{4,0},{6,2},{8,12},{10,14},{12,8},{14,10},{16,20},{18,... | collective-permute-start | bytes 6291464 | tf_op jit(solution)/shard_map/ppermute | solution.py:64
  119.0 103.0 %collective-permute-start.1 = (bf16[512,2048]{1,0:T(8,128)(2,1)}, bf16[512,2048]{1,0:T(8,128)(2,1)}, u32[]{:S(2)}, u32[]{:S(2)}) collective-permute-start(bf16[512,2048]{1,0:T(8,128)(2,1)} %all-gather.8.cloned.1.call-done), channel_id=1, source_target_pairs={{0,4},{2,6},{4,0},{6,2},{8,12},{10,14},{12,8},{14,10},{16,20},{18,... | collective-permute-start | bytes 6291464 | tf_op jit(solution)/shard_map/ppermute | solution.py:64
  125.8 211.9 %collective-permute-start.9 = (bf16[512,2048]{1,0:T(8,128)(2,1)}, bf16[512,2048]{1,0:T(8,128)(2,1)}, u32[]{:S(2)}, u32[]{:S(2)}) collective-permute-start(bf16[512,2048]{1,0:T(8,128)(2,1)} %all-gather.12.cloned.1.call-done), channel_id=1, source_target_pairs={{0,2},{2,0},{4,6},{6,4},{8,10},{10,8},{12,14},{14,12},{16,18},{18,... | collective-permute-start | bytes 6291464 | tf_op jit(solution)/shard_map/ppermute | solution.py:61
  132.1 208.8 %collective-permute-start.2 = (bf16[512,2048]{1,0:T(8,128)(2,1)}, bf16[512,2048]{1,0:T(8,128)(2,1)}, u32[]{:S(2)}, u32[]{:S(2)}) collective-permute-start(bf16[512,2048]{1,0:T(8,128)(2,1)} %all-gather.8.cloned.1.call-done), channel_id=1, source_target_pairs={{0,2},{2,0},{4,6},{6,4},{8,10},{10,8},{12,14},{14,12},{16,18},{18,... | collective-permute-start | bytes 6291464 | tf_op jit(solution)/shard_map/ppermute | solution.py:61
  153.3 188.1 %collective-permute-start.5 = (bf16[512,2048]{0,1:T(8,128)(2,1)}, bf16[512,2048]{0,1:T(8,128)(2,1)}, u32[]{:S(2)}, u32[]{:S(2)}) collective-permute-start(bf16[512,2048]{0,1:T(8,128)(2,1)} %all-gather.10.cloned.1.call-done), channel_id=1, source_target_pairs={{0,4},{2,6},{4,0},{6,2},{8,12},{10,14},{12,8},{14,10},{16,20},{18,... | collective-permute-start | bytes 6291464 | tf_op jit(solution)/shard_map/ppermute | solution.py:64
  212.2 135.6 %collective-permute-start.16 = (bf16[512,2816]{1,0:T(8,128)(2,1)}, bf16[512,2816]{1,0:T(8,128)(2,1)S(1)}, u32[]{:S(2)}, u32[]{:S(2)}) collective-permute-start(bf16[512,2816]{1,0:T(8,128)(2,1)} %all-gather.16.cloned.1.call-done), channel_id=1, source_target_pairs={{0,4},{2,6},{4,0},{6,2},{8,12},{10,14},{12,8},{14,10},{16,20},{18,... | collective-permute-start | bytes 8650760 | tf_op jit(solution)/shard_map/ppermute | solution.py:64
  222.1 128.2 %collective-permute-start.3 = (bf16[512,2048]{1,0:T(8,128)(2,1)}, bf16[512,2048]{1,0:T(8,128)(2,1)}, u32[]{:S(2)}, u32[]{:S(2)}) collective-permute-start(bf16[512,2048]{1,0:T(8,128)(2,1)} %collective-permute-done.1), channel_id=1, source_target_pairs={{0,2},{2,0},{4,6},{6,4},{8,10},{10,8},{12,14},{14,12},{16,18},{18,... | collective-permute-start | bytes 6291464 | tf_op jit(solution)/shard_map/ppermute | solution.py:61
  347.8 259.9 %collective-permute-start.17 = (bf16[512,2816]{1,0:T(8,128)(2,1)}, bf16[512,2816]{1,0:T(8,128)(2,1)}, u32[]{:S(2)}, u32[]{:S(2)}) collective-permute-start(bf16[512,2816]{1,0:T(8,128)(2,1)} %all-gather.16.cloned.1.call-done), channel_id=1, source_target_pairs={{0,2},{2,0},{4,6},{6,4},{8,10},{10,8},{12,14},{14,12},{16,18},{18,... | collective-permute-start | bytes 8650760 | tf_op jit(solution)/shard_map/ppermute | solution.py:61
  350.3 262.8 %collective-permute-start.13 = (bf16[512,2816]{1,0:T(8,128)(2,1)}, bf16[512,2816]{1,0:T(8,128)(2,1)}, u32[]{:S(2)}, u32[]{:S(2)}) collective-permute-start(bf16[512,2816]{1,0:T(8,128)(2,1)} %all-gather.14.cloned.1.call-done), channel_id=1, source_target_pairs={{0,4},{2,6},{4,0},{6,2},{8,12},{10,14},{12,8},{14,10},{16,20},{18,... | collective-permute-start | bytes 8650760 | tf_op jit(solution)/shard_map/ppermute | solution.py:64
  362.3 256.9 %collective-permute-start.14 = (bf16[512,2816]{1,0:T(8,128)(2,1)}, bf16[512,2816]{1,0:T(8,128)(2,1)}, u32[]{:S(2)}, u32[]{:S(2)}) collective-permute-start(bf16[512,2816]{1,0:T(8,128)(2,1)} %all-gather.14.cloned.1.call-done), channel_id=1, source_target_pairs={{0,2},{2,0},{4,6},{6,4},{8,10},{10,8},{12,14},{14,12},{16,18},{18,... | collective-permute-start | bytes 8650760 | tf_op jit(solution)/shard_map/ppermute | solution.py:61
  365.6 251.1 %collective-permute-start.19 = (bf16[512,2816]{1,0:T(8,128)(2,1)}, bf16[512,2816]{1,0:T(8,128)(2,1)}, u32[]{:S(2)}, u32[]{:S(2)}) collective-permute-start(bf16[512,2816]{1,0:T(8,128)(2,1)} %all-gather.18.cloned.1.call-done), channel_id=1, source_target_pairs={{0,4},{2,6},{4,0},{6,2},{8,12},{10,14},{12,8},{14,10},{16,20},{18,... | collective-permute-start | bytes 8650760 | tf_op jit(solution)/shard_map/ppermute | solution.py:64
  366.3 278.7 %collective-permute-start.20 = (bf16[512,2816]{1,0:T(8,128)(2,1)}, bf16[512,2816]{1,0:T(8,128)(2,1)}, u32[]{:S(2)}, u32[]{:S(2)}) collective-permute-start(bf16[512,2816]{1,0:T(8,128)(2,1)} %all-gather.18.cloned.1.call-done), channel_id=1, source_target_pairs={{0,2},{2,0},{4,6},{6,4},{8,10},{10,8},{12,14},{14,12},{16,18},{18,... | collective-permute-start | bytes 8650760 | tf_op jit(solution)/shard_map/ppermute | solution.py:61
  607.7 31.1 %collective-permute-start.11 = (bf16[320,2048]{1,0:T(8,128)(2,1)S(1)}, bf16[320,2048]{1,0:T(8,128)(2,1)S(1)}, u32[]{:S(2)}, u32[]{:S(2)}) collective-permute-start(bf16[320,2048]{1,0:T(8,128)(2,1)S(1)} %fusion.124), channel_id=1, source_target_pairs={{0,1},{1,0},{2,3},{3,2},{4,5},{5,4},{6,7},{7,6},{8,9},{9,8},{10,11... | collective-permute-start | bytes 3932168 | tf_op jit(solution)/shard_map/ppermute | solution.py:67
  613.1 33.9 %collective-permute-start.18 = (bf16[512,2816]{1,0:T(8,128)(2,1)S(1)}, bf16[512,2816]{1,0:T(8,128)(2,1)S(1)}, u32[]{:S(2)}, u32[]{:S(2)}) collective-permute-start(bf16[512,2816]{1,0:T(8,128)(2,1)S(1)} %copy-done.41), channel_id=1, source_target_pairs={{0,2},{2,0},{4,6},{6,4},{8,10},{10,8},{12,14},{14,12},{16,18},{18,... | collective-permute-start | bytes 8650760 | tf_op jit(solution)/shard_map/ppermute | solution.py:61
  616.7 32.1 %collective-permute-start.15 = (bf16[512,2816]{1,0:T(8,128)(2,1)}, bf16[512,2816]{1,0:T(8,128)(2,1)S(1)}, u32[]{:S(2)}, u32[]{:S(2)}) collective-permute-start(bf16[512,2816]{1,0:T(8,128)(2,1)} %collective-permute-done.13), channel_id=1, source_target_pairs={{0,2},{2,0},{4,6},{6,4},{8,10},{10,8},{12,14},{14,12},{16,18},{18,... | collective-permute-start | bytes 8650760 | tf_op jit(solution)/shard_map/ppermute | solution.py:61
  619.2 31.4 %collective-permute-start.21 = (bf16[512,2816]{1,0:T(8,128)(2,1)}, bf16[512,2816]{1,0:T(8,128)(2,1)S(1)}, u32[]{:S(2)}, u32[]{:S(2)}) collective-permute-start(bf16[512,2816]{1,0:T(8,128)(2,1)} %collective-permute-done.19), channel_id=1, source_target_pairs={{0,2},{2,0},{4,6},{6,4},{8,10},{10,8},{12,14},{14,12},{16,18},{18,... | collective-permute-start | bytes 8650760 | tf_op jit(solution)/shard_map/ppermute | solution.py:61
  643.4 30.3 %collective-permute-start.12 = (bf16[320,2048]{1,0:T(8,128)(2,1)S(1)}, bf16[320,2048]{1,0:T(8,128)(2,1)S(1)}, u32[]{:S(2)}, u32[]{:S(2)}) collective-permute-start(bf16[320,2048]{1,0:T(8,128)(2,1)S(1)} %multiply_convert_fusion.3), channel_id=1, source_target_pairs={{0,1},{1,0},{2,3},{3,2},{4,5},{5,4},{6,7},{7,6},{8,9},{9,8},{10,11... | collective-permute-start | bytes 3932168 | tf_op jit(solution)/shard_map/ppermute | solution.py:67
  744.0 29.5 %collective-permute-start.24 = (bf16[320,2048]{1,0:T(8,128)(2,1)S(1)}, bf16[320,2048]{1,0:T(8,128)(2,1)}, u32[]{:S(2)}, u32[]{:S(2)}) collective-permute-start(bf16[320,2048]{1,0:T(8,128)(2,1)S(1)} %fusion.120), channel_id=1, source_target_pairs={{0,1},{1,0},{2,3},{3,2},{4,5},{5,4},{6,7},{7,6},{8,9},{9,8},{10,11... | collective-permute-start | bytes 3932168 | tf_op jit(solution)/shard_map/ppermute | solution.py:67
  791.7 28.7 %collective-permute-start.25 = (bf16[320,2048]{1,0:T(8,128)(2,1)}, bf16[320,2048]{1,0:T(8,128)(2,1)}, u32[]{:S(2)}, u32[]{:S(2)}) collective-permute-start(bf16[320,2048]{1,0:T(8,128)(2,1)} %get-tuple-element.221), channel_id=1, source_target_pairs={{0,1},{1,0},{2,3},{3,2},{4,5},{5,4},{6,7},{7,6},{8,9},{9,8},{10,11... | collective-permute-start | bytes 3932168 | tf_op jit(solution)/shard_map/ppermute | solution.py:67
  846.4 173.6 %collective-permute-start.34 = (bf16[512,1024]{1,0:T(8,128)(2,1)}, bf16[512,1024]{1,0:T(8,128)(2,1)}, u32[]{:S(2)}, u32[]{:S(2)}) collective-permute-start(bf16[512,1024]{1,0:T(8,128)(2,1)} %add_convert_fusion.11), channel_id=1, source_target_pairs={{0,4},{2,6},{4,0},{6,2},{8,12},{10,14},{12,8},{14,10},{16,20},{18,... | collective-permute-start | bytes 3145736 | tf_op jit(solution)/shard_map/ppermute | solution.py:64
  1013.4 31.4 %collective-permute-start.26 = (bf16[1024,2048]{0,1:T(8,128)(2,1)}, bf16[1024,2048]{0,1:T(8,128)(2,1)}, u32[]{:S(2)}, u32[]{:S(2)}) collective-permute-start(bf16[1024,2048]{0,1:T(8,128)(2,1)} %fusion.85), channel_id=1, source_target_pairs={{0,2},{2,0},{4,6},{6,4},{8,10},{10,8},{12,14},{14,12},{16,18},{18,... | collective-permute-start | bytes 12582920 | tf_op jit(solution)/shard_map/ppermute | solution.py:61
  1023.1 413.5 %reduce-scatter.10.cloned.1.call-start = ((), (), s32[]{:S(2)}) async-start(), calls=%async_computation.13 | async-start | bytes 1310720 | tf_op jit(solution)/shard_map/reduce_scatter | solution.py:79
  1040.1 79.0 %collective-permute-start.31 = (bf16[1024,2048]{1,0:T(8,128)(2,1)}, bf16[1024,2048]{1,0:T(8,128)(2,1)}, u32[]{:S(2)}, u32[]{:S(2)}) collective-permute-start(bf16[1024,2048]{1,0:T(8,128)(2,1)} %fusion.86), channel_id=1, source_target_pairs={{0,2},{2,0},{4,6},{6,4},{8,10},{10,8},{12,14},{14,12},{16,18},{18,... | collective-permute-start | bytes 12582920 | tf_op jit(solution)/shard_map/ppermute | solution.py:61
  1043.1 26.1 %collective-permute-start.30 = (bf16[512,1024]{1,0:T(8,128)(2,1)S(1)}, bf16[512,1024]{1,0:T(8,128)(2,1)S(1)}, u32[]{:S(2)}, u32[]{:S(2)}) collective-permute-start(bf16[512,1024]{1,0:T(8,128)(2,1)S(1)} %add_convert_fusion.13), channel_id=1, source_target_pairs={{0,4},{2,6},{4,0},{6,2},{8,12},{10,14},{12,8},{14,10},{16,20},{18,... | collective-permute-start | bytes 3145736 | tf_op jit(solution)/shard_map/ppermute | solution.py:64
  1051.3 62.2 %collective-permute-start.27 = (bf16[512,2048]{0,1:T(8,128)(2,1)S(1)}, bf16[512,2048]{0,1:T(8,128)(2,1)}, u32[]{:S(2)}, u32[]{:S(2)}) collective-permute-start(bf16[512,2048]{0,1:T(8,128)(2,1)S(1)} %slice.300), channel_id=1, source_target_pairs={{0,4},{2,6},{4,0},{6,2},{8,12},{10,14},{12,8},{14,10},{16,20},{18,... | collective-permute-start | bytes 6291464 | tf_op jit(solution)/shard_map/ppermute | solution.py:64
  1071.9 366.5 %reduce-scatter.22.cloned.1.call-start = ((), (), s32[]{:S(2)}) async-start(), calls=%async_computation.19 | async-start | bytes 2621440
  1081.7 102.6 %collective-permute-start.39 = (bf16[1024,2816]{1,0:T(8,128)(2,1)}, bf16[1024,2816]{1,0:T(8,128)(2,1)}, u32[]{:S(2)}, u32[]{:S(2)}) collective-permute-start(bf16[1024,2816]{1,0:T(8,128)(2,1)} %convolution_convert_fusion.1), channel_id=1, source_target_pairs={{0,2},{2,0},{4,6},{6,4},{8,10},{10,8},{12,14},{14,12},{16,18},{18,... | collective-permute-start | bytes 17301512 | tf_op jit(solution)/shard_map/ppermute | solution.py:61
  1118.6 340.0 %reduce-scatter.12.cloned.1.call-start = ((), (), s32[]{:S(2)}) async-start(), calls=%async_computation.14 | async-start | bytes 2621440 | tf_op jit(solution)/shard_map/reduce_scatter | solution.py:79
  1132.0 47.3 %collective-permute-start.32 = (bf16[512,2048]{1,0:T(8,128)(2,1)}, bf16[512,2048]{1,0:T(8,128)(2,1)}, u32[]{:S(2)}, u32[]{:S(2)}) collective-permute-start(bf16[512,2048]{1,0:T(8,128)(2,1)} %add_convert_fusion.8), channel_id=1, source_target_pairs={{0,4},{2,6},{4,0},{6,2},{8,12},{10,14},{12,8},{14,10},{16,20},{18,... | collective-permute-start | bytes 6291464 | tf_op jit(solution)/shard_map/ppermute | solution.py:64
  1141.1 125.1 %collective-permute-start.37 = (bf16[1024,2816]{1,0:T(8,128)(2,1)}, bf16[1024,2816]{1,0:T(8,128)(2,1)}, u32[]{:S(2)}, u32[]{:S(2)}) collective-permute-start(bf16[1024,2816]{1,0:T(8,128)(2,1)} %convolution_convert_fusion.2), channel_id=1, source_target_pairs={{0,2},{2,0},{4,6},{6,4},{8,10},{10,8},{12,14},{14,12},{16,18},{18,... | collective-permute-start | bytes 17301512 | tf_op jit(solution)/shard_map/ppermute | solution.py:61
  1184.0 286.5 %reduce-scatter.20.cloned.1.call-start = ((), (), s32[]{:S(2)}) async-start(), calls=%async_computation.18 | async-start | bytes 3604480 | tf_op jit(solution)/shard_map/reduce_scatter | solution.py:79
  1190.0 62.9 %collective-permute-start.40 = (bf16[512,2816]{1,0:T(8,128)(2,1)S(1)}, bf16[512,2816]{1,0:T(8,128)(2,1)S(1)}, u32[]{:S(2)}, u32[]{:S(2)}) collective-permute-start(bf16[512,2816]{1,0:T(8,128)(2,1)S(1)} %add_convert_fusion.2), channel_id=1, source_target_pairs={{0,4},{2,6},{4,0},{6,2},{8,12},{10,14},{12,8},{14,10},{16,20},{18,... | collective-permute-start | bytes 8650760 | tf_op jit(solution)/shard_map/ppermute | solution.py:64
  1257.4 215.6 %reduce-scatter.18.cloned.1.call-start = ((), (), s32[]{:S(2)}) async-start(), calls=%async_computation.17 | async-start | bytes 3604480 | tf_op jit(solution)/shard_map/reduce_scatter | solution.py:79
  1266.1 74.3 %collective-permute-start.35 = (bf16[1024,2816]{1,0:T(8,128)(2,1)}, bf16[1024,2816]{1,0:T(8,128)(2,1)}, u32[]{:S(2)}, u32[]{:S(2)}) collective-permute-start(bf16[1024,2816]{1,0:T(8,128)(2,1)} %convolution_convert_fusion.3), channel_id=1, source_target_pairs={{0,2},{2,0},{4,6},{6,4},{8,10},{10,8},{12,14},{14,12},{16,18},{18,... | collective-permute-start | bytes 17301512 | tf_op jit(solution)/shard_map/ppermute | solution.py:61
  1270.5 65.0 %collective-permute-start.38 = (bf16[512,2816]{1,0:T(8,128)(2,1)S(1)}, bf16[512,2816]{1,0:T(8,128)(2,1)S(1)}, u32[]{:S(2)}, u32[]{:S(2)}) collective-permute-start(bf16[512,2816]{1,0:T(8,128)(2,1)S(1)} %add_convert_fusion.4), channel_id=1, source_target_pairs={{0,4},{2,6},{4,0},{6,2},{8,12},{10,14},{12,8},{14,10},{16,20},{18,... | collective-permute-start | bytes 8650760 | tf_op jit(solution)/shard_map/ppermute | solution.py:64
  1339.9 135.3 %reduce-scatter.16.cloned.1.call-start = ((), (), s32[]{:S(2)}) async-start(), calls=%async_computation.16 | async-start | bytes 3604480 | tf_op jit(solution)/shard_map/reduce_scatter | solution.py:79
  1347.7 64.2 %collective-permute-start.36 = (bf16[512,2816]{1,0:T(8,128)(2,1)}, bf16[512,2816]{1,0:T(8,128)(2,1)S(1)}, u32[]{:S(2)}, u32[]{:S(2)}) collective-permute-start(bf16[512,2816]{1,0:T(8,128)(2,1)} %add_convert_fusion.6), channel_id=1, source_target_pairs={{0,4},{2,6},{4,0},{6,2},{8,12},{10,14},{12,8},{14,10},{16,20},{18,... | collective-permute-start | bytes 8650760 | tf_op jit(solution)/shard_map/ppermute | solution.py:64
  1357.2 59.9 %collective-permute-start.22 = (bf16[320,2048]{1,0:T(8,128)(2,1)}, bf16[320,2048]{1,0:T(8,128)(2,1)}, u32[]{:S(2)}, u32[]{:S(2)}) collective-permute-start(bf16[320,2048]{1,0:T(8,128)(2,1)} %convolution_convert_fusion.4), channel_id=1, source_target_pairs={{0,1},{1,0},{2,3},{3,2},{4,5},{5,4},{6,7},{7,6},{8,9},{9,8},{10,11... | collective-permute-start | bytes 3932168 | tf_op jit(solution)/shard_map/ppermute | solution.py:67
  1457.3 29.6 %collective-permute-start.28 = (bf16[320,2048]{1,0:T(8,128)(2,1)}, bf16[320,2048]{1,0:T(8,128)(2,1)S(1)}, u32[]{:S(2)}, u32[]{:S(2)}) collective-permute-start(bf16[320,2048]{1,0:T(8,128)(2,1)} %fusion.121), channel_id=1, source_target_pairs={{0,1},{1,0},{2,3},{3,2},{4,5},{5,4},{6,7},{7,6},{8,9},{9,8},{10,11... | collective-permute-start | bytes 3932168 | tf_op jit(solution)/shard_map/ppermute | solution.py:67
  (92 other events, 2081.1 us)
Sparse Core Ops, SparseCore 0:
  10.2 48.6 all-gather.11
  61.0 45.0 all-gather.7
  108.3 44.9 all-gather.9
  154.7 57.3 all-gather.15
  213.6 57.8 all-gather.13
  272.9 57.8 all-gather.17
  1023.2 24.9 reduce-scatter.13
  1072.0 24.8 reduce-scatter.9
  1118.7 41.5 reduce-scatter.21
  1184.2 41.1 reduce-scatter.11
  1257.5 53.4 reduce-scatter.19
  1340.1 53.3 reduce-scatter.17
  1416.5 53.2 reduce-scatter.15

commit v2 on v1

v2 whole, which is shorter than its diff:
```python
import jax
import jax.numpy as jnp
from jax import lax
from jax.experimental import pallas as pl
from jax.experimental.pallas import tpu as pltpu
from jax.sharding import PartitionSpec as P

D = 2048
DK = 128
DV = 256

norm_eps = 1e-06
head_eps = 1e-05
lambda_init = 0.2
masked_value = -1e30
f32 = jnp.float32
bf16 = jnp.bfloat16
CHUNK = 256


def inv_rms(entries, eps_value):
    return lax.rsqrt(jnp.mean(entries * entries, axis=-1, keepdims=True) + eps_value)


def norm_back(entries, inverse, gain_row, incoming):
    scaled = gain_row * incoming
    return inverse * scaled - entries * inverse**3 * jnp.mean(
        entries * scaled, axis=-1, keepdims=True
    )


def plain_product(first_arg, second_arg):
    return jnp.dot(first_arg, second_arg, preferred_element_type=f32)


def rows_product(first_arg, second_arg):
    return lax.dot_general(
        first_arg, second_arg, (((0,), (0,)), ((), ())), preferred_element_type=f32
    )


def cols_product(first_arg, second_arg):
    return lax.dot_general(
        first_arg, second_arg, (((1,), (1,)), ((), ())), preferred_element_type=f32
    )


def together(*values):
    return lax.optimization_barrier(values)


def after(value, *others):
    if not others:
        return value
    return lax.optimization_barrier((value,) + others)[0]


class Places:
    def __init__(self):
        self.count = lax.axis_size("dp")
        self.upper = self.count // 4
        index = lax.axis_index("dp")
        self.index = index
        self.core = index % 2
        self.side = (index // 2) % 2
        self.tensor = lax.axis_index("tensor")
        self.upper_groups = [
            [low + 4 * high for high in range(self.upper)] for low in range(4)
        ]
        self.core_pairs = [(k, k ^ 1) for k in range(self.count)]
        self.side_pairs = [(k, k ^ 2) for k in range(self.count)]

    def swap_core(self, value):
        return lax.ppermute(value, "dp", self.core_pairs)

    def swap_side(self, value):
        return lax.ppermute(value, "dp", self.side_pairs)

    def swap_tensor(self, value):
        return lax.ppermute(value, "tensor", [(0, 1), (1, 0)])

    def gather_upper(self, shard):
        return lax.all_gather(
            shard, "dp", axis=0, tiled=True, axis_index_groups=self.upper_groups
        )

    def gather_near(self, here, *others):
        here = after(here, *others)
        aside = self.swap_side(here)
        return [here, aside, self.swap_core(here), self.swap_core(aside)]

    def sum_small(self, value):
        step = 1
        while step < self.count:
            value = value + lax.ppermute(
                value, "dp", [(k, k ^ step) for k in range(self.count)]
            )
            step *= 2
        return value

    def block_order(self, value):
        parts = value.reshape((2, 2, self.upper) + value.shape[1:])
        parts = self.flip(self.flip(parts, 0, self.core), 1, self.side)
        order = (2, 1, 0) + tuple(range(3, parts.ndim))
        return jnp.transpose(parts, order).reshape(value.shape)

    def scatter_upper(self, value):
        return lax.psum_scatter(
            value, "dp", scatter_dimension=0, tiled=True, axis_index_groups=self.upper_groups
        )

    def far_part(self, first_arg, second_arg):
        half = first_arg.shape[1] // 2
        return rows_product(first_arg[:, half:], second_arg).astype(bf16)

    def aside_part(self, first_arg, second_arg, far):
        half, quarter = first_arg.shape[1] // 2, first_arg.shape[1] // 4
        aside = rows_product(first_arg[:, quarter:half], second_arg) + far[quarter:].astype(f32)
        return aside.astype(bf16)

    def near_part(self, first_arg, second_arg, far, aside):
        quarter = first_arg.shape[1] // 4
        near = rows_product(first_arg[:, :quarter], second_arg) + far[:quarter].astype(f32)
        return (near + aside.astype(f32)).astype(bf16)

    def flip(self, value, axis, bit):
        return jnp.where(bit == 1, jnp.flip(value, axis), value)

    def to_relative(self, value):
        lead = value.shape[:-1]
        parts = value.reshape(lead + (self.upper, 2, 2, value.shape[-1] // self.count))
        k = len(lead)
        order = tuple(range(k)) + (k + 2, k + 1, k, k + 3)
        parts = jnp.transpose(parts, order)
        parts = self.flip(self.flip(parts, k, self.core), k + 1, self.side)
        return parts.reshape(value.shape)

    def from_relative(self, value):
        lead = value.shape[:-1]
        parts = value.reshape(lead + (2, 2, self.upper, value.shape[-1] // self.count))
        k = len(lead)
        parts = self.flip(self.flip(parts, k, self.core), k + 1, self.side)
        order = tuple(range(k)) + (k + 2, k + 1, k, k + 3)
        return jnp.transpose(parts, order).reshape(value.shape)

    def relative_blocks(self):
        spot = jnp.arange(self.count, dtype=jnp.int32)
        core = spot // (2 * self.upper)
        side = (spot // self.upper) % 2
        high = spot % self.upper
        return high * 4 + (side ^ self.side) * 2 + (core ^ self.core)

    def own_half(self, rows):
        half = rows.shape[0] // 2
        return lax.dynamic_slice_in_dim(rows, self.tensor * half, half, 0)

    def other_half(self, rows):
        half = rows.shape[0] // 2
        return lax.dynamic_slice_in_dim(rows, (1 - self.tensor) * half, half, 0)

    def in_order(self, own, other):
        return jnp.where(
            self.tensor == 0,
            jnp.concatenate([own, other], axis=0),
            jnp.concatenate([other, own], axis=0),
        )


def dot_nt(first, second):
    return lax.dot_general(first, second, (((1,), (1,)), ((), ())), preferred_element_type=f32)


def dot_nn(first, second):
    return lax.dot_general(first, second, (((1,), (0,)), ((), ())), preferred_element_type=f32)


def dot_tn(first, second):
    return lax.dot_general(first, second, (((0,), (0,)), ((), ())), preferred_element_type=f32)


def forward_kernel(
    prompt_len, top_rows, first_head, lam_ref, q_ref, kv_ref, gain_ref, spot_ref, reach_ref, low_ref, high_ref,
    out_ref, vec_ref, lse_ref, one_ref, two_ref, stat_ref,
):
    lam = lam_ref[first_head + pl.program_id(0)]
    rows, keys = q_ref.shape[0], kv_ref.shape[0]
    scale = DK ** (-0.5)
    scores = (one_ref, two_ref)

    def chunk_scores(chunk):
        for comp in range(2):
            lanes = slice(comp * DK, (comp + 1) * DK)
            scores[comp][chunk] = dot_nt(q_ref[:, lanes], kv_ref[pl.ds(chunk * CHUNK, CHUNK), lanes])

    def prompt_chunk(chunk, tops):
        chunk_scores(chunk)
        spots = spot_ref[chunk]
        for comp in range(2):
            ref = scores[comp]
            for part in range(CHUNK // 128):
                lanes = slice(part * 128, (part + 1) * 128)
                ref[chunk, :top_rows, lanes] = jnp.where(
                    spots[:, lanes] <= reach_ref[...], ref[chunk, :top_rows, lanes], masked_value
                )
        return 0

    def cont_chunk(chunk, tops):
        chunk_scores(chunk)
        first = chunk * CHUNK - prompt_len
        for part in range(CHUNK // 128):
            lanes = slice(part * 128, (part + 1) * 128)
            spot = lax.broadcasted_iota(jnp.int32, (rows, 128), 1) + (first + part * 128)
            allowed = (spot >= low_ref[...]) & (spot <= high_ref[...])
            for comp in range(2):
                ref = scores[comp]
                ref[chunk, :, lanes] = jnp.where(allowed, ref[chunk, :, lanes], masked_value)
        return 0

    first_cont = prompt_len // CHUNK
    count = keys // CHUNK
    lax.fori_loop(0, first_cont, prompt_chunk, 0)
    lax.fori_loop(first_cont, count, cont_chunk, 0)

    ROWS = 32
    def row_block(block, carry):
        span = pl.ds(pl.multiple_of(block * ROWS, ROWS), ROWS)
        totals = []
        for comp in range(2):
            ref = scores[comp]
            top = ref[0, span, :128]
            for chunk in range(count):
                for part in range(CHUNK // 128):
                    if chunk + part > 0:
                        top = jnp.maximum(top, ref[chunk, span, part * 128 : (part + 1) * 128])
            top = jnp.max(top, axis=1, keepdims=True)
            total = jnp.zeros((ROWS, 128), f32)
            for chunk in range(count):
                for part in range(CHUNK // 128):
                    lanes = slice(part * 128, (part + 1) * 128)
                    terms = jnp.exp((ref[chunk, span, lanes] - top) * scale)
                    total = total + terms
                    ref[chunk, span, lanes] = terms
            total = jnp.sum(total, axis=1, keepdims=True)
            totals.append(total)
            stat_ref[comp, span, :] = jnp.broadcast_to(top * scale + jnp.log(total), (ROWS, 128))
        first = 1.0 / totals[0]
        second = lam / totals[1]
        for chunk in range(count):
            for part in range(CHUNK // 128):
                lanes = slice(part * 128, (part + 1) * 128)
                one_ref[chunk, span, lanes] = (
                    one_ref[chunk, span, lanes] * first - two_ref[chunk, span, lanes] * second
                )
        return carry

    lax.fori_loop(0, rows // ROWS, row_block, 0)

    turn = (lax.broadcasted_iota(jnp.int32, (8, 128), 1) == 0).astype(f32)
    for comp in range(2):
        lse_ref[0, comp * 8 : (comp + 1) * 8, :] = lax.dot_general(
            turn,
            stat_ref[comp],
            (((1,), (1,)), ((), ())),
            precision=lax.Precision.HIGHEST,
            preferred_element_type=f32,
        )
    out_ref[...] = jnp.zeros_like(out_ref)

    def mix(chunk, carry):
        out_ref[...] += dot_nn(
            one_ref[chunk].astype(bf16), kv_ref[pl.ds(chunk * CHUNK, CHUNK), 2 * DK :]
        )
        return carry

    lax.fori_loop(0, count, mix, 0)
    out = out_ref[...]
    inverse = lax.rsqrt(jnp.mean(out * out, axis=1, keepdims=True) + head_eps)
    vec_ref[...] = (out * inverse * gain_ref[...] * (1.0 - lambda_init)).astype(bf16)


def backward_kernel(
    prompt_len, top_rows, lam_ref, q_ref, kv_ref, gain_ref, vec_ref, out_ref, lse_ref, spot_ref, reach_ref,
    dq_ref, dkv_ref, sums_ref, one_ref, two_ref, mix_ref, grad_ref, turn_ref,
):
    head = pl.program_id(0)
    lam = lam_ref[head]
    rows, keys = q_ref.shape[0], kv_ref.shape[0]
    scale = DK ** (-0.5)
    out = out_ref[...]
    vec = vec_ref[...]
    inverse = lax.rsqrt(jnp.mean(out * out, axis=1, keepdims=True) + head_eps)
    plain = vec * out * inverse * (1.0 - lambda_init)
    scaled = vec * gain_ref[...] * (1.0 - lambda_init)
    grad_ref[...] = (
        inverse * scaled - out * inverse**3 * jnp.mean(out * scaled, axis=1, keepdims=True)
    ).astype(bf16)
    gain_part = jnp.sum(plain, axis=0, keepdims=True)
    grad = grad_ref[...]
    count = keys // CHUNK
    first_cont = prompt_len // CHUNK

    def weigh(chunk):
        span = pl.ds(pl.multiple_of(chunk * CHUNK, CHUNK), CHUNK)
        for comp, ref in ((0, one_ref), (1, two_ref)):
            lanes = slice(comp * DK, (comp + 1) * DK)
            scores = dot_nt(kv_ref[span, lanes], q_ref[:, lanes])
            ref[chunk] = jnp.exp(scores * scale - lse_ref[0, 8 * comp : 8 * comp + 1, :])
        mix_ref[chunk] = dot_nt(kv_ref[span, 2 * DK :], grad)

    def gather_sums(chunk, sums):
        span = pl.ds(pl.multiple_of(chunk * CHUNK, CHUNK), CHUNK)
        one, two, mix = one_ref[chunk], two_ref[chunk], mix_ref[chunk]
        mixed = (one - lam * two).astype(bf16)
        dkv_ref[span, 2 * DK :] = dot_nn(mixed, grad).astype(bf16)
        return (
            sums[0] + jnp.sum((one * mix).reshape(CHUNK // 8, 8, rows), axis=0),
            sums[1] + jnp.sum((two * mix).reshape(CHUNK // 8, 8, rows), axis=0),
        )

    def prompt_chunk(chunk, sums):
        weigh(chunk)
        allowed = spot_ref[pl.ds(chunk * CHUNK, CHUNK), :top_rows] <= reach_ref[0:1, :top_rows]
        for ref in (one_ref, two_ref):
            ref[chunk, :, :top_rows] = jnp.where(allowed, ref[chunk, :, :top_rows], 0.0)
        return gather_sums(chunk, sums)

    def cont_chunk(chunk, sums):
        weigh(chunk)
        spot = lax.broadcasted_iota(jnp.int32, (CHUNK, rows), 0) + (chunk * CHUNK - prompt_len)
        allowed = (spot >= reach_ref[1:2, :]) & (spot <= reach_ref[2:3, :])
        for ref in (one_ref, two_ref):
            ref[chunk] = jnp.where(allowed, ref[chunk], 0.0)
        return gather_sums(chunk, sums)

    sums = (jnp.zeros((8, rows), f32), jnp.zeros((8, rows), f32))
    sums = lax.fori_loop(0, first_cont, prompt_chunk, sums)
    sums = lax.fori_loop(first_cont, count, cont_chunk, sums)
    first = jnp.sum(sums[0], axis=0, keepdims=True)
    second = jnp.sum(sums[1], axis=0, keepdims=True)
    sums_ref[0, 0:1, :] = gain_part
    sums_ref[0, 1:2, :] = jnp.broadcast_to(-jnp.sum(second, axis=1, keepdims=True), (1, DV))
    turn_ref[...] = jnp.zeros_like(turn_ref)

    def back(chunk, carry):
        span = pl.ds(pl.multiple_of(chunk * CHUNK, CHUNK), CHUNK)
        mix = mix_ref[chunk]
        grads = (
            (one_ref[chunk] * (mix - first)).astype(bf16),
            (two_ref[chunk] * ((mix - second) * (-lam))).astype(bf16),
        )
        for comp in range(2):
            lanes = slice(comp * DK, (comp + 1) * DK)
            dkv_ref[span, lanes] = (dot_nn(grads[comp], q_ref[:, lanes]) * scale).astype(bf16)
            turn_ref[lanes, :] += dot_tn(kv_ref[span, lanes], grads[comp])
        return carry

    lax.fori_loop(0, count, back, 0)
    dq_ref[...] = (turn_ref[...] * scale).astype(bf16)


def attend(queries, keys_values, lam_vec, gain_rows, prompt_spots, bounds, prompt_part, span):
    first, heads = span[0], span[1] - span[0]
    rows, keys = queries.shape[0], keys_values.shape[0]
    prompt_len = prompt_spots.shape[0]
    top_rows = min(rows, -(-prompt_part // 16) * 16)
    wide = [jnp.broadcast_to(bound[:, None], (rows, 128)) for bound in bounds]
    count = keys // CHUNK
    return pl.pallas_call(
        lambda *refs: forward_kernel(prompt_len, top_rows, first, *refs),
        grid=(heads,),
        in_specs=[
            pl.BlockSpec(memory_space=pltpu.SMEM),
            pl.BlockSpec((rows, 2 * DK), lambda h: (0, h + first)),
            pl.BlockSpec((keys, 2 * DK + DV), lambda h: (0, h + first)),
            pl.BlockSpec((1, DV), lambda h: (0, h + first)),
            pl.BlockSpec((prompt_len // CHUNK, 1, CHUNK), lambda h: (0, 0, 0)),
            pl.BlockSpec((top_rows, 128), lambda h: (0, 0)),
            pl.BlockSpec((rows, 128), lambda h: (0, 0)),
            pl.BlockSpec((rows, 128), lambda h: (0, 0)),
        ],
        out_specs=[
            pl.BlockSpec((rows, DV), lambda h: (0, h)),
            pl.BlockSpec((rows, DV), lambda h: (0, h)),
            pl.BlockSpec((1, 16, rows), lambda h: (h, 0, 0)),
        ],
        out_shape=[
            jax.ShapeDtypeStruct((rows, heads * DV), f32),
            jax.ShapeDtypeStruct((rows, heads * DV), bf16),
            jax.ShapeDtypeStruct((heads, 16, rows), f32),
        ],
        scratch_shapes=[
            pltpu.VMEM((count, rows, CHUNK), f32),
            pltpu.VMEM((count, rows, CHUNK), f32),
            pltpu.VMEM((2, rows, 128), f32),
        ],
        compiler_params=pltpu.CompilerParams(vmem_limit_bytes=56 * 2**20),
        name="attend",
    )(
        lam_vec,
        queries,
        keys_values,
        gain_rows,
        prompt_spots.reshape(prompt_len // CHUNK, 1, CHUNK),
        wide[0][:top_rows],
        wide[1],
        wide[2],
    )


def attend_back(queries, keys_values, lam_vec, gain_rows, vec_grad, out, lse, prompt_spots, bounds, prompt_part):
    heads = lam_vec.shape[0]
    rows, keys = queries.shape[0], keys_values.shape[0]
    prompt_len = prompt_spots.shape[0]
    top_rows = min(rows, -(-prompt_part // 128) * 128)
    count = keys // CHUNK
    reach = jnp.concatenate([jnp.stack(bounds), jnp.zeros((5, rows), jnp.int32)])
    return pl.pallas_call(
        lambda *refs: backward_kernel(prompt_len, top_rows, *refs),
        grid=(heads,),
        in_specs=[
            pl.BlockSpec(memory_space=pltpu.SMEM),
            pl.BlockSpec((rows, 2 * DK), lambda h: (0, h)),
            pl.BlockSpec((keys, 2 * DK + DV), lambda h: (0, h)),
            pl.BlockSpec((1, DV), lambda h: (0, h)),
            pl.BlockSpec((rows, DV), lambda h: (0, h)),
            pl.BlockSpec((rows, DV), lambda h: (0, h)),
            pl.BlockSpec((1, 16, rows), lambda h: (h, 0, 0)),
            pl.BlockSpec((prompt_len, 128), lambda h: (0, 0)),
            pl.BlockSpec((8, rows), lambda h: (0, 0)),
        ],
        out_specs=[
            pl.BlockSpec((2 * DK, rows), lambda h: (h, 0)),
            pl.BlockSpec((keys, 2 * DK + DV), lambda h: (0, h)),
            pl.BlockSpec((1, 8, DV), lambda h: (h, 0, 0)),
        ],
        out_shape=[
            jax.ShapeDtypeStruct((heads * 2 * DK, rows), bf16),
            jax.ShapeDtypeStruct((keys, heads * (2 * DK + DV)), bf16),
            jax.ShapeDtypeStruct((heads, 8, DV), f32),
        ],
        scratch_shapes=[
            pltpu.VMEM((count, CHUNK, rows), f32),
            pltpu.VMEM((count, CHUNK, rows), f32),
            pltpu.VMEM((count, CHUNK, rows), f32),
            pltpu.VMEM((rows, DV), bf16),
            pltpu.VMEM((2 * DK, rows), f32),
        ],
        compiler_params=pltpu.CompilerParams(vmem_limit_bytes=58 * 2**20),
        name="attend_back",
    )(
        lam_vec,
        queries,
        keys_values,
        gain_rows,
        vec_grad,
        out,
        lse,
        jnp.broadcast_to(prompt_spots[:, None], (prompt_len, 128)),
        reach,
    )


def norm_kernel(count, blocks_ref, swap_ref, *refs):
    *sources, gain_ref, out_ref = refs
    step = pl.program_id(0)
    rows, depth = out_ref.shape
    block = depth // count
    upper = count // 4

    def norm_from(pieces):
        total = jnp.zeros((rows, 1), f32)
        for piece in pieces:
            x = piece[:rows, :].astype(f32)
            total = total + jnp.sum(x * x, axis=1, keepdims=True)
        inverse = lax.rsqrt(total * (1.0 / depth) + norm_eps)
        size = depth // len(pieces)
        for spot in range(count):
            lanes = slice(spot * block, (spot + 1) * block)
            high = spot % upper
            piece = pieces[high * 4 * block // size]
            start = blocks_ref[spot] * block - (high * 4 * block // size) * size
            part = piece[:rows, pl.ds(pl.multiple_of(start, block), block)].astype(f32)
            out_ref[:, lanes] = (part * inverse * gain_ref[:, lanes]).astype(bf16)

    for core in range(2):

        @pl.when((step >= core * 2 * upper) & (step < (core + 1) * 2 * upper))
        def _():
            norm_from(sources[2 * core : 2 * core + 2])

    @pl.when(step >= count)
    def _():
        norm_from(sources[4:5])


def norm_keys(at, prompt_two, prompt_far, tokens_all, gain_row, prompt_part):
    depth = tokens_all.shape[1]
    count, upper = at.count, at.upper
    cont_len = tokens_all.shape[0] - prompt_part
    unit = prompt_two.shape[0] // (4 * upper)
    if (depth // count) % 128 or cont_len % prompt_part or upper % 2:
        cores = []
        for group in (prompt_two, prompt_far):
            parts = group.reshape(2, 2 * upper, unit, depth // 2)[:, :, :prompt_part]
            parts = parts.reshape(2, 2 * upper * prompt_part, depth // 2)
            parts = at.flip(parts, 0, at.tensor)
            cores.append(jnp.concatenate([parts[0], parts[1]], axis=1))
        rows = at.to_relative(jnp.concatenate(cores + [tokens_all[prompt_part:]], axis=0))
        rows = rows.astype(f32)
        return (rows * inv_rms(rows, norm_eps) * gain_row).astype(bf16)

    def spot_of(core, half):
        first = core * 2 * upper
        return lambda i, blocks, swap: (
            (swap[0] ^ half) * 2 * upper + jnp.clip(i - first, 0, 2 * upper - 1),
            0,
        )

    return pl.pallas_call(
        lambda *refs: norm_kernel(count, *refs),
        grid_spec=pltpu.PrefetchScalarGridSpec(
            num_scalar_prefetch=2,
            grid=(count + cont_len // prompt_part,),
            in_specs=[
                pl.BlockSpec((unit, depth // 2), spot_of(core, half))
                for core in range(2)
                for half in range(2)
            ]
            + [
                pl.BlockSpec(
                    (prompt_part, depth),
                    lambda i, blocks, swap: (1 + jnp.maximum(i - count, 0), 0),
                ),
                pl.BlockSpec((1, depth), lambda i, blocks, swap: (0, 0)),
            ],
            out_specs=pl.BlockSpec((prompt_part, depth), lambda i, blocks, swap: (i, 0)),
        ),
        out_shape=jax.ShapeDtypeStruct((prompt_part * count + cont_len, depth), bf16),
        name="norm_keys",
    )(
        at.relative_blocks(),
        at.tensor.reshape(1).astype(jnp.int32),
        prompt_two,
        prompt_two,
        prompt_far,
        prompt_far,
        tokens_all,
        gain_row.reshape(1, depth),
    )


def per_device(
    tokens,
    cotangent,
    cont_ids,
    q_weight,
    k_weight,
    v_weight,
    out_weight,
    attn_gain,
    head_gain,
    lam_q1,
    lam_k1,
    lam_q2,
    lam_k2,
    gate_weight,
    up_weight,
    down_weight,
    ffn_gain,
):
    at = Places()
    local_rows = tokens.shape[0]
    block_rows = 2 * local_rows
    row_ids = cont_ids[0]
    cont_len = row_ids.shape[0]
    prompt_part = block_rows - cont_len
    prompt_len = prompt_part * at.count
    heads = q_weight.shape[1] // (2 * DK)
    width = heads * 2 * DK
    shard_rows = q_weight.shape[0]

    small_parts = (attn_gain, ffn_gain, head_gain, lam_q1, lam_k1, lam_q2, lam_k2)
    small = jnp.concatenate([part.reshape(-1) for part in small_parts])
    half = D // 2
    small_rows = jnp.zeros((16, half), bf16).at[0, : small.size].set(small)
    prompt_sent = lax.ppermute(tokens[:prompt_part, half:], "tensor", [(0, 1)])
    prompt_own = jnp.where(at.tensor == 0, tokens[:prompt_part, :half], prompt_sent)
    prompt_own = jnp.concatenate([prompt_own, small_rows], axis=0)
    prompt_here = at.gather_upper(prompt_own)

    def by_head(weight):
        return weight.reshape(shard_rows, heads, -1)

    kv_here = at.gather_upper(
        after(
            jnp.concatenate([by_head(k_weight), by_head(v_weight)], axis=2).reshape(
                shard_rows, -1
            ),
            prompt_own,
        )
    )
    q_here = at.gather_upper(after(q_weight, prompt_own))
    out_here = at.gather_upper(after(out_weight, prompt_own))
    gate_here = at.gather_upper(after(gate_weight, prompt_own))
    up_here = at.gather_upper(after(up_weight, prompt_own))
    down_here = at.gather_upper(after(down_weight, prompt_own))

    tokens_rel = at.to_relative(tokens)
    cot_rel = at.to_relative(cotangent)
    prompt_here, tokens_rel, cot_rel = together(prompt_here, tokens_rel, cot_rel)
    prompt_pair = jnp.concatenate([prompt_here, at.swap_side(prompt_here)], axis=0)
    prompt_turned = at.swap_tensor(prompt_pair)
    kv_here = after(kv_here, prompt_pair)
    kv_side, kv_near = at.swap_side(kv_here), at.swap_core(kv_here)
    tokens_turned = at.swap_tensor(after(tokens, prompt_turned))
    prompt_two = jnp.concatenate([prompt_pair, prompt_turned], axis=0)
    prompt_far = at.swap_core(prompt_two)
    prompt_far, kv_side = together(prompt_far, kv_side)
    kv_far = at.swap_core(kv_side)
    q_here = after(q_here, kv_side)
    q_side, q_near = at.swap_side(q_here), at.swap_core(q_here)
    tokens_all = at.in_order(tokens, tokens_turned)

    small_all = jnp.concatenate(
        [
            group.reshape(2, 2 * at.upper, -1, half)[0, :, prompt_part, : small.size]
            for group in (prompt_two, prompt_far)
        ],
        axis=0,
    ).astype(f32)
    small_full = []
    start = 0
    for part in small_parts:
        small_full.append(
            small_all[:, start : start + part.size].reshape((at.count,) + part.shape)
        )
        start += part.size
    attn_gain_row = small_full[0].reshape(-1)
    ffn_gain_row = small_full[1].reshape(-1)
    head_gain_row = at.block_order(small_full[2]).reshape(DV, heads).T.reshape(1, heads * DV)
    first_exp = jnp.exp(jnp.sum(small_full[3] * small_full[4], axis=(0, 1)))
    second_exp = jnp.exp(jnp.sum(small_full[5] * small_full[6], axis=(0, 1)))
    lam_vec = first_exp - second_exp + lambda_init

    prompt_spots = (
        at.relative_blocks()[:, None] * prompt_part
        + jnp.arange(prompt_part, dtype=jnp.int32)[None]
    ).reshape(-1)
    cont_spot = jnp.arange(cont_len, dtype=jnp.int32)
    earlier = jnp.sum((row_ids[None, :] < row_ids[:, None]).astype(jnp.int32), axis=1)
    far_spot = jnp.full((prompt_part,), prompt_len + cont_len, jnp.int32)
    reach = jnp.concatenate(
        [
            at.index * prompt_part + jnp.arange(prompt_part, dtype=jnp.int32),
            jnp.full((cont_len,), prompt_len, jnp.int32),
        ]
    )
    bounds = (
        reach,
        jnp.concatenate([far_spot, earlier]),
        jnp.concatenate([jnp.full((prompt_part,), -1, jnp.int32), cont_spot]),
    )

    tokens_f32 = tokens_rel.astype(f32)
    normed_keys = norm_keys(at, prompt_two, prompt_far, tokens_all, attn_gain_row, prompt_part)
    normed_keys, kv_far, kv_near = together(normed_keys, kv_far, kv_near)
    own_block = lax.dynamic_slice_in_dim(
        normed_keys, (at.index // 4) * prompt_part, prompt_part, 0
    )
    normed = jnp.concatenate([own_block, normed_keys[prompt_len:]], axis=0)
    kv_full = jnp.concatenate([kv_here, kv_side, kv_near, kv_far], axis=0)
    keys_values = plain_product(normed_keys, kv_full).astype(bf16)
    keys_values, normed, q_side, q_near = together(keys_values, normed, q_side, q_near)
    q_far = at.swap_core(q_side)
    out_here = after(out_here, q_side)
    out_side, out_near = at.swap_side(out_here), at.swap_core(out_here)
    q_full = jnp.concatenate([q_here, q_side, q_near, q_far], axis=0)
    queries = plain_product(normed, q_full).astype(bf16)
    fixed = (lam_vec, head_gain_row, prompt_spots, bounds, prompt_part)
    middle = heads // 2
    first_out, first_vec, first_lse = attend(queries, keys_values, *fixed, (0, middle))
    first_vec, out_side, out_near, gate_here = together(first_vec, out_side, out_near, gate_here)
    out_far = at.swap_core(out_side)
    gate_side, gate_near = at.swap_side(gate_here), at.swap_core(gate_here)
    second_out, second_vec, second_lse = attend(
        after(queries, first_vec), keys_values, *fixed, (middle, heads)
    )
    second_vec, out_far, gate_near = together(second_vec, out_far, gate_near)
    heads_out = jnp.concatenate([first_out, second_out], axis=1)
    lse = jnp.concatenate([first_lse, second_lse], axis=0)
    attn_vec = jnp.concatenate([first_vec, second_vec], axis=1)
    out_full = jnp.concatenate([out_here, out_side, out_near, out_far], axis=0)
    attn_own, attn_other = at.own_half(attn_vec), at.other_half(attn_vec)
    out_send = cols_product(attn_other, out_full).astype(bf16)
    out_sent = at.swap_tensor(out_send)
    out_part = cols_product(after(attn_own, out_send), out_full)
    attn_two = jnp.concatenate([attn_own, attn_other], axis=0)
    out_sent, out_part, gate_side, up_here, attn_two = together(
        out_sent, out_part, gate_side, up_here, attn_two
    )
    gate_far = at.swap_core(gate_side)
    up_side, up_near = at.swap_side(up_here), at.swap_core(up_here)
    residual = tokens_f32 + (out_part + out_sent.astype(f32))

    inv_second = inv_rms(residual, norm_eps)
    ffn_own = (residual * inv_second * ffn_gain_row).astype(bf16)
    ffn_turned = at.swap_tensor(ffn_own)
    cot_turned = at.swap_tensor(after(cot_rel, ffn_own))
    ffn_turned, gate_far, up_near = together(ffn_turned, gate_far, up_near)
    ffn_in = jnp.concatenate([ffn_own, ffn_turned], axis=0)
    cot_rows = jnp.concatenate([cot_rel, cot_turned], axis=0)
    gate_full = jnp.concatenate([gate_here, gate_side, gate_near, gate_far], axis=0)
    gate_proj = plain_product(ffn_in, gate_full)
    gate_proj, up_side, down_here, cot_rows = together(gate_proj, up_side, down_here, cot_rows)
    up_far = at.swap_core(up_side)
    down_side, down_near = at.swap_side(down_here), at.swap_core(down_here)
    up_full = jnp.concatenate([up_here, up_side, up_near, up_far], axis=0)
    up_proj = plain_product(ffn_in, up_full)
    gate_sigmoid = jax.nn.sigmoid(gate_proj)
    hidden = (gate_proj * gate_sigmoid * up_proj).astype(bf16)

    down_send = at.far_part(cot_rows, hidden)
    down_grad_far = at.swap_core(down_send)
    down_send, down_side, down_near = together(down_send, down_side, down_near)
    down_far = at.swap_core(down_side)
    down_grad_side = at.aside_part(cot_rows, hidden, after(down_grad_far, down_side))
    down_grad_aside = at.swap_side(down_grad_side)
    down_full = jnp.concatenate([down_here, down_side, down_near, down_far], axis=0)
    hidden_grad = plain_product(after(cot_rows, down_grad_side), down_full)
    gate_grad = (
        hidden_grad * up_proj * gate_sigmoid * (1.0 + gate_proj * (1.0 - gate_sigmoid))
    ).astype(bf16)
    up_grad = (hidden_grad * gate_proj * gate_sigmoid).astype(bf16)

    def back_ffn(one, two):
        return cols_product(one, gate_full) + cols_product(two, up_full)

    ffn_send = back_ffn(gate_grad[local_rows:], up_grad[local_rows:]).astype(bf16)
    ffn_sent = at.swap_tensor(ffn_send)
    gate_send = at.far_part(ffn_in, after(gate_grad, ffn_send))
    gate_grad_far = at.swap_core(gate_send)
    ffn_part = back_ffn(after(gate_grad[:local_rows], gate_send), up_grad[:local_rows])
    ffn_part, ffn_sent, gate_grad_far = together(ffn_part, ffn_sent, gate_grad_far)
    ffn_in_grad = ffn_part + ffn_sent.astype(f32)
    residual_grad = cot_rel.astype(f32) + norm_back(
        residual, inv_second, ffn_gain_row, ffn_in_grad
    )

    branch_own = residual_grad.astype(bf16)
    branch_sent = at.swap_tensor(branch_own)
    gate_grad_side = at.aside_part(ffn_in, gate_grad, after(gate_grad_far, branch_own))
    up_send = at.far_part(ffn_in, after(up_grad, gate_grad_side))
    up_grad_far = at.swap_core(up_send)
    up_send, branch_sent, down_grad_aside = together(up_send, branch_sent, down_grad_aside)
    gate_grad_aside = at.swap_side(after(gate_grad_side, down_grad_aside))
    branch = jnp.concatenate([branch_own, branch_sent], axis=0)
    out_grad_send = at.far_part(branch, attn_two)
    out_grad_far = at.swap_core(out_grad_send)
    down_last = at.near_part(
        cot_rows, after(hidden, out_grad_send), down_grad_far, down_grad_aside
    )
    grad_down = at.scatter_upper(down_last)
    up_grad_side = at.aside_part(ffn_in, after(up_grad, down_last), up_grad_far)
    up_grad_aside = at.swap_side(up_grad_side)
    vec_two = plain_product(after(branch, up_grad_side), out_full)
    out_grad_side = at.aside_part(branch, after(attn_two, vec_two), out_grad_far)
    out_grad_aside = at.swap_side(out_grad_side)
    vec_grad = at.in_order(vec_two[:local_rows], vec_two[local_rows:])
    queries_grad, kv_grad, head_sums = attend_back(
        queries,
        keys_values,
        lam_vec,
        head_gain_row,
        after(vec_grad, out_grad_side),
        heads_out,
        lse,
        prompt_spots,
        bounds,
        prompt_part,
    )
    queries_grad, kv_grad, head_sums, gate_grad_aside = together(
        queries_grad, kv_grad, head_sums, gate_grad_aside
    )
    queries_grad = queries_grad.T

    two, four = prompt_len // 2, prompt_len // 4
    prompt_send = kv_grad[two:prompt_len]
    prompt_grad_far = at.swap_core(prompt_send)
    kv_send = at.far_part(normed_keys, after(kv_grad, prompt_send))
    kv_grad_far = at.swap_core(kv_send)
    kv_send, prompt_grad_far = together(kv_send, prompt_grad_far)
    prompt_side = (kv_grad[four:two].astype(f32) + prompt_grad_far[four:].astype(f32)).astype(bf16)
    prompt_aside = at.swap_side(prompt_side)
    gate_last = at.near_part(
        ffn_in, after(gate_grad, prompt_side), gate_grad_far, gate_grad_aside
    )
    grad_gate = at.scatter_upper(gate_last)
    gate_last, kv_grad_far = together(gate_last, kv_grad_far)
    kv_grad_side = at.aside_part(normed_keys, kv_grad, kv_grad_far)
    kv_grad_aside = at.swap_side(kv_grad_side)
    q_send = at.far_part(normed, after(queries_grad, kv_grad_side))
    q_grad_far = at.swap_core(q_send)
    up_last = at.near_part(ffn_in, up_grad, up_grad_far, after(up_grad_aside, q_send))
    grad_up = at.scatter_upper(up_last)
    q_grad_side = at.aside_part(normed, queries_grad, after(q_grad_far, up_last))
    q_grad_aside = at.swap_side(q_grad_side)

    hidden_late = after(hidden, q_grad_side)
    output_send = cols_product(hidden_late[local_rows:], down_full).astype(bf16)
    output_sent = at.swap_tensor(output_send)
    output_part = cols_product(hidden_late[:local_rows], down_full)
    output_part, output_sent, prompt_aside = together(output_part, output_sent, prompt_aside)
    output = at.from_relative((residual + (output_part + output_sent.astype(f32))).astype(bf16))

    prompt_last = (
        kv_grad[:four].astype(f32)
        + prompt_grad_far[:four].astype(f32)
        + prompt_aside.astype(f32)
    ).astype(bf16)
    prompt_grad = at.scatter_upper(prompt_last)
    out_last = at.near_part(
        branch, after(attn_two, prompt_last), out_grad_far, out_grad_aside
    )
    grad_out = at.scatter_upper(out_last)
    kv_last = at.near_part(
        normed_keys, kv_grad, kv_grad_far, after(kv_grad_aside, out_last)
    )
    grad_kv = at.scatter_upper(kv_last)
    q_last = at.near_part(normed, queries_grad, q_grad_far, after(q_grad_aside, kv_last))
    grad_q = at.scatter_upper(q_last)
    here_grad = jnp.concatenate([after(prompt_grad, q_last), kv_grad[prompt_len:]], axis=0)

    def back_attn(half_of):
        return cols_product(half_of(queries_grad), q_full) + cols_product(
            half_of(here_grad), kv_full
        )

    normed_send = back_attn(at.other_half).astype(bf16)
    normed_sent = at.swap_tensor(normed_send)
    normed_grad = back_attn(at.own_half) + normed_sent.astype(f32)
    inv_first = inv_rms(tokens_f32, norm_eps)
    tokens_grad = residual_grad + norm_back(tokens_f32, inv_first, attn_gain_row, normed_grad)
    tokens_grad = at.from_relative(tokens_grad.astype(bf16))

    def row_sum(grad, weight):
        return jnp.sum(grad.astype(f32) * weight.astype(f32), axis=1)

    head_sums = at.sum_small(jnp.concatenate([head_sums[:, 0], head_sums[:, 1]], axis=1))
    head_gain_sum, lam_sum = head_sums[:, :DV], head_sums[:, DV]
    head_rows = head_gain.shape[0]
    grad_head_gain = lax.dynamic_slice_in_dim(head_gain_sum.T, at.index * head_rows, head_rows, 0)
    one_scale, two_scale = lam_sum * first_exp, -lam_sum * second_exp
    grad_q = grad_q.astype(f32)
    grad_kv = grad_kv.astype(f32).reshape(shard_rows, heads, -1)
    grad_k = grad_kv[:, :, : 2 * DK].reshape(shard_rows, -1)
    grad_v = grad_kv[:, :, 2 * DK :].reshape(shard_rows, -1)
    attn_gain_part = row_sum(grad_q, q_weight) + row_sum(grad_k, k_weight) + row_sum(grad_v, v_weight)
    ffn_gain_part = row_sum(grad_gate, gate_weight) + row_sum(grad_up, up_weight)
    attn_gain_sum = attn_gain_part + at.swap_tensor(attn_gain_part)
    ffn_gain_sum = ffn_gain_part + at.swap_tensor(ffn_gain_part)
    return (
        output,
        tokens_grad,
        grad_q,
        grad_k,
        grad_v,
        grad_out.astype(f32),
        attn_gain_sum / attn_gain.astype(f32),
        grad_head_gain,
        one_scale * lam_k1.astype(f32),
        one_scale * lam_q1.astype(f32),
        two_scale * lam_k2.astype(f32),
        two_scale * lam_q2.astype(f32),
        grad_gate.astype(f32),
        grad_up.astype(f32),
        grad_down.astype(f32),
        ffn_gain_sum / ffn_gain.astype(f32),
    )


def solution(mesh):
    rows = P(("dp", "tensor"), None)
    both = P("dp", "tensor")
    placed = (
        (rows, rows, P("dp", None))
        + (both,) * 4
        + (P("dp"),)
        + (both,) * 5
        + (both,) * 3
        + (P("dp"),)
    )
    return jax.shard_map(
        per_device,
        mesh=mesh,
        in_specs=placed,
        out_specs=(rows, rows)
        + (both,) * 4
        + (P("dp"),)
        + (both,) * 5
        + (both,) * 3
        + (P("dp"),),
        check_vma=False,
    )
```

time: 1590 us -> 1260 us (0.79)
  matrix products: 490 us -> 275 us
  other arithmetic: 224 us -> 87.1 us
  Pallas kernels: 0 us -> 130 us
  blocking collectives: 125 us -> 0 us
  waiting for transfers between devices: 537 us -> 573 us
  local copies, waits for them, and re-layouts: 152 us -> 129 us
    all_gather x6 -> x7, waiting for transfers between devices: 184 us -> 24.3 us  [gather_upper(): lax.all_gather(shard, 'dp', axis=0, tiled=True, axis_index_groups=self.up...]
    pallas_call x0 -> x4, Pallas kernels: none -> 130 us  [the longest x2 58.8 us: attend(): pl.pallas_call(lambda *refs: forward_kernel(prompt_len, top_rows, first,...]
    dot_general x20 -> x0, matrix products: 125 us -> none  [the longest x8 75.4 us: head_scores(): jnp.einsum('qcd,kcd->cqk', query_head, key_head, preferred_element_type=f32)]
    reduce_scatter x6 -> x7, waiting for transfers between devices: 0.03 us -> 105 us  [scatter_upper(): lax.psum_scatter(value, 'dp', scatter_dimension=0, tiled=True, axis_index...]
    psum x2 -> x0, blocking collectives: 62.6 us -> none  [the longest x1 57.7 us: per_device(): lax.psum((at.from_relative(attn_gain_part), at.from_relative(ffn_gain_par...]
    unnamed x1 -> x0, blocking collectives: 62.3 us -> none
    dot_general x16 -> x12, matrix products: 140 us -> 84.2 us  [cols_product(): lax.dot_general(first_arg, second_arg, (((1,), (1,)), ((), ())), preferre...]
    ppermute x8 -> x11, waiting for transfers between devices: 93.2 us -> 143 us  [swap_tensor(): return lax.ppermute(value, 'tensor', [(0, 1), (1, 0)])]
  transfers between devices with their start and end apart: 54 -> 64, of which waited for: 16 -> 24; matrix products, arithmetic and copies ran while one was open for 46% -> 30% of each run, Pallas kernels for 0% -> 10%
where the time goes in v2:
time: 1260 us; the launch traced here: 1250 us
  waiting for transfers between devices  573 us (45%)
  matrix products  275 us (22%)
  Pallas kernels  130 us (10%)
  local copies, waits for them, and re-layouts  129 us (10%)
  other arithmetic  87.1 us (7%)
  starting transfers between devices  44.5 us (4%)
  between operations  15.8 us (1%)
    ppermute x14, waiting for transfers between devices, swap_side(): return lax.ppermute(value, 'dp', self.side_pairs)  291 us
    ppermute x11, waiting for transfers between devices, swap_tensor(): return lax.ppermute(value, 'tensor', [(0, 1), (1, 0)])  143 us
    dot_general x18, matrix products, rows_product(): lax.dot_general(first_arg, second_arg, (((0,), (0,)), ((), ())), preferre...  111 us
    reduce_scatter x7, waiting for transfers between devices, scatter_upper(): lax.psum_scatter(value, 'dp', scatter_dimension=0, tiled=True, axis_index...  105 us
    dot_general x12, matrix products, cols_product(): lax.dot_general(first_arg, second_arg, (((1,), (1,)), ((), ())), preferre...  84.2 us
    dot_general x6, matrix products, plain_product(): return jnp.dot(first_arg, second_arg, preferred_element_type=f32)  79.3 us
    unnamed x209, local copies, waits for them, and re-layouts  61 us
    pallas_call x2, Pallas kernels, attend(): pl.pallas_call(lambda *refs: forward_kernel(prompt_len, top_rows, first,...  58.8 us
  transfers between devices with their start and end apart: 64, of which 24 were waited for; matrix products, arithmetic and copies ran while one was open for 30% of the time, Pallas kernels for 10%

profile of v2, /device:TPU:0, one launch (start us, length us, event | category | flops | bytes accessed | tf_op | source)
XLA Modules:
  0.0 1254.6 jit_solution(8402659998442469805)
XLA Ops:
  38.0 15.3 %all-gather.8.cloned.1.call-done = bf16[576,1024]{1,0:T(8,128)(2,1)} async-done(((bf16[144,1024]{1,0:T(8,128)(2,1)}), bf16[576,1024]{1,0:T(8,128)(2,1)}) %all-gather.8.cloned.1.call-update) | async-done | bytes 1179664 | tf_op jit(solution)/shard_map/all_gather | solution.py:83
  57.8 22.9 %collective-permute-done.1 = bf16[576,1024]{1,0:T(8,128)(2,1)S(1)} collective-permute-done((bf16[576,1024]{1,0:T(8,128)(2,1)}, bf16[576,1024]{1,0:T(8,128)(2,1)S(1)}, u32[]{:S(2)}, u32[]{:S(2)}) %collective-permute-start.1) | collective-permute-done | bytes 1179680 | tf_op jit(solution)/shard_map/ppermute | solution.py:77
  85.5 48.7 %collective-permute-done.2 = bf16[1152,1024]{1,0:T(8,128)(2,1)} collective-permute-done((bf16[1152,1024]{1,0:T(8,128)(2,1)}, bf16[1152,1024]{1,0:T(8,128)(2,1)}, u32[]{:S(2)}, u32[]{:S(2)}) %collective-permute-start.2) | collective-permute-done | bytes 2359328 | tf_op jit(solution)/shard_map/ppermute | solution.py:80
  140.8 45.2 %collective-permute-done.4 = bf16[512,2048]{1,0:T(8,128)(2,1)S(1)} collective-permute-done((bf16[512,2048]{1,0:T(8,128)(2,1)}, bf16[512,2048]{1,0:T(8,128)(2,1)S(1)}, u32[]{:S(2)}, u32[]{:S(2)}) %collective-permute-start.4) | collective-permute-done | bytes 2097184 | tf_op jit(solution)/shard_map/ppermute | solution.py:77
  198.9 18.6 %norm_keys.1 = bf16[2560,2048]{1,0:T(8,128)(2,1)} custom-call(s32[16]{0:T(128)} %get-tuple-element.221.refs_0_, s32[1]{0:T(128)} %bitcast.6.refs_1_, bf16[2304,1024]{1,0:T(8,128)(2,1)} %constant_dynamic-update-slice_fusion.2.refs_2_.refs_3_, bf16[2304,1024]{1,0:T(8,128)(2,1)} %constant_dynamic-update-slice_fusion.2.refs_2_.refs_3_, ...), custom_call_target="tpu_custom_call" | custom-call | tf_op jit(solution)/shard_map/norm_keys/pallas_call | solution.py:519
  226.1 26.7 %convolution_convert_fusion.refs_2_ = bf16[2560,2048]{1,0:T(8,128)(2,1)} fusion(bf16[2560,2048]{1,0:T(8,128)(2,1)S(1)} %copy-done.12, bf16[2048,2048]{1,0:T(8,128)(2,1)} %constant_dynamic-update-slice_fusion.5), kind=kOutput, calls=%fused_computation | convolution fusion | flops 21480079360 | bytes 29360128 | tf_op jit(solution)/shard_map/dot_general | solution.py:33
  266.7 6.1 convolution_convert_fusion.8.refs_1_
  275.3 29.6 %attend.2 = (f32[640,512]{1,0:T(8,128)}, bf16[640,512]{1,0:T(8,128)(2,1)}, f32[2,16,640]{2,1,0:T(8,128)}) custom-call(f32[4]{0:T(128)} %subtract_add_fusion.1.refs_0_, bf16[640,1024]{1,0:T(8,128)(2,1)} %convolution_convert_fusion.8.refs_1_, bf16[2560,2048]{1,0:T(8,128)(2,1)} %convolution_convert_fusion.refs_2_, f32[1,1024]{1,0:T(1,128)} %bitcast.107, ...), custom_call_target="tpu_custom_call" | custom-call | tf_op jit(solution)/shard_map/attend/pallas_call | solution.py:368
  309.5 29.2 %attend.3 = (f32[640,512]{1,0:T(8,128)}, bf16[640,512]{1,0:T(8,128)(2,1)}, f32[2,16,640]{2,1,0:T(8,128)}) custom-call(f32[4]{0:T(128)} %subtract_add_fusion.1.refs_0_, bf16[640,1024]{1,0:T(8,128)(2,1)} %convolution_convert_fusion.8.refs_1_, bf16[2560,2048]{1,0:T(8,128)(2,1)} %convolution_convert_fusion.refs_2_, f32[1,1024]{1,0:T(1,128)} %bitcast.108, ...), custom_call_target="tpu_custom_call" | custom-call | tf_op jit(solution)/shard_map/attend/pallas_call | solution.py:368
  356.6 9.0 all-gather.18.cloned.1.call-done
  370.8 10.7 collective-permute-done.15
  392.8 26.1 %collective-permute-done.21 = bf16[320,2048]{1,0:T(8,128)(2,1)S(1)} collective-permute-done((bf16[320,2048]{1,0:T(8,128)(2,1)S(1)}, bf16[320,2048]{1,0:T(8,128)(2,1)S(1)}, u32[]{:S(2)}, u32[]{:S(2)}) %collective-permute-start.21) | collective-permute-done | bytes 1310752 | tf_op jit(solution)/shard_map/ppermute | solution.py:80
  420.7 24.8 %collective-permute-done.17 = bf16[320,2048]{1,0:T(8,128)(2,1)S(1)} collective-permute-done((bf16[320,2048]{1,0:T(8,128)(2,1)S(1)}, bf16[320,2048]{1,0:T(8,128)(2,1)S(1)}, u32[]{:S(2)}, u32[]{:S(2)}) %collective-permute-start.17) | collective-permute-done | bytes 1310752 | tf_op jit(solution)/shard_map/ppermute | solution.py:80
  452.2 10.8 fusion.27
  477.6 16.1 %multiply_convert_fusion.2 = (bf16[640,2816]{1,0:T(8,128)(2,1)S(1)}, f32[640,2816]{1,0:T(8,128)}) fusion(f32[640,2816]{1,0:T(8,128)} %fusion.27, bf16[2048,2816]{1,0:T(8,128)(2,1)} %constant_dynamic-update-slice_fusion.23, bf16[320,2048]{1,0:T(8,128)(2,1)S(1)} %copy-done.7, bf16[320,2048]{1,0:T(8,128)(2,1)S(1)} %copy-done.1), kind=kOutput, calls=%fused_computation.3 | convolution fusion | flops 7398031360 | bytes 32178176 | tf_op jit(solution)/shard_map/dot_general | solution.py:33
  493.7 6.9 convolution_convert_fusion.3
  501.1 30.7 %collective-permute-done.24 = bf16[512,2816]{1,0:T(8,128)(2,1)} collective-permute-done((bf16[512,2816]{1,0:T(8,128)(2,1)S(1)}, bf16[512,2816]{1,0:T(8,128)(2,1)}, u32[]{:S(2)}, u32[]{:S(2)}) %collective-permute-start.24) | collective-permute-done | bytes 2883616 | tf_op jit(solution)/shard_map/ppermute | solution.py:77
  544.3 16.6 %multiply_convert_fusion.1 = (bf16[640,2816]{1,0:T(8,128)(2,1)S(1)}, bf16[640,2816]{1,0:T(8,128)(2,1)}) fusion(f32[640,2816]{1,0:T(8,128)} %fusion.27, f32[640,2816]{1,0:T(8,128)} %get-tuple-element.252, bf16[640,2048]{1,0:T(8,128)(2,1)S(1)} %copy-done.25, bf16[2048,2816]{1,0:T(8,128)(2,1)} %copy-done.56), kind=kOutput, calls=%fused_computation.2 | convolution fusion | flops 7405404160 | bytes 35782656 | tf_op jit(solution)/shard_map/dot_general | solution.py:33
  560.9 11.5 fusion.20
  572.5 13.3 %fusion.7 = bf16[320,2048]{1,0:T(8,128)(2,1)} fusion(f32[320,2048]{1,0:T(8,128)} %fusion.20, bf16[2048,2816]{1,0:T(8,128)(2,1)} %copy-done.55, bf16[640,2816]{1,0:T(8,128)(2,1)S(1)} %get-tuple-element.195), kind=kOutput, calls=%fused_computation.47 | convolution fusion | flops 3692298240 | bytes 17268736 | tf_op jit(solution)/shard_map/dot_general | solution.py:43
  585.8 7.0 convolution_convert_fusion.2
  594.4 8.7 fusion.18
  604.6 9.7 convolution_add_fusion.2
  614.3 9.9 collective-permute-done.27
  629.1 6.4 add_convert_fusion.4
  635.6 6.8 convolution_convert_fusion.1
  647.9 59.5 %collective-permute-done.30 = bf16[512,2816]{1,0:T(8,128)(2,1)S(1)} collective-permute-done((bf16[512,2816]{1,0:T(8,128)(2,1)S(1)}, bf16[512,2816]{1,0:T(8,128)(2,1)S(1)}, u32[]{:S(2)}, u32[]{:S(2)}) %collective-permute-start.30) | collective-permute-done | bytes 2883616 | tf_op jit(solution)/shard_map/ppermute | solution.py:77
  711.2 5.6 add_convert_fusion.3
  719.3 7.1 add_convert_fusion.2
  738.2 53.1 %attend_back.1 = (bf16[1024,640]{1,0:T(8,128)(2,1)}, bf16[2560,2048]{1,0:T(8,128)(2,1)}, f32[4,8,256]{2,1,0:T(8,128)}) custom-call(f32[4]{0:T(128)} %subtract_add_fusion.1.refs_0_, bf16[640,1024]{1,0:T(8,128)(2,1)} %convolution_convert_fusion.8.refs_1_, bf16[2560,2048]{1,0:T(8,128)(2,1)} %convolution_convert_fusion.refs_2_, f32[1,1024]{1,0:T(1,128)} %bitcast.109, ...), custom_call_target="tpu_custom_call" | custom-call | tf_op jit(solution)/shard_map/attend_back/pallas_call | solution.py:417
  796.4 16.8 %fusion.2 = bf16[1024,2048]{1,0:T(8,128)(2,1)} fusion(bf16[2560,2048]{1,0:T(8,128)(2,1)} %get-tuple-element.193, bf16[2560,2048]{1,0:T(8,128)(2,1)} %norm_keys.1), kind=kOutput, calls=%fused_computation.24 | convolution fusion | flops 10739515392 | bytes 19922944 | tf_op jit(solution)/shard_map/dot_general | solution.py:37
  814.0 7.2 fusion.98
  835.4 10.6 add_convert_fusion.8
  849.2 36.9 %collective-permute-done.37 = bf16[512,2816]{1,0:T(8,128)(2,1)} collective-permute-done((bf16[512,2816]{1,0:T(8,128)(2,1)}, bf16[512,2816]{1,0:T(8,128)(2,1)}, u32[]{:S(2)}, u32[]{:S(2)}) %collective-permute-start.37) | collective-permute-done | bytes 2883616 | tf_op jit(solution)/shard_map/ppermute | solution.py:77
  886.1 6.8 add_convert_fusion
  893.8 10.7 fusion.15
  909.8 9.3 convolution_convert_fusion.5
  925.7 8.7 fusion.24
  934.9 40.7 %collective-permute-done.39 = bf16[512,2048]{1,0:T(8,128)(2,1)S(1)} collective-permute-done((bf16[512,2048]{1,0:T(8,128)(2,1)S(1)}, bf16[512,2048]{1,0:T(8,128)(2,1)S(1)}, u32[]{:S(2)}, u32[]{:S(2)}) %collective-permute-start.39) | collective-permute-done | bytes 2097184 | tf_op jit(solution)/shard_map/ppermute | solution.py:77
  986.0 34.6 %collective-permute-done.41 = bf16[512,2048]{1,0:T(8,128)(2,1)} collective-permute-done((bf16[512,2048]{1,0:T(8,128)(2,1)}, bf16[512,2048]{1,0:T(8,128)(2,1)}, u32[]{:S(2)}, u32[]{:S(2)}) %collective-permute-start.41) | collective-permute-done | bytes 2097184 | tf_op jit(solution)/shard_map/ppermute | solution.py:77
  1020.7 5.9 add_convert_fusion.6
  1026.6 15.7 %collective-permute-done.40 = bf16[512,1024]{1,0:T(8,128)(2,1)} collective-permute-done((bf16[512,1024]{1,0:T(8,128)(2,1)}, bf16[512,1024]{1,0:T(8,128)(2,1)}, u32[]{:S(2)}, u32[]{:S(2)}) %collective-permute-start.40) | collective-permute-done | bytes 1048608 | tf_op jit(solution)/shard_map/ppermute | solution.py:77
  1082.6 19.6 %reduce-scatter.14.cloned.1.call-done = bf16[128,1024]{1,0:T(8,128)(2,1)} async-done(((bf16[512,1024]{1,0:T(8,128)(2,1)}), bf16[128,1024]{1,0:T(8,128)(2,1)}) %reduce-scatter.14.cloned.1.call-update) | async-done | bytes 262160 | tf_op jit(solution)/shard_map/reduce_scatter | solution.py:108
  1104.6 42.5 %reduce-scatter.12.cloned.1.call-done = bf16[128,2048]{1,0:T(8,128)(2,1)} async-done(((bf16[512,2048]{1,0:T(8,128)(2,1)}), bf16[128,2048]{1,0:T(8,128)(2,1)}) %reduce-scatter.12.cloned.1.call-update) | async-done | bytes 524304 | tf_op jit(solution)/shard_map/reduce_scatter | solution.py:108
  1149.4 43.2 %reduce-scatter.8.cloned.1.call-done = bf16[128,2048]{1,0:T(8,128)(2,1)} async-done(((bf16[512,2048]{1,0:T(8,128)(2,1)}), bf16[128,2048]{1,0:T(8,128)(2,1)}) %reduce-scatter.8.cloned.1.call-update) | async-done | bytes 524304 | tf_op jit(solution)/shard_map/reduce_scatter | solution.py:108
  1192.6 5.9 fusion.31
  1203.1 5.4 fusion.34
  1208.6 22.7 %collective-permute-done.44 = f32[128]{0:T(128)S(1)} collective-permute-done((f32[128]{0:T(128)S(1)}, f32[128]{0:T(128)S(1)}, u32[]{:S(2)}, u32[]{:S(2)}) %collective-permute-start.44) | collective-permute-done | bytes 544 | tf_op jit(solution)/shard_map/ppermute | solution.py:80
  (479 shorter events, 302.9 us)
Async XLA Ops:
  7.2 46.1 %all-gather.8.cloned.1.call-start = ((), (), s32[]{:S(2)}) async-start(), calls=%async_computation.7 | async-start | bytes 1474560 | tf_op jit(solution)/shard_map/all_gather | solution.py:83
  20.7 117.0 %all-gather.10.cloned.1.call-start = ((), (), s32[]{:S(2)}) async-start(), calls=%async_computation.8 | async-start | bytes 2621440 | tf_op jit(solution)/shard_map/all_gather | solution.py:83
  82.5 51.8 %collective-permute-start.2 = (bf16[1152,1024]{1,0:T(8,128)(2,1)}, bf16[1152,1024]{1,0:T(8,128)(2,1)}, u32[]{:S(2)}, u32[]{:S(2)}) collective-permute-start(bf16[1152,1024]{1,0:T(8,128)(2,1)} %get-tuple-element.232), channel_id=1, source_target_pairs={{0,1},{1,0},{2,3},{3,2},{4,5},{5,4},{6,7},{7,6},{8,9},{9,8},{10,11... | collective-permute-start | bytes 7077896 | tf_op jit(solution)/shard_map/ppermute | solution.py:80
  85.5 110.1 %all-gather.12.cloned.1.call-start = ((), (), s32[]{:S(2)}) async-start(), calls=%async_computation.9 | async-start | bytes 1310720 | tf_op jit(solution)/shard_map/all_gather | solution.py:83
  137.6 48.4 %collective-permute-start.3 = (bf16[2304,1024]{1,0:T(8,128)(2,1)}, bf16[2304,1024]{1,0:T(8,128)(2,1)}, u32[]{:S(2)}, u32[]{:S(2)}) collective-permute-start(bf16[2304,1024]{1,0:T(8,128)(2,1)} %constant_dynamic-update-slice_fusion.2.refs_2_.refs_3_), channel_id=1, source_target_pairs={{0,2},{2,0},{4,6},{6,4},{8,10},{10,8},{12,14},{14,12},{16,18},{18,... | collective-permute-start | bytes 14155784 | tf_op jit(solution)/shard_map/ppermute | solution.py:74
  137.6 121.7 %all-gather.14.cloned.1.call-start = ((), (), s32[]{:S(2)}) async-start(), calls=%async_computation.10 | async-start | bytes 1310720 | tf_op jit(solution)/shard_map/all_gather | solution.py:83
  137.7 48.3 %collective-permute-start.4 = (bf16[512,2048]{1,0:T(8,128)(2,1)}, bf16[512,2048]{1,0:T(8,128)(2,1)S(1)}, u32[]{:S(2)}, u32[]{:S(2)}) collective-permute-start(bf16[512,2048]{1,0:T(8,128)(2,1)} %all-gather.10.cloned.1.call-done), channel_id=1, source_target_pairs={{0,4},{2,6},{4,0},{6,2},{8,12},{10,14},{12,8},{14,10},{16,20},{18,... | collective-permute-start | bytes 6291464 | tf_op jit(solution)/shard_map/ppermute | solution.py:77
  139.2 165.7 %all-gather.16.cloned.1.call-start = ((), (), s32[]{:S(2)}) async-start(), calls=%async_computation.11 | async-start | bytes 3604480 | tf_op jit(solution)/shard_map/all_gather | solution.py:83
  139.3 52.6 %collective-permute-start.5 = (bf16[320,2048]{1,0:T(8,128)(2,1)S(1)}, bf16[320,2048]{1,0:T(8,128)(2,1)}, u32[]{:S(2)}, u32[]{:S(2)}) collective-permute-start(bf16[320,2048]{1,0:T(8,128)(2,1)S(1)} %copy-done.19), channel_id=1, source_target_pairs={{0,1},{1,0},{2,3},{3,2},{4,5},{5,4},{6,7},{7,6},{8,9},{9,8},{10,11... | collective-permute-start | bytes 3932168 | tf_op jit(solution)/shard_map/ppermute | solution.py:80
  140.8 78.2 %collective-permute-start.7 = (bf16[512,2048]{1,0:T(8,128)(2,1)}, bf16[512,2048]{1,0:T(8,128)(2,1)}, u32[]{:S(2)}, u32[]{:S(2)}) collective-permute-start(bf16[512,2048]{1,0:T(8,128)(2,1)} %all-gather.10.cloned.1.call-done), channel_id=1, source_target_pairs={{0,2},{2,0},{4,6},{6,4},{8,10},{10,8},{12,14},{14,12},{16,18},{18,... | collective-permute-start | bytes 6291464 | tf_op jit(solution)/shard_map/ppermute | solution.py:74
  186.0 33.0 %collective-permute-start.6 = (bf16[512,2048]{1,0:T(8,128)(2,1)S(1)}, bf16[512,2048]{1,0:T(8,128)(2,1)}, u32[]{:S(2)}, u32[]{:S(2)}) collective-permute-start(bf16[512,2048]{1,0:T(8,128)(2,1)S(1)} %collective-permute-done.4), channel_id=1, source_target_pairs={{0,2},{2,0},{4,6},{6,4},{8,10},{10,8},{12,14},{14,12},{16,18},{18,... | collective-permute-start | bytes 6291464 | tf_op jit(solution)/shard_map/ppermute | solution.py:74
  187.6 178.0 %all-gather.18.cloned.1.call-start = ((), (), s32[]{:S(2)}) async-start(), calls=%async_computation.12 | async-start | bytes 3604480 | tf_op jit(solution)/shard_map/all_gather | solution.py:83
  195.6 59.2 %collective-permute-start.8 = (bf16[512,1024]{1,0:T(8,128)(2,1)}, bf16[512,1024]{1,0:T(8,128)(2,1)}, u32[]{:S(2)}, u32[]{:S(2)}) collective-permute-start(bf16[512,1024]{1,0:T(8,128)(2,1)} %all-gather.12.cloned.1.call-done), channel_id=1, source_target_pairs={{0,4},{2,6},{4,0},{6,2},{8,12},{10,14},{12,8},{14,10},{16,20},{18,... | collective-permute-start | bytes 3145736 | tf_op jit(solution)/shard_map/ppermute | solution.py:77
  197.1 57.7 %collective-permute-start.9 = (bf16[512,1024]{1,0:T(8,128)(2,1)}, bf16[512,1024]{1,0:T(8,128)(2,1)}, u32[]{:S(2)}, u32[]{:S(2)}) collective-permute-start(bf16[512,1024]{1,0:T(8,128)(2,1)} %all-gather.12.cloned.1.call-done), channel_id=1, source_target_pairs={{0,2},{2,0},{4,6},{6,4},{8,10},{10,8},{12,14},{14,12},{16,18},{18,... | collective-permute-start | bytes 3145736 | tf_op jit(solution)/shard_map/ppermute | solution.py:74
  259.3 45.6 %collective-permute-start.11 = (bf16[512,1024]{1,0:T(8,128)(2,1)}, bf16[512,1024]{1,0:T(8,128)(2,1)}, u32[]{:S(2)}, u32[]{:S(2)}) collective-permute-start(bf16[512,1024]{1,0:T(8,128)(2,1)} %all-gather.14.cloned.1.call-done), channel_id=1, source_target_pairs={{0,4},{2,6},{4,0},{6,2},{8,12},{10,14},{12,8},{14,10},{16,20},{18,... | collective-permute-start | bytes 3145736 | tf_op jit(solution)/shard_map/ppermute | solution.py:77
  259.9 45.0 %collective-permute-start.12 = (bf16[512,1024]{1,0:T(8,128)(2,1)}, bf16[512,1024]{1,0:T(8,128)(2,1)}, u32[]{:S(2)}, u32[]{:S(2)}) collective-permute-start(bf16[512,1024]{1,0:T(8,128)(2,1)} %all-gather.14.cloned.1.call-done), channel_id=1, source_target_pairs={{0,2},{2,0},{4,6},{6,4},{8,10},{10,8},{12,14},{14,12},{16,18},{18,... | collective-permute-start | bytes 3145736 | tf_op jit(solution)/shard_map/ppermute | solution.py:74
  304.9 38.5 %collective-permute-start.14 = (bf16[512,2816]{1,0:T(8,128)(2,1)}, bf16[512,2816]{1,0:T(8,128)(2,1)S(1)}, u32[]{:S(2)}, u32[]{:S(2)}) collective-permute-start(bf16[512,2816]{1,0:T(8,128)(2,1)} %all-gather.16.cloned.1.call-done), channel_id=1, source_target_pairs={{0,2},{2,0},{4,6},{6,4},{8,10},{10,8},{12,14},{14,12},{16,18},{18,... | collective-permute-start | bytes 8650760 | tf_op jit(solution)/shard_map/ppermute | solution.py:74
  305.5 157.6 %all-gather.20.cloned.1.call-start = ((), (), s32[]{:S(2)}) async-start(), calls=%async_computation.13 | async-start | bytes 3604480 | tf_op jit(solution)/shard_map/all_gather | solution.py:83
  305.5 37.9 %collective-permute-start.13 = (bf16[512,1024]{1,0:T(8,128)(2,1)}, bf16[512,1024]{1,0:T(8,128)(2,1)}, u32[]{:S(2)}, u32[]{:S(2)}) collective-permute-start(bf16[512,1024]{1,0:T(8,128)(2,1)} %collective-permute-done.11), channel_id=1, source_target_pairs={{0,2},{2,0},{4,6},{6,4},{8,10},{10,8},{12,14},{14,12},{16,18},{18,... | collective-permute-start | bytes 3145736 | tf_op jit(solution)/shard_map/ppermute | solution.py:74
  305.6 65.2 %collective-permute-start.16 = (bf16[512,2816]{1,0:T(8,128)(2,1)}, bf16[512,2816]{1,0:T(8,128)(2,1)}, u32[]{:S(2)}, u32[]{:S(2)}) collective-permute-start(bf16[512,2816]{1,0:T(8,128)(2,1)} %all-gather.16.cloned.1.call-done), channel_id=1, source_target_pairs={{0,4},{2,6},{4,0},{6,2},{8,12},{10,14},{12,8},{14,10},{16,20},{18,... | collective-permute-start | bytes 8650760 | tf_op jit(solution)/shard_map/ppermute | solution.py:77
  381.6 64.0 %collective-permute-start.18 = (bf16[512,2816]{1,0:T(8,128)(2,1)}, bf16[512,2816]{1,0:T(8,128)(2,1)}, u32[]{:S(2)}, u32[]{:S(2)}) collective-permute-start(bf16[512,2816]{1,0:T(8,128)(2,1)} %collective-permute-done.16), channel_id=1, source_target_pairs={{0,2},{2,0},{4,6},{6,4},{8,10},{10,8},{12,14},{14,12},{16,18},{18,... | collective-permute-start | bytes 8650760 | tf_op jit(solution)/shard_map/ppermute | solution.py:74
  381.6 64.0 %collective-permute-start.19 = (bf16[512,2816]{1,0:T(8,128)(2,1)}, bf16[512,2816]{1,0:T(8,128)(2,1)}, u32[]{:S(2)}, u32[]{:S(2)}) collective-permute-start(bf16[512,2816]{1,0:T(8,128)(2,1)} %all-gather.18.cloned.1.call-done), channel_id=1, source_target_pairs={{0,2},{2,0},{4,6},{6,4},{8,10},{10,8},{12,14},{14,12},{16,18},{18,... | collective-permute-start | bytes 8650760 | tf_op jit(solution)/shard_map/ppermute | solution.py:74
  382.6 682.1 %reduce-scatter.20.cloned.1.call-start = ((), (), s32[]{:S(2)}) async-start(), calls=%async_computation.20 | async-start | bytes 3604480 | tf_op jit(solution)/shard_map/reduce_scatter | solution.py:108
  387.2 31.7 %collective-permute-start.21 = (bf16[320,2048]{1,0:T(8,128)(2,1)S(1)}, bf16[320,2048]{1,0:T(8,128)(2,1)S(1)}, u32[]{:S(2)}, u32[]{:S(2)}) collective-permute-start(bf16[320,2048]{1,0:T(8,128)(2,1)S(1)} %copy-done.16), channel_id=1, source_target_pairs={{0,1},{1,0},{2,3},{3,2},{4,5},{5,4},{6,7},{7,6},{8,9},{9,8},{10,11... | collective-permute-start | bytes 3932168 | tf_op jit(solution)/shard_map/ppermute | solution.py:80
  388.7 56.8 %collective-permute-start.17 = (bf16[320,2048]{1,0:T(8,128)(2,1)S(1)}, bf16[320,2048]{1,0:T(8,128)(2,1)S(1)}, u32[]{:S(2)}, u32[]{:S(2)}) collective-permute-start(bf16[320,2048]{1,0:T(8,128)(2,1)S(1)} %multiply_convert_fusion.3), channel_id=1, source_target_pairs={{0,1},{1,0},{2,3},{3,2},{4,5},{5,4},{6,7},{7,6},{8,9},{9,8},{10,11... | collective-permute-start | bytes 3932168 | tf_op jit(solution)/shard_map/ppermute | solution.py:80
  389.4 73.6 %collective-permute-start.20 = (bf16[512,2816]{1,0:T(8,128)(2,1)}, bf16[512,2816]{1,0:T(8,128)(2,1)}, u32[]{:S(2)}, u32[]{:S(2)}) collective-permute-start(bf16[512,2816]{1,0:T(8,128)(2,1)} %all-gather.18.cloned.1.call-done), channel_id=1, source_target_pairs={{0,4},{2,6},{4,0},{6,2},{8,12},{10,14},{12,8},{14,10},{16,20},{18,... | collective-permute-start | bytes 8650760 | tf_op jit(solution)/shard_map/ppermute | solution.py:77
  466.9 64.8 %collective-permute-start.24 = (bf16[512,2816]{1,0:T(8,128)(2,1)S(1)}, bf16[512,2816]{1,0:T(8,128)(2,1)}, u32[]{:S(2)}, u32[]{:S(2)}) collective-permute-start(bf16[512,2816]{1,0:T(8,128)(2,1)S(1)} %copy-done.35), channel_id=1, source_target_pairs={{0,4},{2,6},{4,0},{6,2},{8,12},{10,14},{12,8},{14,10},{16,20},{18,... | collective-permute-start | bytes 8650760 | tf_op jit(solution)/shard_map/ppermute | solution.py:77
  467.6 64.2 %collective-permute-start.25 = (bf16[512,2816]{1,0:T(8,128)(2,1)S(1)}, bf16[512,2816]{1,0:T(8,128)(2,1)}, u32[]{:S(2)}, u32[]{:S(2)}) collective-permute-start(bf16[512,2816]{1,0:T(8,128)(2,1)S(1)} %copy-done.35), channel_id=1, source_target_pairs={{0,2},{2,0},{4,6},{6,4},{8,10},{10,8},{12,14},{14,12},{16,18},{18,... | collective-permute-start | bytes 8650760 | tf_op jit(solution)/shard_map/ppermute | solution.py:74
  500.6 36.9 %collective-permute-start.23 = (bf16[1024,2816]{1,0:T(8,128)(2,1)}, bf16[1024,2816]{1,0:T(8,128)(2,1)S(1)}, u32[]{:S(2)}, u32[]{:S(2)}) collective-permute-start(bf16[1024,2816]{1,0:T(8,128)(2,1)} %convolution_convert_fusion.3), channel_id=1, source_target_pairs={{0,2},{2,0},{4,6},{6,4},{8,10},{10,8},{12,14},{14,12},{16,18},{18,... | collective-permute-start | bytes 17301512 | tf_op jit(solution)/shard_map/ppermute | solution.py:74
  592.8 31.4 %collective-permute-start.28 = (bf16[1024,2816]{1,0:T(8,128)(2,1)}, bf16[1024,2816]{1,0:T(8,128)(2,1)}, u32[]{:S(2)}, u32[]{:S(2)}) collective-permute-start(bf16[1024,2816]{1,0:T(8,128)(2,1)} %convolution_convert_fusion.2), channel_id=1, source_target_pairs={{0,2},{2,0},{4,6},{6,4},{8,10},{10,8},{12,14},{14,12},{16,18},{18,... | collective-permute-start | bytes 17301512 | tf_op jit(solution)/shard_map/ppermute | solution.py:74
  592.9 31.3 %collective-permute-start.27 = (bf16[320,2048]{1,0:T(8,128)(2,1)}, bf16[320,2048]{1,0:T(8,128)(2,1)S(1)}, u32[]{:S(2)}, u32[]{:S(2)}) collective-permute-start(bf16[320,2048]{1,0:T(8,128)(2,1)} %fusion.7), channel_id=1, source_target_pairs={{0,1},{1,0},{2,3},{3,2},{4,5},{5,4},{6,7},{7,6},{8,9},{9,8},{10,11... | collective-permute-start | bytes 3932168 | tf_op jit(solution)/shard_map/ppermute | solution.py:80
  642.4 76.7 %collective-permute-start.31 = (bf16[1024,2816]{1,0:T(8,128)(2,1)}, bf16[1024,2816]{1,0:T(8,128)(2,1)}, u32[]{:S(2)}, u32[]{:S(2)}) collective-permute-start(bf16[1024,2816]{1,0:T(8,128)(2,1)} %convolution_convert_fusion.1), channel_id=1, source_target_pairs={{0,2},{2,0},{4,6},{6,4},{8,10},{10,8},{12,14},{14,12},{16,18},{18,... | collective-permute-start | bytes 17301512 | tf_op jit(solution)/shard_map/ppermute | solution.py:74
  642.5 64.9 %collective-permute-start.30 = (bf16[512,2816]{1,0:T(8,128)(2,1)S(1)}, bf16[512,2816]{1,0:T(8,128)(2,1)S(1)}, u32[]{:S(2)}, u32[]{:S(2)}) collective-permute-start(bf16[512,2816]{1,0:T(8,128)(2,1)S(1)} %copy-done.38), channel_id=1, source_target_pairs={{0,4},{2,6},{4,0},{6,2},{8,12},{10,14},{12,8},{14,10},{16,20},{18,... | collective-permute-start | bytes 8650760 | tf_op jit(solution)/shard_map/ppermute | solution.py:77
  643.1 64.2 %collective-permute-start.29 = (bf16[320,2048]{1,0:T(8,128)(2,1)S(1)}, bf16[320,2048]{1,0:T(8,128)(2,1)S(1)}, u32[]{:S(2)}, u32[]{:S(2)}) collective-permute-start(bf16[320,2048]{1,0:T(8,128)(2,1)S(1)} %get-tuple-element.222), channel_id=1, source_target_pairs={{0,1},{1,0},{2,3},{3,2},{4,5},{5,4},{6,7},{7,6},{8,9},{9,8},{10,11... | collective-permute-start | bytes 3932168 | tf_op jit(solution)/shard_map/ppermute | solution.py:80
  710.6 80.7 %collective-permute-start.33 = (bf16[512,2816]{1,0:T(8,128)(2,1)}, bf16[512,2816]{1,0:T(8,128)(2,1)}, u32[]{:S(2)}, u32[]{:S(2)}) collective-permute-start(bf16[512,2816]{1,0:T(8,128)(2,1)} %add_convert_fusion.4), channel_id=1, source_target_pairs={{0,4},{2,6},{4,0},{6,2},{8,12},{10,14},{12,8},{14,10},{16,20},{18,... | collective-permute-start | bytes 8650760 | tf_op jit(solution)/shard_map/ppermute | solution.py:77
  813.6 260.9 %reduce-scatter.18.cloned.1.call-start = ((), (), s32[]{:S(2)}) async-start(), calls=%async_computation.19 | async-start | bytes 3604480 | tf_op jit(solution)/shard_map/reduce_scatter | solution.py:108
  821.2 64.9 %collective-permute-start.37 = (bf16[512,2816]{1,0:T(8,128)(2,1)}, bf16[512,2816]{1,0:T(8,128)(2,1)}, u32[]{:S(2)}, u32[]{:S(2)}) collective-permute-start(bf16[512,2816]{1,0:T(8,128)(2,1)} %add_convert_fusion.2), channel_id=1, source_target_pairs={{0,4},{2,6},{4,0},{6,2},{8,12},{10,14},{12,8},{14,10},{16,20},{18,... | collective-permute-start | bytes 8650760 | tf_op jit(solution)/shard_map/ppermute | solution.py:77
  892.9 184.0 %reduce-scatter.16.cloned.1.call-start = ((), (), s32[]{:S(2)}) async-start(), calls=%async_computation.18 | async-start | bytes 3604480 | tf_op jit(solution)/shard_map/reduce_scatter | solution.py:108
  893.5 187.3 %reduce-scatter.10.cloned.1.call-start = ((), (), s32[]{:S(2)}) async-start(), calls=%async_computation.15 | async-start | bytes 1310720 | tf_op jit(solution)/shard_map/reduce_scatter | solution.py:108
  904.5 78.5 %collective-permute-start.42 = (bf16[512,1024]{1,0:T(8,128)(2,1)}, bf16[512,1024]{1,0:T(8,128)(2,1)}, u32[]{:S(2)}, u32[]{:S(2)}) collective-permute-start(bf16[512,1024]{1,0:T(8,128)(2,1)} %add_convert_fusion.14), channel_id=1, source_target_pairs={{0,4},{2,6},{4,0},{6,2},{8,12},{10,14},{12,8},{14,10},{16,20},{18,... | collective-permute-start | bytes 3145736 | tf_op jit(solution)/shard_map/ppermute | solution.py:77
  905.9 69.8 %collective-permute-start.39 = (bf16[512,2048]{1,0:T(8,128)(2,1)S(1)}, bf16[512,2048]{1,0:T(8,128)(2,1)S(1)}, u32[]{:S(2)}, u32[]{:S(2)}) collective-permute-start(bf16[512,2048]{1,0:T(8,128)(2,1)S(1)} %copy-done.39), channel_id=1, source_target_pairs={{0,4},{2,6},{4,0},{6,2},{8,12},{10,14},{12,8},{14,10},{16,20},{18,... | collective-permute-start | bytes 6291464 | tf_op jit(solution)/shard_map/ppermute | solution.py:77
  919.1 56.5 %collective-permute-start.38 = (bf16[320,2048]{1,0:T(8,128)(2,1)}, bf16[320,2048]{1,0:T(8,128)(2,1)}, u32[]{:S(2)}, u32[]{:S(2)}) collective-permute-start(bf16[320,2048]{1,0:T(8,128)(2,1)} %convolution_convert_fusion.5), channel_id=1, source_target_pairs={{0,1},{1,0},{2,3},{3,2},{4,5},{5,4},{6,7},{7,6},{8,9},{9,8},{10,11... | collective-permute-start | bytes 3932168 | tf_op jit(solution)/shard_map/ppermute | solution.py:80
  924.2 96.5 %collective-permute-start.41 = (bf16[512,2048]{1,0:T(8,128)(2,1)}, bf16[512,2048]{1,0:T(8,128)(2,1)}, u32[]{:S(2)}, u32[]{:S(2)}) collective-permute-start(bf16[512,2048]{1,0:T(8,128)(2,1)} %add_convert_fusion.8), channel_id=1, source_target_pairs={{0,4},{2,6},{4,0},{6,2},{8,12},{10,14},{12,8},{14,10},{16,20},{18,... | collective-permute-start | bytes 6291464 | tf_op jit(solution)/shard_map/ppermute | solution.py:77
  934.4 107.9 %collective-permute-start.40 = (bf16[512,1024]{1,0:T(8,128)(2,1)}, bf16[512,1024]{1,0:T(8,128)(2,1)}, u32[]{:S(2)}, u32[]{:S(2)}) collective-permute-start(bf16[512,1024]{1,0:T(8,128)(2,1)} %add_convert_fusion.13), channel_id=1, source_target_pairs={{0,4},{2,6},{4,0},{6,2},{8,12},{10,14},{12,8},{14,10},{16,20},{18,... | collective-permute-start | bytes 3145736 | tf_op jit(solution)/shard_map/ppermute | solution.py:77
  1045.9 56.3 %reduce-scatter.14.cloned.1.call-start = ((), (), s32[]{:S(2)}) async-start(), calls=%async_computation.17 | async-start | bytes 1310720 | tf_op jit(solution)/shard_map/reduce_scatter | solution.py:108
  1046.5 100.6 %reduce-scatter.12.cloned.1.call-start = ((), (), s32[]{:S(2)}) async-start(), calls=%async_computation.16 | async-start | bytes 2621440 | tf_op jit(solution)/shard_map/reduce_scatter | solution.py:108
  1047.3 145.3 %reduce-scatter.8.cloned.1.call-start = ((), (), s32[]{:S(2)}) async-start(), calls=%async_computation.14 | async-start | bytes 2621440 | tf_op jit(solution)/shard_map/reduce_scatter | solution.py:108
  1200.7 31.0 %collective-permute-start.43 = (bf16[320,2048]{1,0:T(8,128)(2,1)S(1)}, bf16[320,2048]{1,0:T(8,128)(2,1)S(1)}, u32[]{:S(2)}, u32[]{:S(2)}) collective-permute-start(bf16[320,2048]{1,0:T(8,128)(2,1)S(1)} %fusion.8), channel_id=1, source_target_pairs={{0,1},{1,0},{2,3},{3,2},{4,5},{5,4},{6,7},{7,6},{8,9},{9,8},{10,11... | collective-permute-start | bytes 3932168 | tf_op jit(solution)/shard_map/ppermute | solution.py:80
  (106 other events, 1785.6 us)
Sparse Core Ops, SparseCore 0:
  20.8 32.4 all-gather.7
  85.6 44.8 all-gather.9
  137.7 28.7 all-gather.11
  167.9 27.4 all-gather.13
  196.8 58.6 all-gather.15
  305.6 59.8 all-gather.17
  382.2 58.9 all-gather.19
  813.7 56.8 reduce-scatter.19
  893.0 56.8 reduce-scatter.17
  952.0 56.0 reduce-scatter.15
  1046.0 28.0 reduce-scatter.9
  1076.4 25.8 reduce-scatter.13
  1104.5 42.5 reduce-scatter.11
  1149.4 43.1 reduce-scatter.7

commit v3 on v2

--- a/solution.py
+++ b/solution.py
@@ -109,18 +109,19 @@
             value, "dp", scatter_dimension=0, tiled=True, axis_index_groups=self.upper_groups
         )
 
-    def far_part(self, first_arg, second_arg):
-        half = first_arg.shape[1] // 2
-        return rows_product(first_arg[:, half:], second_arg).astype(bf16)
+    def product_part(self, first_arg, second_arg, part):
+        quarter = first_arg.shape[1] // 4
+        return rows_product(first_arg[:, part * quarter : (part + 1) * quarter], second_arg)
+
+    def far_part(self, first_arg, second_arg, part):
+        send = self.product_part(first_arg, second_arg, part).astype(bf16)
+        return self.swap_core(send), send
 
     def aside_part(self, first_arg, second_arg, far):
-        half, quarter = first_arg.shape[1] // 2, first_arg.shape[1] // 4
-        aside = rows_product(first_arg[:, quarter:half], second_arg) + far[quarter:].astype(f32)
-        return aside.astype(bf16)
+        return (self.product_part(first_arg, second_arg, 1) + far.astype(f32)).astype(bf16)
 
     def near_part(self, first_arg, second_arg, far, aside):
-        quarter = first_arg.shape[1] // 4
-        near = rows_product(first_arg[:, :quarter], second_arg) + far[:quarter].astype(f32)
+        near = self.product_part(first_arg, second_arg, 0) + far.astype(f32)
         return (near + aside.astype(f32)).astype(bf16)
 
     def flip(self, value, axis, bit):
@@ -279,11 +280,10 @@
 
 
 def backward_kernel(
-    prompt_len, top_rows, lam_ref, q_ref, kv_ref, gain_ref, vec_ref, out_ref, lse_ref, spot_ref, reach_ref,
+    prompt_len, top_rows, first_head, lam_ref, q_ref, kv_ref, gain_ref, vec_ref, out_ref, lse_ref, spot_ref, reach_ref,
     dq_ref, dkv_ref, sums_ref, one_ref, two_ref, mix_ref, grad_ref, turn_ref,
 ):
-    head = pl.program_id(0)
-    lam = lam_ref[head]
+    lam = lam_ref[first_head + pl.program_id(0)]
     rows, keys = q_ref.shape[0], kv_ref.shape[0]
     scale = DK ** (-0.5)
     out = out_ref[...]
@@ -395,6 +395,9 @@
         ],
         compiler_params=pltpu.CompilerParams(vmem_limit_bytes=56 * 2**20),
         name="attend",
+        cost_estimate=pl.CostEstimate(
+            flops=12_000_000_000, transcendentals=0, bytes_accessed=0
+        ),
     )(
         lam_vec,
         queries,
@@ -407,24 +410,26 @@
     )
 
 
-def attend_back(queries, keys_values, lam_vec, gain_rows, vec_grad, out, lse, prompt_spots, bounds, prompt_part):
-    heads = lam_vec.shape[0]
+def attend_back(
+    queries, keys_values, lam_vec, gain_rows, vec_grad, out, lse, prompt_spots, bounds, prompt_part, span
+):
+    first, heads = span[0], span[1] - span[0]
     rows, keys = queries.shape[0], keys_values.shape[0]
     prompt_len = prompt_spots.shape[0]
     top_rows = min(rows, -(-prompt_part // 128) * 128)
     count = keys // CHUNK
     reach = jnp.concatenate([jnp.stack(bounds), jnp.zeros((5, rows), jnp.int32)])
     return pl.pallas_call(
-        lambda *refs: backward_kernel(prompt_len, top_rows, *refs),
+        lambda *refs: backward_kernel(prompt_len, top_rows, first, *refs),
         grid=(heads,),
         in_specs=[
             pl.BlockSpec(memory_space=pltpu.SMEM),
-            pl.BlockSpec((rows, 2 * DK), lambda h: (0, h)),
-            pl.BlockSpec((keys, 2 * DK + DV), lambda h: (0, h)),
-            pl.BlockSpec((1, DV), lambda h: (0, h)),
-            pl.BlockSpec((rows, DV), lambda h: (0, h)),
-            pl.BlockSpec((rows, DV), lambda h: (0, h)),
-            pl.BlockSpec((1, 16, rows), lambda h: (h, 0, 0)),
+            pl.BlockSpec((rows, 2 * DK), lambda h: (0, h + first)),
+            pl.BlockSpec((keys, 2 * DK + DV), lambda h: (0, h + first)),
+            pl.BlockSpec((1, DV), lambda h: (0, h + first)),
+            pl.BlockSpec((rows, DV), lambda h: (0, h + first)),
+            pl.BlockSpec((rows, DV), lambda h: (0, h + first)),
+            pl.BlockSpec((1, 16, rows), lambda h: (h + first, 0, 0)),
             pl.BlockSpec((prompt_len, 128), lambda h: (0, 0)),
             pl.BlockSpec((8, rows), lambda h: (0, 0)),
         ],
@@ -447,6 +452,9 @@
         ],
         compiler_params=pltpu.CompilerParams(vmem_limit_bytes=58 * 2**20),
         name="attend_back",
+        cost_estimate=pl.CostEstimate(
+            flops=24_000_000_000, transcendentals=0, bytes_accessed=0
+        ),
     )(
         lam_vec,
         queries,
@@ -466,6 +474,7 @@
     rows, depth = out_ref.shape
     block = depth // count
     upper = count // 4
+    straight = swap_ref[0] == 0
 
     def norm_from(pieces):
         total = jnp.zeros((rows, 1), f32)
@@ -476,11 +485,12 @@
         size = depth // len(pieces)
         for spot in range(count):
             lanes = slice(spot * block, (spot + 1) * block)
-            high = spot % upper
-            piece = pieces[high * 4 * block // size]
-            start = blocks_ref[spot] * block - (high * 4 * block // size) * size
-            part = piece[:rows, pl.ds(pl.multiple_of(start, block), block)].astype(f32)
-            out_ref[:, lanes] = (part * inverse * gain_ref[:, lanes]).astype(bf16)
+            side = (spot % upper) * 4 * block // size
+            start = pl.multiple_of(blocks_ref[spot] * block - side * size, block)
+            part = pieces[side][:rows, pl.ds(start, block)]
+            if len(pieces) == 2:
+                part = jnp.where(straight, part, pieces[1 - side][:rows, pl.ds(start, block)])
+            out_ref[:, lanes] = (part.astype(f32) * inverse * gain_ref[:, lanes]).astype(bf16)
 
     for core in range(2):
 
@@ -493,28 +503,24 @@
         norm_from(sources[4:5])
 
 
-def norm_keys(at, prompt_two, prompt_far, tokens_all, gain_row, prompt_part):
+def norm_keys(at, prompt_groups, tokens_all, gain_row, prompt_part):
     depth = tokens_all.shape[1]
     count, upper = at.count, at.upper
     cont_len = tokens_all.shape[0] - prompt_part
-    unit = prompt_two.shape[0] // (4 * upper)
+    unit = prompt_groups[0].shape[0] // (2 * upper)
     if (depth // count) % 128 or cont_len % prompt_part or upper % 2:
         cores = []
-        for group in (prompt_two, prompt_far):
-            parts = group.reshape(2, 2 * upper, unit, depth // 2)[:, :, :prompt_part]
-            parts = parts.reshape(2, 2 * upper * prompt_part, depth // 2)
-            parts = at.flip(parts, 0, at.tensor)
+        for pair in (prompt_groups[:2], prompt_groups[2:]):
+            parts = jnp.stack([part.reshape(2 * upper, unit, -1)[:, :prompt_part] for part in pair])
+            parts = at.flip(parts.reshape(2, 2 * upper * prompt_part, depth // 2), 0, at.tensor)
             cores.append(jnp.concatenate([parts[0], parts[1]], axis=1))
         rows = at.to_relative(jnp.concatenate(cores + [tokens_all[prompt_part:]], axis=0))
         rows = rows.astype(f32)
         return (rows * inv_rms(rows, norm_eps) * gain_row).astype(bf16)
 
-    def spot_of(core, half):
+    def spot_of(core):
         first = core * 2 * upper
-        return lambda i, blocks, swap: (
-            (swap[0] ^ half) * 2 * upper + jnp.clip(i - first, 0, 2 * upper - 1),
-            0,
-        )
+        return lambda i, blocks, swap: (jnp.clip(i - first, 0, 2 * upper - 1), 0)
 
     return pl.pallas_call(
         lambda *refs: norm_kernel(count, *refs),
@@ -522,9 +528,7 @@
             num_scalar_prefetch=2,
             grid=(count + cont_len // prompt_part,),
             in_specs=[
-                pl.BlockSpec((unit, depth // 2), spot_of(core, half))
-                for core in range(2)
-                for half in range(2)
+                pl.BlockSpec((unit, depth // 2), spot_of(core)) for core in (0, 0, 1, 1)
             ]
             + [
                 pl.BlockSpec(
@@ -537,13 +541,11 @@
         ),
         out_shape=jax.ShapeDtypeStruct((prompt_part * count + cont_len, depth), bf16),
         name="norm_keys",
+        cost_estimate=pl.CostEstimate(flops=8_000_000_000, transcendentals=0, bytes_accessed=0),
     )(
         at.relative_blocks(),
         at.tensor.reshape(1).astype(jnp.int32),
-        prompt_two,
-        prompt_two,
-        prompt_far,
-        prompt_far,
+        *prompt_groups,
         tokens_all,
         gain_row.reshape(1, depth),
     )
@@ -607,24 +609,29 @@
 
     tokens_rel = at.to_relative(tokens)
     cot_rel = at.to_relative(cotangent)
-    prompt_here, tokens_rel, cot_rel = together(prompt_here, tokens_rel, cot_rel)
+    tokens_turned = at.swap_tensor(after(tokens, prompt_own))
+    prompt_here, tokens_rel, cot_rel, tokens_turned = together(
+        prompt_here, tokens_rel, cot_rel, tokens_turned
+    )
     prompt_pair = jnp.concatenate([prompt_here, at.swap_side(prompt_here)], axis=0)
     prompt_turned = at.swap_tensor(prompt_pair)
+    prompt_far = at.swap_core(prompt_pair)
     kv_here = after(kv_here, prompt_pair)
     kv_side, kv_near = at.swap_side(kv_here), at.swap_core(kv_here)
-    tokens_turned = at.swap_tensor(after(tokens, prompt_turned))
-    prompt_two = jnp.concatenate([prompt_pair, prompt_turned], axis=0)
-    prompt_far = at.swap_core(prompt_two)
-    prompt_far, kv_side = together(prompt_far, kv_side)
+    prompt_turned, kv_side_early = together(prompt_turned, kv_near)
+    kv_near = kv_side_early
+    prompt_far_turned = at.swap_core(prompt_turned)
+    kv_side, q_here = together(kv_side, q_here)
     kv_far = at.swap_core(kv_side)
-    q_here = after(q_here, kv_side)
     q_side, q_near = at.swap_side(q_here), at.swap_core(q_here)
+    prompt_far, prompt_far_turned = together(prompt_far, after(prompt_far_turned, kv_side))
     tokens_all = at.in_order(tokens, tokens_turned)
+    cot_turned = at.swap_tensor(after(cot_rel, prompt_far_turned))
 
     small_all = jnp.concatenate(
         [
-            group.reshape(2, 2 * at.upper, -1, half)[0, :, prompt_part, : small.size]
-            for group in (prompt_two, prompt_far)
+            group.reshape(2 * at.upper, -1, half)[:, prompt_part, : small.size]
+            for group in (prompt_pair, prompt_far)
         ],
         axis=0,
     ).astype(f32)
@@ -662,30 +669,35 @@
     )
 
     tokens_f32 = tokens_rel.astype(f32)
-    normed_keys = norm_keys(at, prompt_two, prompt_far, tokens_all, attn_gain_row, prompt_part)
-    normed_keys, kv_far, kv_near = together(normed_keys, kv_far, kv_near)
+    prompt_groups = (prompt_pair, prompt_turned, prompt_far, prompt_far_turned)
+    normed_keys = norm_keys(at, prompt_groups, tokens_all, attn_gain_row, prompt_part)
+    kv_near, kv_far = after(kv_near, normed_keys), after(kv_far, normed_keys)
+    kv_full = jnp.concatenate([kv_here, kv_side, kv_near, kv_far], axis=0)
+    kv_full, q_side, out_here = together(kv_full, q_side, out_here)
+    q_far = at.swap_core(q_side)
+    out_side, out_near = at.swap_side(out_here), at.swap_core(out_here)
     own_block = lax.dynamic_slice_in_dim(
         normed_keys, (at.index // 4) * prompt_part, prompt_part, 0
     )
     normed = jnp.concatenate([own_block, normed_keys[prompt_len:]], axis=0)
-    kv_full = jnp.concatenate([kv_here, kv_side, kv_near, kv_far], axis=0)
     keys_values = plain_product(normed_keys, kv_full).astype(bf16)
-    keys_values, normed, q_side, q_near = together(keys_values, normed, q_side, q_near)
-    q_far = at.swap_core(q_side)
-    out_here = after(out_here, q_side)
-    out_side, out_near = at.swap_side(out_here), at.swap_core(out_here)
+    q_near, q_far = after(q_near, keys_values), after(q_far, keys_values)
     q_full = jnp.concatenate([q_here, q_side, q_near, q_far], axis=0)
-    queries = plain_product(normed, q_full).astype(bf16)
+    queries = plain_product(after(normed, keys_values), q_full).astype(bf16)
     fixed = (lam_vec, head_gain_row, prompt_spots, bounds, prompt_part)
     middle = heads // 2
-    first_out, first_vec, first_lse = attend(queries, keys_values, *fixed, (0, middle))
-    first_vec, out_side, out_near, gate_here = together(first_vec, out_side, out_near, gate_here)
+    queries, out_side, gate_here = together(queries, out_side, gate_here)
     out_far = at.swap_core(out_side)
     gate_side, gate_near = at.swap_side(gate_here), at.swap_core(gate_here)
+    first_out, first_vec, first_lse = attend(queries, keys_values, *fixed, (0, middle))
+    first_vec, cot_turned = together(first_vec, cot_turned)
     second_out, second_vec, second_lse = attend(
         after(queries, first_vec), keys_values, *fixed, (middle, heads)
     )
-    second_vec, out_far, gate_near = together(second_vec, out_far, gate_near)
+    second_vec, up_here, gate_side = together(second_vec, up_here, gate_side)
+    up_side, up_near = at.swap_side(up_here), at.swap_core(up_here)
+    gate_far = at.swap_core(gate_side)
+    out_near, out_far = after(out_near, second_vec), after(out_far, second_vec)
     heads_out = jnp.concatenate([first_out, second_out], axis=1)
     lse = jnp.concatenate([first_lse, second_lse], axis=0)
     attn_vec = jnp.concatenate([first_vec, second_vec], axis=1)
@@ -695,38 +707,39 @@
     out_sent = at.swap_tensor(out_send)
     out_part = cols_product(after(attn_own, out_send), out_full)
     attn_two = jnp.concatenate([attn_own, attn_other], axis=0)
-    out_sent, out_part, gate_side, up_here, attn_two = together(
-        out_sent, out_part, gate_side, up_here, attn_two
-    )
-    gate_far = at.swap_core(gate_side)
-    up_side, up_near = at.swap_side(up_here), at.swap_core(up_here)
+    out_part, attn_two = together(out_part, attn_two)
+    out_sent = after(out_sent, out_part)
     residual = tokens_f32 + (out_part + out_sent.astype(f32))
 
     inv_second = inv_rms(residual, norm_eps)
     ffn_own = (residual * inv_second * ffn_gain_row).astype(bf16)
     ffn_turned = at.swap_tensor(ffn_own)
-    cot_turned = at.swap_tensor(after(cot_rel, ffn_own))
-    ffn_turned, gate_far, up_near = together(ffn_turned, gate_far, up_near)
-    ffn_in = jnp.concatenate([ffn_own, ffn_turned], axis=0)
-    cot_rows = jnp.concatenate([cot_rel, cot_turned], axis=0)
+    gate_near, gate_far = after(gate_near, ffn_own), after(gate_far, ffn_own)
     gate_full = jnp.concatenate([gate_here, gate_side, gate_near, gate_far], axis=0)
-    gate_proj = plain_product(ffn_in, gate_full)
-    gate_proj, up_side, down_here, cot_rows = together(gate_proj, up_side, down_here, cot_rows)
+    gate_full, down_here, up_side = together(gate_full, down_here, up_side)
     up_far = at.swap_core(up_side)
     down_side, down_near = at.swap_side(down_here), at.swap_core(down_here)
+    ffn_turned = after(ffn_turned, gate_full)
+    ffn_in = jnp.concatenate([ffn_own, ffn_turned], axis=0)
+    gate_proj = plain_product(ffn_in, gate_full)
+    cot_rows = jnp.concatenate([cot_rel, cot_turned], axis=0)
+    up_near, up_far = after(up_near, gate_proj), after(up_far, gate_proj)
     up_full = jnp.concatenate([up_here, up_side, up_near, up_far], axis=0)
-    up_proj = plain_product(ffn_in, up_full)
+    up_proj = plain_product(after(ffn_in, gate_proj), up_full)
     gate_sigmoid = jax.nn.sigmoid(gate_proj)
     hidden = (gate_proj * gate_sigmoid * up_proj).astype(bf16)
 
-    down_send = at.far_part(cot_rows, hidden)
-    down_grad_far = at.swap_core(down_send)
-    down_send, down_side, down_near = together(down_send, down_side, down_near)
+    down_far_aside, down_send = at.far_part(cot_rows, hidden, 3)
+    down_far_keep, down_send = at.far_part(cot_rows, after(hidden, down_send), 2)
+    down_send, down_side = together(down_send, down_side)
+    down_near = after(down_near, down_side)
     down_far = at.swap_core(down_side)
-    down_grad_side = at.aside_part(cot_rows, hidden, after(down_grad_far, down_side))
+    down_far_aside = after(down_far_aside, down_side)
+    down_grad_side = at.aside_part(cot_rows, hidden, down_far_aside)
     down_grad_aside = at.swap_side(down_grad_side)
+    down_near, down_far = after(down_near, down_grad_side), after(down_far, down_grad_side)
     down_full = jnp.concatenate([down_here, down_side, down_near, down_far], axis=0)
-    hidden_grad = plain_product(after(cot_rows, down_grad_side), down_full)
+    hidden_grad = plain_product(cot_rows, down_full)
     gate_grad = (
         hidden_grad * up_proj * gate_sigmoid * (1.0 + gate_proj * (1.0 - gate_sigmoid))
     ).astype(bf16)
@@ -735,100 +748,105 @@
     def back_ffn(one, two):
         return cols_product(one, gate_full) + cols_product(two, up_full)
 
-    ffn_send = back_ffn(gate_grad[local_rows:], up_grad[local_rows:]).astype(bf16)
+    gate_far_aside, gate_send = at.far_part(ffn_in, gate_grad, 3)
+    ffn_send = back_ffn(
+        after(gate_grad[local_rows:], gate_send), up_grad[local_rows:]
+    ).astype(bf16)
     ffn_sent = at.swap_tensor(ffn_send)
-    gate_send = at.far_part(ffn_in, after(gate_grad, ffn_send))
-    gate_grad_far = at.swap_core(gate_send)
-    ffn_part = back_ffn(after(gate_grad[:local_rows], gate_send), up_grad[:local_rows])
-    ffn_part, ffn_sent, gate_grad_far = together(ffn_part, ffn_sent, gate_grad_far)
-    ffn_in_grad = ffn_part + ffn_sent.astype(f32)
+    ffn_part = back_ffn(after(gate_grad[:local_rows], ffn_send), up_grad[:local_rows])
+    gate_far_aside = after(gate_far_aside, ffn_part)
+    gate_grad_side = at.aside_part(ffn_in, gate_grad, gate_far_aside)
+    gate_grad_aside = at.swap_side(gate_grad_side)
+    down_grad_aside = after(down_grad_aside, gate_grad_side)
+    ffn_in_grad = ffn_part + after(ffn_sent, down_grad_aside).astype(f32)
     residual_grad = cot_rel.astype(f32) + norm_back(
         residual, inv_second, ffn_gain_row, ffn_in_grad
     )
 
     branch_own = residual_grad.astype(bf16)
     branch_sent = at.swap_tensor(branch_own)
-    gate_grad_side = at.aside_part(ffn_in, gate_grad, after(gate_grad_far, branch_own))
-    up_send = at.far_part(ffn_in, after(up_grad, gate_grad_side))
-    up_grad_far = at.swap_core(up_send)
-    up_send, branch_sent, down_grad_aside = together(up_send, branch_sent, down_grad_aside)
-    gate_grad_aside = at.swap_side(after(gate_grad_side, down_grad_aside))
-    branch = jnp.concatenate([branch_own, branch_sent], axis=0)
-    out_grad_send = at.far_part(branch, attn_two)
-    out_grad_far = at.swap_core(out_grad_send)
-    down_last = at.near_part(
-        cot_rows, after(hidden, out_grad_send), down_grad_far, down_grad_aside
-    )
+    down_far_keep = after(down_far_keep, branch_own)
+    down_last = at.near_part(cot_rows, hidden, down_far_keep, down_grad_aside)
     grad_down = at.scatter_upper(down_last)
-    up_grad_side = at.aside_part(ffn_in, after(up_grad, down_last), up_grad_far)
-    up_grad_aside = at.swap_side(up_grad_side)
-    vec_two = plain_product(after(branch, up_grad_side), out_full)
-    out_grad_side = at.aside_part(branch, after(attn_two, vec_two), out_grad_far)
-    out_grad_aside = at.swap_side(out_grad_side)
+    up_far_aside, up_send = at.far_part(ffn_in, after(up_grad, down_last), 3)
+    up_far_keep, up_send = at.far_part(ffn_in, after(up_grad, up_send), 2)
+    gate_far_keep, gate_send = at.far_part(ffn_in, after(gate_grad, up_send), 2)
+    up_far_aside = after(up_far_aside, gate_send)
+    up_grad_side = at.aside_part(ffn_in, up_grad, up_far_aside)
+    branch = jnp.concatenate([branch_own, after(branch_sent, up_grad_side)], axis=0)
+    vec_two = plain_product(branch, out_full)
     vec_grad = at.in_order(vec_two[:local_rows], vec_two[local_rows:])
+    vec_grad, gate_far_keep, gate_grad_aside = together(vec_grad, gate_far_keep, gate_grad_aside)
+    up_grad_aside = at.swap_side(after(up_grad_side, gate_grad_aside))
+    gate_last = at.near_part(ffn_in, gate_grad, gate_far_keep, gate_grad_aside)
+    grad_gate = at.scatter_upper(gate_last)
     queries_grad, kv_grad, head_sums = attend_back(
         queries,
         keys_values,
         lam_vec,
         head_gain_row,
-        after(vec_grad, out_grad_side),
+        after(vec_grad, gate_last),
         heads_out,
         lse,
         prompt_spots,
         bounds,
         prompt_part,
-    )
-    queries_grad, kv_grad, head_sums, gate_grad_aside = together(
-        queries_grad, kv_grad, head_sums, gate_grad_aside
+        (0, heads),
+    )
+    queries_grad, kv_grad, head_sums, grad_down = together(
+        queries_grad, kv_grad, head_sums, grad_down
     )
     queries_grad = queries_grad.T
 
-    two, four = prompt_len // 2, prompt_len // 4
-    prompt_send = kv_grad[two:prompt_len]
-    prompt_grad_far = at.swap_core(prompt_send)
-    kv_send = at.far_part(normed_keys, after(kv_grad, prompt_send))
-    kv_grad_far = at.swap_core(kv_send)
-    kv_send, prompt_grad_far = together(kv_send, prompt_grad_far)
-    prompt_side = (kv_grad[four:two].astype(f32) + prompt_grad_far[four:].astype(f32)).astype(bf16)
+    quarter = prompt_len // 4
+
+    def prompt_rows(part):
+        return kv_grad[part * quarter : (part + 1) * quarter]
+
+    prompt_send = prompt_rows(3)
+    prompt_far_aside = at.swap_core(prompt_send)
+    prompt_keep = after(prompt_rows(2), prompt_send)
+    prompt_far_keep = at.swap_core(prompt_keep)
+    kv_far_aside, kv_send = at.far_part(normed_keys, after(kv_grad, prompt_keep), 3)
+    kv_send, up_far_keep, up_grad_aside = together(kv_send, up_far_keep, up_grad_aside)
+    prompt_far_aside = after(prompt_far_aside, up_grad_aside)
+    prompt_side = (prompt_rows(1).astype(f32) + prompt_far_aside.astype(f32)).astype(bf16)
     prompt_aside = at.swap_side(prompt_side)
-    gate_last = at.near_part(
-        ffn_in, after(gate_grad, prompt_side), gate_grad_far, gate_grad_aside
-    )
-    grad_gate = at.scatter_upper(gate_last)
-    gate_last, kv_grad_far = together(gate_last, kv_grad_far)
-    kv_grad_side = at.aside_part(normed_keys, kv_grad, kv_grad_far)
+    up_last = at.near_part(ffn_in, after(up_grad, prompt_side), up_far_keep, up_grad_aside)
+    up_last, grad_gate = together(up_last, grad_gate)
+    grad_up = at.scatter_upper(up_last)
+    kv_far_keep, kv_send = at.far_part(normed_keys, after(kv_grad, up_last), 2)
+    kv_far_aside = after(kv_far_aside, kv_send)
+    kv_grad_side = at.aside_part(normed_keys, kv_grad, kv_far_aside)
     kv_grad_aside = at.swap_side(kv_grad_side)
-    q_send = at.far_part(normed, after(queries_grad, kv_grad_side))
-    q_grad_far = at.swap_core(q_send)
-    up_last = at.near_part(ffn_in, up_grad, up_grad_far, after(up_grad_aside, q_send))
-    grad_up = at.scatter_upper(up_last)
-    q_grad_side = at.aside_part(normed, queries_grad, after(q_grad_far, up_last))
-    q_grad_aside = at.swap_side(q_grad_side)
-
-    hidden_late = after(hidden, q_grad_side)
-    output_send = cols_product(hidden_late[local_rows:], down_full).astype(bf16)
-    output_sent = at.swap_tensor(output_send)
+    q_far_aside, q_send = at.far_part(normed, after(queries_grad, kv_grad_side), 3)
+    q_far_keep, q_send = at.far_part(normed, after(queries_grad, q_send), 2)
+    out_far_aside, out_send_grad = at.far_part(branch, after(attn_two, q_send), 3)
+    out_far_keep, out_send_grad = at.far_part(branch, after(attn_two, out_send_grad), 2)
+    hidden_late = after(hidden, out_send_grad)
     output_part = cols_product(hidden_late[:local_rows], down_full)
-    output_part, output_sent, prompt_aside = together(output_part, output_sent, prompt_aside)
-    output = at.from_relative((residual + (output_part + output_sent.astype(f32))).astype(bf16))
-
+    prompt_far_keep, prompt_aside = together(after(prompt_far_keep, output_part), prompt_aside)
     prompt_last = (
-        kv_grad[:four].astype(f32)
-        + prompt_grad_far[:four].astype(f32)
-        + prompt_aside.astype(f32)
+        prompt_rows(0).astype(f32) + prompt_far_keep.astype(f32) + prompt_aside.astype(f32)
     ).astype(bf16)
     prompt_grad = at.scatter_upper(prompt_last)
-    out_last = at.near_part(
-        branch, after(attn_two, prompt_last), out_grad_far, out_grad_aside
-    )
-    grad_out = at.scatter_upper(out_last)
-    kv_last = at.near_part(
-        normed_keys, kv_grad, kv_grad_far, after(kv_grad_aside, out_last)
-    )
+    q_far_aside = after(q_far_aside, prompt_last)
+    q_grad_side = at.aside_part(normed, queries_grad, q_far_aside)
+    q_grad_aside = at.swap_side(q_grad_side)
+    out_far_aside = after(out_far_aside, q_grad_side)
+    out_grad_side = at.aside_part(branch, attn_two, out_far_aside)
+    out_grad_aside = at.swap_side(out_grad_side)
+    output_send = cols_product(after(hidden_late, out_grad_side)[local_rows:], down_full).astype(bf16)
+    output_sent = at.swap_tensor(output_send)
+    kv_far_keep, kv_grad_aside = together(after(kv_far_keep, output_send), kv_grad_aside)
+    kv_last = at.near_part(normed_keys, kv_grad, kv_far_keep, kv_grad_aside)
     grad_kv = at.scatter_upper(kv_last)
-    q_last = at.near_part(normed, queries_grad, q_grad_far, after(q_grad_aside, kv_last))
+    output_sent, grad_up, q_far_keep = together(after(output_sent, kv_last), grad_up, q_far_keep)
+    q_far_keep, q_grad_aside = together(q_far_keep, q_grad_aside)
+    q_last = at.near_part(normed, queries_grad, q_far_keep, q_grad_aside)
     grad_q = at.scatter_upper(q_last)
-    here_grad = jnp.concatenate([after(prompt_grad, q_last), kv_grad[prompt_len:]], axis=0)
+    prompt_grad = after(prompt_grad, q_last)
+    here_grad = jnp.concatenate([prompt_grad, kv_grad[prompt_len:]], axis=0)
 
     def back_attn(half_of):
         return cols_product(half_of(queries_grad), q_full) + cols_product(
@@ -837,10 +855,15 @@
 
     normed_send = back_attn(at.other_half).astype(bf16)
     normed_sent = at.swap_tensor(normed_send)
-    normed_grad = back_attn(at.own_half) + normed_sent.astype(f32)
+    out_far_keep, out_grad_aside = together(after(out_far_keep, normed_send), out_grad_aside)
+    out_last = at.near_part(branch, attn_two, out_far_keep, out_grad_aside)
+    grad_out = at.scatter_upper(out_last)
+    normed_part = back_attn(lambda rows: at.own_half(after(rows, out_last)))
+    normed_grad = normed_part + normed_sent.astype(f32)
     inv_first = inv_rms(tokens_f32, norm_eps)
     tokens_grad = residual_grad + norm_back(tokens_f32, inv_first, attn_gain_row, normed_grad)
     tokens_grad = at.from_relative(tokens_grad.astype(bf16))
+    output = at.from_relative((residual + (output_part + output_sent.astype(f32))).astype(bf16))
 
     def row_sum(grad, weight):
         return jnp.sum(grad.astype(f32) * weight.astype(f32), axis=1)
@@ -864,7 +887,7 @@
         grad_q,
         grad_k,
         grad_v,
-        grad_out.astype(f32),
+        after(grad_out, attn_gain_sum).astype(f32),
         attn_gain_sum / attn_gain.astype(f32),
         grad_head_gain,
         one_scale * lam_k1.astype(f32),

time: 1260 us -> 966 us (0.77)
  waiting for transfers between devices: 573 us -> 283 us
  local copies, waits for them, and re-layouts: 129 us -> 113 us
    ppermute x14, waiting for transfers between devices: 291 us -> 153 us  [swap_side(): return lax.ppermute(value, 'dp', self.side_pairs)]
    reduce_scatter x7, waiting for transfers between devices: 105 us -> 0.05 us  [scatter_upper(): lax.psum_scatter(value, 'dp', scatter_dimension=0, tiled=True, axis_index...]
    ppermute x11, waiting for transfers between devices: 143 us -> 106 us  [swap_tensor(): return lax.ppermute(value, 'tensor', [(0, 1), (1, 0)])]
    concatenate x2 -> x4, other arithmetic: 4.01 us -> 23.5 us  [the longest x1 14.5 us: per_device(): jnp.concatenate([gate_here, gate_side, gate_near, gate_far], axis=0)]
    convert_element_type x5 -> x3, other arithmetic: 24.9 us -> 9.94 us  [near_part(): return (near + aside.astype(f32)).astype(bf16)]
    unnamed x209 -> x206, local copies, waits for them, and re-layouts: 61 us -> 46.5 us
    dot_general x18 -> x24, matrix products: 111 us -> 115 us  [rows_product(): lax.dot_general(first_arg, second_arg, (((0,), (0,)), ((), ())), preferre...]
  transfers between devices with their start and end apart: 64 -> 72, of which waited for: 24 -> 21; matrix products, arithmetic and copies ran while one was open for 30% -> 48% of each run, Pallas kernels for 10% -> 14%
where the time goes in v3:
time: 966 us; the launch traced here: 956 us
  waiting for transfers between devices  283 us (29%)
  matrix products  283 us (29%)
  Pallas kernels  132 us (14%)
  local copies, waits for them, and re-layouts  113 us (12%)
  other arithmetic  88.5 us (9%)
  starting transfers between devices  41.5 us (4%)
  between operations  15.9 us (2%)
    ppermute x14, waiting for transfers between devices, swap_side(): return lax.ppermute(value, 'dp', self.side_pairs)  153 us
    dot_general x24, matrix products, rows_product(): lax.dot_general(first_arg, second_arg, (((0,), (0,)), ((), ())), preferre...  115 us
    ppermute x11, waiting for transfers between devices, swap_tensor(): return lax.ppermute(value, 'tensor', [(0, 1), (1, 0)])  106 us
    dot_general x12, matrix products, cols_product(): lax.dot_general(first_arg, second_arg, (((1,), (1,)), ((), ())), preferre...  87.4 us
    dot_general x6, matrix products, plain_product(): return jnp.dot(first_arg, second_arg, preferred_element_type=f32)  80 us
    pallas_call x2, Pallas kernels, attend(): pl.pallas_call(lambda *refs: forward_kernel(prompt_len, top_rows, first,...  58.9 us
    pallas_call x1, Pallas kernels, attend_back(): pl.pallas_call(lambda *refs: backward_kernel(prompt_len, top_rows, first,...  53.1 us
    unnamed x206, local copies, waits for them, and re-layouts  46.5 us
  transfers between devices with their start and end apart: 72, of which 21 were waited for; matrix products, arithmetic and copies ran while one was open for 48% of the time, Pallas kernels for 14%

profile of v3, /device:TPU:0, one launch (start us, length us, event | category | flops | bytes accessed | tf_op | source)
XLA Modules:
  0.0 955.6 jit_solution(6961532932233482127)
XLA Ops:
  8.2 4.9 collective-permute-start
  43.9 11.9 %collective-permute-done.1 = bf16[320,2048]{1,0:T(8,128)(2,1)} collective-permute-done((bf16[320,2048]{1,0:T(8,128)(2,1)}, bf16[320,2048]{1,0:T(8,128)(2,1)}, u32[]{:S(2)}, u32[]{:S(2)}) %collective-permute-start.1) | collective-permute-done | bytes 1310752 | tf_op jit(solution)/shard_map/ppermute | solution.py:80
  59.7 22.6 %collective-permute-done.2 = bf16[576,1024]{1,0:T(8,128)(2,1)} collective-permute-done((bf16[576,1024]{1,0:T(8,128)(2,1)}, bf16[576,1024]{1,0:T(8,128)(2,1)}, u32[]{:S(2)}, u32[]{:S(2)}) %collective-permute-start.2) | collective-permute-done | bytes 1179680 | tf_op jit(solution)/shard_map/ppermute | solution.py:77
  86.0 14.4 %all-gather.10.cloned.1.call-done = bf16[512,2048]{1,0:T(8,128)(2,1)} async-done(((bf16[128,2048]{1,0:T(8,128)(2,1)}), bf16[512,2048]{1,0:T(8,128)(2,1)}) %all-gather.10.cloned.1.call-update) | async-done | bytes 2097168 | tf_op jit(solution)/shard_map/all_gather | solution.py:83
  104.9 30.7 %collective-permute-done.4.refs_3_ = bf16[1152,1024]{1,0:T(8,128)(2,1)} collective-permute-done((bf16[1152,1024]{1,0:T(8,128)(2,1)}, bf16[1152,1024]{1,0:T(8,128)(2,1)}, u32[]{:S(2)}, u32[]{:S(2)}) %collective-permute-start.4) | collective-permute-done | bytes 2359328 | tf_op jit(solution)/shard_map/ppermute | solution.py:80
  136.4 12.4 %collective-permute-done.7 = bf16[512,2048]{1,0:T(8,128)(2,1)} collective-permute-done((bf16[512,2048]{1,0:T(8,128)(2,1)}, bf16[512,2048]{1,0:T(8,128)(2,1)}, u32[]{:S(2)}, u32[]{:S(2)}) %collective-permute-start.7) | collective-permute-done | bytes 2097184 | tf_op jit(solution)/shard_map/ppermute | solution.py:77
  161.1 19.5 %norm_keys.1 = bf16[2560,2048]{1,0:T(8,128)(2,1)} custom-call(s32[16]{0:T(128)} %get-tuple-element.289.refs_0_, s32[1]{0:T(128)} %bitcast.6.refs_1_, bf16[1152,1024]{1,0:T(8,128)(2,1)} %constant_dynamic-update-slice_fusion.refs_2_, bf16[1152,1024]{1,0:T(8,128)(2,1)} %collective-permute-done.4.refs_3_, bf16[1152,1024]{1,0:T(8,128)(2,1)} %collective-permute-done.3.refs_4_, ...), custom_call_target="tpu_custom_call" | custom-call | flops 8000000000 | tf_op jit(solution)/shard_map/norm_keys/pallas_call | solution.py:525
  180.7 7.0 pad_maximum_fusion.1
  188.5 27.9 %convolution_convert_fusion.refs_2_ = bf16[2560,2048]{1,0:T(8,128)(2,1)} fusion(bf16[2560,2048]{1,0:T(8,128)(2,1)} %norm_keys.1, bf16[2048,2048]{1,0:T(8,128)(2,1)} %pad_maximum_fusion.1), kind=kOutput, calls=%fused_computation.1 | convolution fusion | flops 21480079360 | bytes 29360128 | tf_op jit(solution)/shard_map/dot_general | solution.py:33
  244.8 29.2 %attend.2 = (f32[640,512]{1,0:T(8,128)}, bf16[640,512]{1,0:T(8,128)(2,1)}, f32[2,16,640]{2,1,0:T(8,128)}) custom-call(f32[4]{0:T(128)} %subtract_add_fusion.1.refs_0_, bf16[640,1024]{1,0:T(8,128)(2,1)} %convolution_convert_fusion.11.refs_1_, bf16[2560,2048]{1,0:T(8,128)(2,1)} %convolution_convert_fusion.refs_2_, f32[1,1024]{1,0:T(1,128)} %bitcast.120, ...), custom_call_target="tpu_custom_call" | custom-call | flops 12000000000 | tf_op jit(solution)/shard_map/attend/pallas_call | solution.py:368
  276.0 29.8 %attend.3 = (f32[640,512]{1,0:T(8,128)}, bf16[640,512]{1,0:T(8,128)(2,1)}, f32[2,16,640]{2,1,0:T(8,128)}) custom-call(f32[4]{0:T(128)} %subtract_add_fusion.1.refs_0_, bf16[640,1024]{1,0:T(8,128)(2,1)} %convolution_convert_fusion.11.refs_1_, bf16[2560,2048]{1,0:T(8,128)(2,1)} %convolution_convert_fusion.refs_2_, f32[1,1024]{1,0:T(1,128)} %bitcast.121, ...), custom_call_target="tpu_custom_call" | custom-call | flops 12000000000 | tf_op jit(solution)/shard_map/attend/pallas_call | solution.py:368
  322.4 23.3 %collective-permute-done.17 = bf16[320,2048]{1,0:T(8,128)(2,1)S(1)} collective-permute-done((bf16[320,2048]{1,0:T(8,128)(2,1)S(1)}, bf16[320,2048]{1,0:T(8,128)(2,1)S(1)}, u32[]{:S(2)}, u32[]{:S(2)}) %collective-permute-start.17) | collective-permute-done | bytes 1310752 | tf_op jit(solution)/shard_map/ppermute | solution.py:80
  349.1 14.5 %pad_maximum_fusion = bf16[2048,2816]{1,0:T(8,128)(2,1)} fusion(bf16[512,2816]{1,0:T(8,128)(2,1)S(1)} %collective-permute-done.20, bf16[512,2816]{1,0:T(8,128)(2,1)} %collective-permute-done.19, bf16[512,2816]{1,0:T(8,128)(2,1)} %collective-permute-done.14, bf16[512,2816]{1,0:T(8,128)(2,1)S(1)} %copy-done.42), kind=kLoop, calls=%fused_computation | loop fusion | flops 46137344 | bytes 23068672 | tf_op jit(solution)/shard_map/concatenate | solution.py:718
  363.6 20.2 %collective-permute-done.21 = bf16[512,2816]{1,0:T(8,128)(2,1)} collective-permute-done((bf16[512,2816]{1,0:T(8,128)(2,1)}, bf16[512,2816]{1,0:T(8,128)(2,1)}, u32[]{:S(2)}, u32[]{:S(2)}) %collective-permute-start.21) | collective-permute-done | bytes 2883616 | tf_op jit(solution)/shard_map/ppermute | solution.py:77
  388.4 13.1 %fusion.131 = f32[640,2816]{1,0:T(8,128)} fusion(bf16[2048,2816]{1,0:T(8,128)(2,1)} %pad_maximum_fusion, bf16[320,2048]{1,0:T(8,128)(2,1)S(1)} %collective-permute-done.18, bf16[320,2048]{1,0:T(8,128)(2,1)S(1)} %multiply_convert_fusion.3), kind=kOutput, calls=%fused_computation.282 | convolution fusion | flops 7387217920 | bytes 21364736 | tf_op jit(solution)/shard_map/dot_general | solution.py:33
  410.6 14.9 %multiply_convert_fusion.2 = (bf16[640,2816]{1,0:T(8,128)(2,1)S(1)}, f32[640,2816]{1,0:T(8,128)}) fusion(f32[640,2816]{1,0:T(8,128)} %fusion.131, bf16[640,2048]{1,0:T(8,128)(2,1)S(1)} %pad_maximum_fusion.3, bf16[2048,2816]{1,0:T(8,128)(2,1)} %constant_dynamic-update-slice_fusion.12), kind=kOutput, calls=%fused_computation.5 | convolution fusion | flops 7392788480 | bytes 32178176 | tf_op jit(solution)/shard_map/dot_general | solution.py:33
  430.0 5.3 convolution_convert_fusion.5
  435.3 17.1 %collective-permute-done.24 = bf16[512,2816]{1,0:T(8,128)(2,1)S(1)} collective-permute-done((bf16[512,2816]{1,0:T(8,128)(2,1)S(1)}, bf16[512,2816]{1,0:T(8,128)(2,1)S(1)}, u32[]{:S(2)}, u32[]{:S(2)}) %collective-permute-start.24) | collective-permute-done | bytes 2883616 | tf_op jit(solution)/shard_map/ppermute | solution.py:77
  453.3 5.2 add_convert_fusion.5
  463.8 17.0 %multiply_convert_fusion.1 = (bf16[640,2816]{1,0:T(8,128)(2,1)S(1)}, bf16[640,2816]{1,0:T(8,128)(2,1)S(1)}) fusion(f32[640,2816]{1,0:T(8,128)} %fusion.131, f32[640,2816]{1,0:T(8,128)} %get-tuple-element.321, bf16[640,2048]{1,0:T(8,128)(2,1)} %constant_dynamic-update-slice_fusion.16, bf16[2048,2816]{1,0:T(8,128)(2,1)} %copy-done.54), kind=kOutput, calls=%fused_computation.4 | convolution fusion | flops 7405404160 | bytes 35782656 | tf_op jit(solution)/shard_map/dot_general | solution.py:33
  487.3 8.6 fusion.18
  495.9 10.5 %fusion.2 = bf16[320,2048]{1,0:T(8,128)(2,1)} fusion(f32[320,2048]{1,0:T(8,128)} %fusion.18, bf16[320,2816]{1,0:T(8,128)(2,1)} %get-tuple-element.211, bf16[2048,2816]{1,0:T(8,128)(2,1)} %pad_maximum_fusion), kind=kOutput, calls=%fused_computation.60 | convolution fusion | flops 3692298240 | bytes 17268736 | tf_op jit(solution)/shard_map/dot_general | solution.py:43
  507.8 8.6 fusion.16
  516.4 13.9 %convolution_add_fusion.2 = f32[320,2048]{1,0:T(8,128)} fusion(f32[320,2048]{1,0:T(8,128)} %fusion.16, bf16[320,2816]{1,0:T(8,128)(2,1)S(1)} %get-tuple-element.212, bf16[2048,2816]{1,0:T(8,128)(2,1)} %pad_maximum_fusion), kind=kOutput, calls=%fused_computation.58 | convolution fusion | flops 3691642880 | bytes 18579456 | tf_op jit(solution)/shard_map/dot_general | solution.py:43
  530.3 6.0 add_convert_fusion.4
  536.3 15.2 %collective-permute-done.29 = bf16[512,2816]{1,0:T(8,128)(2,1)} collective-permute-done((bf16[512,2816]{1,0:T(8,128)(2,1)}, bf16[512,2816]{1,0:T(8,128)(2,1)}, u32[]{:S(2)}, u32[]{:S(2)}) %collective-permute-start.29) | collective-permute-done | bytes 2883616 | tf_op jit(solution)/shard_map/ppermute | solution.py:77
  555.1 7.3 add_convert_fusion.3
  562.6 4.6 convolution_convert_fusion.3
  584.0 21.8 %collective-permute-done.31 = bf16[320,2048]{1,0:T(8,128)(2,1)S(1)} collective-permute-done((bf16[320,2048]{1,0:T(8,128)(2,1)S(1)}, bf16[320,2048]{1,0:T(8,128)(2,1)S(1)}, u32[]{:S(2)}, u32[]{:S(2)}) %collective-permute-start.31) | collective-permute-done | bytes 1310752 | tf_op jit(solution)/shard_map/ppermute | solution.py:80
  611.2 27.8 %collective-permute-done.35 = bf16[512,2816]{1,0:T(8,128)(2,1)S(1)} collective-permute-done((bf16[512,2816]{1,0:T(8,128)(2,1)S(1)}, bf16[512,2816]{1,0:T(8,128)(2,1)S(1)}, u32[]{:S(2)}, u32[]{:S(2)}) %collective-permute-start.35) | collective-permute-done | bytes 2883616 | tf_op jit(solution)/shard_map/ppermute | solution.py:77
  639.0 4.6 add_convert_fusion.1
  645.7 53.1 %attend_back.1 = (bf16[1024,640]{1,0:T(8,128)(2,1)}, bf16[2560,2048]{1,0:T(8,128)(2,1)}, f32[4,8,256]{2,1,0:T(8,128)}) custom-call(f32[4]{0:T(128)} %subtract_add_fusion.1.refs_0_, bf16[640,1024]{1,0:T(8,128)(2,1)} %convolution_convert_fusion.11.refs_1_, bf16[2560,2048]{1,0:T(8,128)(2,1)} %convolution_convert_fusion.refs_2_, f32[1,1024]{1,0:T(1,128)} %bitcast.122, ...), custom_call_target="tpu_custom_call" | custom-call | flops 24000000000 | tf_op jit(solution)/shard_map/attend_back/pallas_call | solution.py:422
  698.8 6.3 fusion.134
  706.2 8.5 convolution_convert_fusion.8
  718.0 7.1 add_convert_fusion
  725.6 10.1 %convolution_convert_fusion.7 = bf16[512,2048]{1,0:T(8,128)(2,1)} fusion(bf16[2560,2048]{1,0:T(8,128)(2,1)} %get-tuple-element.244, bf16[2560,2048]{1,0:T(8,128)(2,1)} %norm_keys.1), kind=kOutput, calls=%fused_computation.52 | convolution fusion | flops 5369757696 | bytes 15204352 | tf_op jit(solution)/shard_map/dot_general | solution.py:37
  735.7 10.6 %add_convert_fusion.8 = bf16[512,2048]{1,0:T(8,128)(2,1)} fusion(bf16[512,2048]{1,0:T(8,128)(2,1)} %collective-permute-done.36, bf16[2560,2048]{1,0:T(8,128)(2,1)} %get-tuple-element.244, bf16[2560,2048]{1,0:T(8,128)(2,1)} %norm_keys.1), kind=kOutput, calls=%fused_computation.30 | convolution fusion | flops 5371854848 | bytes 17301504 | tf_op jit(solution)/shard_map/dot_general | solution.py:37
  755.2 8.7 fusion.21
  765.2 5.6 add_convert_fusion.7
  772.8 9.2 fusion.11
  786.3 9.6 %convolution_convert_fusion.10 = bf16[320,2048]{1,0:T(8,128)(2,1)} fusion(bf16[2048,2816]{1,0:T(8,128)(2,1)} %copy-done.54, bf16[640,2816]{1,0:T(8,128)(2,1)S(1)} %copy-done.14), kind=kOutput, calls=%fused_computation.63 | convolution fusion | flops 3691642880 | bytes 14647296 | tf_op jit(solution)/shard_map/dot_general | solution.py:43
  795.9 24.1 %collective-permute-done.46 = bf16[512,2048]{1,0:T(8,128)(2,1)} collective-permute-done((bf16[512,2048]{1,0:T(8,128)(2,1)}, bf16[512,2048]{1,0:T(8,128)(2,1)}, u32[]{:S(2)}, u32[]{:S(2)}) %collective-permute-start.46) | collective-permute-done | bytes 2097184 | tf_op jit(solution)/shard_map/ppermute | solution.py:77
  845.3 18.3 %collective-permute-done.44 = bf16[320,2048]{1,0:T(8,128)(2,1)} collective-permute-done((bf16[320,2048]{1,0:T(8,128)(2,1)S(1)}, bf16[320,2048]{1,0:T(8,128)(2,1)}, u32[]{:S(2)}, u32[]{:S(2)}) %collective-permute-start.44) | collective-permute-done | bytes 1310752 | tf_op jit(solution)/shard_map/ppermute | solution.py:80
  868.9 6.0 fusion.26
  878.6 9.6 %collective-permute-done.50 = bf16[512,1024]{1,0:T(8,128)(2,1)} collective-permute-done((bf16[512,1024]{1,0:T(8,128)(2,1)}, bf16[512,1024]{1,0:T(8,128)(2,1)}, u32[]{:S(2)}, u32[]{:S(2)}) %collective-permute-start.50) | collective-permute-done | bytes 1048608 | tf_op jit(solution)/shard_map/ppermute | solution.py:77
  896.5 8.1 fusion.28
  918.1 4.8 fusion.5
  938.5 4.5 reshape.325
  (494 shorter events, 265.8 us)
Async XLA Ops:
  7.2 48.6 %all-gather.8.cloned.1.call-start = ((), (), s32[]{:S(2)}) async-start(), calls=%async_computation.7 | async-start | bytes 1474560 | tf_op jit(solution)/shard_map/all_gather | solution.py:83
  20.6 79.8 %all-gather.10.cloned.1.call-start = ((), (), s32[]{:S(2)}) async-start(), calls=%async_computation.8 | async-start | bytes 2621440 | tf_op jit(solution)/shard_map/all_gather | solution.py:83
  23.2 113.2 %all-gather.12.cloned.1.call-start = ((), (), s32[]{:S(2)}) async-start(), calls=%async_computation.9 | async-start | bytes 1310720 | tf_op jit(solution)/shard_map/all_gather | solution.py:83
  23.9 163.8 %all-gather.14.cloned.1.call-start = ((), (), s32[]{:S(2)}) async-start(), calls=%async_computation.10 | async-start | bytes 1310720 | tf_op jit(solution)/shard_map/all_gather | solution.py:83
  24.5 208.0 %all-gather.16.cloned.1.call-start = ((), (), s32[]{:S(2)}) async-start(), calls=%async_computation.11 | async-start | bytes 3604480 | tf_op jit(solution)/shard_map/all_gather | solution.py:83
  25.1 280.7 %all-gather.18.cloned.1.call-start = ((), (), s32[]{:S(2)}) async-start(), calls=%async_computation.12 | async-start | bytes 3604480 | tf_op jit(solution)/shard_map/all_gather | solution.py:83
  25.1 30.6 %collective-permute-start.1 = (bf16[320,2048]{1,0:T(8,128)(2,1)}, bf16[320,2048]{1,0:T(8,128)(2,1)}, u32[]{:S(2)}, u32[]{:S(2)}) collective-permute-start(bf16[320,2048]{1,0:T(8,128)(2,1)} %param.19), channel_id=1, source_target_pairs={{0,1},{1,0},{2,3},{3,2},{4,5},{5,4},{6,7},{7,6},{8,9},{9,8},{10,11... | collective-permute-start | bytes 3932168 | tf_op jit(solution)/shard_map/ppermute | solution.py:80
  57.3 306.3 %all-gather.20.cloned.1.call-start = ((), (), s32[]{:S(2)}) async-start(), calls=%async_computation.13 | async-start | bytes 3604480 | tf_op jit(solution)/shard_map/all_gather | solution.py:83
  84.7 50.9 %collective-permute-start.4 = (bf16[1152,1024]{1,0:T(8,128)(2,1)}, bf16[1152,1024]{1,0:T(8,128)(2,1)}, u32[]{:S(2)}, u32[]{:S(2)}) collective-permute-start(bf16[1152,1024]{1,0:T(8,128)(2,1)} %constant_dynamic-update-slice_fusion.refs_2_), channel_id=1, source_target_pairs={{0,1},{1,0},{2,3},{3,2},{4,5},{5,4},{6,7},{7,6},{8,9},{9,8},{10,11... | collective-permute-start | bytes 7077896 | tf_op jit(solution)/shard_map/ppermute | solution.py:80
  100.4 48.4 %collective-permute-start.7 = (bf16[512,2048]{1,0:T(8,128)(2,1)}, bf16[512,2048]{1,0:T(8,128)(2,1)}, u32[]{:S(2)}, u32[]{:S(2)}) collective-permute-start(bf16[512,2048]{1,0:T(8,128)(2,1)} %all-gather.10.cloned.1.call-done), channel_id=1, source_target_pairs={{0,4},{2,6},{4,0},{6,2},{8,12},{10,14},{12,8},{14,10},{16,20},{18,... | collective-permute-start | bytes 6291464 | tf_op jit(solution)/shard_map/ppermute | solution.py:77
  148.8 31.9 %collective-permute-start.8 = (bf16[512,2048]{1,0:T(8,128)(2,1)}, bf16[512,2048]{1,0:T(8,128)(2,1)}, u32[]{:S(2)}, u32[]{:S(2)}) collective-permute-start(bf16[512,2048]{1,0:T(8,128)(2,1)} %collective-permute-done.7), channel_id=1, source_target_pairs={{0,2},{2,0},{4,6},{6,4},{8,10},{10,8},{12,14},{14,12},{16,18},{18,... | collective-permute-start | bytes 6291464 | tf_op jit(solution)/shard_map/ppermute | solution.py:74
  150.1 548.7 %reduce-scatter.8.cloned.1.call-start = ((), (), s32[]{:S(2)}) async-start(), calls=%async_computation.14 | async-start | bytes 3604480 | tf_op jit(solution)/shard_map/reduce_scatter | solution.py:108
  155.6 32.1 %collective-permute-start.9 = (bf16[512,1024]{1,0:T(8,128)(2,1)}, bf16[512,1024]{1,0:T(8,128)(2,1)}, u32[]{:S(2)}, u32[]{:S(2)}) collective-permute-start(bf16[512,1024]{1,0:T(8,128)(2,1)} %all-gather.12.cloned.1.call-done), channel_id=1, source_target_pairs={{0,4},{2,6},{4,0},{6,2},{8,12},{10,14},{12,8},{14,10},{16,20},{18,... | collective-permute-start | bytes 3145736 | tf_op jit(solution)/shard_map/ppermute | solution.py:77
  157.1 66.7 %collective-permute-start.10 = (bf16[512,1024]{1,0:T(8,128)(2,1)}, bf16[512,1024]{1,0:T(8,128)(2,1)}, u32[]{:S(2)}, u32[]{:S(2)}) collective-permute-start(bf16[512,1024]{1,0:T(8,128)(2,1)} %all-gather.12.cloned.1.call-done), channel_id=1, source_target_pairs={{0,2},{2,0},{4,6},{6,4},{8,10},{10,8},{12,14},{14,12},{16,18},{18,... | collective-permute-start | bytes 3145736 | tf_op jit(solution)/shard_map/ppermute | solution.py:74
  187.7 44.8 %collective-permute-start.12 = (bf16[512,1024]{1,0:T(8,128)(2,1)}, bf16[512,1024]{1,0:T(8,128)(2,1)}, u32[]{:S(2)}, u32[]{:S(2)}) collective-permute-start(bf16[512,1024]{1,0:T(8,128)(2,1)} %all-gather.14.cloned.1.call-done), channel_id=1, source_target_pairs={{0,4},{2,6},{4,0},{6,2},{8,12},{10,14},{12,8},{14,10},{16,20},{18,... | collective-permute-start | bytes 3145736 | tf_op jit(solution)/shard_map/ppermute | solution.py:77
  188.4 117.4 %collective-permute-start.15 = (bf16[512,1024]{1,0:T(8,128)(2,1)}, bf16[512,1024]{1,0:T(8,128)(2,1)}, u32[]{:S(2)}, u32[]{:S(2)}) collective-permute-start(bf16[512,1024]{1,0:T(8,128)(2,1)} %all-gather.14.cloned.1.call-done), channel_id=1, source_target_pairs={{0,2},{2,0},{4,6},{6,4},{8,10},{10,8},{12,14},{14,12},{16,18},{18,... | collective-permute-start | bytes 3145736 | tf_op jit(solution)/shard_map/ppermute | solution.py:74
  232.5 73.3 %collective-permute-start.14 = (bf16[512,2816]{1,0:T(8,128)(2,1)}, bf16[512,2816]{1,0:T(8,128)(2,1)}, u32[]{:S(2)}, u32[]{:S(2)}) collective-permute-start(bf16[512,2816]{1,0:T(8,128)(2,1)} %all-gather.16.cloned.1.call-done), channel_id=1, source_target_pairs={{0,4},{2,6},{4,0},{6,2},{8,12},{10,14},{12,8},{14,10},{16,20},{18,... | collective-permute-start | bytes 8650760 | tf_op jit(solution)/shard_map/ppermute | solution.py:77
  234.3 39.7 %collective-permute-start.13 = (bf16[320,2048]{1,0:T(8,128)(2,1)S(1)}, bf16[320,2048]{1,0:T(8,128)(2,1)}, u32[]{:S(2)}, u32[]{:S(2)}) collective-permute-start(bf16[320,2048]{1,0:T(8,128)(2,1)S(1)} %reshape.316), channel_id=1, source_target_pairs={{0,1},{1,0},{2,3},{3,2},{4,5},{5,4},{6,7},{7,6},{8,9},{9,8},{10,11... | collective-permute-start | bytes 3932168 | tf_op jit(solution)/shard_map/ppermute | solution.py:80
  239.6 109.2 %collective-permute-start.19 = (bf16[512,2816]{1,0:T(8,128)(2,1)}, bf16[512,2816]{1,0:T(8,128)(2,1)}, u32[]{:S(2)}, u32[]{:S(2)}) collective-permute-start(bf16[512,2816]{1,0:T(8,128)(2,1)} %all-gather.16.cloned.1.call-done), channel_id=1, source_target_pairs={{0,2},{2,0},{4,6},{6,4},{8,10},{10,8},{12,14},{14,12},{16,18},{18,... | collective-permute-start | bytes 8650760 | tf_op jit(solution)/shard_map/ppermute | solution.py:74
  239.6 66.2 %collective-permute-start.16 = (bf16[512,1024]{1,0:T(8,128)(2,1)}, bf16[512,1024]{1,0:T(8,128)(2,1)}, u32[]{:S(2)}, u32[]{:S(2)}) collective-permute-start(bf16[512,1024]{1,0:T(8,128)(2,1)} %collective-permute-done.12), channel_id=1, source_target_pairs={{0,2},{2,0},{4,6},{6,4},{8,10},{10,8},{12,14},{14,12},{16,18},{18,... | collective-permute-start | bytes 3145736 | tf_op jit(solution)/shard_map/ppermute | solution.py:74
  305.8 42.9 %collective-permute-start.20 = (bf16[512,2816]{1,0:T(8,128)(2,1)}, bf16[512,2816]{1,0:T(8,128)(2,1)S(1)}, u32[]{:S(2)}, u32[]{:S(2)}) collective-permute-start(bf16[512,2816]{1,0:T(8,128)(2,1)} %collective-permute-done.14), channel_id=1, source_target_pairs={{0,2},{2,0},{4,6},{6,4},{8,10},{10,8},{12,14},{14,12},{16,18},{18,... | collective-permute-start | bytes 8650760 | tf_op jit(solution)/shard_map/ppermute | solution.py:74
  314.5 31.1 %collective-permute-start.17 = (bf16[320,2048]{1,0:T(8,128)(2,1)S(1)}, bf16[320,2048]{1,0:T(8,128)(2,1)S(1)}, u32[]{:S(2)}, u32[]{:S(2)}) collective-permute-start(bf16[320,2048]{1,0:T(8,128)(2,1)S(1)} %convolution_convert_fusion.9), channel_id=1, source_target_pairs={{0,1},{1,0},{2,3},{3,2},{4,5},{5,4},{6,7},{7,6},{8,9},{9,8},{10,11... | collective-permute-start | bytes 3932168 | tf_op jit(solution)/shard_map/ppermute | solution.py:80
  319.0 64.8 %collective-permute-start.21 = (bf16[512,2816]{1,0:T(8,128)(2,1)}, bf16[512,2816]{1,0:T(8,128)(2,1)}, u32[]{:S(2)}, u32[]{:S(2)}) collective-permute-start(bf16[512,2816]{1,0:T(8,128)(2,1)} %all-gather.18.cloned.1.call-done), channel_id=1, source_target_pairs={{0,4},{2,6},{4,0},{6,2},{8,12},{10,14},{12,8},{14,10},{16,20},{18,... | collective-permute-start | bytes 8650760 | tf_op jit(solution)/shard_map/ppermute | solution.py:77
  319.6 81.8 %collective-permute-start.22 = (bf16[512,2816]{1,0:T(8,128)(2,1)}, bf16[512,2816]{1,0:T(8,128)(2,1)}, u32[]{:S(2)}, u32[]{:S(2)}) collective-permute-start(bf16[512,2816]{1,0:T(8,128)(2,1)} %all-gather.18.cloned.1.call-done), channel_id=1, source_target_pairs={{0,2},{2,0},{4,6},{6,4},{8,10},{10,8},{12,14},{14,12},{16,18},{18,... | collective-permute-start | bytes 8650760 | tf_op jit(solution)/shard_map/ppermute | solution.py:74
  348.1 40.2 %collective-permute-start.18 = (bf16[320,2048]{1,0:T(8,128)(2,1)S(1)}, bf16[320,2048]{1,0:T(8,128)(2,1)S(1)}, u32[]{:S(2)}, u32[]{:S(2)}) collective-permute-start(bf16[320,2048]{1,0:T(8,128)(2,1)S(1)} %multiply_convert_fusion.3), channel_id=1, source_target_pairs={{0,1},{1,0},{2,3},{3,2},{4,5},{5,4},{6,7},{7,6},{8,9},{9,8},{10,11... | collective-permute-start | bytes 3932168 | tf_op jit(solution)/shard_map/ppermute | solution.py:80
  387.5 64.9 %collective-permute-start.24 = (bf16[512,2816]{1,0:T(8,128)(2,1)S(1)}, bf16[512,2816]{1,0:T(8,128)(2,1)S(1)}, u32[]{:S(2)}, u32[]{:S(2)}) collective-permute-start(bf16[512,2816]{1,0:T(8,128)(2,1)S(1)} %copy-done.40), channel_id=1, source_target_pairs={{0,4},{2,6},{4,0},{6,2},{8,12},{10,14},{12,8},{14,10},{16,20},{18,... | collective-permute-start | bytes 8650760 | tf_op jit(solution)/shard_map/ppermute | solution.py:77
  388.1 65.0 %collective-permute-start.25 = (bf16[512,2816]{1,0:T(8,128)(2,1)S(1)}, bf16[512,2816]{1,0:T(8,128)(2,1)S(1)}, u32[]{:S(2)}, u32[]{:S(2)}) collective-permute-start(bf16[512,2816]{1,0:T(8,128)(2,1)S(1)} %copy-done.40), channel_id=1, source_target_pairs={{0,2},{2,0},{4,6},{6,4},{8,10},{10,8},{12,14},{14,12},{16,18},{18,... | collective-permute-start | bytes 8650760 | tf_op jit(solution)/shard_map/ppermute | solution.py:74
  452.6 102.5 %collective-permute-start.32 = (bf16[512,2816]{1,0:T(8,128)(2,1)}, bf16[512,2816]{1,0:T(8,128)(2,1)}, u32[]{:S(2)}, u32[]{:S(2)}) collective-permute-start(bf16[512,2816]{1,0:T(8,128)(2,1)} %convolution_convert_fusion.5), channel_id=1, source_target_pairs={{0,2},{2,0},{4,6},{6,4},{8,10},{10,8},{12,14},{14,12},{16,18},{18,... | collective-permute-start | bytes 8650760 | tf_op jit(solution)/shard_map/ppermute | solution.py:74
  486.6 64.8 %collective-permute-start.29 = (bf16[512,2816]{1,0:T(8,128)(2,1)}, bf16[512,2816]{1,0:T(8,128)(2,1)}, u32[]{:S(2)}, u32[]{:S(2)}) collective-permute-start(bf16[512,2816]{1,0:T(8,128)(2,1)} %add_convert_fusion.5), channel_id=1, source_target_pairs={{0,4},{2,6},{4,0},{6,2},{8,12},{10,14},{12,8},{14,10},{16,20},{18,... | collective-permute-start | bytes 8650760 | tf_op jit(solution)/shard_map/ppermute | solution.py:77
  495.9 34.4 %collective-permute-start.30 = (bf16[512,2816]{1,0:T(8,128)(2,1)}, bf16[512,2816]{1,0:T(8,128)(2,1)}, u32[]{:S(2)}, u32[]{:S(2)}) collective-permute-start(bf16[512,2816]{1,0:T(8,128)(2,1)} %convolution_convert_fusion.4), channel_id=1, source_target_pairs={{0,2},{2,0},{4,6},{6,4},{8,10},{10,8},{12,14},{14,12},{16,18},{18,... | collective-permute-start | bytes 8650760 | tf_op jit(solution)/shard_map/ppermute | solution.py:74
  506.4 45.1 %collective-permute-start.28 = (bf16[320,2048]{1,0:T(8,128)(2,1)}, bf16[320,2048]{1,0:T(8,128)(2,1)S(1)}, u32[]{:S(2)}, u32[]{:S(2)}) collective-permute-start(bf16[320,2048]{1,0:T(8,128)(2,1)} %fusion.2), channel_id=1, source_target_pairs={{0,1},{1,0},{2,3},{3,2},{4,5},{5,4},{6,7},{7,6},{8,9},{9,8},{10,11... | collective-permute-start | bytes 3932168 | tf_op jit(solution)/shard_map/ppermute | solution.py:80
  562.4 162.7 %reduce-scatter.10.cloned.1.call-start = ((), (), s32[]{:S(2)}) async-start(), calls=%async_computation.15 | async-start | bytes 3604480 | tf_op jit(solution)/shard_map/reduce_scatter | solution.py:108
  574.0 37.2 %collective-permute-start.34 = (bf16[512,2816]{1,0:T(8,128)(2,1)S(1)}, bf16[512,2816]{1,0:T(8,128)(2,1)S(1)}, u32[]{:S(2)}, u32[]{:S(2)}) collective-permute-start(bf16[512,2816]{1,0:T(8,128)(2,1)S(1)} %convolution_convert_fusion.1), channel_id=1, source_target_pairs={{0,2},{2,0},{4,6},{6,4},{8,10},{10,8},{12,14},{14,12},{16,18},{18,... | collective-permute-start | bytes 8650760 | tf_op jit(solution)/shard_map/ppermute | solution.py:74
  574.6 64.5 %collective-permute-start.35 = (bf16[512,2816]{1,0:T(8,128)(2,1)S(1)}, bf16[512,2816]{1,0:T(8,128)(2,1)S(1)}, u32[]{:S(2)}, u32[]{:S(2)}) collective-permute-start(bf16[512,2816]{1,0:T(8,128)(2,1)S(1)} %copy-done.43), channel_id=1, source_target_pairs={{0,4},{2,6},{4,0},{6,2},{8,12},{10,14},{12,8},{14,10},{16,20},{18,... | collective-permute-start | bytes 8650760 | tf_op jit(solution)/shard_map/ppermute | solution.py:77
  575.3 30.5 %collective-permute-start.31 = (bf16[320,2048]{1,0:T(8,128)(2,1)S(1)}, bf16[320,2048]{1,0:T(8,128)(2,1)S(1)}, u32[]{:S(2)}, u32[]{:S(2)}) collective-permute-start(bf16[320,2048]{1,0:T(8,128)(2,1)S(1)} %copy-done.8), channel_id=1, source_target_pairs={{0,1},{1,0},{2,3},{3,2},{4,5},{5,4},{6,7},{7,6},{8,9},{9,8},{10,11... | collective-permute-start | bytes 3932168 | tf_op jit(solution)/shard_map/ppermute | solution.py:80
  579.9 134.8 %collective-permute-start.38 = (bf16[512,2816]{1,0:T(8,128)(2,1)}, bf16[512,2816]{1,0:T(8,128)(2,1)}, u32[]{:S(2)}, u32[]{:S(2)}) collective-permute-start(bf16[512,2816]{1,0:T(8,128)(2,1)} %convolution_convert_fusion.2), channel_id=1, source_target_pairs={{0,2},{2,0},{4,6},{6,4},{8,10},{10,8},{12,14},{14,12},{16,18},{18,... | collective-permute-start | bytes 8650760 | tf_op jit(solution)/shard_map/ppermute | solution.py:74
  643.6 71.1 %collective-permute-start.39 = (bf16[512,2816]{1,0:T(8,128)(2,1)}, bf16[512,2816]{1,0:T(8,128)(2,1)}, u32[]{:S(2)}, u32[]{:S(2)}) collective-permute-start(bf16[512,2816]{1,0:T(8,128)(2,1)} %add_convert_fusion.2), channel_id=1, source_target_pairs={{0,4},{2,6},{4,0},{6,2},{8,12},{10,14},{12,8},{14,10},{16,20},{18,... | collective-permute-start | bytes 8650760 | tf_op jit(solution)/shard_map/ppermute | solution.py:77
  644.3 219.2 %reduce-scatter.12.cloned.1.call-start = ((), (), s32[]{:S(2)}) async-start(), calls=%async_computation.16 | async-start | bytes 3604480 | tf_op jit(solution)/shard_map/reduce_scatter | solution.py:108
  705.1 58.8 %collective-permute-start.42 = (bf16[512,2048]{1,0:T(8,128)(2,1)}, bf16[512,2048]{1,0:T(8,128)(2,1)}, u32[]{:S(2)}, u32[]{:S(2)}) collective-permute-start(bf16[512,2048]{1,0:T(8,128)(2,1)} %get-tuple-element.236), channel_id=1, source_target_pairs={{0,2},{2,0},{4,6},{6,4},{8,10},{10,8},{12,14},{14,12},{16,18},{18,... | collective-permute-start | bytes 6291464 | tf_op jit(solution)/shard_map/ppermute | solution.py:74
  716.9 48.3 %collective-permute-start.43 = (bf16[512,2048]{1,0:T(8,128)(2,1)}, bf16[512,2048]{1,0:T(8,128)(2,1)}, u32[]{:S(2)}, u32[]{:S(2)}) collective-permute-start(bf16[512,2048]{1,0:T(8,128)(2,1)} %add_convert_fusion.9), channel_id=1, source_target_pairs={{0,4},{2,6},{4,0},{6,2},{8,12},{10,14},{12,8},{14,10},{16,20},{18,... | collective-permute-start | bytes 6291464 | tf_op jit(solution)/shard_map/ppermute | solution.py:77
  725.1 143.8 %reduce-scatter.14.cloned.1.call-start = ((), (), s32[]{:S(2)}) async-start(), calls=%async_computation.17 | async-start | bytes 2621440 | tf_op jit(solution)/shard_map/reduce_scatter | solution.py:108
  770.8 140.8 %reduce-scatter.18.cloned.1.call-start = ((), (), s32[]{:S(2)}) async-start(), calls=%async_computation.19 | async-start | bytes 2621440 | tf_op jit(solution)/shard_map/reduce_scatter | solution.py:108
  771.7 48.3 %collective-permute-start.46 = (bf16[512,2048]{1,0:T(8,128)(2,1)}, bf16[512,2048]{1,0:T(8,128)(2,1)}, u32[]{:S(2)}, u32[]{:S(2)}) collective-permute-start(bf16[512,2048]{1,0:T(8,128)(2,1)} %add_convert_fusion.8), channel_id=1, source_target_pairs={{0,4},{2,6},{4,0},{6,2},{8,12},{10,14},{12,8},{14,10},{16,20},{18,... | collective-permute-start | bytes 6291464 | tf_op jit(solution)/shard_map/ppermute | solution.py:77
  824.1 106.1 %reduce-scatter.16.cloned.1.call-start = ((), (), s32[]{:S(2)}) async-start(), calls=%async_computation.18 | async-start | bytes 1310720 | tf_op jit(solution)/shard_map/reduce_scatter | solution.py:108
  843.3 35.3 %collective-permute-start.48 = (bf16[512,1024]{1,0:T(8,128)(2,1)}, bf16[512,1024]{1,0:T(8,128)(2,1)}, u32[]{:S(2)}, u32[]{:S(2)}) collective-permute-start(bf16[512,1024]{1,0:T(8,128)(2,1)} %convolution_convert_fusion.12), channel_id=1, source_target_pairs={{0,2},{2,0},{4,6},{6,4},{8,10},{10,8},{12,14},{14,12},{16,18},{18,... | collective-permute-start | bytes 3145736 | tf_op jit(solution)/shard_map/ppermute | solution.py:74
  844.7 43.4 %collective-permute-start.50 = (bf16[512,1024]{1,0:T(8,128)(2,1)}, bf16[512,1024]{1,0:T(8,128)(2,1)}, u32[]{:S(2)}, u32[]{:S(2)}) collective-permute-start(bf16[512,1024]{1,0:T(8,128)(2,1)} %add_convert_fusion.13), channel_id=1, source_target_pairs={{0,4},{2,6},{4,0},{6,2},{8,12},{10,14},{12,8},{14,10},{16,20},{18,... | collective-permute-start | bytes 3145736 | tf_op jit(solution)/shard_map/ppermute | solution.py:77
  878.1 39.9 %collective-permute-start.51 = (bf16[320,2048]{1,0:T(8,128)(2,1)}, bf16[320,2048]{1,0:T(8,128)(2,1)}, u32[]{:S(2)}, u32[]{:S(2)}) collective-permute-start(bf16[320,2048]{1,0:T(8,128)(2,1)} %fusion.3), channel_id=1, source_target_pairs={{0,1},{1,0},{2,3},{3,2},{4,5},{5,4},{6,7},{7,6},{8,9},{9,8},{10,11... | collective-permute-start | bytes 3932168 | tf_op jit(solution)/shard_map/ppermute | solution.py:80
  890.0 56.8 %reduce-scatter.20.cloned.1.call-start = ((), (), s32[]{:S(2)}) async-start(), calls=%async_computation.20 | async-start | bytes 1310720 | tf_op jit(solution)/shard_map/reduce_scatter | solution.py:108
  (115 other events, 1959.7 us)
Sparse Core Ops, SparseCore 0:
  20.8 32.4 all-gather.7
  55.4 45.0 all-gather.9
  102.0 26.6 all-gather.11
  130.1 27.4 all-gather.13
  159.0 58.6 all-gather.15
  219.1 57.8 all-gather.17
  278.6 57.9 all-gather.19
  562.5 53.9 reduce-scatter.7
  644.5 54.6 reduce-scatter.9
  725.2 53.9 reduce-scatter.11
  781.5 43.7 reduce-scatter.13
  827.5 43.3 reduce-scatter.17
  890.1 26.3 reduce-scatter.15
  918.7 25.7 reduce-scatter.19

commit v4 on v3

--- a/solution.py
+++ b/solution.py
@@ -15,7 +15,7 @@
 masked_value = -1e30
 f32 = jnp.float32
 bf16 = jnp.bfloat16
-CHUNK = 256
+CHUNK = 512
 
 
 def inv_rms(entries, eps_value):
@@ -84,11 +84,6 @@
             shard, "dp", axis=0, tiled=True, axis_index_groups=self.upper_groups
         )
 
-    def gather_near(self, here, *others):
-        here = after(here, *others)
-        aside = self.swap_side(here)
-        return [here, aside, self.swap_core(here), self.swap_core(aside)]
-
     def sum_small(self, value):
         step = 1
         while step < self.count:
@@ -180,100 +175,73 @@
 
 
 def forward_kernel(
-    prompt_len, top_rows, first_head, lam_ref, q_ref, kv_ref, gain_ref, spot_ref, reach_ref, low_ref, high_ref,
-    out_ref, vec_ref, lse_ref, one_ref, two_ref, stat_ref,
+    prompt_len, top_rows, first_head, lam_ref, q_ref, kv_ref, gain_ref, spot_ref, reach_ref,
+    out_ref, vec_ref, lse_ref, one_ref, two_ref, turn_ref,
 ):
     lam = lam_ref[first_head + pl.program_id(0)]
     rows, keys = q_ref.shape[0], kv_ref.shape[0]
     scale = DK ** (-0.5)
-    scores = (one_ref, two_ref)
-
-    def chunk_scores(chunk):
-        for comp in range(2):
+    count = keys // CHUNK
+    first_cont = prompt_len // CHUNK
+    flipped = rows % 128 == 0
+
+    def span_of(chunk):
+        return pl.ds(pl.multiple_of(chunk * CHUNK, CHUNK), CHUNK)
+
+    def eights(values):
+        return values.reshape(CHUNK // 8, 8, rows)
+
+    def score(chunk, allowed, columns, tops):
+        news = []
+        for comp, ref in ((0, one_ref), (1, two_ref)):
             lanes = slice(comp * DK, (comp + 1) * DK)
-            scores[comp][chunk] = dot_nt(q_ref[:, lanes], kv_ref[pl.ds(chunk * CHUNK, CHUNK), lanes])
+            scores = dot_nt(kv_ref[span_of(chunk), lanes], q_ref[:, lanes])
+            masked = jnp.where(allowed, scores[:, :columns], masked_value)
+            if columns < rows:
+                masked = jnp.concatenate([masked, scores[:, columns:]], axis=1)
+            ref[chunk] = masked
+            news.append(jnp.maximum(tops[comp], jnp.max(eights(masked), axis=0)))
+        return tuple(news)
 
     def prompt_chunk(chunk, tops):
-        chunk_scores(chunk)
-        spots = spot_ref[chunk]
-        for comp in range(2):
-            ref = scores[comp]
-            for part in range(CHUNK // 128):
-                lanes = slice(part * 128, (part + 1) * 128)
-                ref[chunk, :top_rows, lanes] = jnp.where(
-                    spots[:, lanes] <= reach_ref[...], ref[chunk, :top_rows, lanes], masked_value
-                )
-        return 0
+        allowed = spot_ref[span_of(chunk), :top_rows] <= reach_ref[0:1, :top_rows]
+        return score(chunk, allowed, top_rows, tops)
 
     def cont_chunk(chunk, tops):
-        chunk_scores(chunk)
-        first = chunk * CHUNK - prompt_len
-        for part in range(CHUNK // 128):
-            lanes = slice(part * 128, (part + 1) * 128)
-            spot = lax.broadcasted_iota(jnp.int32, (rows, 128), 1) + (first + part * 128)
-            allowed = (spot >= low_ref[...]) & (spot <= high_ref[...])
-            for comp in range(2):
-                ref = scores[comp]
-                ref[chunk, :, lanes] = jnp.where(allowed, ref[chunk, :, lanes], masked_value)
-        return 0
-
-    first_cont = prompt_len // CHUNK
-    count = keys // CHUNK
-    lax.fori_loop(0, first_cont, prompt_chunk, 0)
-    lax.fori_loop(first_cont, count, cont_chunk, 0)
-
-    ROWS = 32
-    def row_block(block, carry):
-        span = pl.ds(pl.multiple_of(block * ROWS, ROWS), ROWS)
-        totals = []
-        for comp in range(2):
-            ref = scores[comp]
-            top = ref[0, span, :128]
-            for chunk in range(count):
-                for part in range(CHUNK // 128):
-                    if chunk + part > 0:
-                        top = jnp.maximum(top, ref[chunk, span, part * 128 : (part + 1) * 128])
-            top = jnp.max(top, axis=1, keepdims=True)
-            total = jnp.zeros((ROWS, 128), f32)
-            for chunk in range(count):
-                for part in range(CHUNK // 128):
-                    lanes = slice(part * 128, (part + 1) * 128)
-                    terms = jnp.exp((ref[chunk, span, lanes] - top) * scale)
-                    total = total + terms
-                    ref[chunk, span, lanes] = terms
-            total = jnp.sum(total, axis=1, keepdims=True)
-            totals.append(total)
-            stat_ref[comp, span, :] = jnp.broadcast_to(top * scale + jnp.log(total), (ROWS, 128))
-        first = 1.0 / totals[0]
-        second = lam / totals[1]
-        for chunk in range(count):
-            for part in range(CHUNK // 128):
-                lanes = slice(part * 128, (part + 1) * 128)
-                one_ref[chunk, span, lanes] = (
-                    one_ref[chunk, span, lanes] * first - two_ref[chunk, span, lanes] * second
-                )
+        spot = lax.broadcasted_iota(jnp.int32, (CHUNK, rows), 0) + (chunk * CHUNK - prompt_len)
+        allowed = (spot >= reach_ref[1:2, :]) & (spot <= reach_ref[2:3, :])
+        return score(chunk, allowed, rows, tops)
+
+    tops = (jnp.full((8, rows), masked_value, f32),) * 2
+    tops = lax.fori_loop(0, first_cont, prompt_chunk, tops, unroll=2)
+    tops = lax.fori_loop(first_cont, count, cont_chunk, tops, unroll=2)
+    tops = [jnp.max(top, axis=0, keepdims=True) * scale for top in tops]
+
+    def weigh(chunk, totals):
+        news = []
+        for comp, ref in ((0, one_ref), (1, two_ref)):
+            terms = jnp.exp(ref[chunk] * scale - tops[comp])
+            ref[chunk] = terms
+            news.append(totals[comp] + jnp.sum(eights(terms), axis=0))
+        return tuple(news)
+
+    totals = lax.fori_loop(0, count, weigh, (jnp.zeros((8, rows), f32),) * 2)
+    totals = [jnp.sum(total, axis=0, keepdims=True) for total in totals]
+    for comp in range(2):
+        lse_ref[0, 8 * comp : 8 * comp + 1, :] = tops[comp] + jnp.log(totals[comp])
+    first, second = 1.0 / totals[0], lam / totals[1]
+    gather = turn_ref if flipped else out_ref
+    gather[...] = jnp.zeros_like(gather)
+
+    def mix(chunk, carry):
+        mixed = (one_ref[chunk] * first - two_ref[chunk] * second).astype(bf16)
+        value = kv_ref[span_of(chunk), 2 * DK :]
+        gather[...] += dot_tn(value, mixed) if flipped else dot_tn(mixed, value)
         return carry
 
-    lax.fori_loop(0, rows // ROWS, row_block, 0)
-
-    turn = (lax.broadcasted_iota(jnp.int32, (8, 128), 1) == 0).astype(f32)
-    for comp in range(2):
-        lse_ref[0, comp * 8 : (comp + 1) * 8, :] = lax.dot_general(
-            turn,
-            stat_ref[comp],
-            (((1,), (1,)), ((), ())),
-            precision=lax.Precision.HIGHEST,
-            preferred_element_type=f32,
-        )
-    out_ref[...] = jnp.zeros_like(out_ref)
-
-    def mix(chunk, carry):
-        out_ref[...] += dot_nn(
-            one_ref[chunk].astype(bf16), kv_ref[pl.ds(chunk * CHUNK, CHUNK), 2 * DK :]
-        )
-        return carry
-
-    lax.fori_loop(0, count, mix, 0)
+    lax.fori_loop(0, count, mix, 0, unroll=2)
+    if flipped:
+        out_ref[...] = jnp.transpose(turn_ref[...])
     out = out_ref[...]
     inverse = lax.rsqrt(jnp.mean(out * out, axis=1, keepdims=True) + head_eps)
     vec_ref[...] = (out * inverse * gain_ref[...] * (1.0 - lambda_init)).astype(bf16)
@@ -333,8 +301,8 @@
         return gather_sums(chunk, sums)
 
     sums = (jnp.zeros((8, rows), f32), jnp.zeros((8, rows), f32))
-    sums = lax.fori_loop(0, first_cont, prompt_chunk, sums)
-    sums = lax.fori_loop(first_cont, count, cont_chunk, sums)
+    sums = lax.fori_loop(0, first_cont, prompt_chunk, sums, unroll=2)
+    sums = lax.fori_loop(first_cont, count, cont_chunk, sums, unroll=2)
     first = jnp.sum(sums[0], axis=0, keepdims=True)
     second = jnp.sum(sums[1], axis=0, keepdims=True)
     sums_ref[0, 0:1, :] = gain_part
@@ -354,7 +322,7 @@
             turn_ref[lanes, :] += dot_tn(kv_ref[span, lanes], grads[comp])
         return carry
 
-    lax.fori_loop(0, count, back, 0)
+    lax.fori_loop(0, count, back, 0, unroll=2)
     dq_ref[...] = (turn_ref[...] * scale).astype(bf16)
 
 
@@ -362,8 +330,7 @@
     first, heads = span[0], span[1] - span[0]
     rows, keys = queries.shape[0], keys_values.shape[0]
     prompt_len = prompt_spots.shape[0]
-    top_rows = min(rows, -(-prompt_part // 16) * 16)
-    wide = [jnp.broadcast_to(bound[:, None], (rows, 128)) for bound in bounds]
+    top_rows = min(rows, -(-prompt_part // 128) * 128)
     count = keys // CHUNK
     return pl.pallas_call(
         lambda *refs: forward_kernel(prompt_len, top_rows, first, *refs),
@@ -373,10 +340,8 @@
             pl.BlockSpec((rows, 2 * DK), lambda h: (0, h + first)),
             pl.BlockSpec((keys, 2 * DK + DV), lambda h: (0, h + first)),
             pl.BlockSpec((1, DV), lambda h: (0, h + first)),
-            pl.BlockSpec((prompt_len // CHUNK, 1, CHUNK), lambda h: (0, 0, 0)),
-            pl.BlockSpec((top_rows, 128), lambda h: (0, 0)),
-            pl.BlockSpec((rows, 128), lambda h: (0, 0)),
-            pl.BlockSpec((rows, 128), lambda h: (0, 0)),
+            pl.BlockSpec((prompt_len, 128), lambda h: (0, 0)),
+            pl.BlockSpec((8, rows), lambda h: (0, 0)),
         ],
         out_specs=[
             pl.BlockSpec((rows, DV), lambda h: (0, h)),
@@ -389,38 +354,34 @@
             jax.ShapeDtypeStruct((heads, 16, rows), f32),
         ],
         scratch_shapes=[
-            pltpu.VMEM((count, rows, CHUNK), f32),
-            pltpu.VMEM((count, rows, CHUNK), f32),
-            pltpu.VMEM((2, rows, 128), f32),
+            pltpu.VMEM((count, CHUNK, rows), f32),
+            pltpu.VMEM((count, CHUNK, rows), f32),
+            pltpu.VMEM((DV, rows), f32),
         ],
         compiler_params=pltpu.CompilerParams(vmem_limit_bytes=56 * 2**20),
         name="attend",
-        cost_estimate=pl.CostEstimate(
-            flops=12_000_000_000, transcendentals=0, bytes_accessed=0
-        ),
+        cost_estimate=pl.CostEstimate(flops=14_000_000_000, transcendentals=0, bytes_accessed=0),
     )(
         lam_vec,
         queries,
         keys_values,
         gain_rows,
-        prompt_spots.reshape(prompt_len // CHUNK, 1, CHUNK),
-        wide[0][:top_rows],
-        wide[1],
-        wide[2],
+        jnp.broadcast_to(prompt_spots[:, None], (prompt_len, 128)),
+        jnp.concatenate([jnp.stack(bounds), jnp.zeros((5, rows), jnp.int32)]),
     )
 
 
 def attend_back(
-    queries, keys_values, lam_vec, gain_rows, vec_grad, out, lse, prompt_spots, bounds, prompt_part, span
+    queries, keys_values, lam_vec, gain_rows, vec_grad, out, lse, prompt_spots, bounds, prompt_part, span, done
 ):
-    first, heads = span[0], span[1] - span[0]
+    first, heads, all_heads = span[0], span[1] - span[0], lam_vec.shape[0]
     rows, keys = queries.shape[0], keys_values.shape[0]
     prompt_len = prompt_spots.shape[0]
     top_rows = min(rows, -(-prompt_part // 128) * 128)
     count = keys // CHUNK
     reach = jnp.concatenate([jnp.stack(bounds), jnp.zeros((5, rows), jnp.int32)])
     return pl.pallas_call(
-        lambda *refs: backward_kernel(prompt_len, top_rows, first, *refs),
+        lambda *refs: backward_kernel(prompt_len, top_rows, first, *refs[:9], *refs[9 + len(done) :]),
         grid=(heads,),
         in_specs=[
             pl.BlockSpec(memory_space=pltpu.SMEM),
@@ -432,17 +393,19 @@
             pl.BlockSpec((1, 16, rows), lambda h: (h + first, 0, 0)),
             pl.BlockSpec((prompt_len, 128), lambda h: (0, 0)),
             pl.BlockSpec((8, rows), lambda h: (0, 0)),
-        ],
+        ]
+        + [pl.BlockSpec(memory_space=pl.ANY)] * len(done),
         out_specs=[
-            pl.BlockSpec((2 * DK, rows), lambda h: (h, 0)),
-            pl.BlockSpec((keys, 2 * DK + DV), lambda h: (0, h)),
-            pl.BlockSpec((1, 8, DV), lambda h: (h, 0, 0)),
+            pl.BlockSpec((2 * DK, rows), lambda h: (h + first, 0)),
+            pl.BlockSpec((keys, 2 * DK + DV), lambda h: (0, h + first)),
+            pl.BlockSpec((1, 8, DV), lambda h: (h + first, 0, 0)),
         ],
         out_shape=[
-            jax.ShapeDtypeStruct((heads * 2 * DK, rows), bf16),
-            jax.ShapeDtypeStruct((keys, heads * (2 * DK + DV)), bf16),
-            jax.ShapeDtypeStruct((heads, 8, DV), f32),
+            jax.ShapeDtypeStruct((all_heads * 2 * DK, rows), bf16),
+            jax.ShapeDtypeStruct((keys, all_heads * (2 * DK + DV)), bf16),
+            jax.ShapeDtypeStruct((all_heads, 8, DV), f32),
         ],
+        input_output_aliases={9 + k: k for k in range(len(done))},
         scratch_shapes=[
             pltpu.VMEM((count, CHUNK, rows), f32),
             pltpu.VMEM((count, CHUNK, rows), f32),
@@ -453,7 +416,7 @@
         compiler_params=pltpu.CompilerParams(vmem_limit_bytes=58 * 2**20),
         name="attend_back",
         cost_estimate=pl.CostEstimate(
-            flops=24_000_000_000, transcendentals=0, bytes_accessed=0
+            flops=0, transcendentals=0, bytes_accessed=0
         ),
     )(
         lam_vec,
@@ -465,88 +428,94 @@
         lse,
         jnp.broadcast_to(prompt_spots[:, None], (prompt_len, 128)),
         reach,
-    )
-
-
-def norm_kernel(count, blocks_ref, swap_ref, *refs):
+        *done,
+    )
+
+
+def norm_kernel(count, unit, blocks_ref, swap_ref, *refs):
     *sources, gain_ref, out_ref = refs
     step = pl.program_id(0)
-    rows, depth = out_ref.shape
+    all_rows, depth = out_ref.shape
     block = depth // count
     upper = count // 4
-    straight = swap_ref[0] == 0
-
-    def norm_from(pieces):
-        total = jnp.zeros((rows, 1), f32)
-        for piece in pieces:
-            x = piece[:rows, :].astype(f32)
-            total = total + jnp.sum(x * x, axis=1, keepdims=True)
-        inverse = lax.rsqrt(total * (1.0 / depth) + norm_eps)
-        size = depth // len(pieces)
-        for spot in range(count):
-            lanes = slice(spot * block, (spot + 1) * block)
-            side = (spot % upper) * 4 * block // size
-            start = pl.multiple_of(blocks_ref[spot] * block - side * size, block)
-            part = pieces[side][:rows, pl.ds(start, block)]
-            if len(pieces) == 2:
-                part = jnp.where(straight, part, pieces[1 - side][:rows, pl.ds(start, block)])
-            out_ref[:, lanes] = (part.astype(f32) * inverse * gain_ref[:, lanes]).astype(bf16)
+    rows = all_rows // upper
+
+    def norm_from(pieces, stride):
+        for part in range(upper):
+            span = slice(part * stride, part * stride + rows)
+            total = jnp.zeros((rows, 128), f32)
+            for piece in pieces:
+                for lane in range(0, piece.shape[1], 128):
+                    x = piece[span, lane : lane + 128].astype(f32)
+                    total = total + x * x
+            total = jnp.sum(total, axis=1, keepdims=True)
+            inverse = jnp.broadcast_to(lax.rsqrt(total * (1.0 / depth) + norm_eps), (rows, block))
+            size = depth // len(pieces)
+            for spot in range(count):
+                lanes = slice(spot * block, (spot + 1) * block)
+                side = (spot % upper) * 4 * block // size
+                start = pl.multiple_of(blocks_ref[spot] * block - side * size, block)
+                x = pieces[side][span, pl.ds(start, block)].astype(f32)
+                out_ref[part * rows : (part + 1) * rows, lanes] = (
+                    x * inverse * gain_ref[:, lanes]
+                ).astype(bf16)
 
     for core in range(2):
-
-        @pl.when((step >= core * 2 * upper) & (step < (core + 1) * 2 * upper))
-        def _():
-            norm_from(sources[2 * core : 2 * core + 2])
-
-    @pl.when(step >= count)
+        for turn in range(2):
+
+            @pl.when((step >= core * 2) & (step < core * 2 + 2) & (swap_ref[0] == turn))
+            def _():
+                pair = sources[2 * core : 2 * core + 2]
+                norm_from(pair[::-1] if turn else pair, unit)
+
+    @pl.when(step >= 4)
     def _():
-        norm_from(sources[4:5])
-
-
-def norm_keys(at, prompt_groups, tokens_all, gain_row, prompt_part):
-    depth = tokens_all.shape[1]
+        norm_from(sources[4:5], rows)
+
+
+def norm_keys(at, prompt_groups, cont_tokens, gain_row, prompt_part):
+    cont_len, depth = cont_tokens.shape
     count, upper = at.count, at.upper
-    cont_len = tokens_all.shape[0] - prompt_part
     unit = prompt_groups[0].shape[0] // (2 * upper)
-    if (depth // count) % 128 or cont_len % prompt_part or upper % 2:
+    group_rows = upper * prompt_part
+    if (depth // count) % 128 or cont_len % group_rows or upper % 2:
         cores = []
         for pair in (prompt_groups[:2], prompt_groups[2:]):
             parts = jnp.stack([part.reshape(2 * upper, unit, -1)[:, :prompt_part] for part in pair])
             parts = at.flip(parts.reshape(2, 2 * upper * prompt_part, depth // 2), 0, at.tensor)
             cores.append(jnp.concatenate([parts[0], parts[1]], axis=1))
-        rows = at.to_relative(jnp.concatenate(cores + [tokens_all[prompt_part:]], axis=0))
+        rows = at.to_relative(jnp.concatenate(cores + [cont_tokens], axis=0))
         rows = rows.astype(f32)
         return (rows * inv_rms(rows, norm_eps) * gain_row).astype(bf16)
 
     def spot_of(core):
-        first = core * 2 * upper
-        return lambda i, blocks, swap: (jnp.clip(i - first, 0, 2 * upper - 1), 0)
+        return lambda i, blocks, swap: (jnp.clip(i - 2 * core, 0, 1), 0)
 
     return pl.pallas_call(
-        lambda *refs: norm_kernel(count, *refs),
+        lambda *refs: norm_kernel(count, unit, *refs),
         grid_spec=pltpu.PrefetchScalarGridSpec(
             num_scalar_prefetch=2,
-            grid=(count + cont_len // prompt_part,),
+            grid=(4 + cont_len // group_rows,),
             in_specs=[
-                pl.BlockSpec((unit, depth // 2), spot_of(core)) for core in (0, 0, 1, 1)
+                pl.BlockSpec((upper * unit, depth // 2), spot_of(core)) for core in (0, 0, 1, 1)
             ]
             + [
                 pl.BlockSpec(
-                    (prompt_part, depth),
-                    lambda i, blocks, swap: (1 + jnp.maximum(i - count, 0), 0),
+                    (group_rows, depth), lambda i, blocks, swap: (jnp.maximum(i - 4, 0), 0)
                 ),
                 pl.BlockSpec((1, depth), lambda i, blocks, swap: (0, 0)),
             ],
-            out_specs=pl.BlockSpec((prompt_part, depth), lambda i, blocks, swap: (i, 0)),
+            out_specs=pl.BlockSpec((group_rows, depth), lambda i, blocks, swap: (i, 0)),
         ),
         out_shape=jax.ShapeDtypeStruct((prompt_part * count + cont_len, depth), bf16),
+        compiler_params=pltpu.CompilerParams(vmem_limit_bytes=56 * 2**20),
         name="norm_keys",
         cost_estimate=pl.CostEstimate(flops=8_000_000_000, transcendentals=0, bytes_accessed=0),
     )(
         at.relative_blocks(),
         at.tensor.reshape(1).astype(jnp.int32),
         *prompt_groups,
-        tokens_all,
+        cont_tokens,
         gain_row.reshape(1, depth),
     )
 
@@ -625,7 +594,7 @@
     kv_far = at.swap_core(kv_side)
     q_side, q_near = at.swap_side(q_here), at.swap_core(q_here)
     prompt_far, prompt_far_turned = together(prompt_far, after(prompt_far_turned, kv_side))
-    tokens_all = at.in_order(tokens, tokens_turned)
+    cont_tokens = at.in_order(tokens, tokens_turned)[prompt_part:]
     cot_turned = at.swap_tensor(after(cot_rel, prompt_far_turned))
 
     small_all = jnp.concatenate(
@@ -670,7 +639,7 @@
 
     tokens_f32 = tokens_rel.astype(f32)
     prompt_groups = (prompt_pair, prompt_turned, prompt_far, prompt_far_turned)
-    normed_keys = norm_keys(at, prompt_groups, tokens_all, attn_gain_row, prompt_part)
+    normed_keys = norm_keys(at, prompt_groups, cont_tokens, attn_gain_row, prompt_part)
     kv_near, kv_far = after(kv_near, normed_keys), after(kv_far, normed_keys)
     kv_full = jnp.concatenate([kv_here, kv_side, kv_near, kv_far], axis=0)
     kv_full, q_side, out_here = together(kv_full, q_side, out_here)
@@ -685,30 +654,22 @@
     q_full = jnp.concatenate([q_here, q_side, q_near, q_far], axis=0)
     queries = plain_product(after(normed, keys_values), q_full).astype(bf16)
     fixed = (lam_vec, head_gain_row, prompt_spots, bounds, prompt_part)
-    middle = heads // 2
     queries, out_side, gate_here = together(queries, out_side, gate_here)
     out_far = at.swap_core(out_side)
     gate_side, gate_near = at.swap_side(gate_here), at.swap_core(gate_here)
-    first_out, first_vec, first_lse = attend(queries, keys_values, *fixed, (0, middle))
-    first_vec, cot_turned = together(first_vec, cot_turned)
-    second_out, second_vec, second_lse = attend(
-        after(queries, first_vec), keys_values, *fixed, (middle, heads)
-    )
-    second_vec, up_here, gate_side = together(second_vec, up_here, gate_side)
-    up_side, up_near = at.swap_side(up_here), at.swap_core(up_here)
-    gate_far = at.swap_core(gate_side)
-    out_near, out_far = after(out_near, second_vec), after(out_far, second_vec)
-    heads_out = jnp.concatenate([first_out, second_out], axis=1)
-    lse = jnp.concatenate([first_lse, second_lse], axis=0)
-    attn_vec = jnp.concatenate([first_vec, second_vec], axis=1)
+    heads_out, attn_vec, lse = attend(queries, keys_values, *fixed, (0, heads))
+    attn_vec, cot_turned = together(attn_vec, cot_turned)
+    out_near, out_far = after(out_near, attn_vec), after(out_far, attn_vec)
     out_full = jnp.concatenate([out_here, out_side, out_near, out_far], axis=0)
     attn_own, attn_other = at.own_half(attn_vec), at.other_half(attn_vec)
     out_send = cols_product(attn_other, out_full).astype(bf16)
     out_sent = at.swap_tensor(out_send)
     out_part = cols_product(after(attn_own, out_send), out_full)
     attn_two = jnp.concatenate([attn_own, attn_other], axis=0)
-    out_part, attn_two = together(out_part, attn_two)
-    out_sent = after(out_sent, out_part)
+    out_part, attn_two, gate_side, up_here = together(out_part, attn_two, gate_side, up_here)
+    up_side, up_near = at.swap_side(up_here), at.swap_core(up_here)
+    gate_far = at.swap_core(gate_side)
+    out_sent = after(out_sent, gate_side)
     residual = tokens_f32 + (out_part + out_sent.astype(f32))
 
     inv_second = inv_rms(residual, norm_eps)
@@ -745,20 +706,24 @@
     ).astype(bf16)
     up_grad = (hidden_grad * gate_proj * gate_sigmoid).astype(bf16)
 
-    def back_ffn(one, two):
-        return cols_product(one, gate_full) + cols_product(two, up_full)
+    def back_ffn(one, two, features=slice(None)):
+        return cols_product(one, gate_full[features]) + cols_product(two, up_full[features])
 
     gate_far_aside, gate_send = at.far_part(ffn_in, gate_grad, 3)
-    ffn_send = back_ffn(
-        after(gate_grad[local_rows:], gate_send), up_grad[local_rows:]
-    ).astype(bf16)
-    ffn_sent = at.swap_tensor(ffn_send)
-    ffn_part = back_ffn(after(gate_grad[:local_rows], ffn_send), up_grad[:local_rows])
-    gate_far_aside = after(gate_far_aside, ffn_part)
+    gate_other, up_other = after(gate_grad[local_rows:], gate_send), up_grad[local_rows:]
+    ffn_sends = [back_ffn(gate_other, up_other, slice(0, half)).astype(bf16)]
+    gate_other, up_other = after(gate_other, ffn_sends[0]), after(up_other, ffn_sends[0])
+    ffn_sends.append(back_ffn(gate_other, up_other, slice(half, D)).astype(bf16))
+    ffn_sent = [at.swap_tensor(send) for send in ffn_sends]
+    ffn_part = cols_product(after(gate_grad[:local_rows], ffn_sends[1]), gate_full)
+    ffn_part, down_grad_aside = together(ffn_part, down_grad_aside)
+    ffn_part = ffn_part + cols_product(after(up_grad[:local_rows], down_grad_aside), up_full)
+    gate_far_keep, gate_send = at.far_part(ffn_in, after(gate_grad, ffn_part), 2)
+    gate_far_aside = after(gate_far_aside, gate_send)
     gate_grad_side = at.aside_part(ffn_in, gate_grad, gate_far_aside)
     gate_grad_aside = at.swap_side(gate_grad_side)
-    down_grad_aside = after(down_grad_aside, gate_grad_side)
-    ffn_in_grad = ffn_part + after(ffn_sent, down_grad_aside).astype(f32)
+    ffn_sent = together(after(ffn_sent[0], gate_grad_side), ffn_sent[1])
+    ffn_in_grad = ffn_part + jnp.concatenate(ffn_sent, axis=1).astype(f32)
     residual_grad = cot_rel.astype(f32) + norm_back(
         residual, inv_second, ffn_gain_row, ffn_in_grad
     )
@@ -770,28 +735,22 @@
     grad_down = at.scatter_upper(down_last)
     up_far_aside, up_send = at.far_part(ffn_in, after(up_grad, down_last), 3)
     up_far_keep, up_send = at.far_part(ffn_in, after(up_grad, up_send), 2)
-    gate_far_keep, gate_send = at.far_part(ffn_in, after(gate_grad, up_send), 2)
-    up_far_aside = after(up_far_aside, gate_send)
-    up_grad_side = at.aside_part(ffn_in, up_grad, up_far_aside)
-    branch = jnp.concatenate([branch_own, after(branch_sent, up_grad_side)], axis=0)
+    branch = jnp.concatenate([branch_own, after(branch_sent, up_send)], axis=0)
     vec_two = plain_product(branch, out_full)
     vec_grad = at.in_order(vec_two[:local_rows], vec_two[local_rows:])
-    vec_grad, gate_far_keep, gate_grad_aside = together(vec_grad, gate_far_keep, gate_grad_aside)
-    up_grad_aside = at.swap_side(after(up_grad_side, gate_grad_aside))
+    middle = heads // 2
+    back_args = (queries, keys_values, lam_vec, head_gain_row)
+    back_fixed = (heads_out, lse, prompt_spots, bounds, prompt_part)
+    half_back = attend_back(*back_args, vec_grad, *back_fixed, (0, middle), ())
+    half_back, gate_grad_aside = together(half_back, gate_grad_aside)
+    gate_far_keep = after(gate_far_keep, gate_grad_aside)
     gate_last = at.near_part(ffn_in, gate_grad, gate_far_keep, gate_grad_aside)
     grad_gate = at.scatter_upper(gate_last)
+    up_far_aside = after(up_far_aside, gate_last)
+    up_grad_side = at.aside_part(ffn_in, up_grad, up_far_aside)
+    up_grad_aside = at.swap_side(up_grad_side)
     queries_grad, kv_grad, head_sums = attend_back(
-        queries,
-        keys_values,
-        lam_vec,
-        head_gain_row,
-        after(vec_grad, gate_last),
-        heads_out,
-        lse,
-        prompt_spots,
-        bounds,
-        prompt_part,
-        (0, heads),
+        *back_args, after(vec_grad, up_grad_side), *back_fixed, (middle, heads), half_back
     )
     queries_grad, kv_grad, head_sums, grad_down = together(
         queries_grad, kv_grad, head_sums, grad_down

time: 966 us -> 923 us (0.955)
  Pallas kernels: 132 us -> 90.2 us
    pallas_call x2 -> x1, Pallas kernels: 58.9 us -> 31.6 us  [attend(): pl.pallas_call(lambda *refs: forward_kernel(prompt_len, top_rows, first,...]
    pallas_call x1 -> x2, Pallas kernels: 53.1 us -> 45 us  [attend_back(): pl.pallas_call(lambda *refs: backward_kernel(prompt_len, top_rows, first,...]
    dot_general x12 -> x14, matrix products: 87.4 us -> 81.4 us  [cols_product(): lax.dot_general(first_arg, second_arg, (((1,), (1,)), ((), ())), preferre...]
    ppermute x11 -> x12, waiting for transfers between devices: 106 us -> 103 us  [swap_tensor(): return lax.ppermute(value, 'tensor', [(0, 1), (1, 0)])]
    unnamed x206 -> x199, local copies, waits for them, and re-layouts: 46.5 us -> 48.6 us
  transfers between devices with their start and end apart: 72 -> 73, of which waited for: 21 -> 22; matrix products, arithmetic and copies ran while one was open for 48% -> 50% of each run, Pallas kernels for 14% -> 10%
where the time goes in v4:
time: 923 us; the launch traced here: 913 us
  waiting for transfers between devices  288 us (31%)
  matrix products  282 us (31%)
  local copies, waits for them, and re-layouts  108 us (12%)
  Pallas kernels  90.2 us (10%)
  other arithmetic  88.9 us (10%)
  starting transfers between devices  39.8 us (4%)
  between operations  15.8 us (2%)
    ppermute x14, waiting for transfers between devices, swap_side(): return lax.ppermute(value, 'dp', self.side_pairs)  159 us
    dot_general x24, matrix products, rows_product(): lax.dot_general(first_arg, second_arg, (((0,), (0,)), ((), ())), preferre...  120 us
    ppermute x12, waiting for transfers between devices, swap_tensor(): return lax.ppermute(value, 'tensor', [(0, 1), (1, 0)])  103 us
    dot_general x14, matrix products, cols_product(): lax.dot_general(first_arg, second_arg, (((1,), (1,)), ((), ())), preferre...  81.4 us
    dot_general x6, matrix products, plain_product(): return jnp.dot(first_arg, second_arg, preferred_element_type=f32)  80.3 us
    unnamed x199, local copies, waits for them, and re-layouts  48.6 us
    pallas_call x2, Pallas kernels, attend_back(): pl.pallas_call(lambda *refs: backward_kernel(prompt_len, top_rows, first,...  45 us
    pallas_call x1, Pallas kernels, attend(): pl.pallas_call(lambda *refs: forward_kernel(prompt_len, top_rows, first,...  31.6 us
  transfers between devices with their start and end apart: 73, of which 22 were waited for; matrix products, arithmetic and copies ran while one was open for 50% of the time, Pallas kernels for 10%

profile of v4, /device:TPU:0, one launch (start us, length us, event | category | flops | bytes accessed | tf_op | source)
XLA Modules:
  0.0 913.5 jit_solution(16962049118300719359)
XLA Ops:
  8.2 4.9 collective-permute-start
  46.5 9.1 collective-permute-done.1
  59.6 22.7 %collective-permute-done.2 = bf16[576,1024]{1,0:T(8,128)(2,1)} collective-permute-done((bf16[576,1024]{1,0:T(8,128)(2,1)}, bf16[576,1024]{1,0:T(8,128)(2,1)}, u32[]{:S(2)}, u32[]{:S(2)}) %collective-permute-start.2) | collective-permute-done | bytes 1179680 | tf_op jit(solution)/shard_map/ppermute | solution.py:77
  86.0 14.5 %all-gather.10.cloned.1.call-done = bf16[512,2048]{1,0:T(8,128)(2,1)} async-done(((bf16[128,2048]{1,0:T(8,128)(2,1)}), bf16[512,2048]{1,0:T(8,128)(2,1)}) %all-gather.10.cloned.1.call-update) | async-done | bytes 2097168 | tf_op jit(solution)/shard_map/all_gather | solution.py:83
  104.9 30.6 %collective-permute-done.4.refs_3_ = bf16[1152,1024]{1,0:T(8,128)(2,1)} collective-permute-done((bf16[1152,1024]{1,0:T(8,128)(2,1)}, bf16[1152,1024]{1,0:T(8,128)(2,1)}, u32[]{:S(2)}, u32[]{:S(2)}) %collective-permute-start.4) | collective-permute-done | bytes 2359328 | tf_op jit(solution)/shard_map/ppermute | solution.py:80
  136.4 12.4 %collective-permute-done.7 = bf16[512,2048]{1,0:T(8,128)(2,1)} collective-permute-done((bf16[512,2048]{1,0:T(8,128)(2,1)}, bf16[512,2048]{1,0:T(8,128)(2,1)}, u32[]{:S(2)}, u32[]{:S(2)}) %collective-permute-start.7) | collective-permute-done | bytes 2097184 | tf_op jit(solution)/shard_map/ppermute | solution.py:77
  161.2 13.5 %norm_keys.1 = bf16[2560,2048]{1,0:T(8,128)(2,1)} custom-call(s32[16]{0:T(128)} %get-tuple-element.303.refs_0_, s32[1]{0:T(128)} %bitcast.6.refs_1_, bf16[1152,1024]{1,0:T(8,128)(2,1)} %constant_dynamic-update-slice_fusion.refs_2_, bf16[1152,1024]{1,0:T(8,128)(2,1)} %collective-permute-done.4.refs_3_, bf16[1152,1024]{1,0:T(8,128)(2,1)} %collective-permute-done.3.refs_4_, ...), custom_call_target="tpu_custom_call" | custom-call | flops 8000000000 | tf_op jit(solution)/shard_map/norm_keys/pallas_call | solution.py:494
  174.7 6.6 pad_maximum_fusion.1
  187.9 28.0 %convolution_convert_fusion.refs_2_ = bf16[2560,2048]{1,0:T(8,128)(2,1)} fusion(bf16[2560,2048]{1,0:T(8,128)(2,1)} %norm_keys.1, bf16[2048,2048]{1,0:T(8,128)(2,1)} %pad_maximum_fusion.1), kind=kOutput, calls=%fused_computation.1 | convolution fusion | flops 21480079360 | bytes 29360128 | tf_op jit(solution)/shard_map/dot_general | solution.py:33
  234.2 31.6 %attend.1 = (f32[640,1024]{1,0:T(8,128)}, bf16[640,1024]{1,0:T(8,128)(2,1)}, f32[4,16,640]{2,1,0:T(8,128)}) custom-call(f32[4]{0:T(128)} %subtract_add_fusion.1.refs_0_, bf16[640,1024]{1,0:T(8,128)(2,1)} %convolution_convert_fusion.11.refs_1_, bf16[2560,2048]{1,0:T(8,128)(2,1)} %convolution_convert_fusion.refs_2_, f32[1,1024]{1,0:T(1,128)} %bitcast.114, ...), custom_call_target="tpu_custom_call" | custom-call | flops 14000000000 | tf_op jit(solution)/shard_map/attend/pallas_call | solution.py:335
  277.0 20.3 %collective-permute-done.16 = bf16[512,2816]{1,0:T(8,128)(2,1)} collective-permute-done((bf16[512,2816]{1,0:T(8,128)(2,1)}, bf16[512,2816]{1,0:T(8,128)(2,1)}, u32[]{:S(2)}, u32[]{:S(2)}) %collective-permute-start.16) | collective-permute-done | bytes 2883616 | tf_op jit(solution)/shard_map/ppermute | solution.py:77
  302.8 25.7 %collective-permute-done.17 = bf16[320,2048]{1,0:T(8,128)(2,1)S(1)} collective-permute-done((bf16[320,2048]{1,0:T(8,128)(2,1)S(1)}, bf16[320,2048]{1,0:T(8,128)(2,1)S(1)}, u32[]{:S(2)}, u32[]{:S(2)}) %collective-permute-start.17) | collective-permute-done | bytes 1310752 | tf_op jit(solution)/shard_map/ppermute | solution.py:80
  332.0 14.6 %pad_maximum_fusion = bf16[2048,2816]{1,0:T(8,128)(2,1)} fusion(bf16[512,2816]{1,0:T(8,128)(2,1)S(1)} %collective-permute-done.20, bf16[512,2816]{1,0:T(8,128)(2,1)} %collective-permute-done.19, bf16[512,2816]{1,0:T(8,128)(2,1)} %collective-permute-done.16, bf16[512,2816]{1,0:T(8,128)(2,1)S(1)} %copy-done.40), kind=kLoop, calls=%fused_computation | loop fusion | flops 46137344 | bytes 23068672 | tf_op jit(solution)/shard_map/concatenate | solution.py:679
  346.6 16.1 %collective-permute-done.21 = bf16[512,2816]{1,0:T(8,128)(2,1)} collective-permute-done((bf16[512,2816]{1,0:T(8,128)(2,1)}, bf16[512,2816]{1,0:T(8,128)(2,1)}, u32[]{:S(2)}, u32[]{:S(2)}) %collective-permute-start.21) | collective-permute-done | bytes 2883616 | tf_op jit(solution)/shard_map/ppermute | solution.py:77
  367.4 13.0 %fusion.138 = f32[640,2816]{1,0:T(8,128)} fusion(bf16[2048,2816]{1,0:T(8,128)(2,1)} %pad_maximum_fusion, bf16[320,2048]{1,0:T(8,128)(2,1)S(1)} %collective-permute-done.18, bf16[320,2048]{1,0:T(8,128)(2,1)S(1)} %multiply_convert_fusion.3), kind=kOutput, calls=%fused_computation.268 | convolution fusion | flops 7387217920 | bytes 21364736 | tf_op jit(solution)/shard_map/dot_general | solution.py:33
  390.3 15.4 %multiply_convert_fusion.2 = (bf16[640,2816]{1,0:T(8,128)(2,1)S(1)}, f32[640,2816]{1,0:T(8,128)}) fusion(f32[640,2816]{1,0:T(8,128)} %fusion.138, bf16[640,2048]{1,0:T(8,128)(2,1)S(1)} %pad_maximum_fusion.3, bf16[2048,2816]{1,0:T(8,128)(2,1)} %constant_dynamic-update-slice_fusion.10), kind=kOutput, calls=%fused_computation.5 | convolution fusion | flops 7392788480 | bytes 32178176 | tf_op jit(solution)/shard_map/dot_general | solution.py:33
  412.4 19.0 %collective-permute-done.24 = bf16[512,2816]{1,0:T(8,128)(2,1)} collective-permute-done((bf16[512,2816]{1,0:T(8,128)(2,1)S(1)}, bf16[512,2816]{1,0:T(8,128)(2,1)}, u32[]{:S(2)}, u32[]{:S(2)}) %collective-permute-start.24) | collective-permute-done | bytes 2883616 | tf_op jit(solution)/shard_map/ppermute | solution.py:77
  445.3 17.0 %multiply_convert_fusion = (bf16[640,2816]{1,0:T(8,128)(2,1)S(1)}, bf16[640,2816]{1,0:T(8,128)(2,1)S(1)}) fusion(f32[640,2816]{1,0:T(8,128)} %fusion.138, f32[640,2816]{1,0:T(8,128)} %get-tuple-element.333, bf16[640,2048]{1,0:T(8,128)(2,1)} %copy-done.34, bf16[2048,2816]{1,0:T(8,128)(2,1)} %copy-done.53), kind=kOutput, calls=%fused_computation.3 | convolution fusion | flops 7405404160 | bytes 35782656 | tf_op jit(solution)/shard_map/dot_general | solution.py:33
  466.2 6.8 fusion
  480.8 4.5 fusion.4
  488.8 7.5 fusion.147
  496.3 6.6 collective-permute-done.28
  502.9 10.2 %fusion.148 = f32[320,2048]{1,0:T(8,128)} fusion(bf16[320,2816]{1,0:T(8,128)(2,1)} %get-tuple-element.219, bf16[2048,2816]{1,0:T(8,128)(2,1)} %constant_dynamic-update-slice_fusion.10), kind=kOutput, calls=%fused_computation.277 | convolution fusion | flops 3690987520 | bytes 15958016 | tf_op jit(solution)/shard_map/dot_general | solution.py:43
  519.3 6.0 add_convert_fusion.4
  530.2 7.2 add_convert_fusion.3
  540.0 6.5 convolution_convert_fusion.2
  550.9 19.0 %collective-permute-done.32 = bf16[320,2048]{1,0:T(8,128)(2,1)S(1)} collective-permute-done((bf16[320,2048]{1,0:T(8,128)(2,1)}, bf16[320,2048]{1,0:T(8,128)(2,1)S(1)}, u32[]{:S(2)}, u32[]{:S(2)}) %collective-permute-start.32) | collective-permute-done | bytes 1310752 | tf_op jit(solution)/shard_map/ppermute | solution.py:80
  575.3 22.5 %attend_back.2 = (bf16[1024,640]{1,0:T(8,128)(2,1)}, bf16[2560,2048]{1,0:T(8,128)(2,1)}, f32[4,8,256]{2,1,0:T(8,128)}) custom-call(f32[4]{0:T(128)} %subtract_add_fusion.1.refs_0_, bf16[640,1024]{1,0:T(8,128)(2,1)} %convolution_convert_fusion.11.refs_1_, bf16[2560,2048]{1,0:T(8,128)(2,1)} %convolution_convert_fusion.refs_2_, f32[1,1024]{1,0:T(1,128)} %bitcast.115, ...), custom_call_target="tpu_custom_call" | custom-call | tf_op jit(solution)/shard_map/attend_back/pallas_call | solution.py:383
  601.9 8.0 add_convert_fusion.2
  610.0 6.9 add_convert_fusion.1
  617.6 22.5 %attend_back.3 = (bf16[1024,640]{1,0:T(8,128)(2,1)}, bf16[2560,2048]{1,0:T(8,128)(2,1)}, f32[4,8,256]{2,1,0:T(8,128)}) custom-call(f32[4]{0:T(128)} %subtract_add_fusion.1.refs_0_, bf16[640,1024]{1,0:T(8,128)(2,1)} %convolution_convert_fusion.11.refs_1_, ...), custom_call_target="tpu_custom_call", output_to_operand_aliasing={{0}: (9, {}), {1}: (10, {}), {2}: (11, {})} | custom-call | tf_op jit(solution)/shard_map/attend_back/pallas_call | solution.py:383
  640.1 6.3 fusion.141
  647.6 8.5 convolution_convert_fusion.8
  656.4 25.8 %collective-permute-done.40 = bf16[512,2816]{1,0:T(8,128)(2,1)} collective-permute-done((bf16[512,2816]{1,0:T(8,128)(2,1)}, bf16[512,2816]{1,0:T(8,128)(2,1)}, u32[]{:S(2)}, u32[]{:S(2)}) %collective-permute-start.40) | collective-permute-done | bytes 2883616 | tf_op jit(solution)/shard_map/ppermute | solution.py:77
  684.8 7.1 add_convert_fusion
  692.0 10.5 %convolution_convert_fusion.7 = bf16[512,2048]{1,0:T(8,128)(2,1)} fusion(bf16[2560,2048]{1,0:T(8,128)(2,1)} %get-tuple-element.254, bf16[2560,2048]{1,0:T(8,128)(2,1)} %norm_keys.1), kind=kOutput, calls=%fused_computation.64 | convolution fusion | flops 5369757696 | bytes 15204352 | tf_op jit(solution)/shard_map/dot_general | solution.py:37
  702.5 10.7 %add_convert_fusion.8 = bf16[512,2048]{1,0:T(8,128)(2,1)} fusion(bf16[512,2048]{1,0:T(8,128)(2,1)} %collective-permute-done.37, bf16[2560,2048]{1,0:T(8,128)(2,1)} %get-tuple-element.254, bf16[2560,2048]{1,0:T(8,128)(2,1)} %norm_keys.1), kind=kOutput, calls=%fused_computation.42 | convolution fusion | flops 5371854848 | bytes 17301504 | tf_op jit(solution)/shard_map/dot_general | solution.py:37
  722.1 8.6 fusion.29
  731.8 5.6 add_convert_fusion.7
  738.6 9.3 %fusion.22 = f32[512,2048]{1,0:T(8,128)S(1)} fusion(bf16[2560,2048]{1,0:T(8,128)(2,1)} %get-tuple-element.254, bf16[2560,2048]{1,0:T(8,128)(2,1)} %norm_keys.1), kind=kOutput, calls=%fused_computation.80 | convolution fusion | flops 5368709120 | bytes 17301504 | tf_op jit(solution)/shard_map/dot_general | solution.py:37
  752.2 9.6 %convolution_convert_fusion.10 = bf16[320,2048]{1,0:T(8,128)(2,1)} fusion(bf16[2048,2816]{1,0:T(8,128)(2,1)} %copy-done.53, bf16[640,2816]{1,0:T(8,128)(2,1)S(1)} %copy-done.18), kind=kOutput, calls=%fused_computation.72 | convolution fusion | flops 3691642880 | bytes 14647296 | tf_op jit(solution)/shard_map/dot_general | solution.py:43
  761.9 24.1 %collective-permute-done.47 = bf16[512,2048]{1,0:T(8,128)(2,1)} collective-permute-done((bf16[512,2048]{1,0:T(8,128)(2,1)}, bf16[512,2048]{1,0:T(8,128)(2,1)}, u32[]{:S(2)}, u32[]{:S(2)}) %collective-permute-start.47) | collective-permute-done | bytes 2097184 | tf_op jit(solution)/shard_map/ppermute | solution.py:77
  786.0 4.7 add_convert_fusion.6
  812.2 18.6 %collective-permute-done.45 = bf16[320,2048]{1,0:T(8,128)(2,1)} collective-permute-done((bf16[320,2048]{1,0:T(8,128)(2,1)S(1)}, bf16[320,2048]{1,0:T(8,128)(2,1)}, u32[]{:S(2)}, u32[]{:S(2)}) %collective-permute-start.45) | collective-permute-done | bytes 1310752 | tf_op jit(solution)/shard_map/ppermute | solution.py:80
  839.9 5.8 fusion.46
  850.0 5.0 collective-permute-done.51
  859.8 8.5 fusion.48
  882.0 4.8 fusion.16
  (484 shorter events, 274.6 us)
Async XLA Ops:
  7.2 48.5 %all-gather.8.cloned.1.call-start = ((), (), s32[]{:S(2)}) async-start(), calls=%async_computation.7 | async-start | bytes 1474560 | tf_op jit(solution)/shard_map/all_gather | solution.py:83
  20.6 79.8 %all-gather.10.cloned.1.call-start = ((), (), s32[]{:S(2)}) async-start(), calls=%async_computation.8 | async-start | bytes 2621440 | tf_op jit(solution)/shard_map/all_gather | solution.py:83
  23.3 113.1 %all-gather.12.cloned.1.call-start = ((), (), s32[]{:S(2)}) async-start(), calls=%async_computation.9 | async-start | bytes 1310720 | tf_op jit(solution)/shard_map/all_gather | solution.py:83
  24.0 157.3 %all-gather.14.cloned.1.call-start = ((), (), s32[]{:S(2)}) async-start(), calls=%async_computation.10 | async-start | bytes 1310720 | tf_op jit(solution)/shard_map/all_gather | solution.py:83
  24.6 207.5 %all-gather.16.cloned.1.call-start = ((), (), s32[]{:S(2)}) async-start(), calls=%async_computation.11 | async-start | bytes 3604480 | tf_op jit(solution)/shard_map/all_gather | solution.py:83
  25.2 251.9 %all-gather.18.cloned.1.call-start = ((), (), s32[]{:S(2)}) async-start(), calls=%async_computation.12 | async-start | bytes 3604480 | tf_op jit(solution)/shard_map/all_gather | solution.py:83
  57.2 289.5 %all-gather.20.cloned.1.call-start = ((), (), s32[]{:S(2)}) async-start(), calls=%async_computation.13 | async-start | bytes 3604480 | tf_op jit(solution)/shard_map/all_gather | solution.py:83
  84.6 50.9 %collective-permute-start.4 = (bf16[1152,1024]{1,0:T(8,128)(2,1)}, bf16[1152,1024]{1,0:T(8,128)(2,1)}, u32[]{:S(2)}, u32[]{:S(2)}) collective-permute-start(bf16[1152,1024]{1,0:T(8,128)(2,1)} %constant_dynamic-update-slice_fusion.refs_2_), channel_id=1, source_target_pairs={{0,1},{1,0},{2,3},{3,2},{4,5},{5,4},{6,7},{7,6},{8,9},{9,8},{10,11... | collective-permute-start | bytes 7077896 | tf_op jit(solution)/shard_map/ppermute | solution.py:80
  100.4 48.4 %collective-permute-start.7 = (bf16[512,2048]{1,0:T(8,128)(2,1)}, bf16[512,2048]{1,0:T(8,128)(2,1)}, u32[]{:S(2)}, u32[]{:S(2)}) collective-permute-start(bf16[512,2048]{1,0:T(8,128)(2,1)} %all-gather.10.cloned.1.call-done), channel_id=1, source_target_pairs={{0,4},{2,6},{4,0},{6,2},{8,12},{10,14},{12,8},{14,10},{16,20},{18,... | collective-permute-start | bytes 6291464 | tf_op jit(solution)/shard_map/ppermute | solution.py:77
  150.2 489.9 %reduce-scatter.8.cloned.1.call-start = ((), (), s32[]{:S(2)}) async-start(), calls=%async_computation.14 | async-start | bytes 3604480 | tf_op jit(solution)/shard_map/reduce_scatter | solution.py:103
  155.3 68.1 %collective-permute-start.10 = (bf16[512,1024]{1,0:T(8,128)(2,1)}, bf16[512,1024]{1,0:T(8,128)(2,1)}, u32[]{:S(2)}, u32[]{:S(2)}) collective-permute-start(bf16[512,1024]{1,0:T(8,128)(2,1)} %all-gather.12.cloned.1.call-done), channel_id=1, source_target_pairs={{0,2},{2,0},{4,6},{6,4},{8,10},{10,8},{12,14},{14,12},{16,18},{18,... | collective-permute-start | bytes 3145736 | tf_op jit(solution)/shard_map/ppermute | solution.py:74
  181.3 85.9 %collective-permute-start.14 = (bf16[512,1024]{1,0:T(8,128)(2,1)}, bf16[512,1024]{1,0:T(8,128)(2,1)}, u32[]{:S(2)}, u32[]{:S(2)}) collective-permute-start(bf16[512,1024]{1,0:T(8,128)(2,1)} %all-gather.14.cloned.1.call-done), channel_id=1, source_target_pairs={{0,2},{2,0},{4,6},{6,4},{8,10},{10,8},{12,14},{14,12},{16,18},{18,... | collective-permute-start | bytes 3145736 | tf_op jit(solution)/shard_map/ppermute | solution.py:74
  181.4 50.7 %collective-permute-start.12 = (bf16[512,1024]{1,0:T(8,128)(2,1)}, bf16[512,1024]{1,0:T(8,128)(2,1)}, u32[]{:S(2)}, u32[]{:S(2)}) collective-permute-start(bf16[512,1024]{1,0:T(8,128)(2,1)} %all-gather.14.cloned.1.call-done), channel_id=1, source_target_pairs={{0,4},{2,6},{4,0},{6,2},{8,12},{10,14},{12,8},{14,10},{16,20},{18,... | collective-permute-start | bytes 3145736 | tf_op jit(solution)/shard_map/ppermute | solution.py:77
  186.1 38.7 %collective-permute-start.11 = (bf16[512,1024]{1,0:T(8,128)(2,1)}, bf16[512,1024]{1,0:T(8,128)(2,1)}, u32[]{:S(2)}, u32[]{:S(2)}) collective-permute-start(bf16[512,1024]{1,0:T(8,128)(2,1)} %collective-permute-done.9), channel_id=1, source_target_pairs={{0,2},{2,0},{4,6},{6,4},{8,10},{10,8},{12,14},{14,12},{16,18},{18,... | collective-permute-start | bytes 3145736 | tf_op jit(solution)/shard_map/ppermute | solution.py:74
  186.4 80.8 %collective-permute-start.13 = (bf16[320,2048]{1,0:T(8,128)(2,1)}, bf16[320,2048]{1,0:T(8,128)(2,1)}, u32[]{:S(2)}, u32[]{:S(2)}) collective-permute-start(bf16[320,2048]{1,0:T(8,128)(2,1)} %reshape.266), channel_id=1, source_target_pairs={{0,1},{1,0},{2,3},{3,2},{4,5},{5,4},{6,7},{7,6},{8,9},{9,8},{10,11... | collective-permute-start | bytes 3932168 | tf_op jit(solution)/shard_map/ppermute | solution.py:80
  232.1 99.4 %collective-permute-start.19 = (bf16[512,2816]{1,0:T(8,128)(2,1)}, bf16[512,2816]{1,0:T(8,128)(2,1)}, u32[]{:S(2)}, u32[]{:S(2)}) collective-permute-start(bf16[512,2816]{1,0:T(8,128)(2,1)} %all-gather.16.cloned.1.call-done), channel_id=1, source_target_pairs={{0,2},{2,0},{4,6},{6,4},{8,10},{10,8},{12,14},{14,12},{16,18},{18,... | collective-permute-start | bytes 8650760 | tf_op jit(solution)/shard_map/ppermute | solution.py:74
  232.1 65.2 %collective-permute-start.16 = (bf16[512,2816]{1,0:T(8,128)(2,1)}, bf16[512,2816]{1,0:T(8,128)(2,1)}, u32[]{:S(2)}, u32[]{:S(2)}) collective-permute-start(bf16[512,2816]{1,0:T(8,128)(2,1)} %all-gather.16.cloned.1.call-done), channel_id=1, source_target_pairs={{0,4},{2,6},{4,0},{6,2},{8,12},{10,14},{12,8},{14,10},{16,20},{18,... | collective-permute-start | bytes 8650760 | tf_op jit(solution)/shard_map/ppermute | solution.py:77
  232.7 37.1 %collective-permute-start.15 = (bf16[512,1024]{1,0:T(8,128)(2,1)}, bf16[512,1024]{1,0:T(8,128)(2,1)S(1)}, u32[]{:S(2)}, u32[]{:S(2)}) collective-permute-start(bf16[512,1024]{1,0:T(8,128)(2,1)} %collective-permute-done.12), channel_id=1, source_target_pairs={{0,2},{2,0},{4,6},{6,4},{8,10},{10,8},{12,14},{14,12},{16,18},{18,... | collective-permute-start | bytes 3145736 | tf_op jit(solution)/shard_map/ppermute | solution.py:74
  297.3 34.2 %collective-permute-start.20 = (bf16[512,2816]{1,0:T(8,128)(2,1)}, bf16[512,2816]{1,0:T(8,128)(2,1)S(1)}, u32[]{:S(2)}, u32[]{:S(2)}) collective-permute-start(bf16[512,2816]{1,0:T(8,128)(2,1)} %collective-permute-done.16), channel_id=1, source_target_pairs={{0,2},{2,0},{4,6},{6,4},{8,10},{10,8},{12,14},{14,12},{16,18},{18,... | collective-permute-start | bytes 8650760 | tf_op jit(solution)/shard_map/ppermute | solution.py:74
  297.8 64.9 %collective-permute-start.21 = (bf16[512,2816]{1,0:T(8,128)(2,1)}, bf16[512,2816]{1,0:T(8,128)(2,1)}, u32[]{:S(2)}, u32[]{:S(2)}) collective-permute-start(bf16[512,2816]{1,0:T(8,128)(2,1)} %all-gather.18.cloned.1.call-done), channel_id=1, source_target_pairs={{0,4},{2,6},{4,0},{6,2},{8,12},{10,14},{12,8},{14,10},{16,20},{18,... | collective-permute-start | bytes 8650760 | tf_op jit(solution)/shard_map/ppermute | solution.py:77
  301.3 79.2 %collective-permute-start.22 = (bf16[512,2816]{1,0:T(8,128)(2,1)}, bf16[512,2816]{1,0:T(8,128)(2,1)}, u32[]{:S(2)}, u32[]{:S(2)}) collective-permute-start(bf16[512,2816]{1,0:T(8,128)(2,1)} %all-gather.18.cloned.1.call-done), channel_id=1, source_target_pairs={{0,2},{2,0},{4,6},{6,4},{8,10},{10,8},{12,14},{14,12},{16,18},{18,... | collective-permute-start | bytes 8650760 | tf_op jit(solution)/shard_map/ppermute | solution.py:74
  331.0 36.4 %collective-permute-start.18 = (bf16[320,2048]{1,0:T(8,128)(2,1)S(1)}, bf16[320,2048]{1,0:T(8,128)(2,1)S(1)}, u32[]{:S(2)}, u32[]{:S(2)}) collective-permute-start(bf16[320,2048]{1,0:T(8,128)(2,1)S(1)} %multiply_convert_fusion.3), channel_id=1, source_target_pairs={{0,1},{1,0},{2,3},{3,2},{4,5},{5,4},{6,7},{7,6},{8,9},{9,8},{10,11... | collective-permute-start | bytes 3932168 | tf_op jit(solution)/shard_map/ppermute | solution.py:80
  366.3 65.8 %collective-permute-start.25 = (bf16[512,2816]{1,0:T(8,128)(2,1)S(1)}, bf16[512,2816]{1,0:T(8,128)(2,1)}, u32[]{:S(2)}, u32[]{:S(2)}) collective-permute-start(bf16[512,2816]{1,0:T(8,128)(2,1)S(1)} %copy-done.36), channel_id=1, source_target_pairs={{0,2},{2,0},{4,6},{6,4},{8,10},{10,8},{12,14},{14,12},{16,18},{18,... | collective-permute-start | bytes 8650760 | tf_op jit(solution)/shard_map/ppermute | solution.py:74
  366.9 64.5 %collective-permute-start.24 = (bf16[512,2816]{1,0:T(8,128)(2,1)S(1)}, bf16[512,2816]{1,0:T(8,128)(2,1)}, u32[]{:S(2)}, u32[]{:S(2)}) collective-permute-start(bf16[512,2816]{1,0:T(8,128)(2,1)S(1)} %copy-done.36), channel_id=1, source_target_pairs={{0,4},{2,6},{4,0},{6,2},{8,12},{10,14},{12,8},{14,10},{16,20},{18,... | collective-permute-start | bytes 8650760 | tf_op jit(solution)/shard_map/ppermute | solution.py:77
  431.5 98.6 %collective-permute-start.33 = (bf16[512,2816]{1,0:T(8,128)(2,1)}, bf16[512,2816]{1,0:T(8,128)(2,1)}, u32[]{:S(2)}, u32[]{:S(2)}) collective-permute-start(bf16[512,2816]{1,0:T(8,128)(2,1)} %convolution_convert_fusion.5), channel_id=1, source_target_pairs={{0,2},{2,0},{4,6},{6,4},{8,10},{10,8},{12,14},{14,12},{16,18},{18,... | collective-permute-start | bytes 8650760 | tf_op jit(solution)/shard_map/ppermute | solution.py:74
  438.2 64.7 %collective-permute-start.28 = (bf16[512,2816]{1,0:T(8,128)(2,1)}, bf16[512,2816]{1,0:T(8,128)(2,1)}, u32[]{:S(2)}, u32[]{:S(2)}) collective-permute-start(bf16[512,2816]{1,0:T(8,128)(2,1)} %add_convert_fusion.5), channel_id=1, source_target_pairs={{0,4},{2,6},{4,0},{6,2},{8,12},{10,14},{12,8},{14,10},{16,20},{18,... | collective-permute-start | bytes 8650760 | tf_op jit(solution)/shard_map/ppermute | solution.py:77
  473.1 46.2 %collective-permute-start.30 = (bf16[512,2816]{1,0:T(8,128)(2,1)S(1)}, bf16[512,2816]{1,0:T(8,128)(2,1)}, u32[]{:S(2)}, u32[]{:S(2)}) collective-permute-start(bf16[512,2816]{1,0:T(8,128)(2,1)S(1)} %convolution_convert_fusion.4), channel_id=1, source_target_pairs={{0,2},{2,0},{4,6},{6,4},{8,10},{10,8},{12,14},{14,12},{16,18},{18,... | collective-permute-start | bytes 8650760 | tf_op jit(solution)/shard_map/ppermute | solution.py:74
  477.3 47.9 %collective-permute-start.29 = (bf16[320,1024]{1,0:T(8,128)(2,1)}, bf16[320,1024]{1,0:T(8,128)(2,1)S(1)}, u32[]{:S(2)}, u32[]{:S(2)}) collective-permute-start(bf16[320,1024]{1,0:T(8,128)(2,1)} %fusion.40), channel_id=1, source_target_pairs={{0,1},{1,0},{2,3},{3,2},{4,5},{5,4},{6,7},{7,6},{8,9},{9,8},{10,11... | collective-permute-start | bytes 1966088 | tf_op jit(solution)/shard_map/ppermute | solution.py:80
  488.3 37.0 %collective-permute-start.31 = (bf16[320,1024]{1,0:T(8,128)(2,1)}, bf16[320,1024]{1,0:T(8,128)(2,1)S(1)}, u32[]{:S(2)}, u32[]{:S(2)}) collective-permute-start(bf16[320,1024]{1,0:T(8,128)(2,1)} %fusion.37), channel_id=1, source_target_pairs={{0,1},{1,0},{2,3},{3,2},{4,5},{5,4},{6,7},{7,6},{8,9},{9,8},{10,11... | collective-permute-start | bytes 1966088 | tf_op jit(solution)/shard_map/ppermute | solution.py:80
  537.4 154.5 %reduce-scatter.10.cloned.1.call-start = ((), (), s32[]{:S(2)}) async-start(), calls=%async_computation.15 | async-start | bytes 3604480 | tf_op jit(solution)/shard_map/reduce_scatter | solution.py:103
  537.9 63.9 %collective-permute-start.36 = (bf16[512,2816]{1,0:T(8,128)(2,1)}, bf16[512,2816]{1,0:T(8,128)(2,1)}, u32[]{:S(2)}, u32[]{:S(2)}) collective-permute-start(bf16[512,2816]{1,0:T(8,128)(2,1)} %add_convert_fusion.4), channel_id=1, source_target_pairs={{0,4},{2,6},{4,0},{6,2},{8,12},{10,14},{12,8},{14,10},{16,20},{18,... | collective-permute-start | bytes 8650760 | tf_op jit(solution)/shard_map/ppermute | solution.py:77
  538.5 63.3 %collective-permute-start.35 = (bf16[512,2816]{1,0:T(8,128)(2,1)}, bf16[512,2816]{1,0:T(8,128)(2,1)}, u32[]{:S(2)}, u32[]{:S(2)}) collective-permute-start(bf16[512,2816]{1,0:T(8,128)(2,1)} %convolution_convert_fusion.3), channel_id=1, source_target_pairs={{0,2},{2,0},{4,6},{6,4},{8,10},{10,8},{12,14},{14,12},{16,18},{18,... | collective-permute-start | bytes 8650760 | tf_op jit(solution)/shard_map/ppermute | solution.py:74
  546.6 63.4 %collective-permute-start.34 = (bf16[512,2816]{1,0:T(8,128)(2,1)}, bf16[512,2816]{1,0:T(8,128)(2,1)}, u32[]{:S(2)}, u32[]{:S(2)}) collective-permute-start(bf16[512,2816]{1,0:T(8,128)(2,1)} %convolution_convert_fusion.2), channel_id=1, source_target_pairs={{0,2},{2,0},{4,6},{6,4},{8,10},{10,8},{12,14},{14,12},{16,18},{18,... | collective-permute-start | bytes 8650760 | tf_op jit(solution)/shard_map/ppermute | solution.py:74
  609.9 220.9 %reduce-scatter.12.cloned.1.call-start = ((), (), s32[]{:S(2)}) async-start(), calls=%async_computation.16 | async-start | bytes 3604480 | tf_op jit(solution)/shard_map/reduce_scatter | solution.py:103
  609.9 46.4 %collective-permute-start.39 = (bf16[512,2816]{1,0:T(8,128)(2,1)}, bf16[512,2816]{1,0:T(8,128)(2,1)}, u32[]{:S(2)}, u32[]{:S(2)}) collective-permute-start(bf16[512,2816]{1,0:T(8,128)(2,1)} %convolution_convert_fusion.1), channel_id=1, source_target_pairs={{0,2},{2,0},{4,6},{6,4},{8,10},{10,8},{12,14},{14,12},{16,18},{18,... | collective-permute-start | bytes 8650760 | tf_op jit(solution)/shard_map/ppermute | solution.py:74
  617.0 65.2 %collective-permute-start.40 = (bf16[512,2816]{1,0:T(8,128)(2,1)}, bf16[512,2816]{1,0:T(8,128)(2,1)}, u32[]{:S(2)}, u32[]{:S(2)}) collective-permute-start(bf16[512,2816]{1,0:T(8,128)(2,1)} %add_convert_fusion.1), channel_id=1, source_target_pairs={{0,4},{2,6},{4,0},{6,2},{8,12},{10,14},{12,8},{14,10},{16,20},{18,... | collective-permute-start | bytes 8650760 | tf_op jit(solution)/shard_map/ppermute | solution.py:77
  646.5 35.7 %collective-permute-start.38 = (bf16[512,2048]{1,0:T(8,128)(2,1)S(1)}, bf16[512,2048]{1,0:T(8,128)(2,1)S(1)}, u32[]{:S(2)}, u32[]{:S(2)}) collective-permute-start(bf16[512,2048]{1,0:T(8,128)(2,1)S(1)} %get-tuple-element.307), channel_id=1, source_target_pairs={{0,2},{2,0},{4,6},{6,4},{8,10},{10,8},{12,14},{14,12},{16,18},{18,... | collective-permute-start | bytes 6291464 | tf_op jit(solution)/shard_map/ppermute | solution.py:74
  646.7 84.0 %collective-permute-start.43 = (bf16[512,2048]{1,0:T(8,128)(2,1)}, bf16[512,2048]{1,0:T(8,128)(2,1)}, u32[]{:S(2)}, u32[]{:S(2)}) collective-permute-start(bf16[512,2048]{1,0:T(8,128)(2,1)} %get-tuple-element.247), channel_id=1, source_target_pairs={{0,2},{2,0},{4,6},{6,4},{8,10},{10,8},{12,14},{14,12},{16,18},{18,... | collective-permute-start | bytes 6291464 | tf_op jit(solution)/shard_map/ppermute | solution.py:74
  656.1 46.4 %collective-permute-start.37 = (bf16[512,2048]{1,0:T(8,128)(2,1)}, bf16[512,2048]{1,0:T(8,128)(2,1)}, u32[]{:S(2)}, u32[]{:S(2)}) collective-permute-start(bf16[512,2048]{1,0:T(8,128)(2,1)} %convolution_convert_fusion.8), channel_id=1, source_target_pairs={{0,2},{2,0},{4,6},{6,4},{8,10},{10,8},{12,14},{14,12},{16,18},{18,... | collective-permute-start | bytes 6291464 | tf_op jit(solution)/shard_map/ppermute | solution.py:74
  684.3 47.6 %collective-permute-start.44 = (bf16[512,2048]{1,0:T(8,128)(2,1)}, bf16[512,2048]{1,0:T(8,128)(2,1)}, u32[]{:S(2)}, u32[]{:S(2)}) collective-permute-start(bf16[512,2048]{1,0:T(8,128)(2,1)} %add_convert_fusion.9), channel_id=1, source_target_pairs={{0,4},{2,6},{4,0},{6,2},{8,12},{10,14},{12,8},{14,10},{16,20},{18,... | collective-permute-start | bytes 6291464 | tf_op jit(solution)/shard_map/ppermute | solution.py:77
  691.9 144.1 %reduce-scatter.14.cloned.1.call-start = ((), (), s32[]{:S(2)}) async-start(), calls=%async_computation.17 | async-start | bytes 2621440 | tf_op jit(solution)/shard_map/reduce_scatter | solution.py:103
  737.4 138.0 %reduce-scatter.18.cloned.1.call-start = ((), (), s32[]{:S(2)}) async-start(), calls=%async_computation.19 | async-start | bytes 2621440 | tf_op jit(solution)/shard_map/reduce_scatter | solution.py:103
  738.1 47.9 %collective-permute-start.47 = (bf16[512,2048]{1,0:T(8,128)(2,1)}, bf16[512,2048]{1,0:T(8,128)(2,1)}, u32[]{:S(2)}, u32[]{:S(2)}) collective-permute-start(bf16[512,2048]{1,0:T(8,128)(2,1)} %add_convert_fusion.8), channel_id=1, source_target_pairs={{0,4},{2,6},{4,0},{6,2},{8,12},{10,14},{12,8},{14,10},{16,20},{18,... | collective-permute-start | bytes 6291464 | tf_op jit(solution)/shard_map/ppermute | solution.py:77
  790.7 103.4 %reduce-scatter.16.cloned.1.call-start = ((), (), s32[]{:S(2)}) async-start(), calls=%async_computation.18 | async-start | bytes 1310720 | tf_op jit(solution)/shard_map/reduce_scatter | solution.py:103
  809.4 40.6 %collective-permute-start.49 = (bf16[512,1024]{1,0:T(8,128)(2,1)}, bf16[512,1024]{1,0:T(8,128)(2,1)}, u32[]{:S(2)}, u32[]{:S(2)}) collective-permute-start(bf16[512,1024]{1,0:T(8,128)(2,1)} %convolution_convert_fusion.12), channel_id=1, source_target_pairs={{0,2},{2,0},{4,6},{6,4},{8,10},{10,8},{12,14},{14,12},{16,18},{18,... | collective-permute-start | bytes 3145736 | tf_op jit(solution)/shard_map/ppermute | solution.py:74
  810.9 44.1 %collective-permute-start.51 = (bf16[512,1024]{1,0:T(8,128)(2,1)}, bf16[512,1024]{1,0:T(8,128)(2,1)}, u32[]{:S(2)}, u32[]{:S(2)}) collective-permute-start(bf16[512,1024]{1,0:T(8,128)(2,1)} %add_convert_fusion.13), channel_id=1, source_target_pairs={{0,4},{2,6},{4,0},{6,2},{8,12},{10,14},{12,8},{14,10},{16,20},{18,... | collective-permute-start | bytes 3145736 | tf_op jit(solution)/shard_map/ppermute | solution.py:77
  836.1 68.6 %reduce-scatter.20.cloned.1.call-start = ((), (), s32[]{:S(2)}) async-start(), calls=%async_computation.20 | async-start | bytes 1310720 | tf_op jit(solution)/shard_map/reduce_scatter | solution.py:103
  838.9 36.0 %collective-permute-start.58 = (f32[128]{0:T(128)S(1)}, f32[128]{0:T(128)S(1)}, u32[]{:S(2)}, u32[]{:S(2)}) collective-permute-start(f32[128]{0:T(128)S(1)} %add.339), channel_id=1, source_target_pairs={{0,1},{1,0},{2,3},{3,2},{4,5},{5,4},{6,7},{7,6},{8,9},{9,8},{10,11... | collective-permute-start | bytes 1544 | tf_op jit(solution)/shard_map/ppermute | solution.py:80
  (113 other events, 1813.8 us)
Sparse Core Ops, SparseCore 0:
  20.8 32.4 all-gather.7
  55.4 45.0 all-gather.9
  102.0 26.6 all-gather.11
  130.1 27.4 all-gather.13
  159.0 58.6 all-gather.15
  219.1 57.8 all-gather.17
  278.6 57.8 all-gather.19
  537.6 54.0 reduce-scatter.7
  610.0 54.0 reduce-scatter.9
  692.1 54.7 reduce-scatter.11
  749.2 43.6 reduce-scatter.13
  795.1 43.3 reduce-scatter.17
  840.8 26.4 reduce-scatter.15
  875.0 25.8 reduce-scatter.19

commit v5 on v4

--- a/solution.py
+++ b/solution.py
@@ -111,6 +111,12 @@
     def far_part(self, first_arg, second_arg, part):
         send = self.product_part(first_arg, second_arg, part).astype(bf16)
         return self.swap_core(send), send
+
+    def far_part_two(self, first_arg, second_arg):
+        send = self.product_part(first_arg, second_arg, 3).astype(bf16)
+        middle = send.shape[0] // 2
+        pieces = [self.swap_core(send[:middle]), self.swap_core(send[middle:])]
+        return jnp.concatenate(pieces, axis=0), send
 
     def aside_part(self, first_arg, second_arg, far):
         return (self.product_part(first_arg, second_arg, 1) + far.astype(f32)).astype(bf16)
@@ -650,13 +656,13 @@
     )
     normed = jnp.concatenate([own_block, normed_keys[prompt_len:]], axis=0)
     keys_values = plain_product(normed_keys, kv_full).astype(bf16)
-    q_near, q_far = after(q_near, keys_values), after(q_far, keys_values)
-    q_full = jnp.concatenate([q_here, q_side, q_near, q_far], axis=0)
+    keys_values, out_side, gate_here = together(keys_values, out_side, gate_here)
+    out_far = at.swap_core(out_side)
+    gate_side, gate_near = at.swap_side(gate_here), at.swap_core(gate_here)
+    q_parts = [after(part, keys_values) for part in (q_here, q_side, q_near, q_far)]
+    q_full = jnp.concatenate(q_parts, axis=0)
     queries = plain_product(after(normed, keys_values), q_full).astype(bf16)
     fixed = (lam_vec, head_gain_row, prompt_spots, bounds, prompt_part)
-    queries, out_side, gate_here = together(queries, out_side, gate_here)
-    out_far = at.swap_core(out_side)
-    gate_side, gate_near = at.swap_side(gate_here), at.swap_core(gate_here)
     heads_out, attn_vec, lse = attend(queries, keys_values, *fixed, (0, heads))
     attn_vec, cot_turned = together(attn_vec, cot_turned)
     out_near, out_far = after(out_near, attn_vec), after(out_far, attn_vec)
@@ -709,20 +715,23 @@
     def back_ffn(one, two, features=slice(None)):
         return cols_product(one, gate_full[features]) + cols_product(two, up_full[features])
 
-    gate_far_aside, gate_send = at.far_part(ffn_in, gate_grad, 3)
+    gate_far_aside, gate_send = at.far_part_two(ffn_in, gate_grad)
     gate_other, up_other = after(gate_grad[local_rows:], gate_send), up_grad[local_rows:]
     ffn_sends = [back_ffn(gate_other, up_other, slice(0, half)).astype(bf16)]
     gate_other, up_other = after(gate_other, ffn_sends[0]), after(up_other, ffn_sends[0])
     ffn_sends.append(back_ffn(gate_other, up_other, slice(half, D)).astype(bf16))
     ffn_sent = [at.swap_tensor(send) for send in ffn_sends]
-    ffn_part = cols_product(after(gate_grad[:local_rows], ffn_sends[1]), gate_full)
-    ffn_part, down_grad_aside = together(ffn_part, down_grad_aside)
-    ffn_part = ffn_part + cols_product(after(up_grad[:local_rows], down_grad_aside), up_full)
-    gate_far_keep, gate_send = at.far_part(ffn_in, after(gate_grad, ffn_part), 2)
-    gate_far_aside = after(gate_far_aside, gate_send)
+    gate_far_aside = after(gate_far_aside, ffn_sends[1])
     gate_grad_side = at.aside_part(ffn_in, gate_grad, gate_far_aside)
     gate_grad_aside = at.swap_side(gate_grad_side)
-    ffn_sent = together(after(ffn_sent[0], gate_grad_side), ffn_sent[1])
+    ffn_part = cols_product(after(gate_grad[:local_rows], gate_grad_side), gate_full)
+    ffn_part, down_grad_aside = together(ffn_part, down_grad_aside)
+    down_far_keep = after(down_far_keep, ffn_part)
+    down_last = at.near_part(cot_rows, hidden, down_far_keep, down_grad_aside)
+    grad_down = at.scatter_upper(down_last)
+    ffn_part = ffn_part + cols_product(after(up_grad[:local_rows], down_last), up_full)
+    gate_far_keep, gate_send = at.far_part(ffn_in, after(gate_grad, ffn_part), 2)
+    ffn_sent = together(after(ffn_sent[0], gate_send), ffn_sent[1])
     ffn_in_grad = ffn_part + jnp.concatenate(ffn_sent, axis=1).astype(f32)
     residual_grad = cot_rel.astype(f32) + norm_back(
         residual, inv_second, ffn_gain_row, ffn_in_grad
@@ -730,19 +739,12 @@
 
     branch_own = residual_grad.astype(bf16)
     branch_sent = at.swap_tensor(branch_own)
-    down_far_keep = after(down_far_keep, branch_own)
-    down_last = at.near_part(cot_rows, hidden, down_far_keep, down_grad_aside)
-    grad_down = at.scatter_upper(down_last)
-    up_far_aside, up_send = at.far_part(ffn_in, after(up_grad, down_last), 3)
+    up_far_aside, up_send = at.far_part_two(ffn_in, after(up_grad, branch_own))
     up_far_keep, up_send = at.far_part(ffn_in, after(up_grad, up_send), 2)
     branch = jnp.concatenate([branch_own, after(branch_sent, up_send)], axis=0)
     vec_two = plain_product(branch, out_full)
     vec_grad = at.in_order(vec_two[:local_rows], vec_two[local_rows:])
-    middle = heads // 2
-    back_args = (queries, keys_values, lam_vec, head_gain_row)
-    back_fixed = (heads_out, lse, prompt_spots, bounds, prompt_part)
-    half_back = attend_back(*back_args, vec_grad, *back_fixed, (0, middle), ())
-    half_back, gate_grad_aside = together(half_back, gate_grad_aside)
+    vec_grad, gate_grad_aside = together(vec_grad, gate_grad_aside)
     gate_far_keep = after(gate_far_keep, gate_grad_aside)
     gate_last = at.near_part(ffn_in, gate_grad, gate_far_keep, gate_grad_aside)
     grad_gate = at.scatter_upper(gate_last)
@@ -750,7 +752,18 @@
     up_grad_side = at.aside_part(ffn_in, up_grad, up_far_aside)
     up_grad_aside = at.swap_side(up_grad_side)
     queries_grad, kv_grad, head_sums = attend_back(
-        *back_args, after(vec_grad, up_grad_side), *back_fixed, (middle, heads), half_back
+        queries,
+        keys_values,
+        lam_vec,
+        head_gain_row,
+        after(vec_grad, up_grad_side),
+        heads_out,
+        lse,
+        prompt_spots,
+        bounds,
+        prompt_part,
+        (0, heads),
+        (),
     )
     queries_grad, kv_grad, head_sums, grad_down = together(
         queries_grad, kv_grad, head_sums, grad_down

time: 923 us -> 880 us (0.953)
  waiting for transfers between devices: 288 us -> 255 us
  matrix products: 282 us -> 267 us
    ppermute x14, waiting for transfers between devices: 159 us -> 128 us  [swap_side(): return lax.ppermute(value, 'dp', self.side_pairs)]
    dot_general x24, matrix products: 120 us -> 106 us  [rows_product(): lax.dot_general(first_arg, second_arg, (((0,), (0,)), ((), ())), preferre...]
    pallas_call x2 -> x1, Pallas kernels: 45 us -> 40 us  [attend_back(): pl.pallas_call(lambda *refs: backward_kernel(prompt_len, top_rows, first,...]
    unnamed x199 -> x223, local copies, waits for them, and re-layouts: 48.6 us -> 46.3 us
  transfers between devices with their start and end apart: 73 -> 75, of which waited for: 22 -> 23; matrix products, arithmetic and copies ran while one was open for 50% -> 52% of each run, Pallas kernels for 10% -> 10%
where the time goes in v5:
time: 880 us; the launch traced here: 870 us
  matrix products  267 us (30%)
  waiting for transfers between devices  255 us (29%)
  local copies, waits for them, and re-layouts  109 us (12%)
  other arithmetic  98 us (11%)
  Pallas kernels  84.9 us (10%)
  starting transfers between devices  40.8 us (5%)
  between operations  15.6 us (2%)
    ppermute x14, waiting for transfers between devices, swap_side(): return lax.ppermute(value, 'dp', self.side_pairs)  128 us
    dot_general x24, matrix products, rows_product(): lax.dot_general(first_arg, second_arg, (((0,), (0,)), ((), ())), preferre...  106 us
    ppermute x12, waiting for transfers between devices, swap_tensor(): return lax.ppermute(value, 'tensor', [(0, 1), (1, 0)])  102 us
    dot_general x14, matrix products, cols_product(): lax.dot_general(first_arg, second_arg, (((1,), (1,)), ((), ())), preferre...  82.6 us
    dot_general x6, matrix products, plain_product(): return jnp.dot(first_arg, second_arg, preferred_element_type=f32)  78.6 us
    unnamed x223, local copies, waits for them, and re-layouts  46.3 us
    pallas_call x1, Pallas kernels, attend_back(): pl.pallas_call(lambda *refs: backward_kernel(prompt_len, top_rows, first,...  40 us
    pallas_call x1, Pallas kernels, attend(): pl.pallas_call(lambda *refs: forward_kernel(prompt_len, top_rows, first,...  31.4 us
  transfers between devices with their start and end apart: 75, of which 23 were waited for; matrix products, arithmetic and copies ran while one was open for 52% of the time, Pallas kernels for 10%

profile of v5, /device:TPU:0, one launch (start us, length us, event | category | flops | bytes accessed | tf_op | source)
XLA Modules:
  0.0 870.1 jit_solution(8195887145259118511)
XLA Ops:
  8.2 4.9 collective-permute-start
  28.5 4.4 reshape.265
  46.5 9.1 %collective-permute-done.1 = bf16[320,2048]{1,0:T(8,128)(2,1)} collective-permute-done((bf16[320,2048]{1,0:T(8,128)(2,1)S(1)}, bf16[320,2048]{1,0:T(8,128)(2,1)}, u32[]{:S(2)}, u32[]{:S(2)}) %collective-permute-start.1) | collective-permute-done | bytes 1310752 | tf_op jit(solution)/shard_map/ppermute | solution.py:80
  59.6 22.5 %collective-permute-done.2 = bf16[576,1024]{1,0:T(8,128)(2,1)S(1)} collective-permute-done((bf16[576,1024]{1,0:T(8,128)(2,1)}, bf16[576,1024]{1,0:T(8,128)(2,1)S(1)}, u32[]{:S(2)}, u32[]{:S(2)}) %collective-permute-start.2) | collective-permute-done | bytes 1179680 | tf_op jit(solution)/shard_map/ppermute | solution.py:77
  84.6 15.8 %all-gather.10.cloned.1.call-done = bf16[512,2048]{1,0:T(8,128)(2,1)} async-done(((bf16[128,2048]{1,0:T(8,128)(2,1)}), bf16[512,2048]{1,0:T(8,128)(2,1)}) %all-gather.10.cloned.1.call-update) | async-done | bytes 2097168 | tf_op jit(solution)/shard_map/all_gather | solution.py:83
  104.9 29.3 %collective-permute-done.4.refs_3_ = bf16[1152,1024]{1,0:T(8,128)(2,1)} collective-permute-done((bf16[1152,1024]{1,0:T(8,128)(2,1)}, bf16[1152,1024]{1,0:T(8,128)(2,1)}, u32[]{:S(2)}, u32[]{:S(2)}) %collective-permute-start.4) | collective-permute-done | bytes 2359328 | tf_op jit(solution)/shard_map/ppermute | solution.py:80
  134.8 14.0 %collective-permute-done.7 = bf16[512,2048]{1,0:T(8,128)(2,1)} collective-permute-done((bf16[512,2048]{1,0:T(8,128)(2,1)}, bf16[512,2048]{1,0:T(8,128)(2,1)}, u32[]{:S(2)}, u32[]{:S(2)}) %collective-permute-start.7) | collective-permute-done | bytes 2097184 | tf_op jit(solution)/shard_map/ppermute | solution.py:77
  159.5 13.6 %norm_keys.1 = bf16[2560,2048]{1,0:T(8,128)(2,1)} custom-call(s32[16]{0:T(128)} %get-tuple-element.297.refs_0_, s32[1]{0:T(128)} %bitcast.6.refs_1_, bf16[1152,1024]{1,0:T(8,128)(2,1)} %constant_dynamic-update-slice_fusion.refs_2_, bf16[1152,1024]{1,0:T(8,128)(2,1)} %collective-permute-done.4.refs_3_, bf16[1152,1024]{1,0:T(8,128)(2,1)} %collective-permute-done.3.refs_4_, ...), custom_call_target="tpu_custom_call" | custom-call | flops 8000000000 | tf_op jit(solution)/shard_map/norm_keys/pallas_call | solution.py:500
  173.1 6.6 pad_maximum_fusion.1
  189.2 28.1 %convolution_convert_fusion.refs_2_ = bf16[2560,2048]{1,0:T(8,128)(2,1)} fusion(bf16[2560,2048]{1,0:T(8,128)(2,1)} %norm_keys.1, bf16[2048,2048]{1,0:T(8,128)(2,1)} %pad_maximum_fusion.1), kind=kOutput, calls=%fused_computation.1 | convolution fusion | flops 21480079360 | bytes 29360128 | tf_op jit(solution)/shard_map/dot_general | solution.py:33
  236.2 31.4 %attend.1 = (f32[640,1024]{1,0:T(8,128)}, bf16[640,1024]{1,0:T(8,128)(2,1)}, f32[4,16,640]{2,1,0:T(8,128)}) custom-call(f32[4]{0:T(128)} %subtract_add_fusion.1.refs_0_, bf16[640,1024]{1,0:T(8,128)(2,1)} %convolution_convert_fusion.11.refs_1_, bf16[2560,2048]{1,0:T(8,128)(2,1)} %convolution_convert_fusion.refs_2_, f32[1,1024]{1,0:T(1,128)} %bitcast.119, ...), custom_call_target="tpu_custom_call" | custom-call | flops 14000000000 | tf_op jit(solution)/shard_map/attend/pallas_call | solution.py:341
  280.7 10.4 %collective-permute-done.16 = bf16[512,2816]{1,0:T(8,128)(2,1)} collective-permute-done((bf16[512,2816]{1,0:T(8,128)(2,1)}, bf16[512,2816]{1,0:T(8,128)(2,1)}, u32[]{:S(2)}, u32[]{:S(2)}) %collective-permute-start.16) | collective-permute-done | bytes 2883616 | tf_op jit(solution)/shard_map/ppermute | solution.py:77
  295.4 27.2 %collective-permute-done.17 = bf16[320,2048]{1,0:T(8,128)(2,1)S(1)} collective-permute-done((bf16[320,2048]{1,0:T(8,128)(2,1)}, bf16[320,2048]{1,0:T(8,128)(2,1)S(1)}, u32[]{:S(2)}, u32[]{:S(2)}) %collective-permute-start.17) | collective-permute-done | bytes 1310752 | tf_op jit(solution)/shard_map/ppermute | solution.py:80
  326.0 14.8 %pad_maximum_fusion = bf16[2048,2816]{1,0:T(8,128)(2,1)} fusion(bf16[512,2816]{1,0:T(8,128)(2,1)S(1)} %collective-permute-done.20, bf16[512,2816]{1,0:T(8,128)(2,1)} %collective-permute-done.19, bf16[512,2816]{1,0:T(8,128)(2,1)} %collective-permute-done.16, bf16[512,2816]{1,0:T(8,128)(2,1)S(1)} %copy-done.47), kind=kLoop, calls=%fused_computation | loop fusion | flops 46137344 | bytes 23068672 | tf_op jit(solution)/shard_map/concatenate | solution.py:685
  340.8 15.8 %collective-permute-done.21 = bf16[512,2816]{1,0:T(8,128)(2,1)} collective-permute-done((bf16[512,2816]{1,0:T(8,128)(2,1)}, bf16[512,2816]{1,0:T(8,128)(2,1)}, u32[]{:S(2)}, u32[]{:S(2)}) %collective-permute-start.21) | collective-permute-done | bytes 2883616 | tf_op jit(solution)/shard_map/ppermute | solution.py:77
  361.2 12.9 %fusion.136 = f32[640,2816]{1,0:T(8,128)} fusion(bf16[2048,2816]{1,0:T(8,128)(2,1)} %pad_maximum_fusion, bf16[320,2048]{1,0:T(8,128)(2,1)S(1)} %collective-permute-done.18, bf16[320,2048]{1,0:T(8,128)(2,1)S(1)} %multiply_convert_fusion.3), kind=kOutput, calls=%fused_computation.271 | convolution fusion | flops 7387217920 | bytes 21364736 | tf_op jit(solution)/shard_map/dot_general | solution.py:33
  384.0 15.2 %multiply_convert_fusion.2 = (bf16[640,2816]{1,0:T(8,128)(2,1)S(1)}, f32[640,2816]{1,0:T(8,128)}) fusion(f32[640,2816]{1,0:T(8,128)} %fusion.136, bf16[640,2048]{1,0:T(8,128)(2,1)S(1)} %pad_maximum_fusion.3, bf16[2048,2816]{1,0:T(8,128)(2,1)} %constant_dynamic-update-slice_fusion.10), kind=kOutput, calls=%fused_computation.5 | convolution fusion | flops 7392788480 | bytes 32178176 | tf_op jit(solution)/shard_map/dot_general | solution.py:33
  406.0 19.2 %collective-permute-done.24 = bf16[512,2816]{1,0:T(8,128)(2,1)} collective-permute-done((bf16[512,2816]{1,0:T(8,128)(2,1)S(1)}, bf16[512,2816]{1,0:T(8,128)(2,1)}, u32[]{:S(2)}, u32[]{:S(2)}) %collective-permute-start.24) | collective-permute-done | bytes 2883616 | tf_op jit(solution)/shard_map/ppermute | solution.py:77
  427.9 5.0 fusion.77
  439.8 4.3 copy-done.62
  444.0 15.3 %multiply_convert_fusion = (bf16[640,2816]{1,0:T(8,128)(2,1)S(1)}, bf16[640,2816]{1,0:T(8,128)(2,1)S(1)}) fusion(f32[640,2816]{1,0:T(8,128)} %fusion.136, f32[640,2816]{1,0:T(8,128)} %get-tuple-element.331, bf16[640,2048]{1,0:T(8,128)(2,1)S(1)} %copy-done.41, bf16[2048,2816]{1,0:T(8,128)(2,1)} %copy-done.62), kind=kOutput, calls=%fused_computation.3 | convolution fusion | flops 7405404160 | bytes 35782656 | tf_op jit(solution)/shard_map/dot_general | solution.py:33
  463.3 5.9 fusion
  472.7 4.4 fusion.40
  491.5 8.9 %fusion.147 = f32[320,2048]{1,0:T(8,128)} fusion(bf16[320,2816]{1,0:T(8,128)(2,1)S(1)} %copy-done.54, bf16[2048,2816]{1,0:T(8,128)(2,1)} %pad_maximum_fusion), kind=kOutput, calls=%fused_computation.281 | convolution fusion | flops 3690987520 | bytes 15958016 | tf_op jit(solution)/shard_map/dot_general | solution.py:43
  502.7 5.4 add_convert_fusion.3
  508.1 10.1 %convolution_add_fusion.2 = f32[320,2048]{1,0:T(8,128)S(1)} fusion(f32[320,2048]{1,0:T(8,128)} %fusion.147, bf16[320,2816]{1,0:T(8,128)(2,1)} %get-tuple-element.220, bf16[2048,2816]{1,0:T(8,128)(2,1)} %constant_dynamic-update-slice_fusion.10), kind=kOutput, calls=%fused_computation.72 | convolution fusion | flops 3691642880 | bytes 18579456 | tf_op jit(solution)/shard_map/dot_general | solution.py:43
  522.8 4.6 fusion.137
  537.8 18.0 %collective-permute-done.34 = bf16[320,2048]{1,0:T(8,128)(2,1)S(1)} collective-permute-done((bf16[320,2048]{1,0:T(8,128)(2,1)S(1)}, bf16[320,2048]{1,0:T(8,128)(2,1)S(1)}, u32[]{:S(2)}, u32[]{:S(2)}) %collective-permute-start.34) | collective-permute-done | bytes 1310752 | tf_op jit(solution)/shard_map/ppermute | solution.py:80
  563.5 6.3 add_convert_fusion.2
  572.8 4.1 add_convert_fusion.1
  577.5 40.0 %attend_back.1 = (bf16[1024,640]{1,0:T(8,128)(2,1)}, bf16[2560,2048]{1,0:T(8,128)(2,1)}, f32[4,8,256]{2,1,0:T(8,128)}) custom-call(f32[4]{0:T(128)} %subtract_add_fusion.1.refs_0_, bf16[640,1024]{1,0:T(8,128)(2,1)} %convolution_convert_fusion.11.refs_1_, bf16[2560,2048]{1,0:T(8,128)(2,1)} %convolution_convert_fusion.refs_2_, f32[1,1024]{1,0:T(1,128)} %bitcast.120, ...), custom_call_target="tpu_custom_call" | custom-call | tf_op jit(solution)/shard_map/attend_back/pallas_call | solution.py:389
  617.5 6.3 fusion.139
  624.9 8.5 convolution_convert_fusion.8
  633.5 7.9 collective-permute-done.42
  644.0 7.1 add_convert_fusion
  651.2 10.3 %convolution_convert_fusion.7 = bf16[512,2048]{1,0:T(8,128)(2,1)} fusion(bf16[2560,2048]{1,0:T(8,128)(2,1)} %get-tuple-element.248, bf16[2560,2048]{1,0:T(8,128)(2,1)} %norm_keys.1), kind=kOutput, calls=%fused_computation.64 | convolution fusion | flops 5369757696 | bytes 15204352 | tf_op jit(solution)/shard_map/dot_general | solution.py:37
  661.5 10.7 %add_convert_fusion.8 = bf16[512,2048]{1,0:T(8,128)(2,1)} fusion(bf16[512,2048]{1,0:T(8,128)(2,1)} %collective-permute-done.39, bf16[2560,2048]{1,0:T(8,128)(2,1)} %get-tuple-element.248, bf16[2560,2048]{1,0:T(8,128)(2,1)} %norm_keys.1), kind=kOutput, calls=%fused_computation.42 | convolution fusion | flops 5371854848 | bytes 17301504 | tf_op jit(solution)/shard_map/dot_general | solution.py:37
  680.9 8.7 fusion.29
  690.1 5.6 add_convert_fusion.7
  697.2 9.4 %fusion.22 = f32[512,2048]{1,0:T(8,128)S(1)} fusion(bf16[2560,2048]{1,0:T(8,128)(2,1)} %get-tuple-element.248, bf16[2560,2048]{1,0:T(8,128)(2,1)} %norm_keys.1), kind=kOutput, calls=%fused_computation.83 | convolution fusion | flops 5368709120 | bytes 17301504 | tf_op jit(solution)/shard_map/dot_general | solution.py:37
  710.8 9.6 %convolution_convert_fusion.10 = bf16[320,2048]{1,0:T(8,128)(2,1)} fusion(bf16[2048,2816]{1,0:T(8,128)(2,1)} %copy-done.62, bf16[640,2816]{1,0:T(8,128)(2,1)S(1)} %copy-done.7), kind=kOutput, calls=%fused_computation.75 | convolution fusion | flops 3691642880 | bytes 14647296 | tf_op jit(solution)/shard_map/dot_general | solution.py:43
  720.4 23.9 %collective-permute-done.49 = bf16[512,2048]{1,0:T(8,128)(2,1)S(1)} collective-permute-done((bf16[512,2048]{1,0:T(8,128)(2,1)}, bf16[512,2048]{1,0:T(8,128)(2,1)S(1)}, u32[]{:S(2)}, u32[]{:S(2)}) %collective-permute-start.49) | collective-permute-done | bytes 2097184 | tf_op jit(solution)/shard_map/ppermute | solution.py:77
  769.7 18.5 %collective-permute-done.47 = bf16[320,2048]{1,0:T(8,128)(2,1)} collective-permute-done((bf16[320,2048]{1,0:T(8,128)(2,1)S(1)}, bf16[320,2048]{1,0:T(8,128)(2,1)}, u32[]{:S(2)}, u32[]{:S(2)}) %collective-permute-start.47) | collective-permute-done | bytes 1310752 | tf_op jit(solution)/shard_map/ppermute | solution.py:80
  796.6 6.1 fusion.46
  807.5 5.0 collective-permute-done.53
  817.3 8.4 fusion.48
  839.3 4.8 fusion.16
  846.6 4.2 reverse_select_fusion.1
  (516 shorter events, 272.1 us)
Async XLA Ops:
  7.2 48.5 %all-gather.8.cloned.1.call-start = ((), (), s32[]{:S(2)}) async-start(), calls=%async_computation.7 | async-start | bytes 1474560 | tf_op jit(solution)/shard_map/all_gather | solution.py:83
  20.6 79.8 %all-gather.10.cloned.1.call-start = ((), (), s32[]{:S(2)}) async-start(), calls=%async_computation.8 | async-start | bytes 2621440 | tf_op jit(solution)/shard_map/all_gather | solution.py:83
  23.3 111.5 %all-gather.12.cloned.1.call-start = ((), (), s32[]{:S(2)}) async-start(), calls=%async_computation.9 | async-start | bytes 1310720 | tf_op jit(solution)/shard_map/all_gather | solution.py:83
  24.0 155.7 %all-gather.14.cloned.1.call-start = ((), (), s32[]{:S(2)}) async-start(), calls=%async_computation.10 | async-start | bytes 1310720 | tf_op jit(solution)/shard_map/all_gather | solution.py:83
  24.6 201.3 %all-gather.16.cloned.1.call-start = ((), (), s32[]{:S(2)}) async-start(), calls=%async_computation.11 | async-start | bytes 3604480 | tf_op jit(solution)/shard_map/all_gather | solution.py:83
  25.2 255.6 %all-gather.18.cloned.1.call-start = ((), (), s32[]{:S(2)}) async-start(), calls=%async_computation.12 | async-start | bytes 3604480 | tf_op jit(solution)/shard_map/all_gather | solution.py:83
  83.2 51.0 %collective-permute-start.4 = (bf16[1152,1024]{1,0:T(8,128)(2,1)}, bf16[1152,1024]{1,0:T(8,128)(2,1)}, u32[]{:S(2)}, u32[]{:S(2)}) collective-permute-start(bf16[1152,1024]{1,0:T(8,128)(2,1)} %constant_dynamic-update-slice_fusion.refs_2_), channel_id=1, source_target_pairs={{0,1},{1,0},{2,3},{3,2},{4,5},{5,4},{6,7},{7,6},{8,9},{9,8},{10,11... | collective-permute-start | bytes 7077896 | tf_op jit(solution)/shard_map/ppermute | solution.py:80
  84.6 256.2 %all-gather.20.cloned.1.call-start = ((), (), s32[]{:S(2)}) async-start(), calls=%async_computation.13 | async-start | bytes 3604480 | tf_op jit(solution)/shard_map/all_gather | solution.py:83
  100.4 48.4 %collective-permute-start.7 = (bf16[512,2048]{1,0:T(8,128)(2,1)}, bf16[512,2048]{1,0:T(8,128)(2,1)}, u32[]{:S(2)}, u32[]{:S(2)}) collective-permute-start(bf16[512,2048]{1,0:T(8,128)(2,1)} %all-gather.10.cloned.1.call-done), channel_id=1, source_target_pairs={{0,4},{2,6},{4,0},{6,2},{8,12},{10,14},{12,8},{14,10},{16,20},{18,... | collective-permute-start | bytes 6291464 | tf_op jit(solution)/shard_map/ppermute | solution.py:77
  151.1 466.4 %reduce-scatter.8.cloned.1.call-start = ((), (), s32[]{:S(2)}) async-start(), calls=%async_computation.14 | async-start | bytes 3604480 | tf_op jit(solution)/shard_map/reduce_scatter | solution.py:103
  155.9 70.7 %collective-permute-start.11 = (bf16[512,1024]{1,0:T(8,128)(2,1)}, bf16[512,1024]{1,0:T(8,128)(2,1)}, u32[]{:S(2)}, u32[]{:S(2)}) collective-permute-start(bf16[512,1024]{1,0:T(8,128)(2,1)} %all-gather.12.cloned.1.call-done), channel_id=1, source_target_pairs={{0,2},{2,0},{4,6},{6,4},{8,10},{10,8},{12,14},{14,12},{16,18},{18,... | collective-permute-start | bytes 3145736 | tf_op jit(solution)/shard_map/ppermute | solution.py:74
  181.8 88.2 %collective-permute-start.14 = (bf16[512,1024]{1,0:T(8,128)(2,1)}, bf16[512,1024]{1,0:T(8,128)(2,1)}, u32[]{:S(2)}, u32[]{:S(2)}) collective-permute-start(bf16[512,1024]{1,0:T(8,128)(2,1)} %all-gather.14.cloned.1.call-done), channel_id=1, source_target_pairs={{0,2},{2,0},{4,6},{6,4},{8,10},{10,8},{12,14},{14,12},{16,18},{18,... | collective-permute-start | bytes 3145736 | tf_op jit(solution)/shard_map/ppermute | solution.py:74
  182.8 43.1 %collective-permute-start.10 = (bf16[512,1024]{1,0:T(8,128)(2,1)}, bf16[512,1024]{1,0:T(8,128)(2,1)}, u32[]{:S(2)}, u32[]{:S(2)}) collective-permute-start(bf16[512,1024]{1,0:T(8,128)(2,1)} %all-gather.14.cloned.1.call-done), channel_id=1, source_target_pairs={{0,4},{2,6},{4,0},{6,2},{8,12},{10,14},{12,8},{14,10},{16,20},{18,... | collective-permute-start | bytes 3145736 | tf_op jit(solution)/shard_map/ppermute | solution.py:77
  187.6 38.5 %collective-permute-start.12 = (bf16[512,1024]{1,0:T(8,128)(2,1)}, bf16[512,1024]{1,0:T(8,128)(2,1)}, u32[]{:S(2)}, u32[]{:S(2)}) collective-permute-start(bf16[512,1024]{1,0:T(8,128)(2,1)} %copy-done.57), channel_id=1, source_target_pairs={{0,2},{2,0},{4,6},{6,4},{8,10},{10,8},{12,14},{14,12},{16,18},{18,... | collective-permute-start | bytes 3145736 | tf_op jit(solution)/shard_map/ppermute | solution.py:74
  187.6 82.4 %collective-permute-start.13 = (bf16[320,2048]{1,0:T(8,128)(2,1)}, bf16[320,2048]{1,0:T(8,128)(2,1)}, u32[]{:S(2)}, u32[]{:S(2)}) collective-permute-start(bf16[320,2048]{1,0:T(8,128)(2,1)} %reshape.266), channel_id=1, source_target_pairs={{0,1},{1,0},{2,3},{3,2},{4,5},{5,4},{6,7},{7,6},{8,9},{9,8},{10,11... | collective-permute-start | bytes 3932168 | tf_op jit(solution)/shard_map/ppermute | solution.py:80
  225.9 99.7 %collective-permute-start.19 = (bf16[512,2816]{1,0:T(8,128)(2,1)}, bf16[512,2816]{1,0:T(8,128)(2,1)}, u32[]{:S(2)}, u32[]{:S(2)}) collective-permute-start(bf16[512,2816]{1,0:T(8,128)(2,1)} %all-gather.16.cloned.1.call-done), channel_id=1, source_target_pairs={{0,2},{2,0},{4,6},{6,4},{8,10},{10,8},{12,14},{14,12},{16,18},{18,... | collective-permute-start | bytes 8650760 | tf_op jit(solution)/shard_map/ppermute | solution.py:74
  226.1 65.0 %collective-permute-start.16 = (bf16[512,2816]{1,0:T(8,128)(2,1)}, bf16[512,2816]{1,0:T(8,128)(2,1)}, u32[]{:S(2)}, u32[]{:S(2)}) collective-permute-start(bf16[512,2816]{1,0:T(8,128)(2,1)} %all-gather.16.cloned.1.call-done), channel_id=1, source_target_pairs={{0,4},{2,6},{4,0},{6,2},{8,12},{10,14},{12,8},{14,10},{16,20},{18,... | collective-permute-start | bytes 8650760 | tf_op jit(solution)/shard_map/ppermute | solution.py:77
  226.6 47.0 %collective-permute-start.15 = (bf16[512,1024]{1,0:T(8,128)(2,1)}, bf16[512,1024]{1,0:T(8,128)(2,1)S(1)}, u32[]{:S(2)}, u32[]{:S(2)}) collective-permute-start(bf16[512,1024]{1,0:T(8,128)(2,1)} %collective-permute-done.10), channel_id=1, source_target_pairs={{0,2},{2,0},{4,6},{6,4},{8,10},{10,8},{12,14},{14,12},{16,18},{18,... | collective-permute-start | bytes 3145736 | tf_op jit(solution)/shard_map/ppermute | solution.py:74
  291.1 34.5 %collective-permute-start.20 = (bf16[512,2816]{1,0:T(8,128)(2,1)}, bf16[512,2816]{1,0:T(8,128)(2,1)S(1)}, u32[]{:S(2)}, u32[]{:S(2)}) collective-permute-start(bf16[512,2816]{1,0:T(8,128)(2,1)} %collective-permute-done.16), channel_id=1, source_target_pairs={{0,2},{2,0},{4,6},{6,4},{8,10},{10,8},{12,14},{14,12},{16,18},{18,... | collective-permute-start | bytes 8650760 | tf_op jit(solution)/shard_map/ppermute | solution.py:74
  291.1 31.4 %collective-permute-start.17 = (bf16[320,2048]{1,0:T(8,128)(2,1)}, bf16[320,2048]{1,0:T(8,128)(2,1)S(1)}, u32[]{:S(2)}, u32[]{:S(2)}) collective-permute-start(bf16[320,2048]{1,0:T(8,128)(2,1)} %convolution_convert_fusion.9), channel_id=1, source_target_pairs={{0,1},{1,0},{2,3},{3,2},{4,5},{5,4},{6,7},{7,6},{8,9},{9,8},{10,11... | collective-permute-start | bytes 3932168 | tf_op jit(solution)/shard_map/ppermute | solution.py:80
  291.6 64.9 %collective-permute-start.21 = (bf16[512,2816]{1,0:T(8,128)(2,1)}, bf16[512,2816]{1,0:T(8,128)(2,1)}, u32[]{:S(2)}, u32[]{:S(2)}) collective-permute-start(bf16[512,2816]{1,0:T(8,128)(2,1)} %all-gather.18.cloned.1.call-done), channel_id=1, source_target_pairs={{0,4},{2,6},{4,0},{6,2},{8,12},{10,14},{12,8},{14,10},{16,20},{18,... | collective-permute-start | bytes 8650760 | tf_op jit(solution)/shard_map/ppermute | solution.py:77
  293.8 80.4 %collective-permute-start.22 = (bf16[512,2816]{1,0:T(8,128)(2,1)}, bf16[512,2816]{1,0:T(8,128)(2,1)}, u32[]{:S(2)}, u32[]{:S(2)}) collective-permute-start(bf16[512,2816]{1,0:T(8,128)(2,1)} %all-gather.18.cloned.1.call-done), channel_id=1, source_target_pairs={{0,2},{2,0},{4,6},{6,4},{8,10},{10,8},{12,14},{14,12},{16,18},{18,... | collective-permute-start | bytes 8650760 | tf_op jit(solution)/shard_map/ppermute | solution.py:74
  325.1 36.2 %collective-permute-start.18 = (bf16[320,2048]{1,0:T(8,128)(2,1)S(1)}, bf16[320,2048]{1,0:T(8,128)(2,1)S(1)}, u32[]{:S(2)}, u32[]{:S(2)}) collective-permute-start(bf16[320,2048]{1,0:T(8,128)(2,1)S(1)} %multiply_convert_fusion.3), channel_id=1, source_target_pairs={{0,1},{1,0},{2,3},{3,2},{4,5},{5,4},{6,7},{7,6},{8,9},{9,8},{10,11... | collective-permute-start | bytes 3932168 | tf_op jit(solution)/shard_map/ppermute | solution.py:80
  360.1 65.8 %collective-permute-start.25 = (bf16[512,2816]{1,0:T(8,128)(2,1)S(1)}, bf16[512,2816]{1,0:T(8,128)(2,1)}, u32[]{:S(2)}, u32[]{:S(2)}) collective-permute-start(bf16[512,2816]{1,0:T(8,128)(2,1)S(1)} %copy-done.43), channel_id=1, source_target_pairs={{0,2},{2,0},{4,6},{6,4},{8,10},{10,8},{12,14},{14,12},{16,18},{18,... | collective-permute-start | bytes 8650760 | tf_op jit(solution)/shard_map/ppermute | solution.py:74
  360.6 64.5 %collective-permute-start.24 = (bf16[512,2816]{1,0:T(8,128)(2,1)S(1)}, bf16[512,2816]{1,0:T(8,128)(2,1)}, u32[]{:S(2)}, u32[]{:S(2)}) collective-permute-start(bf16[512,2816]{1,0:T(8,128)(2,1)S(1)} %copy-done.43), channel_id=1, source_target_pairs={{0,4},{2,6},{4,0},{6,2},{8,12},{10,14},{12,8},{14,10},{16,20},{18,... | collective-permute-start | bytes 8650760 | tf_op jit(solution)/shard_map/ppermute | solution.py:77
  425.3 77.3 %collective-permute-start.31 = (bf16[512,2816]{1,0:T(8,128)(2,1)}, bf16[512,2816]{1,0:T(8,128)(2,1)}, u32[]{:S(2)}, u32[]{:S(2)}) collective-permute-start(bf16[512,2816]{1,0:T(8,128)(2,1)} %convolution_convert_fusion.5), channel_id=1, source_target_pairs={{0,2},{2,0},{4,6},{6,4},{8,10},{10,8},{12,14},{14,12},{16,18},{18,... | collective-permute-start | bytes 8650760 | tf_op jit(solution)/shard_map/ppermute | solution.py:74
  437.0 65.7 %collective-permute-start.30 = (bf16[512,2816]{1,0:T(8,128)(2,1)}, bf16[512,2816]{1,0:T(8,128)(2,1)}, u32[]{:S(2)}, u32[]{:S(2)}) collective-permute-start(bf16[512,2816]{1,0:T(8,128)(2,1)} %add_convert_fusion.5), channel_id=1, source_target_pairs={{0,4},{2,6},{4,0},{6,2},{8,12},{10,14},{12,8},{14,10},{16,20},{18,... | collective-permute-start | bytes 8650760 | tf_op jit(solution)/shard_map/ppermute | solution.py:77
  477.1 43.7 %collective-permute-start.32 = (bf16[320,1024]{1,0:T(8,128)(2,1)}, bf16[320,1024]{1,0:T(8,128)(2,1)S(1)}, u32[]{:S(2)}, u32[]{:S(2)}) collective-permute-start(bf16[320,1024]{1,0:T(8,128)(2,1)} %fusion.40), channel_id=1, source_target_pairs={{0,1},{1,0},{2,3},{3,2},{4,5},{5,4},{6,7},{7,6},{8,9},{9,8},{10,11... | collective-permute-start | bytes 1966088 | tf_op jit(solution)/shard_map/ppermute | solution.py:80
  485.3 35.5 %collective-permute-start.33 = (bf16[320,1024]{1,0:T(8,128)(2,1)}, bf16[320,1024]{1,0:T(8,128)(2,1)}, u32[]{:S(2)}, u32[]{:S(2)}) collective-permute-start(bf16[320,1024]{1,0:T(8,128)(2,1)} %fusion.37), channel_id=1, source_target_pairs={{0,1},{1,0},{2,3},{3,2},{4,5},{5,4},{6,7},{7,6},{8,9},{9,8},{10,11... | collective-permute-start | bytes 1966088 | tf_op jit(solution)/shard_map/ppermute | solution.py:80
  490.1 73.4 %collective-permute-start.35 = (bf16[512,2816]{1,0:T(8,128)(2,1)}, bf16[512,2816]{1,0:T(8,128)(2,1)}, u32[]{:S(2)}, u32[]{:S(2)}) collective-permute-start(bf16[512,2816]{1,0:T(8,128)(2,1)} %add_convert_fusion.4), channel_id=1, source_target_pairs={{0,4},{2,6},{4,0},{6,2},{8,12},{10,14},{12,8},{14,10},{16,20},{18,... | collective-permute-start | bytes 8650760 | tf_op jit(solution)/shard_map/ppermute | solution.py:77
  508.1 143.0 %reduce-scatter.10.cloned.1.call-start = ((), (), s32[]{:S(2)}) async-start(), calls=%async_computation.15 | async-start | bytes 3604480 | tf_op jit(solution)/shard_map/reduce_scatter | solution.py:103
  528.9 34.6 %collective-permute-start.38 = (bf16[512,2816]{1,0:T(8,128)(2,1)S(1)}, bf16[512,2816]{1,0:T(8,128)(2,1)S(1)}, u32[]{:S(2)}, u32[]{:S(2)}) collective-permute-start(bf16[512,2816]{1,0:T(8,128)(2,1)S(1)} %convolution_convert_fusion.3), channel_id=1, source_target_pairs={{0,2},{2,0},{4,6},{6,4},{8,10},{10,8},{12,14},{14,12},{16,18},{18,... | collective-permute-start | bytes 8650760 | tf_op jit(solution)/shard_map/ppermute | solution.py:74
  533.2 36.8 %collective-permute-start.36 = (bf16[256,2816]{1,0:T(8,128)(2,1)}, bf16[256,2816]{1,0:T(8,128)(2,1)}, u32[]{:S(2)}, u32[]{:S(2)}) collective-permute-start(bf16[256,2816]{1,0:T(8,128)(2,1)} %get-tuple-element.307), channel_id=1, source_target_pairs={{0,2},{2,0},{4,6},{6,4},{8,10},{10,8},{12,14},{14,12},{16,18},{18,... | collective-permute-start | bytes 4325384 | tf_op jit(solution)/shard_map/ppermute | solution.py:74
  533.7 36.3 %collective-permute-start.37 = (bf16[256,2816]{1,0:T(8,128)(2,1)}, bf16[256,2816]{1,0:T(8,128)(2,1)}, u32[]{:S(2)}, u32[]{:S(2)}) collective-permute-start(bf16[256,2816]{1,0:T(8,128)(2,1)} %get-tuple-element.308), channel_id=1, source_target_pairs={{0,2},{2,0},{4,6},{6,4},{8,10},{10,8},{12,14},{14,12},{16,18},{18,... | collective-permute-start | bytes 4325384 | tf_op jit(solution)/shard_map/ppermute | solution.py:74
  569.9 218.4 %reduce-scatter.12.cloned.1.call-start = ((), (), s32[]{:S(2)}) async-start(), calls=%async_computation.16 | async-start | bytes 3604480 | tf_op jit(solution)/shard_map/reduce_scatter | solution.py:103
  569.9 63.5 %collective-permute-start.41 = (bf16[512,2816]{1,0:T(8,128)(2,1)}, bf16[512,2816]{1,0:T(8,128)(2,1)}, u32[]{:S(2)}, u32[]{:S(2)}) collective-permute-start(bf16[512,2816]{1,0:T(8,128)(2,1)} %convolution_convert_fusion.1), channel_id=1, source_target_pairs={{0,2},{2,0},{4,6},{6,4},{8,10},{10,8},{12,14},{14,12},{16,18},{18,... | collective-permute-start | bytes 8650760 | tf_op jit(solution)/shard_map/ppermute | solution.py:74
  576.9 64.4 %collective-permute-start.42 = (bf16[512,2816]{1,0:T(8,128)(2,1)}, bf16[512,2816]{1,0:T(8,128)(2,1)}, u32[]{:S(2)}, u32[]{:S(2)}) collective-permute-start(bf16[512,2816]{1,0:T(8,128)(2,1)} %add_convert_fusion.1), channel_id=1, source_target_pairs={{0,4},{2,6},{4,0},{6,2},{8,12},{10,14},{12,8},{14,10},{16,20},{18,... | collective-permute-start | bytes 8650760 | tf_op jit(solution)/shard_map/ppermute | solution.py:77
  623.8 65.8 %collective-permute-start.45 = (bf16[512,2048]{1,0:T(8,128)(2,1)}, bf16[512,2048]{1,0:T(8,128)(2,1)}, u32[]{:S(2)}, u32[]{:S(2)}) collective-permute-start(bf16[512,2048]{1,0:T(8,128)(2,1)} %get-tuple-element.241), channel_id=1, source_target_pairs={{0,2},{2,0},{4,6},{6,4},{8,10},{10,8},{12,14},{14,12},{16,18},{18,... | collective-permute-start | bytes 6291464 | tf_op jit(solution)/shard_map/ppermute | solution.py:74
  643.5 46.7 %collective-permute-start.46 = (bf16[512,2048]{1,0:T(8,128)(2,1)}, bf16[512,2048]{1,0:T(8,128)(2,1)}, u32[]{:S(2)}, u32[]{:S(2)}) collective-permute-start(bf16[512,2048]{1,0:T(8,128)(2,1)} %add_convert_fusion.9), channel_id=1, source_target_pairs={{0,4},{2,6},{4,0},{6,2},{8,12},{10,14},{12,8},{14,10},{16,20},{18,... | collective-permute-start | bytes 6291464 | tf_op jit(solution)/shard_map/ppermute | solution.py:77
  651.1 142.1 %reduce-scatter.14.cloned.1.call-start = ((), (), s32[]{:S(2)}) async-start(), calls=%async_computation.17 | async-start | bytes 2621440 | tf_op jit(solution)/shard_map/reduce_scatter | solution.py:103
  695.8 136.9 %reduce-scatter.18.cloned.1.call-start = ((), (), s32[]{:S(2)}) async-start(), calls=%async_computation.19 | async-start | bytes 2621440 | tf_op jit(solution)/shard_map/reduce_scatter | solution.py:103
  696.4 47.8 %collective-permute-start.49 = (bf16[512,2048]{1,0:T(8,128)(2,1)}, bf16[512,2048]{1,0:T(8,128)(2,1)S(1)}, u32[]{:S(2)}, u32[]{:S(2)}) collective-permute-start(bf16[512,2048]{1,0:T(8,128)(2,1)} %add_convert_fusion.8), channel_id=1, source_target_pairs={{0,4},{2,6},{4,0},{6,2},{8,12},{10,14},{12,8},{14,10},{16,20},{18,... | collective-permute-start | bytes 6291464 | tf_op jit(solution)/shard_map/ppermute | solution.py:77
  748.2 103.3 %reduce-scatter.16.cloned.1.call-start = ((), (), s32[]{:S(2)}) async-start(), calls=%async_computation.18 | async-start | bytes 1310720 | tf_op jit(solution)/shard_map/reduce_scatter | solution.py:103
  767.1 40.4 %collective-permute-start.51 = (bf16[512,1024]{1,0:T(8,128)(2,1)}, bf16[512,1024]{1,0:T(8,128)(2,1)}, u32[]{:S(2)}, u32[]{:S(2)}) collective-permute-start(bf16[512,1024]{1,0:T(8,128)(2,1)} %convolution_convert_fusion.12), channel_id=1, source_target_pairs={{0,2},{2,0},{4,6},{6,4},{8,10},{10,8},{12,14},{14,12},{16,18},{18,... | collective-permute-start | bytes 3145736 | tf_op jit(solution)/shard_map/ppermute | solution.py:74
  768.5 44.0 %collective-permute-start.53 = (bf16[512,1024]{1,0:T(8,128)(2,1)}, bf16[512,1024]{1,0:T(8,128)(2,1)}, u32[]{:S(2)}, u32[]{:S(2)}) collective-permute-start(bf16[512,1024]{1,0:T(8,128)(2,1)} %add_convert_fusion.13), channel_id=1, source_target_pairs={{0,4},{2,6},{4,0},{6,2},{8,12},{10,14},{12,8},{14,10},{16,20},{18,... | collective-permute-start | bytes 3145736 | tf_op jit(solution)/shard_map/ppermute | solution.py:77
  793.2 68.3 %reduce-scatter.20.cloned.1.call-start = ((), (), s32[]{:S(2)}) async-start(), calls=%async_computation.20 | async-start | bytes 1310720 | tf_op jit(solution)/shard_map/reduce_scatter | solution.py:103
  796.1 36.1 %collective-permute-start.60 = (f32[128]{0:T(128)S(1)}, f32[128]{0:T(128)S(1)}, u32[]{:S(2)}, u32[]{:S(2)}) collective-permute-start(f32[128]{0:T(128)S(1)} %add.339), channel_id=1, source_target_pairs={{0,1},{1,0},{2,3},{3,2},{4,5},{5,4},{6,7},{7,6},{8,9},{9,8},{10,11... | collective-permute-start | bytes 1544 | tf_op jit(solution)/shard_map/ppermute | solution.py:80
  805.9 33.3 %collective-permute-start.54 = (bf16[320,2048]{1,0:T(8,128)(2,1)}, bf16[320,2048]{1,0:T(8,128)(2,1)}, u32[]{:S(2)}, u32[]{:S(2)}) collective-permute-start(bf16[320,2048]{1,0:T(8,128)(2,1)} %fusion.14), channel_id=1, source_target_pairs={{0,1},{1,0},{2,3},{3,2},{4,5},{5,4},{6,7},{7,6},{8,9},{9,8},{10,11... | collective-permute-start | bytes 3932168 | tf_op jit(solution)/shard_map/ppermute | solution.py:80
  (127 other events, 1970.3 us)
Sparse Core Ops, SparseCore 0:
  20.8 32.4 all-gather.7
  55.4 45.0 all-gather.9
  102.0 26.6 all-gather.11
  130.1 27.4 all-gather.13
  159.0 58.6 all-gather.15
  219.1 57.8 all-gather.17
  278.6 57.8 all-gather.19
  508.2 54.0 reduce-scatter.7
  570.0 54.0 reduce-scatter.9
  651.2 54.9 reduce-scatter.11
  708.5 43.7 reduce-scatter.13
  754.5 43.1 reduce-scatter.17
  800.0 26.4 reduce-scatter.15
  832.3 25.6 reduce-scatter.19

commit v6 on v5

--- a/solution.py
+++ b/solution.py
@@ -366,7 +366,7 @@
         ],
         compiler_params=pltpu.CompilerParams(vmem_limit_bytes=56 * 2**20),
         name="attend",
-        cost_estimate=pl.CostEstimate(flops=14_000_000_000, transcendentals=0, bytes_accessed=0),
+        cost_estimate=pl.CostEstimate(flops=0, transcendentals=0, bytes_accessed=0),
     )(
         lam_vec,
         queries,
@@ -466,36 +466,33 @@
                     x * inverse * gain_ref[:, lanes]
                 ).astype(bf16)
 
-    for core in range(2):
+    for group in range(4):
         for turn in range(2):
 
-            @pl.when((step >= core * 2) & (step < core * 2 + 2) & (swap_ref[0] == turn))
+            @pl.when((step == group) & (swap_ref[0] == turn))
             def _():
-                pair = sources[2 * core : 2 * core + 2]
+                pair = sources[2 * group : 2 * group + 2]
                 norm_from(pair[::-1] if turn else pair, unit)
 
     @pl.when(step >= 4)
     def _():
-        norm_from(sources[4:5], rows)
+        norm_from(sources[8:9], rows)
 
 
 def norm_keys(at, prompt_groups, cont_tokens, gain_row, prompt_part):
     cont_len, depth = cont_tokens.shape
     count, upper = at.count, at.upper
-    unit = prompt_groups[0].shape[0] // (2 * upper)
+    unit = prompt_groups[0][0].shape[0] // upper
     group_rows = upper * prompt_part
     if (depth // count) % 128 or cont_len % group_rows or upper % 2:
-        cores = []
-        for pair in (prompt_groups[:2], prompt_groups[2:]):
-            parts = jnp.stack([part.reshape(2 * upper, unit, -1)[:, :prompt_part] for part in pair])
-            parts = at.flip(parts.reshape(2, 2 * upper * prompt_part, depth // 2), 0, at.tensor)
-            cores.append(jnp.concatenate([parts[0], parts[1]], axis=1))
-        rows = at.to_relative(jnp.concatenate(cores + [cont_tokens], axis=0))
+        groups = []
+        for pair in prompt_groups:
+            parts = jnp.stack([part.reshape(upper, unit, -1)[:, :prompt_part] for part in pair])
+            parts = at.flip(parts.reshape(2, group_rows, depth // 2), 0, at.tensor)
+            groups.append(jnp.concatenate([parts[0], parts[1]], axis=1))
+        rows = at.to_relative(jnp.concatenate(groups + [cont_tokens], axis=0))
         rows = rows.astype(f32)
         return (rows * inv_rms(rows, norm_eps) * gain_row).astype(bf16)
-
-    def spot_of(core):
-        return lambda i, blocks, swap: (jnp.clip(i - 2 * core, 0, 1), 0)
 
     return pl.pallas_call(
         lambda *refs: norm_kernel(count, unit, *refs),
@@ -503,7 +500,8 @@
             num_scalar_prefetch=2,
             grid=(4 + cont_len // group_rows,),
             in_specs=[
-                pl.BlockSpec((upper * unit, depth // 2), spot_of(core)) for core in (0, 0, 1, 1)
+                pl.BlockSpec((upper * unit, depth // 2), lambda i, blocks, swap: (0, 0))
+                for _ in range(8)
             ]
             + [
                 pl.BlockSpec(
@@ -516,11 +514,11 @@
         out_shape=jax.ShapeDtypeStruct((prompt_part * count + cont_len, depth), bf16),
         compiler_params=pltpu.CompilerParams(vmem_limit_bytes=56 * 2**20),
         name="norm_keys",
-        cost_estimate=pl.CostEstimate(flops=8_000_000_000, transcendentals=0, bytes_accessed=0),
+        cost_estimate=pl.CostEstimate(flops=0, transcendentals=0, bytes_accessed=0),
     )(
         at.relative_blocks(),
         at.tensor.reshape(1).astype(jnp.int32),
-        *prompt_groups,
+        *[part for pair in prompt_groups for part in pair],
         cont_tokens,
         gain_row.reshape(1, depth),
     )
@@ -588,25 +586,27 @@
     prompt_here, tokens_rel, cot_rel, tokens_turned = together(
         prompt_here, tokens_rel, cot_rel, tokens_turned
     )
-    prompt_pair = jnp.concatenate([prompt_here, at.swap_side(prompt_here)], axis=0)
-    prompt_turned = at.swap_tensor(prompt_pair)
-    prompt_far = at.swap_core(prompt_pair)
-    kv_here = after(kv_here, prompt_pair)
+    cont_tokens = at.in_order(tokens, tokens_turned)[prompt_part:]
+    here_turned, here_far = at.swap_tensor(prompt_here), at.swap_core(prompt_here)
+    prompt_side = at.swap_side(prompt_here)
+    here_turned, prompt_side, cont_tokens = together(here_turned, prompt_side, cont_tokens)
+    side_turned, side_far = at.swap_tensor(prompt_side), at.swap_core(prompt_side)
+    here_turned_far = at.swap_core(here_turned)
+    kv_here = after(kv_here, prompt_side)
     kv_side, kv_near = at.swap_side(kv_here), at.swap_core(kv_here)
-    prompt_turned, kv_side_early = together(prompt_turned, kv_near)
-    kv_near = kv_side_early
-    prompt_far_turned = at.swap_core(prompt_turned)
-    kv_side, q_here = together(kv_side, q_here)
-    kv_far = at.swap_core(kv_side)
-    q_side, q_near = at.swap_side(q_here), at.swap_core(q_here)
-    prompt_far, prompt_far_turned = together(prompt_far, after(prompt_far_turned, kv_side))
-    cont_tokens = at.in_order(tokens, tokens_turned)[prompt_part:]
-    cot_turned = at.swap_tensor(after(cot_rel, prompt_far_turned))
+    side_turned = after(side_turned, kv_here)
+    side_turned_far = at.swap_core(side_turned)
+    prompt_groups = (
+        (prompt_here, here_turned),
+        (prompt_side, side_turned),
+        (here_far, here_turned_far),
+        (side_far, side_turned_far),
+    )
 
     small_all = jnp.concatenate(
         [
-            group.reshape(2 * at.upper, -1, half)[:, prompt_part, : small.size]
-            for group in (prompt_pair, prompt_far)
+            group[0].reshape(at.upper, -1, half)[:, prompt_part, : small.size]
+            for group in prompt_groups
         ],
         axis=0,
     ).astype(f32)
@@ -644,24 +644,29 @@
     )
 
     tokens_f32 = tokens_rel.astype(f32)
-    prompt_groups = (prompt_pair, prompt_turned, prompt_far, prompt_far_turned)
     normed_keys = norm_keys(at, prompt_groups, cont_tokens, attn_gain_row, prompt_part)
-    kv_near, kv_far = after(kv_near, normed_keys), after(kv_far, normed_keys)
+    normed_keys, kv_side, q_here = together(normed_keys, kv_side, q_here)
+    kv_far = at.swap_core(kv_side)
+    q_side, q_near = at.swap_side(q_here), at.swap_core(q_here)
+    cot_turned = at.swap_tensor(after(cot_rel, normed_keys))
+    kv_near = after(kv_near, kv_side)
     kv_full = jnp.concatenate([kv_here, kv_side, kv_near, kv_far], axis=0)
-    kv_full, q_side, out_here = together(kv_full, q_side, out_here)
+    keys_values = plain_product(normed_keys, kv_full).astype(bf16)
+    keys_values, q_side, out_here, normed_late = together(
+        keys_values, q_side, out_here, normed_keys
+    )
     q_far = at.swap_core(q_side)
     out_side, out_near = at.swap_side(out_here), at.swap_core(out_here)
     own_block = lax.dynamic_slice_in_dim(
-        normed_keys, (at.index // 4) * prompt_part, prompt_part, 0
-    )
-    normed = jnp.concatenate([own_block, normed_keys[prompt_len:]], axis=0)
-    keys_values = plain_product(normed_keys, kv_full).astype(bf16)
-    keys_values, out_side, gate_here = together(keys_values, out_side, gate_here)
-    out_far = at.swap_core(out_side)
-    gate_side, gate_near = at.swap_side(gate_here), at.swap_core(gate_here)
+        normed_late, (at.index // 4) * prompt_part, prompt_part, 0
+    )
+    normed = jnp.concatenate([own_block, normed_late[prompt_len:]], axis=0)
     q_parts = [after(part, keys_values) for part in (q_here, q_side, q_near, q_far)]
     q_full = jnp.concatenate(q_parts, axis=0)
     queries = plain_product(after(normed, keys_values), q_full).astype(bf16)
+    queries, out_side, gate_here = together(queries, out_side, gate_here)
+    out_far = at.swap_core(out_side)
+    gate_side, gate_near = at.swap_side(gate_here), at.swap_core(gate_here)
     fixed = (lam_vec, head_gain_row, prompt_spots, bounds, prompt_part)
     heads_out, attn_vec, lse = attend(queries, keys_values, *fixed, (0, heads))
     attn_vec, cot_turned = together(attn_vec, cot_turned)

time: 880 us -> 871 us (0.990)
  other arithmetic: 98 us -> 88.9 us
    all_gather x7, waiting for transfers between devices: 15.8 us -> 46.8 us  [gather_upper(): lax.all_gather(shard, 'dp', axis=0, tiled=True, axis_index_groups=self.up...]
    ppermute x12 -> x13, waiting for transfers between devices: 102 us -> 80.4 us  [swap_tensor(): return lax.ppermute(value, 'tensor', [(0, 1), (1, 0)])]
    ppermute x14, waiting for transfers between devices: 128 us -> 115 us  [swap_side(): return lax.ppermute(value, 'dp', self.side_pairs)]
    unnamed x223 -> x225, local copies, waits for them, and re-layouts: 46.3 us -> 51.4 us
  transfers between devices with their start and end apart: 75 -> 78, of which waited for: 23 -> 26; matrix products, arithmetic and copies ran while one was open for 52% -> 52% of each run, Pallas kernels for 10% -> 10%
where the time goes in v6:
time: 871 us; the launch traced here: 862 us
  matrix products  263 us (30%)
  waiting for transfers between devices  248 us (28%)
  local copies, waits for them, and re-layouts  114 us (13%)
  other arithmetic  88.9 us (10%)
  Pallas kernels  84.6 us (10%)
  starting transfers between devices  48.7 us (6%)
  between operations  15.6 us (2%)
    ppermute x14, waiting for transfers between devices, swap_side(): return lax.ppermute(value, 'dp', self.side_pairs)  115 us
    dot_general x24, matrix products, rows_product(): lax.dot_general(first_arg, second_arg, (((0,), (0,)), ((), ())), preferre...  106 us
    dot_general x14, matrix products, cols_product(): lax.dot_general(first_arg, second_arg, (((1,), (1,)), ((), ())), preferre...  82.6 us
    ppermute x13, waiting for transfers between devices, swap_tensor(): return lax.ppermute(value, 'tensor', [(0, 1), (1, 0)])  80.4 us
    dot_general x6, matrix products, plain_product(): return jnp.dot(first_arg, second_arg, preferred_element_type=f32)  74.8 us
    unnamed x225, local copies, waits for them, and re-layouts  51.4 us
    all_gather x7, waiting for transfers between devices, gather_upper(): lax.all_gather(shard, 'dp', axis=0, tiled=True, axis_index_groups=self.up...  46.8 us
    pallas_call x1, Pallas kernels, attend_back(): pl.pallas_call(lambda *refs: backward_kernel(prompt_len, top_rows, first,...  40 us
  transfers between devices with their start and end apart: 78, of which 26 were waited for; matrix products, arithmetic and copies ran while one was open for 52% of the time, Pallas kernels for 10%

profile of v6, /device:TPU:0, one launch (start us, length us, event | category | flops | bytes accessed | tf_op | source)
XLA Modules:
  0.0 862.5 jit_solution(9536903049068137635)
XLA Ops:
  8.2 4.9 collective-permute-start
  44.5 10.1 %collective-permute-done.1 = bf16[320,2048]{1,0:T(8,128)(2,1)} collective-permute-done((bf16[320,2048]{1,0:T(8,128)(2,1)}, bf16[320,2048]{1,0:T(8,128)(2,1)}, u32[]{:S(2)}, u32[]{:S(2)}) %collective-permute-start.1) | collective-permute-done | bytes 1310752 | tf_op jit(solution)/shard_map/ppermute | solution.py:80
  58.3 4.6 fusion.27.refs_10_
  62.8 18.3 %collective-permute-done.3.refs_4_ = bf16[576,1024]{1,0:T(8,128)(2,1)} collective-permute-done((bf16[576,1024]{1,0:T(8,128)(2,1)}, bf16[576,1024]{1,0:T(8,128)(2,1)}, u32[]{:S(2)}, u32[]{:S(2)}) %collective-permute-start.3) | collective-permute-done | bytes 1179680 | tf_op jit(solution)/shard_map/ppermute | solution.py:77
  83.9 16.5 %all-gather.10.cloned.1.call-done = bf16[512,2048]{1,0:T(8,128)(2,1)} async-done(((bf16[128,2048]{1,0:T(8,128)(2,1)}), bf16[512,2048]{1,0:T(8,128)(2,1)}) %all-gather.10.cloned.1.call-update) | async-done | bytes 2097168 | tf_op jit(solution)/shard_map/all_gather | solution.py:83
  102.4 5.4 collective-permute-done.6.refs_5_
  112.8 12.9 %norm_keys.1 = bf16[2560,2048]{1,0:T(8,128)(2,1)} custom-call(s32[16]{0:T(128)} %get-tuple-element.297.refs_0_, s32[1]{0:T(128)} %bitcast.10.refs_1_, bf16[576,1024]{1,0:T(8,128)(2,1)} %all-gather.8.cloned.1.call-done.refs_2_, bf16[576,1024]{1,0:T(8,128)(2,1)} %collective-permute-done.2.refs_3_, bf16[576,1024]{1,0:T(8,128)(2,1)} %collective-permute-done.3.refs_4_, ...), custom_call_target="tpu_custom_call" | custom-call | tf_op jit(solution)/shard_map/norm_keys/pallas_call | solution.py:497
  128.7 19.4 %collective-permute-done.9 = bf16[512,2048]{1,0:T(8,128)(2,1)} collective-permute-done((bf16[512,2048]{1,0:T(8,128)(2,1)}, bf16[512,2048]{1,0:T(8,128)(2,1)}, u32[]{:S(2)}, u32[]{:S(2)}) %collective-permute-start.9) | collective-permute-done | bytes 2097184 | tf_op jit(solution)/shard_map/ppermute | solution.py:77
  161.7 24.3 %convolution_convert_fusion.refs_2_ = bf16[2560,2048]{1,0:T(8,128)(2,1)} fusion(bf16[2560,2048]{1,0:T(8,128)(2,1)S(1)} %copy-done.29, bf16[2048,2048]{1,0:T(8,128)(2,1)S(1)} %constant_dynamic-update-slice_fusion), kind=kOutput, calls=%fused_computation.1 | convolution fusion | flops 21480079360 | bytes 29360128 | tf_op jit(solution)/shard_map/dot_general | solution.py:33
  203.8 13.9 %all-gather.16.cloned.1.call-done = bf16[512,2816]{1,0:T(8,128)(2,1)} async-done(((bf16[128,2816]{1,0:T(8,128)(2,1)}), bf16[512,2816]{1,0:T(8,128)(2,1)}) %all-gather.16.cloned.1.call-update) | async-done | bytes 2883600 | tf_op jit(solution)/shard_map/all_gather | solution.py:83
  225.6 31.7 %attend.1 = (f32[640,1024]{1,0:T(8,128)}, bf16[640,1024]{1,0:T(8,128)(2,1)}, f32[4,16,640]{2,1,0:T(8,128)}) custom-call(f32[4]{0:T(128)} %subtract_add_fusion.1.refs_0_, bf16[640,1024]{1,0:T(8,128)(2,1)} %convolution_convert_fusion.11.refs_1_, bf16[2560,2048]{1,0:T(8,128)(2,1)} %convolution_convert_fusion.refs_2_, f32[1,1024]{1,0:T(1,128)} %bitcast.127, ...), custom_call_target="tpu_custom_call" | custom-call | tf_op jit(solution)/shard_map/attend/pallas_call | solution.py:341
  268.2 8.8 %all-gather.18.cloned.1.call-done = bf16[512,2816]{1,0:T(8,128)(2,1)} async-done(((bf16[128,2816]{1,0:T(8,128)(2,1)}), bf16[512,2816]{1,0:T(8,128)(2,1)}) %all-gather.18.cloned.1.call-update) | async-done | bytes 2883600 | tf_op jit(solution)/shard_map/all_gather | solution.py:83
  277.0 5.2 collective-permute-done.19
  288.4 25.2 %collective-permute-done.20 = bf16[320,2048]{1,0:T(8,128)(2,1)S(1)} collective-permute-done((bf16[320,2048]{1,0:T(8,128)(2,1)}, bf16[320,2048]{1,0:T(8,128)(2,1)S(1)}, u32[]{:S(2)}, u32[]{:S(2)}) %collective-permute-start.20) | collective-permute-done | bytes 1310752 | tf_op jit(solution)/shard_map/ppermute | solution.py:80
  317.7 14.4 %pad_maximum_fusion = bf16[2048,2816]{1,0:T(8,128)(2,1)} fusion(bf16[512,2816]{1,0:T(8,128)(2,1)S(1)} %collective-permute-done.23, bf16[512,2816]{1,0:T(8,128)(2,1)} %collective-permute-done.22, bf16[512,2816]{1,0:T(8,128)(2,1)} %collective-permute-done.19, bf16[512,2816]{1,0:T(8,128)(2,1)S(1)} %copy-done.47), kind=kLoop, calls=%fused_computation | loop fusion | flops 46137344 | bytes 23068672 | tf_op jit(solution)/shard_map/concatenate | solution.py:690
  332.1 4.4 all-gather.20.cloned.1.call-done
  336.5 12.1 %collective-permute-done.24 = bf16[512,2816]{1,0:T(8,128)(2,1)} collective-permute-done((bf16[512,2816]{1,0:T(8,128)(2,1)}, bf16[512,2816]{1,0:T(8,128)(2,1)}, u32[]{:S(2)}, u32[]{:S(2)}) %collective-permute-start.24) | collective-permute-done | bytes 2883616 | tf_op jit(solution)/shard_map/ppermute | solution.py:77
  354.2 13.1 %fusion.136 = f32[640,2816]{1,0:T(8,128)} fusion(bf16[2048,2816]{1,0:T(8,128)(2,1)} %pad_maximum_fusion, bf16[320,2048]{1,0:T(8,128)(2,1)S(1)} %collective-permute-done.21, bf16[320,2048]{1,0:T(8,128)(2,1)S(1)} %multiply_convert_fusion.3), kind=kOutput, calls=%fused_computation.274 | convolution fusion | flops 7387217920 | bytes 21364736 | tf_op jit(solution)/shard_map/dot_general | solution.py:33
  377.1 15.1 %multiply_convert_fusion.2 = (bf16[640,2816]{1,0:T(8,128)(2,1)S(1)}, f32[640,2816]{1,0:T(8,128)}) fusion(f32[640,2816]{1,0:T(8,128)} %fusion.136, bf16[640,2048]{1,0:T(8,128)(2,1)S(1)} %pad_maximum_fusion.2, bf16[2048,2816]{1,0:T(8,128)(2,1)} %constant_dynamic-update-slice_fusion.12), kind=kOutput, calls=%fused_computation.4 | convolution fusion | flops 7392788480 | bytes 32178176 | tf_op jit(solution)/shard_map/dot_general | solution.py:33
  398.9 18.3 %collective-permute-done.27 = bf16[512,2816]{1,0:T(8,128)(2,1)} collective-permute-done((bf16[512,2816]{1,0:T(8,128)(2,1)S(1)}, bf16[512,2816]{1,0:T(8,128)(2,1)}, u32[]{:S(2)}, u32[]{:S(2)}) %collective-permute-start.27) | collective-permute-done | bytes 2883616 | tf_op jit(solution)/shard_map/ppermute | solution.py:77
  420.0 5.0 fusion.77
  432.7 4.3 copy-done.63
  437.0 15.3 %multiply_convert_fusion = (bf16[640,2816]{1,0:T(8,128)(2,1)S(1)}, bf16[640,2816]{1,0:T(8,128)(2,1)S(1)}) fusion(f32[640,2816]{1,0:T(8,128)} %fusion.136, f32[640,2816]{1,0:T(8,128)} %get-tuple-element.331, bf16[640,2048]{1,0:T(8,128)(2,1)S(1)} %copy-done.41, bf16[2048,2816]{1,0:T(8,128)(2,1)} %copy-done.63), kind=kOutput, calls=%fused_computation.2 | convolution fusion | flops 7405404160 | bytes 35782656 | tf_op jit(solution)/shard_map/dot_general | solution.py:33
  456.3 5.9 fusion
  465.6 4.4 fusion.40
  483.5 8.9 %fusion.147 = f32[320,2048]{1,0:T(8,128)} fusion(bf16[320,2816]{1,0:T(8,128)(2,1)S(1)} %copy-done.52, bf16[2048,2816]{1,0:T(8,128)(2,1)} %pad_maximum_fusion), kind=kOutput, calls=%fused_computation.284 | convolution fusion | flops 3690987520 | bytes 15958016 | tf_op jit(solution)/shard_map/dot_general | solution.py:43
  494.7 5.4 add_convert_fusion.3
  500.2 10.1 %convolution_add_fusion.2 = f32[320,2048]{1,0:T(8,128)S(1)} fusion(f32[320,2048]{1,0:T(8,128)} %fusion.147, bf16[320,2816]{1,0:T(8,128)(2,1)} %get-tuple-element.220, bf16[2048,2816]{1,0:T(8,128)(2,1)} %constant_dynamic-update-slice_fusion.12), kind=kOutput, calls=%fused_computation.71 | convolution fusion | flops 3691642880 | bytes 18579456 | tf_op jit(solution)/shard_map/dot_general | solution.py:43
  514.9 4.6 fusion.137
  528.6 19.2 %collective-permute-done.37 = bf16[320,2048]{1,0:T(8,128)(2,1)S(1)} collective-permute-done((bf16[320,2048]{1,0:T(8,128)(2,1)S(1)}, bf16[320,2048]{1,0:T(8,128)(2,1)S(1)}, u32[]{:S(2)}, u32[]{:S(2)}) %collective-permute-start.37) | collective-permute-done | bytes 1310752 | tf_op jit(solution)/shard_map/ppermute | solution.py:80
  555.6 6.3 add_convert_fusion.2
  570.4 40.0 %attend_back.1 = (bf16[1024,640]{1,0:T(8,128)(2,1)}, bf16[2560,2048]{1,0:T(8,128)(2,1)}, f32[4,8,256]{2,1,0:T(8,128)}) custom-call(f32[4]{0:T(128)} %subtract_add_fusion.1.refs_0_, bf16[640,1024]{1,0:T(8,128)(2,1)} %convolution_convert_fusion.11.refs_1_, bf16[2560,2048]{1,0:T(8,128)(2,1)} %convolution_convert_fusion.refs_2_, f32[1,1024]{1,0:T(1,128)} %bitcast.128, ...), custom_call_target="tpu_custom_call" | custom-call | tf_op jit(solution)/shard_map/attend_back/pallas_call | solution.py:389
  610.5 6.3 fusion.139
  617.9 8.5 convolution_convert_fusion.8
  626.5 6.9 collective-permute-done.45
  637.0 7.1 add_convert_fusion
  644.1 10.6 %convolution_convert_fusion.7 = bf16[512,2048]{1,0:T(8,128)(2,1)} fusion(bf16[2560,2048]{1,0:T(8,128)(2,1)} %get-tuple-element.248, bf16[2560,2048]{1,0:T(8,128)(2,1)} %norm_keys.1), kind=kOutput, calls=%fused_computation.63 | convolution fusion | flops 5369757696 | bytes 15204352 | tf_op jit(solution)/shard_map/dot_general | solution.py:37
  654.8 10.6 %add_convert_fusion.8 = bf16[512,2048]{1,0:T(8,128)(2,1)} fusion(bf16[512,2048]{1,0:T(8,128)(2,1)} %collective-permute-done.42, bf16[2560,2048]{1,0:T(8,128)(2,1)} %get-tuple-element.248, bf16[2560,2048]{1,0:T(8,128)(2,1)} %norm_keys.1), kind=kOutput, calls=%fused_computation.41 | convolution fusion | flops 5371854848 | bytes 17301504 | tf_op jit(solution)/shard_map/dot_general | solution.py:37
  674.0 8.7 %fusion.29 = f32[320,2048]{1,0:T(8,128)} fusion(bf16[2048,2816]{1,0:T(8,128)(2,1)} %copy-done.63, bf16[640,2816]{1,0:T(8,128)(2,1)S(1)} %copy-done.6), kind=kOutput, calls=%fused_computation.115 | convolution fusion | flops 3690987520 | bytes 15958016 | tf_op jit(solution)/shard_map/dot_general | solution.py:43
  682.8 5.6 add_convert_fusion.7
  689.9 9.3 %fusion.22 = f32[512,2048]{1,0:T(8,128)S(1)} fusion(bf16[2560,2048]{1,0:T(8,128)(2,1)} %get-tuple-element.248, bf16[2560,2048]{1,0:T(8,128)(2,1)} %norm_keys.1), kind=kOutput, calls=%fused_computation.84 | convolution fusion | flops 5368709120 | bytes 17301504 | tf_op jit(solution)/shard_map/dot_general | solution.py:37
  703.4 9.7 %convolution_convert_fusion.10 = bf16[320,2048]{1,0:T(8,128)(2,1)} fusion(bf16[2048,2816]{1,0:T(8,128)(2,1)} %copy-done.63, bf16[640,2816]{1,0:T(8,128)(2,1)S(1)} %copy-done.7), kind=kOutput, calls=%fused_computation.74 | convolution fusion | flops 3691642880 | bytes 14647296 | tf_op jit(solution)/shard_map/dot_general | solution.py:43
  713.1 23.8 %collective-permute-done.52 = bf16[512,2048]{1,0:T(8,128)(2,1)S(1)} collective-permute-done((bf16[512,2048]{1,0:T(8,128)(2,1)}, bf16[512,2048]{1,0:T(8,128)(2,1)S(1)}, u32[]{:S(2)}, u32[]{:S(2)}) %collective-permute-start.52) | collective-permute-done | bytes 2097184 | tf_op jit(solution)/shard_map/ppermute | solution.py:77
  761.2 19.3 %collective-permute-done.50 = bf16[320,2048]{1,0:T(8,128)(2,1)} collective-permute-done((bf16[320,2048]{1,0:T(8,128)(2,1)S(1)}, bf16[320,2048]{1,0:T(8,128)(2,1)}, u32[]{:S(2)}, u32[]{:S(2)}) %collective-permute-start.50) | collective-permute-done | bytes 1310752 | tf_op jit(solution)/shard_map/ppermute | solution.py:80
  789.0 6.0 fusion.46
  799.0 5.1 collective-permute-done.56
  808.8 8.4 fusion.48
  830.7 4.8 fusion.16
  (524 shorter events, 288.2 us)
Async XLA Ops:
  7.2 47.4 %all-gather.8.cloned.1.call-start = ((), (), s32[]{:S(2)}) async-start(), calls=%async_computation.7 | async-start | bytes 1474560 | tf_op jit(solution)/shard_map/all_gather | solution.py:83
  20.6 79.8 %all-gather.10.cloned.1.call-start = ((), (), s32[]{:S(2)}) async-start(), calls=%async_computation.8 | async-start | bytes 2621440 | tf_op jit(solution)/shard_map/all_gather | solution.py:83
  23.2 105.5 %all-gather.12.cloned.1.call-start = ((), (), s32[]{:S(2)}) async-start(), calls=%async_computation.9 | async-start | bytes 1310720 | tf_op jit(solution)/shard_map/all_gather | solution.py:83
  23.9 162.0 %all-gather.14.cloned.1.call-start = ((), (), s32[]{:S(2)}) async-start(), calls=%async_computation.10 | async-start | bytes 1310720 | tf_op jit(solution)/shard_map/all_gather | solution.py:83
  24.0 30.6 %collective-permute-start.1 = (bf16[320,2048]{1,0:T(8,128)(2,1)}, bf16[320,2048]{1,0:T(8,128)(2,1)}, u32[]{:S(2)}, u32[]{:S(2)}) collective-permute-start(bf16[320,2048]{1,0:T(8,128)(2,1)} %param.19), channel_id=1, source_target_pairs={{0,1},{1,0},{2,3},{3,2},{4,5},{5,4},{6,7},{7,6},{8,9},{9,8},{10,11... | collective-permute-start | bytes 3932168 | tf_op jit(solution)/shard_map/ppermute | solution.py:80
  33.7 184.0 %all-gather.16.cloned.1.call-start = ((), (), s32[]{:S(2)}) async-start(), calls=%async_computation.11 | async-start | bytes 3604480 | tf_op jit(solution)/shard_map/all_gather | solution.py:83
  57.8 219.2 %all-gather.18.cloned.1.call-start = ((), (), s32[]{:S(2)}) async-start(), calls=%async_computation.12 | async-start | bytes 3604480 | tf_op jit(solution)/shard_map/all_gather | solution.py:83
  100.4 47.7 %collective-permute-start.9 = (bf16[512,2048]{1,0:T(8,128)(2,1)}, bf16[512,2048]{1,0:T(8,128)(2,1)}, u32[]{:S(2)}, u32[]{:S(2)}) collective-permute-start(bf16[512,2048]{1,0:T(8,128)(2,1)} %all-gather.10.cloned.1.call-done), channel_id=1, source_target_pairs={{0,4},{2,6},{4,0},{6,2},{8,12},{10,14},{12,8},{14,10},{16,20},{18,... | collective-permute-start | bytes 6291464 | tf_op jit(solution)/shard_map/ppermute | solution.py:77
  107.8 44.7 %collective-permute-start.10 = (bf16[512,2048]{1,0:T(8,128)(2,1)}, bf16[512,2048]{1,0:T(8,128)(2,1)}, u32[]{:S(2)}, u32[]{:S(2)}) collective-permute-start(bf16[512,2048]{1,0:T(8,128)(2,1)} %all-gather.10.cloned.1.call-done), channel_id=1, source_target_pairs={{0,2},{2,0},{4,6},{6,4},{8,10},{10,8},{12,14},{14,12},{16,18},{18,... | collective-permute-start | bytes 6291464 | tf_op jit(solution)/shard_map/ppermute | solution.py:74
  148.5 188.0 %all-gather.20.cloned.1.call-start = ((), (), s32[]{:S(2)}) async-start(), calls=%async_computation.13 | async-start | bytes 3604480 | tf_op jit(solution)/shard_map/all_gather | solution.py:83
  150.5 44.7 %collective-permute-start.13 = (bf16[512,1024]{1,0:T(8,128)(2,1)}, bf16[512,1024]{1,0:T(8,128)(2,1)}, u32[]{:S(2)}, u32[]{:S(2)}) collective-permute-start(bf16[512,1024]{1,0:T(8,128)(2,1)} %all-gather.12.cloned.1.call-done), channel_id=1, source_target_pairs={{0,2},{2,0},{4,6},{6,4},{8,10},{10,8},{12,14},{14,12},{16,18},{18,... | collective-permute-start | bytes 3145736 | tf_op jit(solution)/shard_map/ppermute | solution.py:74
  151.0 34.9 %collective-permute-start.12 = (bf16[512,1024]{1,0:T(8,128)(2,1)}, bf16[512,1024]{1,0:T(8,128)(2,1)}, u32[]{:S(2)}, u32[]{:S(2)}) collective-permute-start(bf16[512,1024]{1,0:T(8,128)(2,1)} %all-gather.12.cloned.1.call-done), channel_id=1, source_target_pairs={{0,4},{2,6},{4,0},{6,2},{8,12},{10,14},{12,8},{14,10},{16,20},{18,... | collective-permute-start | bytes 3145736 | tf_op jit(solution)/shard_map/ppermute | solution.py:77
  186.0 71.2 %collective-permute-start.16 = (bf16[320,2048]{1,0:T(8,128)(2,1)S(1)}, bf16[320,2048]{1,0:T(8,128)(2,1)}, u32[]{:S(2)}, u32[]{:S(2)}) collective-permute-start(bf16[320,2048]{1,0:T(8,128)(2,1)S(1)} %reshape.272), channel_id=1, source_target_pairs={{0,1},{1,0},{2,3},{3,2},{4,5},{5,4},{6,7},{7,6},{8,9},{9,8},{10,11... | collective-permute-start | bytes 3932168 | tf_op jit(solution)/shard_map/ppermute | solution.py:80
  217.7 64.5 %collective-permute-start.19 = (bf16[512,2816]{1,0:T(8,128)(2,1)}, bf16[512,2816]{1,0:T(8,128)(2,1)}, u32[]{:S(2)}, u32[]{:S(2)}) collective-permute-start(bf16[512,2816]{1,0:T(8,128)(2,1)} %all-gather.16.cloned.1.call-done), channel_id=1, source_target_pairs={{0,4},{2,6},{4,0},{6,2},{8,12},{10,14},{12,8},{14,10},{16,20},{18,... | collective-permute-start | bytes 8650760 | tf_op jit(solution)/shard_map/ppermute | solution.py:77
  219.9 37.4 %collective-permute-start.17 = (bf16[512,1024]{1,0:T(8,128)(2,1)}, bf16[512,1024]{1,0:T(8,128)(2,1)}, u32[]{:S(2)}, u32[]{:S(2)}) collective-permute-start(bf16[512,1024]{1,0:T(8,128)(2,1)} %all-gather.14.cloned.1.call-done), channel_id=1, source_target_pairs={{0,2},{2,0},{4,6},{6,4},{8,10},{10,8},{12,14},{14,12},{16,18},{18,... | collective-permute-start | bytes 3145736 | tf_op jit(solution)/shard_map/ppermute | solution.py:74
  220.0 390.5 %reduce-scatter.8.cloned.1.call-start = ((), (), s32[]{:S(2)}) async-start(), calls=%async_computation.14 | async-start | bytes 3604480 | tf_op jit(solution)/shard_map/reduce_scatter | solution.py:103
  220.9 40.4 %collective-permute-start.18 = (bf16[512,1024]{1,0:T(8,128)(2,1)}, bf16[512,1024]{1,0:T(8,128)(2,1)}, u32[]{:S(2)}, u32[]{:S(2)}) collective-permute-start(bf16[512,1024]{1,0:T(8,128)(2,1)} %collective-permute-done.15), channel_id=1, source_target_pairs={{0,2},{2,0},{4,6},{6,4},{8,10},{10,8},{12,14},{14,12},{16,18},{18,... | collective-permute-start | bytes 3145736 | tf_op jit(solution)/shard_map/ppermute | solution.py:74
  224.2 93.5 %collective-permute-start.22 = (bf16[512,2816]{1,0:T(8,128)(2,1)}, bf16[512,2816]{1,0:T(8,128)(2,1)}, u32[]{:S(2)}, u32[]{:S(2)}) collective-permute-start(bf16[512,2816]{1,0:T(8,128)(2,1)} %all-gather.16.cloned.1.call-done), channel_id=1, source_target_pairs={{0,2},{2,0},{4,6},{6,4},{8,10},{10,8},{12,14},{14,12},{16,18},{18,... | collective-permute-start | bytes 8650760 | tf_op jit(solution)/shard_map/ppermute | solution.py:74
  282.2 35.4 %collective-permute-start.23 = (bf16[512,2816]{1,0:T(8,128)(2,1)}, bf16[512,2816]{1,0:T(8,128)(2,1)S(1)}, u32[]{:S(2)}, u32[]{:S(2)}) collective-permute-start(bf16[512,2816]{1,0:T(8,128)(2,1)} %collective-permute-done.19), channel_id=1, source_target_pairs={{0,2},{2,0},{4,6},{6,4},{8,10},{10,8},{12,14},{14,12},{16,18},{18,... | collective-permute-start | bytes 8650760 | tf_op jit(solution)/shard_map/ppermute | solution.py:74
  282.2 31.4 %collective-permute-start.20 = (bf16[320,2048]{1,0:T(8,128)(2,1)}, bf16[320,2048]{1,0:T(8,128)(2,1)S(1)}, u32[]{:S(2)}, u32[]{:S(2)}) collective-permute-start(bf16[320,2048]{1,0:T(8,128)(2,1)} %convolution_convert_fusion.9), channel_id=1, source_target_pairs={{0,1},{1,0},{2,3},{3,2},{4,5},{5,4},{6,7},{7,6},{8,9},{9,8},{10,11... | collective-permute-start | bytes 3932168 | tf_op jit(solution)/shard_map/ppermute | solution.py:80
  283.7 64.9 %collective-permute-start.24 = (bf16[512,2816]{1,0:T(8,128)(2,1)}, bf16[512,2816]{1,0:T(8,128)(2,1)}, u32[]{:S(2)}, u32[]{:S(2)}) collective-permute-start(bf16[512,2816]{1,0:T(8,128)(2,1)} %all-gather.18.cloned.1.call-done), channel_id=1, source_target_pairs={{0,4},{2,6},{4,0},{6,2},{8,12},{10,14},{12,8},{14,10},{16,20},{18,... | collective-permute-start | bytes 8650760 | tf_op jit(solution)/shard_map/ppermute | solution.py:77
  286.8 80.5 %collective-permute-start.25 = (bf16[512,2816]{1,0:T(8,128)(2,1)}, bf16[512,2816]{1,0:T(8,128)(2,1)}, u32[]{:S(2)}, u32[]{:S(2)}) collective-permute-start(bf16[512,2816]{1,0:T(8,128)(2,1)} %all-gather.18.cloned.1.call-done), channel_id=1, source_target_pairs={{0,2},{2,0},{4,6},{6,4},{8,10},{10,8},{12,14},{14,12},{16,18},{18,... | collective-permute-start | bytes 8650760 | tf_op jit(solution)/shard_map/ppermute | solution.py:74
  316.1 38.0 %collective-permute-start.21 = (bf16[320,2048]{1,0:T(8,128)(2,1)S(1)}, bf16[320,2048]{1,0:T(8,128)(2,1)S(1)}, u32[]{:S(2)}, u32[]{:S(2)}) collective-permute-start(bf16[320,2048]{1,0:T(8,128)(2,1)S(1)} %multiply_convert_fusion.3), channel_id=1, source_target_pairs={{0,1},{1,0},{2,3},{3,2},{4,5},{5,4},{6,7},{7,6},{8,9},{9,8},{10,11... | collective-permute-start | bytes 3932168 | tf_op jit(solution)/shard_map/ppermute | solution.py:80
  352.2 65.8 %collective-permute-start.28 = (bf16[512,2816]{1,0:T(8,128)(2,1)S(1)}, bf16[512,2816]{1,0:T(8,128)(2,1)}, u32[]{:S(2)}, u32[]{:S(2)}) collective-permute-start(bf16[512,2816]{1,0:T(8,128)(2,1)S(1)} %copy-done.43), channel_id=1, source_target_pairs={{0,2},{2,0},{4,6},{6,4},{8,10},{10,8},{12,14},{14,12},{16,18},{18,... | collective-permute-start | bytes 8650760 | tf_op jit(solution)/shard_map/ppermute | solution.py:74
  352.7 64.5 %collective-permute-start.27 = (bf16[512,2816]{1,0:T(8,128)(2,1)S(1)}, bf16[512,2816]{1,0:T(8,128)(2,1)}, u32[]{:S(2)}, u32[]{:S(2)}) collective-permute-start(bf16[512,2816]{1,0:T(8,128)(2,1)S(1)} %copy-done.43), channel_id=1, source_target_pairs={{0,4},{2,6},{4,0},{6,2},{8,12},{10,14},{12,8},{14,10},{16,20},{18,... | collective-permute-start | bytes 8650760 | tf_op jit(solution)/shard_map/ppermute | solution.py:77
  417.4 77.3 %collective-permute-start.34 = (bf16[512,2816]{1,0:T(8,128)(2,1)}, bf16[512,2816]{1,0:T(8,128)(2,1)}, u32[]{:S(2)}, u32[]{:S(2)}) collective-permute-start(bf16[512,2816]{1,0:T(8,128)(2,1)} %convolution_convert_fusion.5), channel_id=1, source_target_pairs={{0,2},{2,0},{4,6},{6,4},{8,10},{10,8},{12,14},{14,12},{16,18},{18,... | collective-permute-start | bytes 8650760 | tf_op jit(solution)/shard_map/ppermute | solution.py:74
  429.0 65.7 %collective-permute-start.33 = (bf16[512,2816]{1,0:T(8,128)(2,1)}, bf16[512,2816]{1,0:T(8,128)(2,1)}, u32[]{:S(2)}, u32[]{:S(2)}) collective-permute-start(bf16[512,2816]{1,0:T(8,128)(2,1)} %add_convert_fusion.5), channel_id=1, source_target_pairs={{0,4},{2,6},{4,0},{6,2},{8,12},{10,14},{12,8},{14,10},{16,20},{18,... | collective-permute-start | bytes 8650760 | tf_op jit(solution)/shard_map/ppermute | solution.py:77
  469.9 42.9 %collective-permute-start.35 = (bf16[320,1024]{1,0:T(8,128)(2,1)}, bf16[320,1024]{1,0:T(8,128)(2,1)S(1)}, u32[]{:S(2)}, u32[]{:S(2)}) collective-permute-start(bf16[320,1024]{1,0:T(8,128)(2,1)} %fusion.40), channel_id=1, source_target_pairs={{0,1},{1,0},{2,3},{3,2},{4,5},{5,4},{6,7},{7,6},{8,9},{9,8},{10,11... | collective-permute-start | bytes 1966088 | tf_op jit(solution)/shard_map/ppermute | solution.py:80
  477.3 35.6 %collective-permute-start.36 = (bf16[320,1024]{1,0:T(8,128)(2,1)}, bf16[320,1024]{1,0:T(8,128)(2,1)}, u32[]{:S(2)}, u32[]{:S(2)}) collective-permute-start(bf16[320,1024]{1,0:T(8,128)(2,1)} %fusion.37), channel_id=1, source_target_pairs={{0,1},{1,0},{2,3},{3,2},{4,5},{5,4},{6,7},{7,6},{8,9},{9,8},{10,11... | collective-permute-start | bytes 1966088 | tf_op jit(solution)/shard_map/ppermute | solution.py:80
  483.0 72.6 %collective-permute-start.38 = (bf16[512,2816]{1,0:T(8,128)(2,1)}, bf16[512,2816]{1,0:T(8,128)(2,1)}, u32[]{:S(2)}, u32[]{:S(2)}) collective-permute-start(bf16[512,2816]{1,0:T(8,128)(2,1)} %add_convert_fusion.4), channel_id=1, source_target_pairs={{0,4},{2,6},{4,0},{6,2},{8,12},{10,14},{12,8},{14,10},{16,20},{18,... | collective-permute-start | bytes 8650760 | tf_op jit(solution)/shard_map/ppermute | solution.py:77
  500.1 143.9 %reduce-scatter.10.cloned.1.call-start = ((), (), s32[]{:S(2)}) async-start(), calls=%async_computation.15 | async-start | bytes 3604480 | tf_op jit(solution)/shard_map/reduce_scatter | solution.py:103
  519.8 35.8 %collective-permute-start.41 = (bf16[512,2816]{1,0:T(8,128)(2,1)S(1)}, bf16[512,2816]{1,0:T(8,128)(2,1)S(1)}, u32[]{:S(2)}, u32[]{:S(2)}) collective-permute-start(bf16[512,2816]{1,0:T(8,128)(2,1)S(1)} %convolution_convert_fusion.3), channel_id=1, source_target_pairs={{0,2},{2,0},{4,6},{6,4},{8,10},{10,8},{12,14},{14,12},{16,18},{18,... | collective-permute-start | bytes 8650760 | tf_op jit(solution)/shard_map/ppermute | solution.py:74
  524.0 38.0 %collective-permute-start.39 = (bf16[256,2816]{1,0:T(8,128)(2,1)}, bf16[256,2816]{1,0:T(8,128)(2,1)}, u32[]{:S(2)}, u32[]{:S(2)}) collective-permute-start(bf16[256,2816]{1,0:T(8,128)(2,1)} %get-tuple-element.307), channel_id=1, source_target_pairs={{0,2},{2,0},{4,6},{6,4},{8,10},{10,8},{12,14},{14,12},{16,18},{18,... | collective-permute-start | bytes 4325384 | tf_op jit(solution)/shard_map/ppermute | solution.py:74
  524.5 37.5 %collective-permute-start.40 = (bf16[256,2816]{1,0:T(8,128)(2,1)}, bf16[256,2816]{1,0:T(8,128)(2,1)}, u32[]{:S(2)}, u32[]{:S(2)}) collective-permute-start(bf16[256,2816]{1,0:T(8,128)(2,1)} %get-tuple-element.308), channel_id=1, source_target_pairs={{0,2},{2,0},{4,6},{6,4},{8,10},{10,8},{12,14},{14,12},{16,18},{18,... | collective-permute-start | bytes 4325384 | tf_op jit(solution)/shard_map/ppermute | solution.py:74
  561.9 218.6 %reduce-scatter.12.cloned.1.call-start = ((), (), s32[]{:S(2)}) async-start(), calls=%async_computation.16 | async-start | bytes 3604480 | tf_op jit(solution)/shard_map/reduce_scatter | solution.py:103
  561.9 64.5 %collective-permute-start.44 = (bf16[512,2816]{1,0:T(8,128)(2,1)}, bf16[512,2816]{1,0:T(8,128)(2,1)}, u32[]{:S(2)}, u32[]{:S(2)}) collective-permute-start(bf16[512,2816]{1,0:T(8,128)(2,1)} %convolution_convert_fusion.1), channel_id=1, source_target_pairs={{0,2},{2,0},{4,6},{6,4},{8,10},{10,8},{12,14},{14,12},{16,18},{18,... | collective-permute-start | bytes 8650760 | tf_op jit(solution)/shard_map/ppermute | solution.py:74
  569.0 64.4 %collective-permute-start.45 = (bf16[512,2816]{1,0:T(8,128)(2,1)}, bf16[512,2816]{1,0:T(8,128)(2,1)}, u32[]{:S(2)}, u32[]{:S(2)}) collective-permute-start(bf16[512,2816]{1,0:T(8,128)(2,1)} %add_convert_fusion.1), channel_id=1, source_target_pairs={{0,4},{2,6},{4,0},{6,2},{8,12},{10,14},{12,8},{14,10},{16,20},{18,... | collective-permute-start | bytes 8650760 | tf_op jit(solution)/shard_map/ppermute | solution.py:77
  616.8 65.9 %collective-permute-start.48 = (bf16[512,2048]{1,0:T(8,128)(2,1)}, bf16[512,2048]{1,0:T(8,128)(2,1)}, u32[]{:S(2)}, u32[]{:S(2)}) collective-permute-start(bf16[512,2048]{1,0:T(8,128)(2,1)} %get-tuple-element.241), channel_id=1, source_target_pairs={{0,2},{2,0},{4,6},{6,4},{8,10},{10,8},{12,14},{14,12},{16,18},{18,... | collective-permute-start | bytes 6291464 | tf_op jit(solution)/shard_map/ppermute | solution.py:74
  635.5 47.3 %collective-permute-start.49 = (bf16[512,2048]{1,0:T(8,128)(2,1)}, bf16[512,2048]{1,0:T(8,128)(2,1)}, u32[]{:S(2)}, u32[]{:S(2)}) collective-permute-start(bf16[512,2048]{1,0:T(8,128)(2,1)} %add_convert_fusion.9), channel_id=1, source_target_pairs={{0,4},{2,6},{4,0},{6,2},{8,12},{10,14},{12,8},{14,10},{16,20},{18,... | collective-permute-start | bytes 6291464 | tf_op jit(solution)/shard_map/ppermute | solution.py:77
  644.1 140.6 %reduce-scatter.14.cloned.1.call-start = ((), (), s32[]{:S(2)}) async-start(), calls=%async_computation.17 | async-start | bytes 2621440 | tf_op jit(solution)/shard_map/reduce_scatter | solution.py:103
  688.4 135.8 %reduce-scatter.18.cloned.1.call-start = ((), (), s32[]{:S(2)}) async-start(), calls=%async_computation.19 | async-start | bytes 2621440 | tf_op jit(solution)/shard_map/reduce_scatter | solution.py:103
  689.1 47.8 %collective-permute-start.52 = (bf16[512,2048]{1,0:T(8,128)(2,1)}, bf16[512,2048]{1,0:T(8,128)(2,1)S(1)}, u32[]{:S(2)}, u32[]{:S(2)}) collective-permute-start(bf16[512,2048]{1,0:T(8,128)(2,1)} %add_convert_fusion.8), channel_id=1, source_target_pairs={{0,4},{2,6},{4,0},{6,2},{8,12},{10,14},{12,8},{14,10},{16,20},{18,... | collective-permute-start | bytes 6291464 | tf_op jit(solution)/shard_map/ppermute | solution.py:77
  740.9 102.0 %reduce-scatter.16.cloned.1.call-start = ((), (), s32[]{:S(2)}) async-start(), calls=%async_computation.18 | async-start | bytes 1310720 | tf_op jit(solution)/shard_map/reduce_scatter | solution.py:103
  758.9 40.0 %collective-permute-start.54 = (bf16[512,1024]{1,0:T(8,128)(2,1)}, bf16[512,1024]{1,0:T(8,128)(2,1)}, u32[]{:S(2)}, u32[]{:S(2)}) collective-permute-start(bf16[512,1024]{1,0:T(8,128)(2,1)} %convolution_convert_fusion.12), channel_id=1, source_target_pairs={{0,2},{2,0},{4,6},{6,4},{8,10},{10,8},{12,14},{14,12},{16,18},{18,... | collective-permute-start | bytes 3145736 | tf_op jit(solution)/shard_map/ppermute | solution.py:74
  760.4 43.6 %collective-permute-start.56 = (bf16[512,1024]{1,0:T(8,128)(2,1)}, bf16[512,1024]{1,0:T(8,128)(2,1)}, u32[]{:S(2)}, u32[]{:S(2)}) collective-permute-start(bf16[512,1024]{1,0:T(8,128)(2,1)} %add_convert_fusion.13), channel_id=1, source_target_pairs={{0,4},{2,6},{4,0},{6,2},{8,12},{10,14},{12,8},{14,10},{16,20},{18,... | collective-permute-start | bytes 3145736 | tf_op jit(solution)/shard_map/ppermute | solution.py:77
  784.7 69.2 %reduce-scatter.20.cloned.1.call-start = ((), (), s32[]{:S(2)}) async-start(), calls=%async_computation.20 | async-start | bytes 1310720 | tf_op jit(solution)/shard_map/reduce_scatter | solution.py:103
  787.5 36.1 %collective-permute-start.63 = (f32[128]{0:T(128)S(1)}, f32[128]{0:T(128)S(1)}, u32[]{:S(2)}, u32[]{:S(2)}) collective-permute-start(f32[128]{0:T(128)S(1)} %add.339), channel_id=1, source_target_pairs={{0,1},{1,0},{2,3},{3,2},{4,5},{5,4},{6,7},{7,6},{8,9},{9,8},{10,11... | collective-permute-start | bytes 1544 | tf_op jit(solution)/shard_map/ppermute | solution.py:80
  798.3 32.3 %collective-permute-start.57 = (bf16[320,2048]{1,0:T(8,128)(2,1)}, bf16[320,2048]{1,0:T(8,128)(2,1)}, u32[]{:S(2)}, u32[]{:S(2)}) collective-permute-start(bf16[320,2048]{1,0:T(8,128)(2,1)} %fusion.14), channel_id=1, source_target_pairs={{0,1},{1,0},{2,3},{3,2},{4,5},{5,4},{6,7},{7,6},{8,9},{9,8},{10,11... | collective-permute-start | bytes 3932168 | tf_op jit(solution)/shard_map/ppermute | solution.py:80
  (128 other events, 1998.6 us)
Sparse Core Ops, SparseCore 0:
  20.8 32.4 all-gather.7
  55.4 45.0 all-gather.9
  102.0 26.6 all-gather.11
  130.1 27.4 all-gather.13
  159.0 58.6 all-gather.15
  219.1 57.8 all-gather.17
  278.6 57.8 all-gather.19
  500.2 54.0 reduce-scatter.7
  562.0 54.1 reduce-scatter.9
  644.2 53.2 reduce-scatter.11
  699.8 43.6 reduce-scatter.13
  745.7 43.2 reduce-scatter.17
  791.3 26.4 reduce-scatter.15
  823.8 26.7 reduce-scatter.19

commit v7 on v6

--- a/solution.py
+++ b/solution.py
@@ -574,8 +574,9 @@
             prompt_own,
         )
     )
-    q_here = at.gather_upper(after(q_weight, prompt_own))
-    out_here = at.gather_upper(after(out_weight, prompt_own))
+    joint_here = at.gather_upper(
+        after(jnp.concatenate([q_weight, out_weight], axis=1), prompt_own)
+    )
     gate_here = at.gather_upper(after(gate_weight, prompt_own))
     up_here = at.gather_upper(after(up_weight, prompt_own))
     down_here = at.gather_upper(after(down_weight, prompt_own))
@@ -645,33 +646,30 @@
 
     tokens_f32 = tokens_rel.astype(f32)
     normed_keys = norm_keys(at, prompt_groups, cont_tokens, attn_gain_row, prompt_part)
-    normed_keys, kv_side, q_here = together(normed_keys, kv_side, q_here)
+    normed_keys, kv_side, joint_here = together(normed_keys, kv_side, joint_here)
     kv_far = at.swap_core(kv_side)
-    q_side, q_near = at.swap_side(q_here), at.swap_core(q_here)
+    joint_side, joint_near = at.swap_side(joint_here), at.swap_core(joint_here)
     cot_turned = at.swap_tensor(after(cot_rel, normed_keys))
     kv_near = after(kv_near, kv_side)
     kv_full = jnp.concatenate([kv_here, kv_side, kv_near, kv_far], axis=0)
     keys_values = plain_product(normed_keys, kv_full).astype(bf16)
-    keys_values, q_side, out_here, normed_late = together(
-        keys_values, q_side, out_here, normed_keys
-    )
-    q_far = at.swap_core(q_side)
-    out_side, out_near = at.swap_side(out_here), at.swap_core(out_here)
+    keys_values, joint_side, normed_late = together(keys_values, joint_side, normed_keys)
+    joint_far = at.swap_core(joint_side)
+    joint_far, gate_here = together(joint_far, gate_here)
+    gate_side, gate_near = at.swap_side(gate_here), at.swap_core(gate_here)
+    joint = (joint_here, joint_side, joint_near, joint_far)
     own_block = lax.dynamic_slice_in_dim(
         normed_late, (at.index // 4) * prompt_part, prompt_part, 0
     )
     normed = jnp.concatenate([own_block, normed_late[prompt_len:]], axis=0)
-    q_parts = [after(part, keys_values) for part in (q_here, q_side, q_near, q_far)]
-    q_full = jnp.concatenate(q_parts, axis=0)
+    q_full = jnp.concatenate([after(part, gate_here)[:, :width] for part in joint], axis=0)
+    q_full = lax.optimization_barrier(q_full)
     queries = plain_product(after(normed, keys_values), q_full).astype(bf16)
-    queries, out_side, gate_here = together(queries, out_side, gate_here)
-    out_far = at.swap_core(out_side)
-    gate_side, gate_near = at.swap_side(gate_here), at.swap_core(gate_here)
     fixed = (lam_vec, head_gain_row, prompt_spots, bounds, prompt_part)
     heads_out, attn_vec, lse = attend(queries, keys_values, *fixed, (0, heads))
     attn_vec, cot_turned = together(attn_vec, cot_turned)
-    out_near, out_far = after(out_near, attn_vec), after(out_far, attn_vec)
-    out_full = jnp.concatenate([out_here, out_side, out_near, out_far], axis=0)
+    out_full = jnp.concatenate([after(part, attn_vec)[:, width:] for part in joint], axis=0)
+    out_full = lax.optimization_barrier(out_full)
     attn_own, attn_other = at.own_half(attn_vec), at.other_half(attn_vec)
     out_send = cols_product(attn_other, out_full).astype(bf16)
     out_sent = at.swap_tensor(out_send)
@@ -750,18 +748,18 @@
     vec_two = plain_product(branch, out_full)
     vec_grad = at.in_order(vec_two[:local_rows], vec_two[local_rows:])
     vec_grad, gate_grad_aside = together(vec_grad, gate_grad_aside)
-    gate_far_keep = after(gate_far_keep, gate_grad_aside)
+    up_far_aside = after(up_far_aside, gate_grad_aside)
+    up_grad_side = at.aside_part(ffn_in, up_grad, up_far_aside)
+    up_grad_aside = at.swap_side(up_grad_side)
+    gate_far_keep = after(gate_far_keep, up_grad_side)
     gate_last = at.near_part(ffn_in, gate_grad, gate_far_keep, gate_grad_aside)
     grad_gate = at.scatter_upper(gate_last)
-    up_far_aside = after(up_far_aside, gate_last)
-    up_grad_side = at.aside_part(ffn_in, up_grad, up_far_aside)
-    up_grad_aside = at.swap_side(up_grad_side)
     queries_grad, kv_grad, head_sums = attend_back(
         queries,
         keys_values,
         lam_vec,
         head_gain_row,
-        after(vec_grad, up_grad_side),
+        after(vec_grad, gate_last),
         heads_out,
         lse,
         prompt_spots,

time: 871 us -> 862 us (0.990)
  local copies, waits for them, and re-layouts: 114 us -> 103 us
    unnamed x225, local copies, waits for them, and re-layouts: 51.4 us -> 39.1 us
    slice x0 -> x8, local copies, waits for them, and re-layouts: none -> 10.4 us  [the longest x4 5.25 us: per_device(): after(part, gate_here)[:, :width]]
    all_gather x7 -> x6, waiting for transfers between devices: 46.8 us -> 47.5 us  [gather_upper(): lax.all_gather(shard, 'dp', axis=0, tiled=True, axis_index_groups=self.up...]
    ppermute x14 -> x13, waiting for transfers between devices: 115 us -> 116 us  [swap_side(): return lax.ppermute(value, 'dp', self.side_pairs)]
    ppermute x14 -> x13, starting transfers between devices: 17.4 us -> 17.5 us  [swap_side(): return lax.ppermute(value, 'dp', self.side_pairs)]
  transfers between devices with their start and end apart: 78 -> 74, of which waited for: 26 -> 27; matrix products, arithmetic and copies ran while one was open for 52% -> 51% of each run, Pallas kernels for 10% -> 10%
where the time goes in v7:
time: 862 us; the launch traced here: 853 us
  matrix products  264 us (31%)
  waiting for transfers between devices  250 us (29%)
  local copies, waits for them, and re-layouts  103 us (12%)
  other arithmetic  84.9 us (10%)
  Pallas kernels  84.4 us (10%)
  starting transfers between devices  51.5 us (6%)
  between operations  15.7 us (2%)
    ppermute x13, waiting for transfers between devices, swap_side(): return lax.ppermute(value, 'dp', self.side_pairs)  116 us
    dot_general x24, matrix products, rows_product(): lax.dot_general(first_arg, second_arg, (((0,), (0,)), ((), ())), preferre...  105 us
    ppermute x13, waiting for transfers between devices, swap_tensor(): return lax.ppermute(value, 'tensor', [(0, 1), (1, 0)])  84.9 us
    dot_general x14, matrix products, cols_product(): lax.dot_general(first_arg, second_arg, (((1,), (1,)), ((), ())), preferre...  83.3 us
    dot_general x6, matrix products, plain_product(): return jnp.dot(first_arg, second_arg, preferred_element_type=f32)  74.9 us
    all_gather x6, waiting for transfers between devices, gather_upper(): lax.all_gather(shard, 'dp', axis=0, tiled=True, axis_index_groups=self.up...  47.5 us
    pallas_call x1, Pallas kernels, attend_back(): pl.pallas_call(lambda *refs: backward_kernel(prompt_len, top_rows, first,...  40.1 us
    unnamed x225, local copies, waits for them, and re-layouts  39.1 us
  transfers between devices with their start and end apart: 74, of which 27 were waited for; matrix products, arithmetic and copies ran while one was open for 51% of the time, Pallas kernels for 10%

profile of v7, /device:TPU:0, one launch (start us, length us, event | category | flops | bytes accessed | tf_op | source)
XLA Modules:
  0.0 853.3 jit_solution(1712883569221471765)
XLA Ops:
  8.2 4.9 collective-permute-start
  27.6 4.4 reshape.271
  43.8 11.0 %collective-permute-done.1 = bf16[320,2048]{1,0:T(8,128)(2,1)} collective-permute-done((bf16[320,2048]{1,0:T(8,128)(2,1)S(1)}, bf16[320,2048]{1,0:T(8,128)(2,1)}, u32[]{:S(2)}, u32[]{:S(2)}) %collective-permute-start.1) | collective-permute-done | bytes 1310752 | tf_op jit(solution)/shard_map/ppermute | solution.py:80
  62.2 19.3 %collective-permute-done.3.refs_4_ = bf16[576,1024]{1,0:T(8,128)(2,1)} collective-permute-done((bf16[576,1024]{1,0:T(8,128)(2,1)}, bf16[576,1024]{1,0:T(8,128)(2,1)}, u32[]{:S(2)}, u32[]{:S(2)}) %collective-permute-start.3) | collective-permute-done | bytes 1179680 | tf_op jit(solution)/shard_map/ppermute | solution.py:77
  84.0 16.5 %all-gather.9.cloned.1.call-done = bf16[512,2048]{1,0:T(8,128)(2,1)} async-done(((bf16[128,2048]{1,0:T(8,128)(2,1)}), bf16[512,2048]{1,0:T(8,128)(2,1)}) %all-gather.9.cloned.1.call-update) | async-done | bytes 2097168 | tf_op jit(solution)/shard_map/all_gather | solution.py:83
  102.4 5.6 collective-permute-done.6.refs_5_
  112.7 12.8 %norm_keys.1 = bf16[2560,2048]{1,0:T(8,128)(2,1)} custom-call(s32[16]{0:T(128)} %get-tuple-element.294.refs_0_, s32[1]{0:T(128)} %bitcast.10.refs_1_, bf16[576,1024]{1,0:T(8,128)(2,1)} %all-gather.7.cloned.1.call-done.refs_2_, bf16[576,1024]{1,0:T(8,128)(2,1)} %collective-permute-done.2.refs_3_, bf16[576,1024]{1,0:T(8,128)(2,1)} %collective-permute-done.3.refs_4_, ...), custom_call_target="tpu_custom_call" | custom-call | tf_op jit(solution)/shard_map/norm_keys/pallas_call | solution.py:497
  125.6 21.7 %all-gather.11.cloned.1.call-done = bf16[512,2048]{1,0:T(8,128)(2,1)} async-done(((bf16[128,2048]{1,0:T(8,128)(2,1)}), bf16[512,2048]{1,0:T(8,128)(2,1)}) %all-gather.11.cloned.1.call-update) | async-done | bytes 2097168 | tf_op jit(solution)/shard_map/all_gather | solution.py:83
  156.6 24.4 %convolution_convert_fusion.refs_2_ = bf16[2560,2048]{1,0:T(8,128)(2,1)} fusion(bf16[2560,2048]{1,0:T(8,128)(2,1)S(1)} %copy-done.28, bf16[2048,2048]{1,0:T(8,128)(2,1)S(1)} %constant_dynamic-update-slice_fusion), kind=kOutput, calls=%fused_computation.1 | convolution fusion | flops 21480079360 | bytes 29360128 | tf_op jit(solution)/shard_map/dot_general | solution.py:33
  180.9 16.0 %collective-permute-done.12 = bf16[512,2048]{1,0:T(8,128)(2,1)} collective-permute-done((bf16[512,2048]{1,0:T(8,128)(2,1)}, bf16[512,2048]{1,0:T(8,128)(2,1)}, u32[]{:S(2)}, u32[]{:S(2)}) %collective-permute-start.12) | collective-permute-done | bytes 2097184 | tf_op jit(solution)/shard_map/ppermute | solution.py:77
  219.7 31.4 %attend.1 = (f32[640,1024]{1,0:T(8,128)}, bf16[640,1024]{1,0:T(8,128)(2,1)}, f32[4,16,640]{2,1,0:T(8,128)}) custom-call(f32[4]{0:T(128)} %subtract_add_fusion.1.refs_0_, bf16[640,1024]{1,0:T(8,128)(2,1)} %convolution_convert_fusion.11.refs_1_, bf16[2560,2048]{1,0:T(8,128)(2,1)} %convolution_convert_fusion.refs_2_, f32[1,1024]{1,0:T(1,128)} %bitcast.127, ...), custom_call_target="tpu_custom_call" | custom-call | tf_op jit(solution)/shard_map/attend/pallas_call | solution.py:341
  266.0 5.2 collective-permute-done.16
  278.7 23.6 %collective-permute-done.17 = bf16[320,2048]{1,0:T(8,128)(2,1)S(1)} collective-permute-done((bf16[320,2048]{1,0:T(8,128)(2,1)S(1)}, bf16[320,2048]{1,0:T(8,128)(2,1)S(1)}, u32[]{:S(2)}, u32[]{:S(2)}) %collective-permute-start.17) | collective-permute-done | bytes 1310752 | tf_op jit(solution)/shard_map/ppermute | solution.py:80
  306.4 13.4 %pad_maximum_fusion = bf16[2048,2816]{1,0:T(8,128)(2,1)} fusion(bf16[512,2816]{1,0:T(8,128)(2,1)S(1)} %collective-permute-done.20, bf16[512,2816]{1,0:T(8,128)(2,1)} %collective-permute-done.19, bf16[512,2816]{1,0:T(8,128)(2,1)} %collective-permute-done.16, bf16[512,2816]{1,0:T(8,128)(2,1)} %all-gather.13.cloned.1.call-done), kind=kLoop, calls=%fused_computation | loop fusion | flops 46137344 | bytes 23068672 | tf_op jit(solution)/shard_map/concatenate | solution.py:688
  319.8 5.5 all-gather.17.cloned.1.call-done
  325.3 12.3 %collective-permute-done.21 = bf16[512,2816]{1,0:T(8,128)(2,1)} collective-permute-done((bf16[512,2816]{1,0:T(8,128)(2,1)}, bf16[512,2816]{1,0:T(8,128)(2,1)}, u32[]{:S(2)}, u32[]{:S(2)}) %collective-permute-start.21) | collective-permute-done | bytes 2883616 | tf_op jit(solution)/shard_map/ppermute | solution.py:77
  343.1 13.0 %fusion.136 = f32[640,2816]{1,0:T(8,128)} fusion(bf16[2048,2816]{1,0:T(8,128)(2,1)} %pad_maximum_fusion, bf16[320,2048]{1,0:T(8,128)(2,1)S(1)} %collective-permute-done.18, bf16[320,2048]{1,0:T(8,128)(2,1)S(1)} %multiply_convert_fusion.3), kind=kOutput, calls=%fused_computation.269 | convolution fusion | flops 7387217920 | bytes 21364736 | tf_op jit(solution)/shard_map/dot_general | solution.py:33
  365.9 15.2 %multiply_convert_fusion.2 = (bf16[640,2816]{1,0:T(8,128)(2,1)S(1)}, f32[640,2816]{1,0:T(8,128)}) fusion(f32[640,2816]{1,0:T(8,128)} %fusion.136, bf16[640,2048]{1,0:T(8,128)(2,1)S(1)} %pad_maximum_fusion.4, bf16[2048,2816]{1,0:T(8,128)(2,1)} %constant_dynamic-update-slice_fusion.4), kind=kOutput, calls=%fused_computation.4 | convolution fusion | flops 7392788480 | bytes 32178176 | tf_op jit(solution)/shard_map/dot_general | solution.py:33
  383.8 4.1 convolution_convert_fusion.5
  387.9 18.3 %collective-permute-done.24 = bf16[512,2816]{1,0:T(8,128)(2,1)} collective-permute-done((bf16[512,2816]{1,0:T(8,128)(2,1)S(1)}, bf16[512,2816]{1,0:T(8,128)(2,1)}, u32[]{:S(2)}, u32[]{:S(2)}) %collective-permute-start.24) | collective-permute-done | bytes 2883616 | tf_op jit(solution)/shard_map/ppermute | solution.py:77
  408.9 5.0 fusion.77
  421.6 4.2 copy-done.70
  425.9 15.3 %multiply_convert_fusion = (bf16[640,2816]{1,0:T(8,128)(2,1)S(1)}, bf16[640,2816]{1,0:T(8,128)(2,1)S(1)}) fusion(f32[640,2816]{1,0:T(8,128)} %fusion.136, f32[640,2816]{1,0:T(8,128)} %get-tuple-element.328, bf16[640,2048]{1,0:T(8,128)(2,1)S(1)} %copy-done.39, bf16[2048,2816]{1,0:T(8,128)(2,1)} %copy-done.70), kind=kOutput, calls=%fused_computation.2 | convolution fusion | flops 7405404160 | bytes 35782656 | tf_op jit(solution)/shard_map/dot_general | solution.py:33
  445.2 5.9 fusion
  454.5 4.4 fusion.40
  472.5 8.9 %fusion.147 = f32[320,2048]{1,0:T(8,128)} fusion(bf16[320,2816]{1,0:T(8,128)(2,1)S(1)} %copy-done.56, bf16[2048,2816]{1,0:T(8,128)(2,1)} %pad_maximum_fusion), kind=kOutput, calls=%fused_computation.279 | convolution fusion | flops 3690987520 | bytes 15958016 | tf_op jit(solution)/shard_map/dot_general | solution.py:43
  483.6 5.4 add_convert_fusion.3
  489.1 10.1 %convolution_add_fusion.2 = f32[320,2048]{1,0:T(8,128)S(1)} fusion(f32[320,2048]{1,0:T(8,128)} %fusion.147, bf16[320,2816]{1,0:T(8,128)(2,1)} %get-tuple-element.217, bf16[2048,2816]{1,0:T(8,128)(2,1)} %constant_dynamic-update-slice_fusion.4), kind=kOutput, calls=%fused_computation.73 | convolution fusion | flops 3691642880 | bytes 18579456 | tf_op jit(solution)/shard_map/dot_general | solution.py:43
  503.7 5.0 fusion.137
  512.3 4.1 convolution_convert_fusion.1
  516.4 20.6 %collective-permute-done.34 = bf16[320,2048]{1,0:T(8,128)(2,1)S(1)} collective-permute-done((bf16[320,2048]{1,0:T(8,128)(2,1)S(1)}, bf16[320,2048]{1,0:T(8,128)(2,1)S(1)}, u32[]{:S(2)}, u32[]{:S(2)}) %collective-permute-start.34) | collective-permute-done | bytes 1310752 | tf_op jit(solution)/shard_map/ppermute | solution.py:80
  548.7 6.3 add_convert_fusion.1
  557.1 40.1 %attend_back.1 = (bf16[1024,640]{1,0:T(8,128)(2,1)}, bf16[2560,2048]{1,0:T(8,128)(2,1)}, f32[4,8,256]{2,1,0:T(8,128)}) custom-call(f32[4]{0:T(128)} %subtract_add_fusion.1.refs_0_, bf16[640,1024]{1,0:T(8,128)(2,1)} %convolution_convert_fusion.11.refs_1_, bf16[2560,2048]{1,0:T(8,128)(2,1)} %convolution_convert_fusion.refs_2_, f32[1,1024]{1,0:T(1,128)} %bitcast.128, ...), custom_call_target="tpu_custom_call" | custom-call | tf_op jit(solution)/shard_map/attend_back/pallas_call | solution.py:389
  597.3 6.3 fusion.139
  604.7 8.6 %convolution_convert_fusion.8 = bf16[512,2048]{1,0:T(8,128)(2,1)} fusion(bf16[2560,2048]{1,0:T(8,128)(2,1)S(1)} %copy-done.32, bf16[2560,2048]{1,0:T(8,128)(2,1)} %norm_keys.1), kind=kOutput, calls=%fused_computation.66 | convolution fusion | flops 5369757696 | bytes 15204352 | tf_op jit(solution)/shard_map/dot_general | solution.py:37
  613.4 7.4 collective-permute-done.42
  624.4 7.1 add_convert_fusion
  631.7 10.5 %convolution_convert_fusion.7 = bf16[512,2048]{1,0:T(8,128)(2,1)} fusion(bf16[2560,2048]{1,0:T(8,128)(2,1)} %get-tuple-element.245, bf16[2560,2048]{1,0:T(8,128)(2,1)} %norm_keys.1), kind=kOutput, calls=%fused_computation.65 | convolution fusion | flops 5369757696 | bytes 15204352 | tf_op jit(solution)/shard_map/dot_general | solution.py:37
  642.2 10.6 %add_convert_fusion.8 = bf16[512,2048]{1,0:T(8,128)(2,1)} fusion(bf16[512,2048]{1,0:T(8,128)(2,1)} %collective-permute-done.39, bf16[2560,2048]{1,0:T(8,128)(2,1)} %get-tuple-element.245, bf16[2560,2048]{1,0:T(8,128)(2,1)} %norm_keys.1), kind=kOutput, calls=%fused_computation.43 | convolution fusion | flops 5371854848 | bytes 17301504 | tf_op jit(solution)/shard_map/dot_general | solution.py:37
  661.4 8.7 %fusion.29 = f32[320,2048]{1,0:T(8,128)} fusion(bf16[2048,2816]{1,0:T(8,128)(2,1)} %copy-done.70, bf16[640,2816]{1,0:T(8,128)(2,1)S(1)} %copy-done.6), kind=kOutput, calls=%fused_computation.117 | convolution fusion | flops 3690987520 | bytes 15958016 | tf_op jit(solution)/shard_map/dot_general | solution.py:43
  670.4 5.6 add_convert_fusion.7
  678.4 9.2 %fusion.22 = f32[512,2048]{1,0:T(8,128)S(1)} fusion(bf16[2560,2048]{1,0:T(8,128)(2,1)} %get-tuple-element.245, bf16[2560,2048]{1,0:T(8,128)(2,1)} %norm_keys.1), kind=kOutput, calls=%fused_computation.86 | convolution fusion | flops 5368709120 | bytes 17301504 | tf_op jit(solution)/shard_map/dot_general | solution.py:37
  691.7 9.6 %convolution_convert_fusion.10 = bf16[320,2048]{1,0:T(8,128)(2,1)} fusion(bf16[2048,2816]{1,0:T(8,128)(2,1)} %copy-done.70, bf16[640,2816]{1,0:T(8,128)(2,1)S(1)} %copy-done.7), kind=kOutput, calls=%fused_computation.76 | convolution fusion | flops 3691642880 | bytes 14647296 | tf_op jit(solution)/shard_map/dot_general | solution.py:43
  701.4 23.3 %collective-permute-done.49 = bf16[512,2048]{1,0:T(8,128)(2,1)S(1)} collective-permute-done((bf16[512,2048]{1,0:T(8,128)(2,1)}, bf16[512,2048]{1,0:T(8,128)(2,1)S(1)}, u32[]{:S(2)}, u32[]{:S(2)}) %collective-permute-start.49) | collective-permute-done | bytes 2097184 | tf_op jit(solution)/shard_map/ppermute | solution.py:77
  751.0 20.6 %collective-permute-done.47 = bf16[320,2048]{1,0:T(8,128)(2,1)} collective-permute-done((bf16[320,2048]{1,0:T(8,128)(2,1)S(1)}, bf16[320,2048]{1,0:T(8,128)(2,1)}, u32[]{:S(2)}, u32[]{:S(2)}) %collective-permute-start.47) | collective-permute-done | bytes 1310752 | tf_op jit(solution)/shard_map/ppermute | solution.py:80
  775.0 8.7 %fusion.14 = bf16[320,2048]{1,0:T(8,128)(2,1)} fusion(f32[320,2048]{1,0:T(8,128)} %fusion.50, bf16[2048,2048]{1,0:T(8,128)(2,1)} %copy-done.74, s32[]{:T(128)S(6)} %select_n.174, bf16[512,2048]{1,0:T(8,128)(2,1)} %get-tuple-element.297, bf16[128,2048]{1,0:T(8,128)(2,1)} %reduce-scatter.14.cloned.1.call-done), kind=kOutput, calls=%fused_computation.74 | convolution fusion | flops 2688286720 | bytes 14942212 | tf_op jit(solution)/shard_map/dot_general | solution.py:43
  785.3 8.5 collective-permute-done.53
  818.9 8.1 fusion.16
  (524 shorter events, 270.9 us)
Async XLA Ops:
  7.2 47.6 %all-gather.7.cloned.1.call-start = ((), (), s32[]{:S(2)}) async-start(), calls=%async_computation.7 | async-start | bytes 1474560 | tf_op jit(solution)/shard_map/all_gather | solution.py:83
  20.7 79.7 %all-gather.9.cloned.1.call-start = ((), (), s32[]{:S(2)}) async-start(), calls=%async_computation.8 | async-start | bytes 2621440 | tf_op jit(solution)/shard_map/all_gather | solution.py:83
  23.4 123.9 %all-gather.11.cloned.1.call-start = ((), (), s32[]{:S(2)}) async-start(), calls=%async_computation.9 | async-start | bytes 2621440 | tf_op jit(solution)/shard_map/all_gather | solution.py:83
  24.3 182.3 %all-gather.13.cloned.1.call-start = ((), (), s32[]{:S(2)}) async-start(), calls=%async_computation.10 | async-start | bytes 3604480 | tf_op jit(solution)/shard_map/all_gather | solution.py:83
  24.3 30.4 %collective-permute-start.1 = (bf16[320,2048]{1,0:T(8,128)(2,1)S(1)}, bf16[320,2048]{1,0:T(8,128)(2,1)}, u32[]{:S(2)}, u32[]{:S(2)}) collective-permute-start(bf16[320,2048]{1,0:T(8,128)(2,1)S(1)} %copy-done.37), channel_id=1, source_target_pairs={{0,1},{1,0},{2,3},{3,2},{4,5},{5,4},{6,7},{7,6},{8,9},{9,8},{10,11... | collective-permute-start | bytes 3932168 | tf_op jit(solution)/shard_map/ppermute | solution.py:80
  54.8 26.7 %collective-permute-start.3 = (bf16[576,1024]{1,0:T(8,128)(2,1)}, bf16[576,1024]{1,0:T(8,128)(2,1)}, u32[]{:S(2)}, u32[]{:S(2)}) collective-permute-start(bf16[576,1024]{1,0:T(8,128)(2,1)} %all-gather.7.cloned.1.call-done.refs_2_), channel_id=1, source_target_pairs={{0,4},{2,6},{4,0},{6,2},{8,12},{10,14},{12,8},{14,10},{16,20},{18,... | collective-permute-start | bytes 3538952 | tf_op jit(solution)/shard_map/ppermute | solution.py:77
  57.9 208.1 %all-gather.15.cloned.1.call-start = ((), (), s32[]{:S(2)}) async-start(), calls=%async_computation.11 | async-start | bytes 3604480 | tf_op jit(solution)/shard_map/all_gather | solution.py:83
  100.4 47.7 %collective-permute-start.9 = (bf16[512,2048]{1,0:T(8,128)(2,1)}, bf16[512,2048]{1,0:T(8,128)(2,1)}, u32[]{:S(2)}, u32[]{:S(2)}) collective-permute-start(bf16[512,2048]{1,0:T(8,128)(2,1)} %all-gather.9.cloned.1.call-done), channel_id=1, source_target_pairs={{0,4},{2,6},{4,0},{6,2},{8,12},{10,14},{12,8},{14,10},{16,20},{18,... | collective-permute-start | bytes 6291464 | tf_op jit(solution)/shard_map/ppermute | solution.py:77
  108.0 40.5 %collective-permute-start.10 = (bf16[512,2048]{1,0:T(8,128)(2,1)}, bf16[512,2048]{1,0:T(8,128)(2,1)}, u32[]{:S(2)}, u32[]{:S(2)}) collective-permute-start(bf16[512,2048]{1,0:T(8,128)(2,1)} %all-gather.9.cloned.1.call-done), channel_id=1, source_target_pairs={{0,2},{2,0},{4,6},{6,4},{8,10},{10,8},{12,14},{14,12},{16,18},{18,... | collective-permute-start | bytes 6291464 | tf_op jit(solution)/shard_map/ppermute | solution.py:74
  148.1 177.1 %all-gather.17.cloned.1.call-start = ((), (), s32[]{:S(2)}) async-start(), calls=%async_computation.12 | async-start | bytes 3604480 | tf_op jit(solution)/shard_map/all_gather | solution.py:83
  148.5 48.4 %collective-permute-start.12 = (bf16[512,2048]{1,0:T(8,128)(2,1)}, bf16[512,2048]{1,0:T(8,128)(2,1)}, u32[]{:S(2)}, u32[]{:S(2)}) collective-permute-start(bf16[512,2048]{1,0:T(8,128)(2,1)} %all-gather.11.cloned.1.call-done), channel_id=1, source_target_pairs={{0,4},{2,6},{4,0},{6,2},{8,12},{10,14},{12,8},{14,10},{16,20},{18,... | collective-permute-start | bytes 6291464 | tf_op jit(solution)/shard_map/ppermute | solution.py:77
  198.6 398.6 %reduce-scatter.8.cloned.1.call-start = ((), (), s32[]{:S(2)}) async-start(), calls=%async_computation.13 | async-start | bytes 3604480 | tf_op jit(solution)/shard_map/reduce_scatter | solution.py:103
  200.6 50.5 %collective-permute-start.15 = (bf16[320,2048]{1,0:T(8,128)(2,1)}, bf16[320,2048]{1,0:T(8,128)(2,1)}, u32[]{:S(2)}, u32[]{:S(2)}) collective-permute-start(bf16[320,2048]{1,0:T(8,128)(2,1)} %reshape.272), channel_id=1, source_target_pairs={{0,1},{1,0},{2,3},{3,2},{4,5},{5,4},{6,7},{7,6},{8,9},{9,8},{10,11... | collective-permute-start | bytes 3932168 | tf_op jit(solution)/shard_map/ppermute | solution.py:80
  206.6 64.5 %collective-permute-start.16 = (bf16[512,2816]{1,0:T(8,128)(2,1)}, bf16[512,2816]{1,0:T(8,128)(2,1)}, u32[]{:S(2)}, u32[]{:S(2)}) collective-permute-start(bf16[512,2816]{1,0:T(8,128)(2,1)} %all-gather.13.cloned.1.call-done), channel_id=1, source_target_pairs={{0,4},{2,6},{4,0},{6,2},{8,12},{10,14},{12,8},{14,10},{16,20},{18,... | collective-permute-start | bytes 8650760 | tf_op jit(solution)/shard_map/ppermute | solution.py:77
  208.3 98.1 %collective-permute-start.19 = (bf16[512,2816]{1,0:T(8,128)(2,1)}, bf16[512,2816]{1,0:T(8,128)(2,1)}, u32[]{:S(2)}, u32[]{:S(2)}) collective-permute-start(bf16[512,2816]{1,0:T(8,128)(2,1)} %all-gather.13.cloned.1.call-done), channel_id=1, source_target_pairs={{0,2},{2,0},{4,6},{6,4},{8,10},{10,8},{12,14},{14,12},{16,18},{18,... | collective-permute-start | bytes 8650760 | tf_op jit(solution)/shard_map/ppermute | solution.py:74
  271.1 35.2 %collective-permute-start.20 = (bf16[512,2816]{1,0:T(8,128)(2,1)}, bf16[512,2816]{1,0:T(8,128)(2,1)S(1)}, u32[]{:S(2)}, u32[]{:S(2)}) collective-permute-start(bf16[512,2816]{1,0:T(8,128)(2,1)} %collective-permute-done.16), channel_id=1, source_target_pairs={{0,2},{2,0},{4,6},{6,4},{8,10},{10,8},{12,14},{14,12},{16,18},{18,... | collective-permute-start | bytes 8650760 | tf_op jit(solution)/shard_map/ppermute | solution.py:74
  271.1 31.2 %collective-permute-start.17 = (bf16[320,2048]{1,0:T(8,128)(2,1)S(1)}, bf16[320,2048]{1,0:T(8,128)(2,1)S(1)}, u32[]{:S(2)}, u32[]{:S(2)}) collective-permute-start(bf16[320,2048]{1,0:T(8,128)(2,1)S(1)} %convolution_convert_fusion.9), channel_id=1, source_target_pairs={{0,1},{1,0},{2,3},{3,2},{4,5},{5,4},{6,7},{7,6},{8,9},{9,8},{10,11... | collective-permute-start | bytes 3932168 | tf_op jit(solution)/shard_map/ppermute | solution.py:80
  272.6 64.9 %collective-permute-start.21 = (bf16[512,2816]{1,0:T(8,128)(2,1)}, bf16[512,2816]{1,0:T(8,128)(2,1)}, u32[]{:S(2)}, u32[]{:S(2)}) collective-permute-start(bf16[512,2816]{1,0:T(8,128)(2,1)} %all-gather.15.cloned.1.call-done), channel_id=1, source_target_pairs={{0,4},{2,6},{4,0},{6,2},{8,12},{10,14},{12,8},{14,10},{16,20},{18,... | collective-permute-start | bytes 8650760 | tf_op jit(solution)/shard_map/ppermute | solution.py:77
  277.1 79.0 %collective-permute-start.22 = (bf16[512,2816]{1,0:T(8,128)(2,1)}, bf16[512,2816]{1,0:T(8,128)(2,1)}, u32[]{:S(2)}, u32[]{:S(2)}) collective-permute-start(bf16[512,2816]{1,0:T(8,128)(2,1)} %all-gather.15.cloned.1.call-done), channel_id=1, source_target_pairs={{0,2},{2,0},{4,6},{6,4},{8,10},{10,8},{12,14},{14,12},{16,18},{18,... | collective-permute-start | bytes 8650760 | tf_op jit(solution)/shard_map/ppermute | solution.py:74
  304.8 38.3 %collective-permute-start.18 = (bf16[320,2048]{1,0:T(8,128)(2,1)S(1)}, bf16[320,2048]{1,0:T(8,128)(2,1)S(1)}, u32[]{:S(2)}, u32[]{:S(2)}) collective-permute-start(bf16[320,2048]{1,0:T(8,128)(2,1)S(1)} %multiply_convert_fusion.3), channel_id=1, source_target_pairs={{0,1},{1,0},{2,3},{3,2},{4,5},{5,4},{6,7},{7,6},{8,9},{9,8},{10,11... | collective-permute-start | bytes 3932168 | tf_op jit(solution)/shard_map/ppermute | solution.py:80
  341.1 65.8 %collective-permute-start.25 = (bf16[512,2816]{1,0:T(8,128)(2,1)S(1)}, bf16[512,2816]{1,0:T(8,128)(2,1)}, u32[]{:S(2)}, u32[]{:S(2)}) collective-permute-start(bf16[512,2816]{1,0:T(8,128)(2,1)S(1)} %copy-done.46), channel_id=1, source_target_pairs={{0,2},{2,0},{4,6},{6,4},{8,10},{10,8},{12,14},{14,12},{16,18},{18,... | collective-permute-start | bytes 8650760 | tf_op jit(solution)/shard_map/ppermute | solution.py:74
  341.6 64.5 %collective-permute-start.24 = (bf16[512,2816]{1,0:T(8,128)(2,1)S(1)}, bf16[512,2816]{1,0:T(8,128)(2,1)}, u32[]{:S(2)}, u32[]{:S(2)}) collective-permute-start(bf16[512,2816]{1,0:T(8,128)(2,1)S(1)} %copy-done.46), channel_id=1, source_target_pairs={{0,4},{2,6},{4,0},{6,2},{8,12},{10,14},{12,8},{14,10},{16,20},{18,... | collective-permute-start | bytes 8650760 | tf_op jit(solution)/shard_map/ppermute | solution.py:77
  383.7 30.2 %collective-permute-start.26 = (bf16[512,2816]{1,0:T(8,128)(2,1)S(1)}, bf16[512,2816]{1,0:T(8,128)(2,1)S(1)}, u32[]{:S(2)}, u32[]{:S(2)}) collective-permute-start(bf16[512,2816]{1,0:T(8,128)(2,1)S(1)} %convolution_convert_fusion.6), channel_id=1, source_target_pairs={{0,2},{2,0},{4,6},{6,4},{8,10},{10,8},{12,14},{14,12},{16,18},{18,... | collective-permute-start | bytes 8650760 | tf_op jit(solution)/shard_map/ppermute | solution.py:74
  406.3 77.3 %collective-permute-start.31 = (bf16[512,2816]{1,0:T(8,128)(2,1)}, bf16[512,2816]{1,0:T(8,128)(2,1)}, u32[]{:S(2)}, u32[]{:S(2)}) collective-permute-start(bf16[512,2816]{1,0:T(8,128)(2,1)} %convolution_convert_fusion.5), channel_id=1, source_target_pairs={{0,2},{2,0},{4,6},{6,4},{8,10},{10,8},{12,14},{14,12},{16,18},{18,... | collective-permute-start | bytes 8650760 | tf_op jit(solution)/shard_map/ppermute | solution.py:74
  418.0 65.7 %collective-permute-start.30 = (bf16[512,2816]{1,0:T(8,128)(2,1)}, bf16[512,2816]{1,0:T(8,128)(2,1)}, u32[]{:S(2)}, u32[]{:S(2)}) collective-permute-start(bf16[512,2816]{1,0:T(8,128)(2,1)} %add_convert_fusion.5), channel_id=1, source_target_pairs={{0,4},{2,6},{4,0},{6,2},{8,12},{10,14},{12,8},{14,10},{16,20},{18,... | collective-permute-start | bytes 8650760 | tf_op jit(solution)/shard_map/ppermute | solution.py:77
  458.9 42.9 %collective-permute-start.32 = (bf16[320,1024]{1,0:T(8,128)(2,1)}, bf16[320,1024]{1,0:T(8,128)(2,1)S(1)}, u32[]{:S(2)}, u32[]{:S(2)}) collective-permute-start(bf16[320,1024]{1,0:T(8,128)(2,1)} %fusion.40), channel_id=1, source_target_pairs={{0,1},{1,0},{2,3},{3,2},{4,5},{5,4},{6,7},{7,6},{8,9},{9,8},{10,11... | collective-permute-start | bytes 1966088 | tf_op jit(solution)/shard_map/ppermute | solution.py:80
  466.2 35.6 %collective-permute-start.33 = (bf16[320,1024]{1,0:T(8,128)(2,1)}, bf16[320,1024]{1,0:T(8,128)(2,1)}, u32[]{:S(2)}, u32[]{:S(2)}) collective-permute-start(bf16[320,1024]{1,0:T(8,128)(2,1)} %fusion.37), channel_id=1, source_target_pairs={{0,1},{1,0},{2,3},{3,2},{4,5},{5,4},{6,7},{7,6},{8,9},{9,8},{10,11... | collective-permute-start | bytes 1966088 | tf_op jit(solution)/shard_map/ppermute | solution.py:80
  471.9 72.6 %collective-permute-start.35 = (bf16[512,2816]{1,0:T(8,128)(2,1)}, bf16[512,2816]{1,0:T(8,128)(2,1)}, u32[]{:S(2)}, u32[]{:S(2)}) collective-permute-start(bf16[512,2816]{1,0:T(8,128)(2,1)} %add_convert_fusion.4), channel_id=1, source_target_pairs={{0,4},{2,6},{4,0},{6,2},{8,12},{10,14},{12,8},{14,10},{16,20},{18,... | collective-permute-start | bytes 8650760 | tf_op jit(solution)/shard_map/ppermute | solution.py:77
  489.0 142.4 %reduce-scatter.10.cloned.1.call-start = ((), (), s32[]{:S(2)}) async-start(), calls=%async_computation.14 | async-start | bytes 3604480 | tf_op jit(solution)/shard_map/reduce_scatter | solution.py:103
  508.7 28.3 %collective-permute-start.34 = (bf16[320,2048]{1,0:T(8,128)(2,1)S(1)}, bf16[320,2048]{1,0:T(8,128)(2,1)S(1)}, u32[]{:S(2)}, u32[]{:S(2)}) collective-permute-start(bf16[320,2048]{1,0:T(8,128)(2,1)S(1)} %get-tuple-element.289), channel_id=1, source_target_pairs={{0,1},{1,0},{2,3},{3,2},{4,5},{5,4},{6,7},{7,6},{8,9},{9,8},{10,11... | collective-permute-start | bytes 3932168 | tf_op jit(solution)/shard_map/ppermute | solution.py:80
  509.0 39.7 %collective-permute-start.36 = (bf16[512,2816]{1,0:T(8,128)(2,1)S(1)}, bf16[512,2816]{1,0:T(8,128)(2,1)S(1)}, u32[]{:S(2)}, u32[]{:S(2)}) collective-permute-start(bf16[512,2816]{1,0:T(8,128)(2,1)S(1)} %convolution_convert_fusion.3), channel_id=1, source_target_pairs={{0,2},{2,0},{4,6},{6,4},{8,10},{10,8},{12,14},{14,12},{16,18},{18,... | collective-permute-start | bytes 8650760 | tf_op jit(solution)/shard_map/ppermute | solution.py:74
  511.7 32.8 %collective-permute-start.37 = (bf16[256,2816]{1,0:T(8,128)(2,1)S(1)}, bf16[256,2816]{1,0:T(8,128)(2,1)S(1)}, u32[]{:S(2)}, u32[]{:S(2)}) collective-permute-start(bf16[256,2816]{1,0:T(8,128)(2,1)S(1)} %get-tuple-element.304), channel_id=1, source_target_pairs={{0,2},{2,0},{4,6},{6,4},{8,10},{10,8},{12,14},{14,12},{16,18},{18,... | collective-permute-start | bytes 4325384 | tf_op jit(solution)/shard_map/ppermute | solution.py:74
  512.2 32.2 %collective-permute-start.38 = (bf16[256,2816]{1,0:T(8,128)(2,1)S(1)}, bf16[256,2816]{1,0:T(8,128)(2,1)S(1)}, u32[]{:S(2)}, u32[]{:S(2)}) collective-permute-start(bf16[256,2816]{1,0:T(8,128)(2,1)S(1)} %get-tuple-element.305), channel_id=1, source_target_pairs={{0,2},{2,0},{4,6},{6,4},{8,10},{10,8},{12,14},{14,12},{16,18},{18,... | collective-permute-start | bytes 4325384 | tf_op jit(solution)/shard_map/ppermute | solution.py:74
  555.1 216.5 %reduce-scatter.12.cloned.1.call-start = ((), (), s32[]{:S(2)}) async-start(), calls=%async_computation.15 | async-start | bytes 3604480 | tf_op jit(solution)/shard_map/reduce_scatter | solution.py:103
  555.5 57.9 %collective-permute-start.41 = (bf16[512,2816]{1,0:T(8,128)(2,1)}, bf16[512,2816]{1,0:T(8,128)(2,1)}, u32[]{:S(2)}, u32[]{:S(2)}) collective-permute-start(bf16[512,2816]{1,0:T(8,128)(2,1)} %convolution_convert_fusion.1), channel_id=1, source_target_pairs={{0,2},{2,0},{4,6},{6,4},{8,10},{10,8},{12,14},{14,12},{16,18},{18,... | collective-permute-start | bytes 8650760 | tf_op jit(solution)/shard_map/ppermute | solution.py:74
  555.6 65.2 %collective-permute-start.42 = (bf16[512,2816]{1,0:T(8,128)(2,1)}, bf16[512,2816]{1,0:T(8,128)(2,1)}, u32[]{:S(2)}, u32[]{:S(2)}) collective-permute-start(bf16[512,2816]{1,0:T(8,128)(2,1)} %add_convert_fusion.2), channel_id=1, source_target_pairs={{0,4},{2,6},{4,0},{6,2},{8,12},{10,14},{12,8},{14,10},{16,20},{18,... | collective-permute-start | bytes 8650760 | tf_op jit(solution)/shard_map/ppermute | solution.py:77
  603.7 66.4 %collective-permute-start.45 = (bf16[512,2048]{1,0:T(8,128)(2,1)}, bf16[512,2048]{1,0:T(8,128)(2,1)}, u32[]{:S(2)}, u32[]{:S(2)}) collective-permute-start(bf16[512,2048]{1,0:T(8,128)(2,1)} %get-tuple-element.238), channel_id=1, source_target_pairs={{0,2},{2,0},{4,6},{6,4},{8,10},{10,8},{12,14},{14,12},{16,18},{18,... | collective-permute-start | bytes 6291464 | tf_op jit(solution)/shard_map/ppermute | solution.py:74
  613.3 28.9 %collective-permute-start.39 = (bf16[512,2048]{1,0:T(8,128)(2,1)}, bf16[512,2048]{1,0:T(8,128)(2,1)}, u32[]{:S(2)}, u32[]{:S(2)}) collective-permute-start(bf16[512,2048]{1,0:T(8,128)(2,1)} %convolution_convert_fusion.8), channel_id=1, source_target_pairs={{0,2},{2,0},{4,6},{6,4},{8,10},{10,8},{12,14},{14,12},{16,18},{18,... | collective-permute-start | bytes 6291464 | tf_op jit(solution)/shard_map/ppermute | solution.py:74
  622.9 47.5 %collective-permute-start.46 = (bf16[512,2048]{1,0:T(8,128)(2,1)}, bf16[512,2048]{1,0:T(8,128)(2,1)}, u32[]{:S(2)}, u32[]{:S(2)}) collective-permute-start(bf16[512,2048]{1,0:T(8,128)(2,1)} %add_convert_fusion.9), channel_id=1, source_target_pairs={{0,4},{2,6},{4,0},{6,2},{8,12},{10,14},{12,8},{14,10},{16,20},{18,... | collective-permute-start | bytes 6291464 | tf_op jit(solution)/shard_map/ppermute | solution.py:77
  631.5 143.0 %reduce-scatter.14.cloned.1.call-start = ((), (), s32[]{:S(2)}) async-start(), calls=%async_computation.16 | async-start | bytes 2621440 | tf_op jit(solution)/shard_map/reduce_scatter | solution.py:103
  676.0 138.4 %reduce-scatter.18.cloned.1.call-start = ((), (), s32[]{:S(2)}) async-start(), calls=%async_computation.18 | async-start | bytes 2621440 | tf_op jit(solution)/shard_map/reduce_scatter | solution.py:103
  676.9 47.8 %collective-permute-start.49 = (bf16[512,2048]{1,0:T(8,128)(2,1)}, bf16[512,2048]{1,0:T(8,128)(2,1)S(1)}, u32[]{:S(2)}, u32[]{:S(2)}) collective-permute-start(bf16[512,2048]{1,0:T(8,128)(2,1)} %add_convert_fusion.8), channel_id=1, source_target_pairs={{0,4},{2,6},{4,0},{6,2},{8,12},{10,14},{12,8},{14,10},{16,20},{18,... | collective-permute-start | bytes 6291464 | tf_op jit(solution)/shard_map/ppermute | solution.py:77
  728.7 104.7 %reduce-scatter.16.cloned.1.call-start = ((), (), s32[]{:S(2)}) async-start(), calls=%async_computation.17 | async-start | bytes 1310720 | tf_op jit(solution)/shard_map/reduce_scatter | solution.py:103
  741.2 30.4 %collective-permute-start.47 = (bf16[320,2048]{1,0:T(8,128)(2,1)S(1)}, bf16[320,2048]{1,0:T(8,128)(2,1)}, u32[]{:S(2)}, u32[]{:S(2)}) collective-permute-start(bf16[320,2048]{1,0:T(8,128)(2,1)S(1)} %copy-done.95), channel_id=1, source_target_pairs={{0,1},{1,0},{2,3},{3,2},{4,5},{5,4},{6,7},{7,6},{8,9},{9,8},{10,11... | collective-permute-start | bytes 3932168 | tf_op jit(solution)/shard_map/ppermute | solution.py:80
  748.0 37.3 %collective-permute-start.51 = (bf16[512,1024]{1,0:T(8,128)(2,1)}, bf16[512,1024]{1,0:T(8,128)(2,1)}, u32[]{:S(2)}, u32[]{:S(2)}) collective-permute-start(bf16[512,1024]{1,0:T(8,128)(2,1)} %convolution_convert_fusion.12), channel_id=1, source_target_pairs={{0,2},{2,0},{4,6},{6,4},{8,10},{10,8},{12,14},{14,12},{16,18},{18,... | collective-permute-start | bytes 3145736 | tf_op jit(solution)/shard_map/ppermute | solution.py:74
  749.4 44.3 %collective-permute-start.53 = (bf16[512,1024]{1,0:T(8,128)(2,1)}, bf16[512,1024]{1,0:T(8,128)(2,1)}, u32[]{:S(2)}, u32[]{:S(2)}) collective-permute-start(bf16[512,1024]{1,0:T(8,128)(2,1)} %add_convert_fusion.13), channel_id=1, source_target_pairs={{0,4},{2,6},{4,0},{6,2},{8,12},{10,14},{12,8},{14,10},{16,20},{18,... | collective-permute-start | bytes 3145736 | tf_op jit(solution)/shard_map/ppermute | solution.py:77
  774.5 70.2 %reduce-scatter.20.cloned.1.call-start = ((), (), s32[]{:S(2)}) async-start(), calls=%async_computation.19 | async-start | bytes 1310720 | tf_op jit(solution)/shard_map/reduce_scatter | solution.py:103
  783.7 33.3 %collective-permute-start.54 = (bf16[320,2048]{1,0:T(8,128)(2,1)}, bf16[320,2048]{1,0:T(8,128)(2,1)}, u32[]{:S(2)}, u32[]{:S(2)}) collective-permute-start(bf16[320,2048]{1,0:T(8,128)(2,1)} %fusion.14), channel_id=1, source_target_pairs={{0,1},{1,0},{2,3},{3,2},{4,5},{5,4},{6,7},{7,6},{8,9},{9,8},{10,11... | collective-permute-start | bytes 3932168 | tf_op jit(solution)/shard_map/ppermute | solution.py:80
  (127 other events, 1454.4 us)
Sparse Core Ops, SparseCore 0:
  20.8 32.3 all-gather.6
  55.4 45.0 all-gather.8
  102.6 44.6 all-gather.10
  148.7 57.8 all-gather.12
  208.1 57.8 all-gather.14
  267.4 57.8 all-gather.16
  489.2 54.0 reduce-scatter.7
  555.2 54.0 reduce-scatter.9
  631.6 53.2 reduce-scatter.11
  687.0 43.6 reduce-scatter.13
  733.1 43.3 reduce-scatter.17
  778.7 26.4 reduce-scatter.15
  811.8 26.0 reduce-scatter.19
